TPU v7x, 32 devices: a whole 2x2x4 slice. The times are simulated.
32 devices in a mesh: rep: 2 (over x), fsdp: 16 (over z, y, core).
Axes of the slice: x: 2, y: 2, z: 4, core: 2. Of those that a mesh axis runs over, the one named last changes fastest.
Arguments:
- tokens: bfloat16 [4, 1024, 2048], P('rep', 'fsdp'), may hold values from -6 to 6
- segment_ids: int32 [4, 1024], P('rep', 'fsdp'), may hold values from 0 to 1, never falling along the last dimension, each value on 1 to 768 neighbouring positions
- norm_gains: bfloat16 [2048, 2], P('fsdp'), may hold values from 0.5 to 1.5
- attn_weight: bfloat16 [2048, 4608], P('fsdp'), may hold values from -0.79549513 to 0.79549513
- adapter: bfloat16 [2048, 768], P('fsdp'), may hold values from -0.125 to 0.125
- ffn_weight: bfloat16 [16384, 3, 2048], P('fsdp'), may hold values from -0.125 to 0.125
- ffn_adapter: bfloat16 [16384, 256], P('fsdp'), may hold values from -0.046875 to 0.046875
- cotangent: bfloat16 [4, 1024, 2048], P('rep', 'fsdp'), may hold values from -6 to 6
Outputs:
- block_output: bfloat16 [4, 1024, 2048], P('rep', 'fsdp')
- input_grad: bfloat16 [4, 1024, 2048], P('rep', 'fsdp')
- gains_grad: float32 [2048, 2], P('fsdp')
- attn_grad: float32 [2048, 4608], P('fsdp')
- adapter_grad: float32 [2048, 768], P('fsdp')
- ffn_grad: float32 [16384, 3, 2048], P('fsdp')
- ffn_adapter_grad: float32 [16384, 256], P('fsdp')
Inputs may be any that keep to these rules, and one draw needn't show every extreme that they name: `segment_ids`: in each sequence the ids never fall and each id of 0 to 1 marks one document of 1 to 768 tokens.
All inputs are finite; a program needn't handle non-finite values.
Results may differ from a plain program's by a relative error of at most 0.019.
Values may be sent and summed in bfloat16 or wider, within the bound.
A program may use at most 448 MiB of HBM per device.

v0:
```python
import jax
import jax.numpy as jnp
from jax import lax
from jax.sharding import PartitionSpec as P

HEADS = 8
HD = 256
RANK = 256


epsilon = 1e-06


def rms_scale(values, gain_col):
    return (
        values * lax.rsqrt(jnp.mean(values * values, axis=-1, keepdims=True) + epsilon) * gain_col
    )


def angles_of(positions):
    inverse_freq = 10000.0 ** (-2.0 * jnp.arange(HD // 2, dtype=jnp.float32) / HD)
    return positions.astype(jnp.float32)[:, None] * inverse_freq[None, :]


def rotate(field_in, angles):
    half_dim = field_in.shape[-1] // 2
    cosine = jnp.cos(angles)
    sine_part = jnp.sin(angles)
    lower_half = field_in[..., :half_dim]
    upper_half = field_in[..., half_dim:]
    return jnp.concatenate(
        [
            lower_half * cosine - upper_half * sine_part,
            upper_half * cosine + lower_half * sine_part,
        ],
        axis=-1,
    )


def gelu_tanh(values):
    return jax.nn.gelu(values, approximate=True)


def contract(left_op, right_op, left_dim, right_dim):
    return lax.dot_general(
        left_op,
        right_op,
        (((left_dim,), (right_dim,)), ((), ())),
        preferred_element_type=jnp.float32,
    )


def local(
    tokens, segment_ids, norm_gains, attn_weight, adapter, ffn_weight, ffn_adapter, cotangent
):
    micro_count, local_len, model_dim = tokens.shape
    shards = lax.axis_size("fsdp")
    seq_len = local_len * shards
    offset = lax.axis_index("fsdp") * local_len
    q_width = HEADS * HD
    kv_end = q_width + 2 * HD
    score_scale = HD ** (-0.5)
    hidden_cols = ffn_weight.shape[0]
    attn_rows = attn_weight.shape[0]
    attn_cols = attn_weight.shape[1]
    seg_whole = lax.all_gather(segment_ids, "fsdp", axis=1, tiled=True)
    down_pair = jnp.concatenate([ffn_weight[:, 2, :], ffn_adapter], axis=1)
    gate_up = jnp.concatenate([ffn_weight[:, 0, :], ffn_weight[:, 1, :]], axis=0)
    key_index = jnp.arange(seq_len, dtype=jnp.int32)
    query_index = offset + jnp.arange(local_len, dtype=jnp.int32)

    def fetch_each():
        return (
            lax.all_gather(norm_gains, "fsdp", axis=0, tiled=True),
            lax.all_gather(attn_weight, "fsdp", axis=0, tiled=True),
            lax.all_gather(adapter, "fsdp", axis=0, tiled=True),
        )

    gain_acc = jnp.zeros((attn_rows, 2), jnp.float32)
    attn_acc = jnp.zeros((attn_rows, attn_cols), jnp.float32)
    adapt_acc = jnp.zeros((attn_rows, 3 * RANK), jnp.float32)
    ffn_acc = jnp.zeros((hidden_cols, 3, model_dim), jnp.float32)
    ffn_low_acc = jnp.zeros((hidden_cols, RANK), jnp.float32)
    block_out = []
    input_grads = []
    for micro_idx in range(micro_count):
        params = fetch_each()
        gain_full, attn_full, adapt_full = params
        gain_two = gain_full.astype(jnp.float32)
        hidden_in = tokens[micro_idx].astype(jnp.float32)
        seg_all = seg_whole[micro_idx]
        seg_mine = segment_ids[micro_idx]
        before = jnp.sum((seg_all[None, :] < seg_mine[:, None]).astype(jnp.int32), axis=1)
        angles = angles_of(query_index - before)
        normed, norm_back_one = jax.vjp(rms_scale, hidden_in, gain_two[:, 0])
        normed_low = normed.astype(jnp.bfloat16)
        projected = jnp.dot(normed_low, attn_full[:, :kv_end], preferred_element_type=jnp.float32)
        query_low = jnp.dot(
            normed_low, adapt_full[:, :RANK], preferred_element_type=jnp.float32
        ).astype(jnp.bfloat16)
        query_pre = projected[:, :q_width] + contract(
            query_low, adapt_full[:, RANK : 2 * RANK], 1, 1
        )
        queries = rotate(query_pre.reshape(local_len, HEADS, HD), angles[:, None, :]).astype(
            jnp.bfloat16
        )
        queries = queries.reshape(local_len * HEADS, HD)
        keys_low = rotate(projected[:, q_width : q_width + HD], angles).astype(jnp.bfloat16)
        values_low = projected[:, q_width + HD :].astype(jnp.bfloat16)
        kv_all = lax.all_gather(
            jnp.concatenate([keys_low, values_low], axis=1), "fsdp", axis=0, tiled=True
        )
        keys_all = kv_all[:, :HD]
        values_all = kv_all[:, HD:]
        allowed = (
            (seg_mine[:, None] == seg_all[None, :]) & (key_index[None, :] <= query_index[:, None])
        )[:, None, :]
        scores = (contract(queries, keys_all, 1, 1) * score_scale).reshape(
            local_len, HEADS, seq_len
        )
        scores = jnp.where(allowed, scores, -1e30)
        top_score = jnp.max(scores, axis=-1, keepdims=True)
        exp_scores = jnp.exp(scores - top_score)
        weights = exp_scores / jnp.sum(exp_scores, axis=-1, keepdims=True)
        weights_low = weights.astype(jnp.bfloat16).reshape(local_len * HEADS, seq_len)
        context = jnp.dot(weights_low, values_all, preferred_element_type=jnp.float32)
        context = context.reshape(local_len, q_width).astype(jnp.bfloat16)
        mixed_sum = hidden_in + contract(context, attn_full[:, kv_end:], 1, 1)
        normed_two, norm_back_two = jax.vjp(rms_scale, mixed_sum, gain_two[:, 1])
        inputs_all = lax.all_gather(normed_two.astype(jnp.bfloat16), "fsdp", axis=0, tiled=True)
        gate_pre = contract(inputs_all, ffn_weight[:, 0, :], 1, 1)
        up_pre = contract(inputs_all, ffn_weight[:, 1, :], 1, 1)
        activated, gelu_back = jax.vjp(gelu_tanh, gate_pre)
        hidden_act = (activated * up_pre).astype(jnp.bfloat16)
        down_mine = lax.psum_scatter(
            jnp.dot(hidden_act, down_pair, preferred_element_type=jnp.float32),
            "fsdp",
            scatter_dimension=0,
            tiled=True,
        )
        down_low = down_mine[:, model_dim:].astype(jnp.bfloat16)
        result = (
            mixed_sum
            + down_mine[:, :model_dim]
            + contract(down_low, adapt_full[:, 2 * RANK :], 1, 1)
        )
        block_out.append(result.astype(jnp.bfloat16))
        params_back = fetch_each()
        gain_back, attn_back, adapt_back = params_back
        cot_low = cotangent[micro_idx]
        cot_full = cot_low.astype(jnp.float32)
        low_grad = jnp.dot(
            cot_low, adapt_back[:, 2 * RANK :], preferred_element_type=jnp.float32
        ).astype(jnp.bfloat16)
        bd_grad = contract(cot_low, down_low, 0, 0)
        cot_all = lax.all_gather(
            jnp.concatenate([cot_low, low_grad], axis=1), "fsdp", axis=0, tiled=True
        )
        hidden_grad = contract(cot_all, down_pair, 1, 1)
        gate_grad = gelu_back(hidden_grad * up_pre)[0].astype(jnp.bfloat16)
        up_grad = (hidden_grad * activated).astype(jnp.bfloat16)
        pair_grad = jnp.concatenate([gate_grad, up_grad], axis=1)
        ffn_acc = ffn_acc + jnp.stack(
            [
                contract(gate_grad, inputs_all, 0, 0),
                contract(up_grad, inputs_all, 0, 0),
                contract(hidden_act, cot_all[:, :model_dim], 0, 0),
            ],
            axis=1,
        )
        ffn_low_acc = ffn_low_acc + contract(hidden_act, cot_all[:, model_dim:], 0, 0)
        normed_two_grad = lax.psum_scatter(
            jnp.dot(pair_grad, gate_up, preferred_element_type=jnp.float32),
            "fsdp",
            scatter_dimension=0,
            tiled=True,
        )
        mixed_part, gain_two_grad = norm_back_two(normed_two_grad)
        mixed_grad = cot_full + mixed_part
        out_grad_low = mixed_grad.astype(jnp.bfloat16)
        wout_grad = contract(out_grad_low, context, 0, 0)
        context_grad = jnp.dot(
            out_grad_low, attn_back[:, kv_end:], preferred_element_type=jnp.float32
        )
        context_rows = context_grad.astype(jnp.bfloat16).reshape(local_len * HEADS, HD)
        prob_grad = contract(context_rows, values_all, 1, 1).reshape(local_len, HEADS, seq_len)
        score_grad = weights * (prob_grad - jnp.sum(weights * prob_grad, axis=-1, keepdims=True))
        score_grad = score_grad.astype(jnp.bfloat16).reshape(local_len * HEADS, seq_len)
        query_grad = jnp.dot(score_grad, keys_all, preferred_element_type=jnp.float32) * score_scale
        query_grad = query_grad.reshape(local_len, HEADS, HD)
        kv_grad = lax.psum_scatter(
            jnp.concatenate(
                [
                    contract(score_grad, queries, 0, 0) * score_scale,
                    contract(weights_low, context_rows, 0, 0),
                ],
                axis=1,
            ),
            "fsdp",
            scatter_dimension=0,
            tiled=True,
        )
        query_pre_grad = (
            rotate(query_grad, -angles[:, None, :]).reshape(local_len, q_width).astype(jnp.bfloat16)
        )
        key_grad = rotate(kv_grad[:, :HD], -angles).astype(jnp.bfloat16)
        value_grad = kv_grad[:, HD:].astype(jnp.bfloat16)
        rank_grad = jnp.dot(
            query_pre_grad, adapt_back[:, RANK : 2 * RANK], preferred_element_type=jnp.float32
        )
        rank_grad = rank_grad.astype(jnp.bfloat16)
        proj_grad = jnp.concatenate([query_pre_grad, key_grad, value_grad], axis=1)
        normed_grad = contract(proj_grad, attn_back[:, :kv_end], 1, 1) + contract(
            rank_grad, adapt_back[:, :RANK], 1, 1
        )
        hidden_part, gain_one_grad = norm_back_one(normed_grad)
        input_grads.append((mixed_grad + hidden_part).astype(jnp.bfloat16))
        attn_now = jnp.concatenate([contract(normed_low, proj_grad, 0, 0), wout_grad], axis=1)
        adapt_now = jnp.concatenate(
            [
                contract(normed_low, rank_grad, 0, 0),
                contract(query_pre_grad, query_low, 0, 0),
                bd_grad,
            ],
            axis=1,
        )
        gain_now = jnp.stack([gain_one_grad, gain_two_grad], axis=1)
        gain_part, attn_part, adapt_part = (
            lax.psum_scatter(gain_now, "fsdp", scatter_dimension=0, tiled=True),
            lax.psum_scatter(attn_now, "fsdp", scatter_dimension=0, tiled=True),
            lax.psum_scatter(adapt_now, "fsdp", scatter_dimension=0, tiled=True),
        )
        gain_acc = gain_acc + gain_part
        attn_acc = attn_acc + attn_part
        adapt_acc = adapt_acc + adapt_part
    totals = (
        lax.psum(gain_acc.astype(jnp.bfloat16), "rep").astype(jnp.float32),
        lax.psum(attn_acc.astype(jnp.bfloat16), "rep").astype(jnp.float32),
        lax.psum(adapt_acc.astype(jnp.bfloat16), "rep").astype(jnp.float32),
        lax.psum(ffn_acc.astype(jnp.bfloat16), "rep").astype(jnp.float32),
        lax.psum(ffn_low_acc.astype(jnp.bfloat16), "rep").astype(jnp.float32),
    )
    return (
        jnp.stack(block_out),
        jnp.stack(input_grads),
        totals[0],
        totals[1],
        totals[2],
        totals[3],
        totals[4],
    )


def solution(mesh):
    placed = (
        P("rep", "fsdp", None),
        P("rep", "fsdp"),
        P("fsdp", None),
        P("fsdp", None),
        P("fsdp", None),
        P("fsdp", None, None),
        P("fsdp", None),
        P("rep", "fsdp", None),
    )
    return jax.shard_map(
        local,
        mesh=mesh,
        in_specs=placed,
        out_specs=(
            P("rep", "fsdp", None),
            P("rep", "fsdp", None),
            P("fsdp", None),
            P("fsdp", None),
            P("fsdp", None),
            P("fsdp", None, None),
            P("fsdp", None),
        ),
        check_vma=False,
    )
```

profile of v0, /device:TPU:0, one launch (start us, length us, event | category | flops | bytes accessed | tf_op | source)
XLA Modules:
  0.0 1928.2 jit_solution(1377653447556384146)
XLA Ops:
  8.7 23.7 %all-gather = s32[16,64,2]{1,2,0:T(2,128)S(1)} all-gather(s32[1,64,2]{1,2,0:T(2,128)} %bitcast.272), channel_id=1, replica_groups=mesh['rep'=2,'fsdp'=16] {'fsdp'}, dimensions={0}, use_global_device_ids=true | all-gather | bytes 8704 | tf_op jit(solution)/shard_map/all_gather | solution.py:66
  32.5 18.2 all_gather.38
  53.2 58.1 %all-gather.10.cloned.1.call-done = bf16[2048,4608]{1,0:T(8,128)(2,1)} async-done(((bf16[128,4608]{1,0:T(8,128)(2,1)}), bf16[2048,4608]{1,0:T(8,128)(2,1)}) %all-gather.10.cloned.1.call-update) | async-done | bytes 18874384 | tf_op jit(solution)/shard_map/all_gather | solution.py:75
  111.3 6.1 fusion.7
  117.5 6.1 fusion.5
  126.3 32.8 %all-gather.12.cloned.1.call-done = bf16[2048,768]{1,0:T(8,128)(2,1)} async-done(((bf16[128,768]{1,0:T(8,128)(2,1)}), bf16[2048,768]{1,0:T(8,128)(2,1)}) %all-gather.12.cloned.1.call-update) | async-done | bytes 3145744 | tf_op jit(solution)/shard_map/all_gather | solution.py:76
  165.2 32.9 %all-gather.14.cloned.1.call-done = bf16[1024,512]{1,0:T(8,128)(2,1)} async-done(((bf16[64,512]{1,0:T(8,128)(2,1)}), bf16[1024,512]{1,0:T(8,128)(2,1)}) %all-gather.14.cloned.1.call-update) | async-done | bytes 1048592 | tf_op jit(solution)/shard_map/all_gather | solution.py:110
  202.9 6.2 multiply_reduce_fusion.7
  211.0 9.0 slice_bitcast_fusion.2
  220.0 32.9 %all-gather.22.cloned.1.call-done = bf16[1024,2304]{1,0:T(8,128)(2,1)} async-done(((bf16[64,2304]{1,0:T(8,128)(2,1)}), bf16[1024,2304]{1,0:T(8,128)(2,1)}) %all-gather.22.cloned.1.call-update) | async-done | bytes 4718608 | tf_op jit(solution)/shard_map/all_gather | solution.py:156
  252.9 9.7 fusion.164
  264.2 40.3 %all-gather.16.cloned.1.call-done = bf16[1024,2048]{1,0:T(8,128)(2,1)} async-done(((bf16[64,2048]{1,0:T(8,128)(2,1)}), bf16[1024,2048]{1,0:T(8,128)(2,1)}) %all-gather.16.cloned.1.call-update) | async-done | bytes 4194320 | tf_op jit(solution)/shard_map/all_gather | solution.py:130
  304.4 8.0 fusion.180
  312.5 11.8 fusion.25
  326.2 11.5 fusion.10
  351.8 7.7 multiply_reduce_fusion.6
  360.1 89.9 %reduce-scatter.16.cloned.1.call-done = f32[64,2048]{1,0:T(8,128)} async-done(((f32[1024,2048]{1,0:T(8,128)}), f32[64,2048]{1,0:T(8,128)}) %reduce-scatter.16.cloned.1.call-update) | async-done | bytes 524304 | tf_op jit(solution)/shard_map/reduce_scatter | solution.py:172
  450.0 2.7 multiply_reduce_fusion.3
  452.8 52.9 %all-gather.24.cloned.1.call-done = bf16[1024,2304]{1,0:T(8,128)(2,1)} async-done(((bf16[64,2304]{1,0:T(8,128)(2,1)}), bf16[1024,2304]{1,0:T(8,128)(2,1)}) %all-gather.24.cloned.1.call-update) | async-done | bytes 4718608 | tf_op jit(solution)/shard_map/all_gather | solution.py:156
  505.6 9.7 fusion.163
  515.3 41.5 %all-gather.20.cloned.1.call-done = bf16[1024,2048]{1,0:T(8,128)(2,1)} async-done(((bf16[64,2048]{1,0:T(8,128)(2,1)}), bf16[1024,2048]{1,0:T(8,128)(2,1)}) %all-gather.20.cloned.1.call-update) | async-done | bytes 4194320 | tf_op jit(solution)/shard_map/all_gather | solution.py:130
  556.8 8.1 fusion.179
  564.9 11.8 fusion.32
  578.8 11.5 fusion.9
  591.3 10.1 fusion.166
  601.5 10.6 fusion.165
  615.5 76.9 %reduce-scatter.20.cloned.1.call-done = f32[64,2048]{1,0:T(8,128)} async-done(((f32[1024,2048]{1,0:T(8,128)}), f32[64,2048]{1,0:T(8,128)}) %reduce-scatter.20.cloned.1.call-update) | async-done | bytes 524304 | tf_op jit(solution)/shard_map/reduce_scatter | solution.py:172
  694.2 2.4 fusion.94
  697.4 5.7 fusion.49
  705.8 2.1 multiply_reduce_fusion.1
  712.2 95.3 %reduce-scatter.12.cloned.1.call-done = f32[64,2304]{1,0:T(8,128)} async-done(((f32[1024,2304]{1,0:T(8,128)}), f32[64,2304]{1,0:T(8,128)}) %reduce-scatter.12.cloned.1.call-update) | async-done | bytes 589840 | tf_op jit(solution)/shard_map/reduce_scatter | solution.py:135
  807.4 2.6 convolution_bitcast_fusion.7
  810.0 5.1 fusion.52
  817.0 2.0 multiply_reduce_fusion
  822.7 2.1 fusion.71
  825.1 2.0 fusion.70
  835.2 87.6 %reduce-scatter.14.cloned.1.call-done = f32[64,2304]{1,0:T(8,128)} async-done(((f32[1024,2304]{1,0:T(8,128)}), f32[64,2304]{1,0:T(8,128)}) %reduce-scatter.14.cloned.1.call-update) | async-done | bytes 589840 | tf_op jit(solution)/shard_map/reduce_scatter | solution.py:135
  924.3 6.6 maximum_add_fusion.2
  931.2 9.6 fusion.137
  940.8 8.1 fusion.140
  948.9 39.1 %reduce-scatter.18.cloned.1.call-done = f32[64,512]{1,0:T(8,128)} async-done(((f32[1024,512]{1,0:T(8,128)}), f32[64,512]{1,0:T(8,128)}) %reduce-scatter.18.cloned.1.call-update) | async-done | bytes 131088 | tf_op jit(solution)/shard_map/reduce_scatter | solution.py:191
  988.9 63.5 %reduce-scatter.22.cloned.1.call-done = f32[64,512]{1,0:T(8,128)} async-done(((f32[1024,512]{1,0:T(8,128)}), f32[64,512]{1,0:T(8,128)}) %reduce-scatter.22.cloned.1.call-update) | async-done | bytes 131088 | tf_op jit(solution)/shard_map/reduce_scatter | solution.py:191
  1054.4 4.0 fusion.144
  1058.5 9.8 fusion.143
  1068.3 31.7 %maximum_add_fusion = f32[2048,4608]{1,0:T(8,128)} fusion(f32[2048,2048]{1,0:T(8,128)} %fusion.140, f32[2048,2560]{1,0:T(8,128)S(1)} %fusion.144, f32[2048,2048]{1,0:T(8,128)} %fusion.137, f32[2048,2560]{1,0:T(8,128)} %fusion.143), kind=kLoop, calls=%fused_computation | loop fusion | flops 28311552 | bytes 113246208 | tf_op jit(solution)/shard_map/add | solution.py:234
  1100.5 3.5 fusion.105
  1104.0 6.5 convolution_bitcast_fusion.3
  1110.5 4.5 convolution_bitcast_fusion.5
  1115.1 6.4 convolution_bitcast_fusion.4
  1121.6 6.8 convolution_bitcast_fusion
  1128.4 10.7 convolution_bitcast_fusion.2
  1139.1 6.9 convolution_bitcast_fusion.1
  1146.0 17.5 fusion
  1163.5 7.9 fusion.1
  1171.8 8.1 fusion.3
  1183.0 4.2 fusion.69
  1188.9 319.0 %reduce-scatter.24.cloned.1.call-done = f32[128,4608]{1,0:T(8,128)} async-done(((f32[2048,4608]{1,0:T(8,128)}), f32[128,4608]{1,0:T(8,128)}) %reduce-scatter.24.cloned.1.call-update) | async-done | bytes 2359312 | tf_op jit(solution)/shard_map/reduce_scatter | solution.py:230
  1508.0 2.8 convert_element_type.239
  1516.5 52.3 %reduce-scatter.28.cloned.1.call-done = f32[128,2]{1,0:T(8,128)} async-done(((f32[2048,2]{1,0:T(8,128)}), f32[128,2]{1,0:T(8,128)}) %reduce-scatter.28.cloned.1.call-update) | async-done | bytes 1040
  1569.7 4.9 psum.35
  1575.2 324.8 %all-reduce.3.cloned.1.call-done = (bf16[128,768]{0,1:T(8,128)(2,1)}, bf16[128,4608]{1,0:T(8,128)(2,1)}, bf16[1024,3,2048]{2,0,1:T(8,128)(2,1)}, bf16[1024,256]{1,0:T(8,128)(2,1)}) async-done(((bf16[128,768]{0,1:T(8,128)(2,1)}, bf16[128,4608]{1,0:T(8,128)(2,1)}, bf16[1024,3,2048]{2,0,1:T(8,128)(2,1)}, bf16[1024,256]{1,0:T(8,128)(2,1)}), (bf16[128,768]{0,1:T(8,128)(2,1)}, bf16[128,4608]{1,0:T(8,128)(2,1)}, ...) | async-done | bytes 14483472 | tf_op jit(solution)/shard_map/psum | solution.py:239
  1901.7 2.1 convert_element_type.246
  1903.8 2.9 convert_element_type.240
  1906.7 14.4 convert_element_type.244
  (355 shorter events, 86.2 us)
Async XLA Ops:
  7.2 104.1 %all-gather.10.cloned.1.call-start = ((), (), s32[]{:S(2)}) async-start(), calls=%async_computation.9 | async-start | bytes 20054016 | tf_op jit(solution)/shard_map/all_gather | solution.py:75
  7.9 151.2 %all-gather.12.cloned.1.call-start = ((), (), s32[]{:S(2)}) async-start(), calls=%async_computation.10 | async-start | bytes 3342336 | tf_op jit(solution)/shard_map/all_gather | solution.py:76
  8.6 189.4 %all-gather.14.cloned.1.call-start = ((), (), s32[]{:S(2)}) async-start(), calls=%async_computation.11 | async-start | bytes 1114112 | tf_op jit(solution)/shard_map/all_gather | solution.py:110
  50.7 72.9 %copy-start.84 = (f32[128]{0:T(128)}, f32[128]{0:T(128)S(1)}, u32[]{:S(2)}) copy-start(f32[128]{0:T(128)S(1)} %multiply_power_fusion) | copy-start | bytes 1540
  53.1 64.3 %copy-start.85 = (f32[64]{0:T(128)}, f32[64]{0:T(128)S(1)}, u32[]{:S(2)}) copy-start(f32[64]{0:T(128)S(1)} %get-tuple-element.38) | copy-start | bytes 772
  53.1 64.3 %copy-start.87 = (f32[64]{0:T(128)}, f32[64]{0:T(128)S(1)}, u32[]{:S(2)}) copy-start(f32[64]{0:T(128)S(1)} %get-tuple-element.39) | copy-start | bytes 772
  53.1 64.3 %copy-start.78 = (f32[64]{0:T(128)}, f32[64]{0:T(128)S(1)}, u32[]{:S(2)}) copy-start(f32[64]{0:T(128)S(1)} %get-tuple-element.120) | copy-start | bytes 772
  53.1 108.5 %copy-start.76 = (f32[64]{0:T(128)}, f32[64]{0:T(128)S(1)}, u32[]{:S(2)}) copy-start(f32[64]{0:T(128)S(1)} %get-tuple-element.119) | copy-start | bytes 772
  53.1 70.5 %copy-start.80 = (f32[64]{0:T(128)}, f32[64]{0:T(128)S(1)}, u32[]{:S(2)}) copy-start(f32[64]{0:T(128)S(1)} %get-tuple-element.117) | copy-start | bytes 772
  53.1 70.5 %copy-start.81 = (f32[64]{0:T(128)}, f32[64]{0:T(128)S(1)}, u32[]{:S(2)}) copy-start(f32[64]{0:T(128)S(1)} %get-tuple-element.118) | copy-start | bytes 772
  117.5 8.1 copy-start.15
  125.5 127.4 %all-gather.22.cloned.1.call-start = ((), (), s32[]{:S(2)}) async-start(), calls=%async_computation.17 | async-start | bytes 5013504 | tf_op jit(solution)/shard_map/all_gather | solution.py:156
  161.4 143.1 %all-gather.16.cloned.1.call-start = ((), (), s32[]{:S(2)}) async-start(), calls=%async_computation.12 | async-start | bytes 4456448 | tf_op jit(solution)/shard_map/all_gather | solution.py:130
  163.2 37.4 %copy-start.37 = (bf16[64,256]{1,0:T(8,128)(2,1)}, bf16[64,256]{1,0:T(8,128)(2,1)S(1)}, u32[]{:S(2)}) copy-start(bf16[64,256]{1,0:T(8,128)(2,1)S(1)} %convolution_convert_fusion.7) | copy-start | bytes 98308
  165.1 35.4 %copy-start.45 = (bf16[64,8,128]{2,1,0:T(8,128)(2,1)}, bf16[64,8,128]{2,1,0:T(8,128)(2,1)S(1)}, u32[]{:S(2)}) copy-start(bf16[64,8,128]{2,1,0:T(8,128)(2,1)S(1)} %get-tuple-element.61) | copy-start | bytes 393220
  165.2 35.4 %copy-start.47 = (bf16[64,8,128]{2,1,0:T(8,128)(2,1)}, bf16[64,8,128]{2,1,0:T(8,128)(2,1)S(1)}, u32[]{:S(2)}) copy-start(bf16[64,8,128]{2,1,0:T(8,128)(2,1)S(1)} %get-tuple-element.62) | copy-start | bytes 393220
  209.1 485.1 %copy-start.8 = (f32[64,2048]{1,0:T(8,128)}, f32[64,2048]{1,0:T(8,128)S(1)}, u32[]{:S(2)}) copy-start(f32[64,2048]{1,0:T(8,128)S(1)} %get-tuple-element.109) | copy-start | bytes 1572868
  209.7 10.3 copy-start.82
  210.5 134.3 %all-gather.18.cloned.1.call-start = ((), (), s32[]{:S(2)}) async-start(), calls=%async_computation.14 | async-start | bytes 1114112 | tf_op jit(solution)/shard_map/all_gather | solution.py:110
  252.9 10.6 copy-start.62
  252.9 10.6 copy-start.63
  264.1 185.9 %reduce-scatter.16.cloned.1.call-start = ((), (), s32[]{:S(2)}) async-start(), calls=%async_computation.18 | async-start | bytes 8912896 | tf_op jit(solution)/shard_map/reduce_scatter | solution.py:172
  304.4 8.0 copy-start.89
  312.5 13.8 copy-start.20
  312.5 13.8 copy-start.22
  337.8 167.9 %all-gather.24.cloned.1.call-start = ((), (), s32[]{:S(2)}) async-start(), calls=%async_computation.20 | async-start | bytes 5013504 | tf_op jit(solution)/shard_map/all_gather | solution.py:156
  340.2 216.6 %all-gather.20.cloned.1.call-start = ((), (), s32[]{:S(2)}) async-start(), calls=%async_computation.15 | async-start | bytes 4456448 | tf_op jit(solution)/shard_map/all_gather | solution.py:130
  351.8 7.7 copy-start.31
  452.7 239.7 %reduce-scatter.20.cloned.1.call-start = ((), (), s32[]{:S(2)}) async-start(), calls=%async_computation.21 | async-start | bytes 8912896 | tf_op jit(solution)/shard_map/reduce_scatter | solution.py:172
  556.8 8.1 copy-start.91
  564.9 13.9 copy-start.21
  564.9 13.9 copy-start.23
  590.3 217.1 %reduce-scatter.12.cloned.1.call-start = ((), (), s32[]{:S(2)}) async-start(), calls=%async_computation.13 | async-start | bytes 10027008 | tf_op jit(solution)/shard_map/reduce_scatter | solution.py:135
  601.4 321.4 %reduce-scatter.14.cloned.1.call-start = ((), (), s32[]{:S(2)}) async-start(), calls=%async_computation.16 | async-start | bytes 10027008 | tf_op jit(solution)/shard_map/reduce_scatter | solution.py:135
  612.0 80.4 %copy-start.9 = (f32[64,2048]{1,0:T(8,128)S(1)}, f32[64,2048]{1,0:T(8,128)}, u32[]{:S(2)}) copy-start(f32[64,2048]{1,0:T(8,128)} %get-tuple-element.111) | copy-start | bytes 1572868
  612.1 82.2 %copy-start.100 = (f32[64]{0:T(128)S(1)}, f32[64]{0:T(128)}, u32[]{:S(2)}) copy-start(f32[64]{0:T(128)} %copy-done.99) | copy-start | bytes 772
  612.1 82.2 %copy-start.83 = (f32[64]{0:T(128)S(1)}, f32[64]{0:T(128)}, u32[]{:S(2)}) copy-start(f32[64]{0:T(128)} %copy-done.82) | copy-start | bytes 772
  612.1 375.9 %reduce-scatter.18.cloned.1.call-start = ((), (), s32[]{:S(2)}) async-start(), calls=%async_computation.19 | async-start | bytes 2228224 | tf_op jit(solution)/shard_map/reduce_scatter | solution.py:191
  697.4 7.9 copy-start.18
  710.3 97.1 %copy-start.16 = (bf16[2,64,2048]{2,1,0:T(8,128)(2,1)S(1)}, bf16[2,64,2048]{2,1,0:T(8,128)(2,1)}, u32[]{:S(2)}) copy-start(bf16[2,64,2048]{2,1,0:T(8,128)(2,1)} %param.15) | copy-start | bytes 1572868
  710.3 99.7 %copy-start.13 = (f32[64,2048]{1,0:T(8,128)S(1)}, f32[64,2048]{1,0:T(8,128)}, u32[]{:S(2)}) copy-start(f32[64,2048]{1,0:T(8,128)} %get-tuple-element.68) | copy-start | bytes 1572868
  711.9 340.5 %reduce-scatter.22.cloned.1.call-start = ((), (), s32[]{:S(2)}) async-start(), calls=%async_computation.22 | async-start | bytes 2228224 | tf_op jit(solution)/shard_map/reduce_scatter | solution.py:191
  810.0 7.0 copy-start.1
  810.0 7.0 copy-start.41
  810.0 7.0 copy-start.42
  822.7 364.5 %reduce-scatter.26.cloned.1.call-start = ((), (), s32[]{:S(2)}) async-start(), calls=%async_computation.24 | async-start | bytes 6684672 | tf_op jit(solution)/shard_map/reduce_scatter | solution.py:231
  930.9 577.1 %reduce-scatter.24.cloned.1.call-start = ((), (), s32[]{:S(2)}) async-start(), calls=%async_computation.23 | async-start | bytes 40108032 | tf_op jit(solution)/shard_map/reduce_scatter | solution.py:230
  931.2 9.7 copy-start.11
  931.2 9.6 copy-start.30
  1100.0 468.7 %reduce-scatter.28.cloned.1.call-start = ((), (), s32[]{:S(2)}) async-start(), calls=%async_computation.25 | async-start | bytes 1114112
  1104.0 6.5 copy-start.90
  1104.0 6.5 copy-start.105
  1110.5 11.0 slice-start
  1128.3 10.7 copy-start.92
  1128.4 10.7 copy-start.107
  1146.0 17.5 copy-start.26
  1146.0 17.5 copy-start.59
  1146.0 17.5 copy-start.61
  1171.8 8.2 copy-start.27
  1171.8 8.2 copy-start.6
  1171.8 8.2 copy-start.65
  1171.8 9.7 copy-start.66
  1171.8 9.7 copy-start.67
  1182.9 717.0 %all-reduce.3.cloned.1.call-start = ((), (), s32[]{:S(2)}) async-start(), calls=%async_computation.26 | async-start | bytes 28966912 | tf_op jit(solution)/shard_map/psum | solution.py:239
  (65 other events, 205.0 us)
Sparse Core Ops, SparseCore 0:
  9.6 101.6 all-gather.9
  113.6 45.4 all-gather.11
  161.8 36.1 all-gather.13
  200.8 52.0 all-gather.21
  255.5 48.9 all-gather.15
  306.5 36.3 all-gather.17
  347.5 102.4 reduce-scatter.15
  452.8 52.7 all-gather.23
  507.8 48.9 all-gather.19
  590.4 101.9 reduce-scatter.19
  696.5 110.8 reduce-scatter.11
  811.9 110.8 reduce-scatter.13
  926.6 61.4 reduce-scatter.17
  991.6 60.7 reduce-scatter.21
  1056.2 83.9 reduce-scatter.25
  1144.2 363.6 reduce-scatter.23
  1512.0 56.7 reduce-scatter.27
  1571.9 328.0 all-reduce.2
where the time goes:
time: 1940 us; the launch traced here: 1930 us
  waiting for transfers between devices  1440 us (74%)
  matrix products  281 us (14%)
  other arithmetic  106 us (5%)
  blocking collectives  46.8 us (2%)
  local copies, waits for them, and re-layouts  35.4 us (2%)
    psum x1, waiting for transfers between devices, local(): lax.psum(adapt_acc.astype(jnp.bfloat16), 'rep').astype(jnp.float32)  325 us
    reduce_scatter x1, waiting for transfers between devices, local(): lax.psum_scatter(attn_now, 'fsdp', scatter_dimension=0, tiled=True)  319 us
    dot_general x42, matrix products, contract(): lax.dot_general(left_op, right_op, (((left_dim,), (right_dim,)), ((), ())...  201 us
    reduce_scatter x2, waiting for transfers between devices, local(): lax.psum_scatter(jnp.dot(hidden_act, down_pair, preferred_element_type=jn...  183 us
    reduce_scatter x2, waiting for transfers between devices, local(): lax.psum_scatter(jnp.dot(pair_grad, gate_up, preferred_element_type=jnp.f...  167 us
    reduce_scatter x2, waiting for transfers between devices, local(): lax.psum_scatter(jnp.concatenate([contract(score_grad, queries, 0, 0) * s...  103 us
    all_gather x2, waiting for transfers between devices, local(): lax.all_gather(jnp.concatenate([cot_low, low_grad], axis=1), 'fsdp', axis...  85.8 us
    all_gather x2, waiting for transfers between devices, local(): lax.all_gather(normed_two.astype(jnp.bfloat16), 'fsdp', axis=0, tiled=True)  81.7 us
  transfers between devices with their start and end apart: 18, of which 16 were waited for; matrix products, arithmetic and copies ran while one was open for 19% of the time, Pallas kernels for 0%

commit v1 on v0

v1 whole, which is shorter than its diff:
```python
import jax
import jax.numpy as jnp
from jax import lax
from jax.sharding import PartitionSpec as P

HEADS = 8
HD = 256
RANK = 256
CHUNKS = 4


epsilon = 1e-06


def rms_scale(values, gain_col):
    return (
        values * lax.rsqrt(jnp.mean(values * values, axis=-1, keepdims=True) + epsilon) * gain_col
    )


def angles_of(positions):
    inverse_freq = 10000.0 ** (-2.0 * jnp.arange(HD // 2, dtype=jnp.float32) / HD)
    return positions.astype(jnp.float32)[..., None] * inverse_freq


def rotate(field_in, angles):
    half_dim = field_in.shape[-1] // 2
    cosine = jnp.cos(angles)
    sine_part = jnp.sin(angles)
    lower_half = field_in[..., :half_dim]
    upper_half = field_in[..., half_dim:]
    return jnp.concatenate(
        [
            lower_half * cosine - upper_half * sine_part,
            upper_half * cosine + lower_half * sine_part,
        ],
        axis=-1,
    )


def gelu_tanh(values):
    return jax.nn.gelu(values, approximate=True)


def contract(left_op, right_op, left_dim, right_dim):
    return lax.dot_general(
        left_op,
        right_op,
        (((left_dim,), (right_dim,)), ((), ())),
        preferred_element_type=jnp.float32,
    )


def batched(left_op, right_op, left_dim, right_dim):
    return lax.dot_general(
        left_op,
        right_op,
        (((left_dim,), (right_dim,)), ((0,), (0,))),
        preferred_element_type=jnp.float32,
    )


def low(values):
    return values.astype(jnp.bfloat16)


def gather_rows(values):
    return lax.all_gather(values, "fsdp", axis=values.ndim - 2, tiled=True)


def sum_rows(values):
    return lax.psum_scatter(values, "fsdp", scatter_dimension=1, tiled=True)


def swap_rep(values):
    return lax.ppermute(values, "rep", [(0, 1), (1, 0)])


def local(
    tokens, segment_ids, norm_gains, attn_weight, adapter, ffn_weight, ffn_adapter, cotangent
):
    micro, local_len, model_dim = tokens.shape
    shards = lax.axis_size("fsdp")
    me = lax.axis_index("fsdp")
    seq_len = local_len * shards
    offset = me * local_len
    count = micro * local_len
    every = micro * seq_len
    q_width = HEADS * HD
    kv_end = q_width + 2 * HD
    score_scale = HD ** (-0.5)
    hidden_cols = ffn_weight.shape[0]
    attn_rows = attn_weight.shape[0]

    seg_cols = count // attn_rows
    seg_block = low(segment_ids).reshape(attn_rows, seg_cols)
    spare = jnp.zeros((attn_rows, 128 - 2 - seg_cols), jnp.bfloat16)
    first = gather_rows(
        jnp.concatenate(
            [
                attn_weight[:, :kv_end],
                adapter[:, : 2 * RANK],
                norm_gains,
                seg_block,
                spare,
            ],
            axis=1,
        )
    )
    second = gather_rows(jnp.concatenate([attn_weight[:, kv_end:], adapter[:, 2 * RANK :]], axis=1))
    extra = kv_end + 2 * RANK
    w_proj = first[:, :kv_end]
    a_q = first[:, kv_end : kv_end + RANK]
    bq_t = first[:, kv_end + RANK : extra]
    gain_two = first[:, extra : extra + 2].astype(jnp.float32)
    seg_all = first[:, extra + 2 : extra + 2 + seg_cols].reshape(shards, micro, local_len)
    seg_all = seg_all.transpose(1, 0, 2).reshape(micro, seq_len).astype(jnp.int32)
    w_out = second[:, :q_width]
    bd_t = second[:, q_width:]
    cot_all = gather_rows(cotangent).reshape(every, model_dim)

    hidden_in = tokens.reshape(count, model_dim).astype(jnp.float32)
    key_index = jnp.arange(seq_len, dtype=jnp.int32)
    query_index = offset + jnp.arange(local_len, dtype=jnp.int32)
    before = jnp.sum(
        (seg_all[:, None, :] < segment_ids[:, :, None]).astype(jnp.int32), axis=2
    )
    angles = angles_of(query_index[None, :] - before).reshape(count, HD // 2)
    normed, norm_back_one = jax.vjp(rms_scale, hidden_in, gain_two[:, 0])
    normed_low = low(normed)
    normed_cols = lax.all_to_all(
        normed_low.reshape(micro, local_len, model_dim), "fsdp", 2, 1, tiled=True
    ).reshape(every, attn_rows)
    projected = contract(normed_low, w_proj, 1, 0)
    query_low = low(contract(normed_low, a_q, 1, 0))
    query_pre = projected[:, :q_width] + contract(query_low, bq_t, 1, 1)
    queries = low(rotate(query_pre.reshape(count, HEADS, HD), angles[:, None, :]))
    queries = queries.reshape(micro, local_len * HEADS, HD)
    keys_low = low(rotate(projected[:, q_width : q_width + HD], angles))
    values_low = low(projected[:, q_width + HD :])
    kv_all = gather_rows(
        jnp.concatenate([keys_low, values_low], axis=1).reshape(micro, local_len, 2 * HD)
    )
    keys_all = kv_all[..., :HD]
    values_all = kv_all[..., HD:]
    allowed = (
        (segment_ids[:, :, None] == seg_all[:, None, :])
        & (key_index[None, None, :] <= query_index[None, :, None])
    )[:, :, None, :]
    scores = (batched(queries, keys_all, 2, 2) * score_scale).reshape(
        micro, local_len, HEADS, seq_len
    )
    scores = jnp.where(allowed, scores, -1e30)
    top_score = jnp.max(scores, axis=-1, keepdims=True)
    exp_scores = jnp.exp(scores - top_score)
    weights = exp_scores / jnp.sum(exp_scores, axis=-1, keepdims=True)
    weights_low = low(weights).reshape(micro, local_len * HEADS, seq_len)
    context = low(batched(weights_low, values_all, 2, 1)).reshape(count, q_width)
    mixed_sum = hidden_in + contract(context, w_out, 1, 1)
    normed_two, norm_back_two = jax.vjp(rms_scale, mixed_sum, gain_two[:, 1])
    inputs_all = gather_rows(low(normed_two).reshape(micro, local_len, model_dim))
    inputs_all = inputs_all.reshape(every, model_dim)
    kept_all = gather_rows(
        jnp.concatenate([context, query_low], axis=1).reshape(micro, local_len, q_width + RANK)
    ).reshape(every, q_width + RANK)
    low_grad_all = low(contract(cot_all, bd_t, 1, 0))

    step = hidden_cols // CHUNKS
    hidden_parts, gate_parts, up_parts, ffn_parts, low_parts = [], [], [], [], []
    for at in range(CHUNKS):
        units = slice(at * step, (at + 1) * step)
        w_gate, w_up, w_down = (ffn_weight[units, j, :] for j in range(3))
        gate_pre = contract(inputs_all, w_gate, 1, 1)
        up_pre = contract(inputs_all, w_up, 1, 1)
        activated, gelu_back = jax.vjp(gelu_tanh, gate_pre)
        hidden_act = low(activated * up_pre)
        hidden_grad = contract(cot_all, w_down, 1, 1) + contract(
            low_grad_all, ffn_adapter[units], 1, 1
        )
        gate_grad = low(gelu_back(hidden_grad * up_pre)[0])
        up_grad = low(hidden_grad * activated)
        mine = low(
            jnp.stack(
                [
                    contract(gate_grad, inputs_all, 0, 0),
                    contract(up_grad, inputs_all, 0, 0),
                    contract(hidden_act, cot_all, 0, 0),
                ],
                axis=0,
            )
        )
        mine_low = low(contract(hidden_act, low_grad_all, 0, 0))
        ffn_parts.append((mine, swap_rep(mine)))
        low_parts.append((mine_low, swap_rep(mine_low)))
        hidden_parts.append(hidden_act)
        gate_parts.append(gate_grad)
        up_parts.append(up_grad)

    gate_grad = jnp.concatenate(gate_parts, axis=1)
    up_grad = jnp.concatenate(up_parts, axis=1)
    hidden_act = jnp.concatenate(hidden_parts, axis=1)
    normed_two_grad = sum_rows(
        low(
            contract(gate_grad, ffn_weight[:, 0, :], 1, 0)
            + contract(up_grad, ffn_weight[:, 1, :], 1, 0)
        ).reshape(micro, seq_len, model_dim)
    )
    normed_two_grad = normed_two_grad.reshape(count, model_dim).astype(jnp.float32)
    down_mine = sum_rows(
        jnp.concatenate(
            [
                low(contract(hidden_act, ffn_weight[:, 2, :], 1, 0)),
                low(contract(hidden_act, ffn_adapter, 1, 0)),
            ],
            axis=1,
        ).reshape(micro, seq_len, model_dim + RANK)
    ).reshape(count, model_dim + RANK)
    down_low = down_mine[:, model_dim:]
    result = (
        mixed_sum + down_mine[:, :model_dim].astype(jnp.float32) + contract(down_low, bd_t, 1, 1)
    )

    cot_full = cotangent.reshape(count, model_dim).astype(jnp.float32)
    mixed_part, gain_two_grad = norm_back_two(normed_two_grad)
    mixed_grad = cot_full + mixed_part
    out_grad_low = low(mixed_grad)
    out_cols = lax.all_to_all(
        out_grad_low.reshape(micro, local_len, model_dim), "fsdp", 2, 1, tiled=True
    ).reshape(every, attn_rows)
    wout_grad = contract(out_cols, kept_all[:, :q_width], 0, 0)
    context_grad = contract(out_grad_low, w_out, 1, 0)
    context_rows = low(context_grad).reshape(micro, local_len * HEADS, HD)
    prob_grad = batched(context_rows, values_all, 2, 2).reshape(micro, local_len, HEADS, seq_len)
    score_grad = weights * (prob_grad - jnp.sum(weights * prob_grad, axis=-1, keepdims=True))
    score_grad = low(score_grad).reshape(micro, local_len * HEADS, seq_len)
    query_grad = batched(score_grad, keys_all, 2, 1) * score_scale
    query_grad = query_grad.reshape(count, HEADS, HD)
    kv_grad = sum_rows(
        low(
            jnp.concatenate(
                [
                    batched(score_grad, queries, 1, 1) * score_scale,
                    batched(weights_low, context_rows, 1, 1),
                ],
                axis=2,
            )
        )
    ).reshape(count, 2 * HD)
    query_pre_grad = low(rotate(query_grad, -angles[:, None, :]).reshape(count, q_width))
    key_grad = low(rotate(kv_grad[:, :HD].astype(jnp.float32), -angles))
    value_grad = kv_grad[:, HD:]
    rank_grad = low(contract(query_pre_grad, bq_t, 1, 0))
    proj_grad = jnp.concatenate([query_pre_grad, key_grad, value_grad], axis=1)
    normed_grad = contract(proj_grad, w_proj, 1, 1) + contract(rank_grad, a_q, 1, 1)
    hidden_part, gain_one_grad = norm_back_one(normed_grad)
    input_grad = low(mixed_grad + hidden_part)

    back_all = gather_rows(
        jnp.concatenate([proj_grad, rank_grad, down_low], axis=1).reshape(
            micro, local_len, kv_end + 2 * RANK
        )
    ).reshape(every, kv_end + 2 * RANK)
    my_cols = me * attn_rows
    attn_in = contract(normed_cols, back_all[:, : kv_end + RANK], 0, 0)
    bq_grad = contract(
        lax.dynamic_slice_in_dim(back_all, my_cols, attn_rows, 1), kept_all[:, q_width:], 0, 0
    )
    bd_grad = contract(
        lax.dynamic_slice_in_dim(cot_all, my_cols, attn_rows, 1),
        back_all[:, kv_end + RANK :],
        0,
        0,
    )
    gain_now = jnp.stack([gain_one_grad, gain_two_grad], axis=1).reshape(shards, attn_rows, 2)
    gain_now = lax.all_to_all(gain_now, "fsdp", 0, 0, tiled=True).sum(axis=0)
    tail = low(jnp.concatenate([attn_in, bq_grad, bd_grad], axis=1))
    tail_out = low(wout_grad)
    tail_gain = low(gain_now)

    def total(mine, other):
        return mine.astype(jnp.float32) + other.astype(jnp.float32)

    tail = total(tail, swap_rep(tail))
    tail_out = total(tail_out, swap_rep(tail_out))
    gains_grad = total(tail_gain, swap_rep(tail_gain))
    attn_grad = jnp.concatenate([tail[:, :kv_end], tail_out], axis=1)
    adapter_grad = tail[:, kv_end:]
    ffn_grad = jnp.concatenate([total(*pair) for pair in ffn_parts], axis=1).transpose(1, 0, 2)
    ffn_low_grad = jnp.concatenate([total(*pair) for pair in low_parts], axis=0)
    return (
        low(result).reshape(micro, local_len, model_dim),
        input_grad.reshape(micro, local_len, model_dim),
        gains_grad,
        attn_grad,
        adapter_grad,
        ffn_grad,
        ffn_low_grad,
    )


def solution(mesh):
    placed = (
        P("rep", "fsdp", None),
        P("rep", "fsdp"),
        P("fsdp", None),
        P("fsdp", None),
        P("fsdp", None),
        P("fsdp", None, None),
        P("fsdp", None),
        P("rep", "fsdp", None),
    )
    return jax.shard_map(
        local,
        mesh=mesh,
        in_specs=placed,
        out_specs=(
            P("rep", "fsdp", None),
            P("rep", "fsdp", None),
            P("fsdp", None),
            P("fsdp", None),
            P("fsdp", None),
            P("fsdp", None, None),
            P("fsdp", None),
        ),
        check_vma=False,
    )
```

time: 1940 us -> 1280 us (0.66)
  waiting for transfers between devices: 1440 us -> 858 us
  blocking collectives: 46.8 us -> 0 us
  other arithmetic: 106 us -> 68.8 us
  matrix products: 281 us -> 246 us
  starting transfers between devices: 2.58 us -> 33.8 us
    reduce_scatter x8 -> x2, waiting for transfers between devices: 771 us -> 198 us  [sum_rows(): return lax.psum_scatter(values, 'fsdp', scatter_dimension=1, tiled=True)]
    psum x1 -> x0, waiting for transfers between devices: 325 us -> none  [local(): lax.psum(adapt_acc.astype(jnp.bfloat16), 'rep').astype(jnp.float32)]
    ppermute x0 -> x11, waiting for transfers between devices: none -> 237 us  [swap_rep(): return lax.ppermute(values, 'rep', [(0, 1), (1, 0)])]
    dot_general x18 -> x6, matrix products: 79.2 us -> 9.74 us  [batched(): lax.dot_general(left_op, right_op, (((left_dim,), (right_dim,)), ((0,), (...]
    all_gather x2 -> x0, blocking collectives: 41.9 us -> none  [the longest x1 23.7 us: local(): seg_whole = lax.all_gather(segment_ids, 'fsdp', axis=1, tiled=True)]
    all_gather x8 -> x7, waiting for transfers between devices: 291 us -> 332 us  [gather_rows(): return lax.all_gather(values, 'fsdp', axis=values.ndim - 2, tiled=True)]
    convert_element_type x13 -> x11, other arithmetic: 45.7 us -> 9.62 us  [the longest x7 6.95 us: low(): return values.astype(jnp.bfloat16)]
    dot_general x42 -> x50, matrix products: 201 us -> 236 us  [contract(): lax.dot_general(left_op, right_op, (((left_dim,), (right_dim,)), ((), ())...]
  transfers between devices with their start and end apart: 18 -> 24, of which waited for: 16 -> 15; matrix products, arithmetic and copies ran while one was open for 19% -> 18% of each run, Pallas kernels for 0% -> 0%
where the time goes in v1:
time: 1280 us; the launch traced here: 1270 us
  waiting for transfers between devices  858 us (67%)
  matrix products  246 us (19%)
  other arithmetic  68.8 us (5%)
  local copies, waits for them, and re-layouts  42.9 us (3%)
  starting transfers between devices  33.8 us (3%)
  between operations  16.7 us (1%)
    all_gather x7, waiting for transfers between devices, gather_rows(): return lax.all_gather(values, 'fsdp', axis=values.ndim - 2, tiled=True)  332 us
    ppermute x11, waiting for transfers between devices, swap_rep(): return lax.ppermute(values, 'rep', [(0, 1), (1, 0)])  237 us
    dot_general x50, matrix products, contract(): lax.dot_general(left_op, right_op, (((left_dim,), (right_dim,)), ((), ())...  236 us
    reduce_scatter x2, waiting for transfers between devices, sum_rows(): return lax.psum_scatter(values, 'fsdp', scatter_dimension=1, tiled=True)  198 us
    unnamed x11, waiting for transfers between devices  65.6 us
  transfers between devices with their start and end apart: 24, of which 15 were waited for; matrix products, arithmetic and copies ran while one was open for 18% of the time, Pallas kernels for 0%

profile of v1, /device:TPU:0, one launch (start us, length us, event | category | flops | bytes accessed | tf_op | source)
XLA Modules:
  0.0 1266.4 jit_solution(10089645762833557371)
XLA Ops:
  13.1 105.5 %all-gather.8.cloned.1.call-done = bf16[2048,3200]{1,0:T(8,128)(2,1)} async-done(((bf16[128,3200]{1,0:T(8,128)(2,1)}), bf16[2048,3200]{1,0:T(8,128)(2,1)}) %all-gather.8.cloned.1.call-update) | async-done | bytes 13107216 | tf_op jit(solution)/shard_map/all_gather | solution.py:68
  121.4 5.6 fusion.5
  136.6 34.2 %all-gather.10.cloned.1.call-done = bf16[2,1024,512]{2,1,0:T(8,128)(2,1)} async-done(((bf16[2,64,512]{2,1,0:T(8,128)(2,1)}), bf16[2,1024,512]{2,1,0:T(8,128)(2,1)}) %all-gather.10.cloned.1.call-update) | async-done | bytes 2097168 | tf_op jit(solution)/shard_map/all_gather | solution.py:68
  178.1 75.3 %all-gather.12.cloned.1.call-done = bf16[2048,2304]{1,0:T(8,128)(2,1)} async-done(((bf16[128,2304]{1,0:T(8,128)(2,1)}), bf16[2048,2304]{1,0:T(8,128)(2,1)}) %all-gather.12.cloned.1.call-update) | async-done | bytes 9437200 | tf_op jit(solution)/shard_map/all_gather | solution.py:68
  253.4 6.4 multiply_reduce_fusion.1
  261.2 67.0 %all-gather.16.cloned.1.call-done = bf16[2,1024,2048]{2,1,0:T(8,128)(2,1)} async-done(((bf16[2,64,2048]{2,1,0:T(8,128)(2,1)}), bf16[2,1024,2048]{2,1,0:T(8,128)(2,1)}) %all-gather.16.cloned.1.call-update) | async-done | bytes 8388624 | tf_op jit(solution)/shard_map/all_gather | solution.py:68
  328.2 7.5 fusion.100
  335.7 5.0 fusion.102
  340.6 4.9 fusion.104
  345.5 4.9 fusion.106
  350.4 3.6 convolution_convert_fusion.14
  354.1 49.7 %all-gather.14.cloned.1.call-done = bf16[2,1024,2048]{2,1,0:T(8,128)(2,1)} async-done(((bf16[2,64,2048]{2,1,0:T(8,128)(2,1)}), bf16[2,1024,2048]{2,1,0:T(8,128)(2,1)}) %all-gather.14.cloned.1.call-update) | async-done | bytes 8388624 | tf_op jit(solution)/shard_map/all_gather | solution.py:68
  403.7 7.9 fusion.110
  411.6 7.4 fusion.108
  419.1 2.5 fusion.114
  421.6 3.9 fusion.112
  430.5 2.7 fusion.122
  435.7 4.9 multiply_convert_fusion.2
  440.7 3.4 multiply_convert_fusion.3
  444.0 3.4 multiply_convert_fusion.4
  447.4 3.4 multiply_convert_fusion.5
  450.8 14.4 %fusion.13 = f32[2048,2048]{1,0:T(8,128)} fusion(bf16[2048,256]{0,1:T(8,128)(2,1)} %get-tuple-element.27, bf16[2048,256]{0,1:T(8,128)(2,1)} %get-tuple-element.24, bf16[2048,256]{0,1:T(8,128)(2,1)} %get-tuple-element.21, bf16[2048,256]{0,1:T(8,128)(2,1)} %get-tuple-element.18, bf16[1024,3,2048]{2,0,1:T(8,128)(2,1)S(1)} %bitcast.272), kind=kOutput, calls=%fused_computation.22 | convolution fusion | flops 8606711808 | bytes 25165824 | tf_op jit(solution)/shard_map/dot_general | solution.py:46
  465.2 16.7 %add_convert_fusion = bf16[2048,2048]{1,0:T(8,128)(2,1)} fusion(f32[2048,2048]{1,0:T(8,128)} %fusion.13, bf16[2048,256]{0,1:T(8,128)(2,1)} %get-tuple-element.26, bf16[2048,256]{0,1:T(8,128)(2,1)} %get-tuple-element.23, bf16[2048,256]{0,1:T(8,128)(2,1)} %get-tuple-element.20, bf16[2048,256]{0,1:T(8,128)(2,1)S(1)} %copy-done.65, bf16[1024,3,2048]{2,0,1:T(8,128)(2,1)} %param.13), kind=kOutput, calls=%fused_computation.2 | convolution fusion | flops 8615100416 | bytes 33554432 | tf_op jit(solution)/shard_map/dot_general | solution.py:46
  481.9 13.9 %convolution_convert_fusion = bf16[2048,2048]{0,1:T(8,128)(2,1)} fusion(bf16[1024,3,2048]{2,0,1:T(8,128)(2,1)} %param.13, bf16[2048,256]{0,1:T(8,128)(2,1)S(1)} %get-tuple-element.28, bf16[2048,256]{0,1:T(8,128)(2,1)} %get-tuple-element.25, bf16[2048,256]{0,1:T(8,128)(2,1)} %get-tuple-element.22, bf16[2048,256]{0,1:T(8,128)(2,1)} %get-tuple-element.19), kind=kOutput, calls=%fused_computation.12 | convolution fusion | flops 8610906112 | bytes 16777216 | tf_op jit(solution)/shard_map/dot_general | solution.py:46
  495.8 88.2 %reduce-scatter.5.cloned.1.call-done = bf16[2,64,2048]{2,1,0:T(8,128)(2,1)} async-done(((bf16[2,1024,2048]{2,1,0:T(8,128)(2,1)}), bf16[2,64,2048]{2,1,0:T(8,128)(2,1)}) %reduce-scatter.5.cloned.1.call-update) | async-done | bytes 524304 | tf_op jit(solution)/shard_map/reduce_scatter | solution.py:72
  588.2 4.6 fusion.53
  593.2 3.2 convolution_convert_fusion.15
  601.4 4.1 copy.59
  605.5 3.3 convolution_convert_fusion.1
  608.8 10.9 pad_maximum_fusion
  619.7 12.7 %copy.70 = bf16[2048,2304]{1,0:T(8,128)(2,1)} copy(bf16[2048,2304]{0,1:T(8,128)(2,1)} %pad_maximum_fusion) | data formatting | bytes 18874368 | tf_op jit(solution)/shard_map/reshape | solution.py:216
  638.4 64.9 %all-reduce.3.cloned.1.call-done = bf16[2,1024,512]{2,0,1:T(2,128)(2,1)} async-done(((bf16[2,1024,512]{2,0,1:T(2,128)(2,1)}), bf16[2,1024,512]{2,0,1:T(2,128)(2,1)}) %all-reduce.3.cloned.1.call-update) | async-done | bytes 2097168
  707.9 110.2 %reduce-scatter.3.cloned.1.call-done = bf16[2,64,2304]{2,1,0:T(8,128)(2,1)} async-done(((bf16[2,1024,2304]{2,1,0:T(8,128)(2,1)}), bf16[2,64,2304]{2,1,0:T(8,128)(2,1)}) %reduce-scatter.3.cloned.1.call-update) | async-done | bytes 589840 | tf_op jit(solution)/shard_map/reduce_scatter | solution.py:72
  822.3 4.4 all-to-all-start.1
  826.7 21.9 %all-to-all-done.1 = bf16[16,2,8192]{2,1,0:T(2,128)(2,1)S(1)} async-done(((bf16[16,2,8192]{2,1,0:T(2,128)(2,1)}), bf16[16,2,8192]{2,1,0:T(2,128)(2,1)S(1)}, u32[]{:S(2)}, u32[]{:S(2)}) %all-to-all-start.1) | async-done | bytes 524320 | tf_op jit(solution)/shard_map/all_to_all | solution.py:131
  850.0 6.2 fusion.49
  856.3 5.9 fusion.48
  868.8 5.8 fusion.45
  874.6 5.8 fusion.44
  881.7 6.1 fusion.43
  887.9 5.8 fusion.42
  893.7 6.0 fusion.41
  901.5 5.9 fusion.40
  907.4 6.1 fusion.39
  914.8 5.7 fusion.38
  925.3 148.2 %collective-permute-done.10 = bf16[256,256]{1,0:T(8,128)(2,1)S(1)} collective-permute-done((bf16[256,256]{1,0:T(8,128)(2,1)S(1)}, bf16[256,256]{1,0:T(8,128)(2,1)S(1)}, u32[]{:S(2)}, u32[]{:S(2)}) %collective-permute-start.10) | collective-permute-done | bytes 131104 | tf_op jit(solution)/shard_map/ppermute | solution.py:76
  1075.1 67.5 %collective-permute-done.9 = bf16[256,256]{1,0:T(8,128)(2,1)S(1)} collective-permute-done((bf16[256,256]{1,0:T(8,128)(2,1)S(1)}, bf16[256,256]{1,0:T(8,128)(2,1)S(1)}, u32[]{:S(2)}, u32[]{:S(2)}) %collective-permute-start.9) | collective-permute-done | bytes 131104 | tf_op jit(solution)/shard_map/ppermute | solution.py:76
  1144.1 3.5 collective-permute-done.8
  1149.1 3.5 collective-permute-done.7
  1153.6 3.2 convert_add_fusion
  1156.8 3.2 convert_add_fusion.1
  1160.0 3.2 convert_add_fusion.2
  1163.3 3.2 convert_add_fusion.3
  1168.7 8.6 all-to-all-start.2
  1177.3 17.8 %maximum_bitcast_fusion = f32[1024,3,2048]{2,0,1:T(8,128)} fusion(f32[3,256,2048]{2,1,0:T(8,128)} %convert_add_fusion, f32[3,256,2048]{2,1,0:T(8,128)} %convert_add_fusion.1, f32[3,256,2048]{2,1,0:T(8,128)} %convert_add_fusion.2, f32[3,256,2048]{2,1,0:T(8,128)} %convert_add_fusion.3), kind=kLoop, calls=%fused_computation.1 | loop fusion | flops 18874368 | bytes 50331648 | tf_op jit(solution)/shard_map/transpose | solution.py:288
  1196.6 5.5 fusion.56
  1203.6 6.2 fusion.3
  1209.8 2.9 fusion.127
  1213.3 6.2 all-to-all-start
  1219.6 2.6 fusion.97
  1222.3 3.8 all-to-all-done
  1230.2 6.0 fusion.34
  1239.7 2.7 fusion.59
  1242.4 14.3 %collective-permute-done.1 = bf16[128,3328]{1,0:T(8,128)(2,1)S(1)} collective-permute-done((bf16[128,3328]{1,0:T(8,128)(2,1)S(1)}, bf16[128,3328]{1,0:T(8,128)(2,1)S(1)}, u32[]{:S(2)}, u32[]{:S(2)}) %collective-permute-start.1) | collective-permute-done | bytes 852000 | tf_op jit(solution)/shard_map/ppermute | solution.py:76
  (317 shorter events, 96.3 us)
Async XLA Ops:
  7.2 111.4 %all-gather.8.cloned.1.call-start = ((), (), s32[]{:S(2)}) async-start(), calls=%async_computation.5 | async-start | bytes 13926400 | tf_op jit(solution)/shard_map/all_gather | solution.py:68
  12.1 158.8 %all-gather.10.cloned.1.call-start = ((), (), s32[]{:S(2)}) async-start(), calls=%async_computation.6 | async-start | bytes 2228224 | tf_op jit(solution)/shard_map/all_gather | solution.py:68
  13.0 107.7 %copy-start.56 = (f32[128]{0:T(128)}, f32[128]{0:T(128)S(1)}, u32[]{:S(2)}) copy-start(f32[128]{0:T(128)S(1)} %add.162) | copy-start | bytes 1540
  13.0 114.0 %copy-start.47 = (f32[128]{0:T(128)}, f32[128]{0:T(128)S(1)}, u32[]{:S(2)}) copy-start(f32[128]{0:T(128)S(1)} %rsqrt.23) | copy-start | bytes 1540
  13.1 116.0 %copy-start.43 = (f32[128]{0:T(128)}, f32[128]{0:T(128)S(1)}, u32[]{:S(2)}) copy-start(f32[128]{0:T(128)S(1)} %multiply_power_fusion) | copy-start | bytes 1540
  120.6 465.4 %copy-start.33 = (f32[2048]{0:T(1024)}, f32[2048]{0:T(1024)S(1)}, u32[]{:S(2)}) copy-start(f32[2048]{0:T(1024)S(1)} %get-tuple-element.11) | copy-start | bytes 24580
  121.4 7.4 copy-start.51
  121.4 9.6 slice-start
  121.4 9.6 slice-start.1
  131.0 122.4 %all-gather.12.cloned.1.call-start = ((), (), s32[]{:S(2)}) async-start(), calls=%async_computation.7 | async-start | bytes 10027008 | tf_op jit(solution)/shard_map/all_gather | solution.py:68
  131.9 196.3 %all-gather.16.cloned.1.call-start = ((), (), s32[]{:S(2)}) async-start(), calls=%async_computation.10 | async-start | bytes 8912896 | tf_op jit(solution)/shard_map/all_gather | solution.py:68
  132.5 271.2 %all-gather.14.cloned.1.call-start = ((), (), s32[]{:S(2)}) async-start(), calls=%async_computation.8 | async-start | bytes 8912896 | tf_op jit(solution)/shard_map/all_gather | solution.py:68
  136.6 38.3 %copy-start.23 = (bf16[128,8,128]{2,1,0:T(8,128)(2,1)}, bf16[128,8,128]{2,1,0:T(8,128)(2,1)S(1)}, u32[]{:S(2)}) copy-start(bf16[128,8,128]{2,1,0:T(8,128)(2,1)S(1)} %get-tuple-element.33) | copy-start | bytes 786436
  136.6 38.3 %copy-start.25 = (bf16[128,8,128]{2,1,0:T(8,128)(2,1)}, bf16[128,8,128]{2,1,0:T(8,128)(2,1)S(1)}, u32[]{:S(2)}) copy-start(bf16[128,8,128]{2,1,0:T(8,128)(2,1)S(1)} %get-tuple-element.34) | copy-start | bytes 786436
  177.8 75.6 %copy-start.14 = (bf16[2,512,256]{2,1,0:T(8,128)(2,1)}, bf16[2,512,256]{2,1,0:T(8,128)(2,1)S(1)}, u32[]{:S(2)}) copy-start(bf16[2,512,256]{2,1,0:T(8,128)(2,1)S(1)} %convolution_convert_fusion.16) | copy-start | bytes 1572868
  259.7 326.3 %copy-start = (f32[128,2048]{1,0:T(8,128)}, f32[128,2048]{1,0:T(8,128)S(1)}, u32[]{:S(2)}) copy-start(f32[128,2048]{1,0:T(8,128)S(1)} %get-tuple-element.48) | copy-start | bytes 3145732
  259.8 326.3 %copy-start.41 = (f32[128]{0:T(128)}, f32[128]{0:T(128)S(1)}, u32[]{:S(2)}) copy-start(f32[128]{0:T(128)S(1)} %fusion.176) | copy-start | bytes 1540
  261.0 323.1 %reduce-scatter.5.cloned.1.call-start = ((), (), s32[]{:S(2)}) async-start(), calls=%async_computation.11 | async-start | bytes 8912896 | tf_op jit(solution)/shard_map/reduce_scatter | solution.py:72
  328.2 7.5 copy-start.38
  354.1 93.4 %copy-start.2 = (bf16[256,2048]{1,0:T(8,128)(2,1)}, bf16[256,2048]{1,0:T(8,128)(2,1)S(1)}, u32[]{:S(2)}) copy-start(bf16[256,2048]{1,0:T(8,128)(2,1)S(1)} %convolution_convert_fusion.14) | copy-start | bytes 3145732
  403.7 15.3 %slice-start.4 = ((s8[12582912]{0:T(1024)(128)(4,1)}), s8[4194304]{0:T(1024)(128)(4,1)S(1)}, s32[]{:S(2)}) async-start(s8[12582912]{0:T(1024)(128)(4,1)} %bitcast.271), calls=%async_computation.19 | async-start | bytes 8388608
  403.7 15.3 %slice-start.5 = ((s8[12582912]{0:T(1024)(128)(4,1)}), s8[4194304]{0:T(1024)(128)(4,1)S(1)}, s32[]{:S(2)}) async-start(s8[12582912]{0:T(1024)(128)(4,1)} %bitcast.271), calls=%async_computation.20 | async-start | bytes 8388608
  403.7 15.3 %slice-start.7 = ((s8[8388608]{0:T(1024)(128)(4,1)}), s8[4194304]{0:T(1024)(128)(4,1)S(1)}, s32[]{:S(2)}) async-start(s8[8388608]{0:T(1024)(128)(4,1)} %bitcast.282), calls=%async_computation.22 | async-start | bytes 8388608
  411.6 7.5 slice-start.6
  411.6 7.5 slice-start.8
  440.6 164.9 %copy-start.18 = (bf16[2048,256]{0,1:T(8,128)(2,1)}, bf16[2048,256]{0,1:T(8,128)(2,1)S(1)}, u32[]{:S(2)}) copy-start(bf16[2048,256]{0,1:T(8,128)(2,1)S(1)} %get-tuple-element.28) | copy-start | bytes 3145732
  450.8 14.4 %copy-start.65 = (bf16[2048,256]{0,1:T(8,128)(2,1)S(1)}, bf16[2048,256]{0,1:T(8,128)(2,1)}, u32[]{:S(2)}) copy-start(bf16[2048,256]{0,1:T(8,128)(2,1)} %get-tuple-element.17) | copy-start | bytes 3145732
  481.9 221.4 %all-reduce.3.cloned.1.call-start = ((), (), s32[]{:S(2)}) async-start(), calls=%async_computation.14 | async-start | bytes 4194304
  481.9 104.1 %copy-start.6 = (bf16[2,64,2048]{2,1,0:T(8,128)(2,1)S(1)}, bf16[2,64,2048]{2,1,0:T(8,128)(2,1)}, u32[]{:S(2)}) copy-start(bf16[2,64,2048]{2,1,0:T(8,128)(2,1)} %param.15) | copy-start | bytes 1572868
  605.5 212.6 %reduce-scatter.3.cloned.1.call-start = ((), (), s32[]{:S(2)}) async-start(), calls=%async_computation.9 | async-start | bytes 10027008 | tf_op jit(solution)/shard_map/reduce_scatter | solution.py:72
  632.5 564.0 %all-gather.20.cloned.1.call-start = ((), (), s32[]{:S(2)}) async-start(), calls=%async_computation.13 | async-start | bytes 10027008 | tf_op jit(solution)/shard_map/all_gather | solution.py:68
  634.7 592.0 %all-gather.18.cloned.1.call-start = ((), (), s32[]{:S(2)}) async-start(), calls=%async_computation.12 | async-start | bytes 13369344 | tf_op jit(solution)/shard_map/all_gather | solution.py:68
  636.0 68.4 %copy-start.44 = (f32[128]{0:T(128)S(1)}, f32[128]{0:T(128)}, u32[]{:S(2)}) copy-start(f32[128]{0:T(128)} %copy-done.43) | copy-start | bytes 1540
  636.0 68.4 %copy-start.46 = (f32[128]{0:T(128)S(1)}, f32[128]{0:T(128)}, u32[]{:S(2)}) copy-start(f32[128]{0:T(128)} %copy-done.45) | copy-start | bytes 1540
  638.0 181.9 %copy-start.5 = (bf16[2,64,2048]{2,1,0:T(8,128)(2,1)S(1)}, bf16[2,64,2048]{2,1,0:T(8,128)(2,1)}, u32[]{:S(2)}) copy-start(bf16[2,64,2048]{2,1,0:T(8,128)(2,1)} %param.8) | copy-start | bytes 1572868
  638.0 181.9 %copy-start.36 = (f32[2048]{0:T(1024)S(1)}, f32[2048]{0:T(1024)}, u32[]{:S(2)}) copy-start(f32[2048]{0:T(1024)} %copy-done.35) | copy-start | bytes 24580
  638.0 181.9 %copy-start.52 = (f32[2,64]{1,0:T(2,128)S(1)}, f32[2,64]{1,0:T(2,128)}, u32[]{:S(2)}) copy-start(f32[2,64]{1,0:T(2,128)} %get-tuple-element.37) | copy-start | bytes 1540
  822.3 26.2 %all-to-all-start.1 = ((bf16[16,2,8192]{2,1,0:T(2,128)(2,1)}), bf16[16,2,8192]{2,1,0:T(2,128)(2,1)S(1)}, u32[]{:S(2)}, u32[]{:S(2)}) async-start(bf16[16,2,8192]{2,1,0:T(2,128)(2,1)} %reshape.417), calls=%async_computation.3 | async-start | bytes 1048576 | tf_op jit(solution)/shard_map/all_to_all | solution.py:131
  850.0 12.1 slice-start.9
  856.2 10.2 slice-start.2
  864.9 288.7 %collective-permute-start.6 = (bf16[3,256,2048]{2,1,0:T(8,128)(2,1)S(1)}, bf16[3,256,2048]{2,1,0:T(8,128)(2,1)S(1)}, u32[]{:S(2)}, u32[]{:S(2)}) collective-permute-start(bf16[3,256,2048]{2,1,0:T(8,128)(2,1)S(1)} %pad_maximum_fusion.5), channel_id=1, source_target_pairs={{0,16},{16,0},{1,17},{17,1},{2,18},{18,2},{3,19},{19,3},{4,20},{20... | collective-permute-start | bytes 9437192 | tf_op jit(solution)/shard_map/ppermute | solution.py:76
  880.8 7.0 copy-start.68
  880.8 276.0 %collective-permute-start.5 = (bf16[3,256,2048]{2,1,0:T(8,128)(2,1)S(1)}, bf16[3,256,2048]{2,1,0:T(8,128)(2,1)S(1)}, u32[]{:S(2)}, u32[]{:S(2)}) collective-permute-start(bf16[3,256,2048]{2,1,0:T(8,128)(2,1)S(1)} %pad_maximum_fusion.4), channel_id=1, source_target_pairs={{0,16},{16,0},{1,17},{17,1},{2,18},{18,2},{3,19},{19,3},{4,20},{20... | collective-permute-start | bytes 9437192 | tf_op jit(solution)/shard_map/ppermute | solution.py:76
  900.0 7.3 copy-start.66
  900.0 260.0 %collective-permute-start.4 = (bf16[3,256,2048]{2,1,0:T(8,128)(2,1)S(1)}, bf16[3,256,2048]{2,1,0:T(8,128)(2,1)S(1)}, u32[]{:S(2)}, u32[]{:S(2)}) collective-permute-start(bf16[3,256,2048]{2,1,0:T(8,128)(2,1)S(1)} %pad_maximum_fusion.3), channel_id=1, source_target_pairs={{0,16},{16,0},{1,17},{17,1},{2,18},{18,2},{3,19},{19,3},{4,20},{20... | collective-permute-start | bytes 9437192 | tf_op jit(solution)/shard_map/ppermute | solution.py:76
  920.9 152.6 %collective-permute-start.10 = (bf16[256,256]{1,0:T(8,128)(2,1)S(1)}, bf16[256,256]{1,0:T(8,128)(2,1)S(1)}, u32[]{:S(2)}, u32[]{:S(2)}) collective-permute-start(bf16[256,256]{1,0:T(8,128)(2,1)S(1)} %convolution_convert_fusion.17), channel_id=1, source_target_pairs={{0,16},{16,0},{1,17},{17,1},{2,18},{18,2},{3,19},{19,3},{4,20},{20... | collective-permute-start | bytes 393224 | tf_op jit(solution)/shard_map/ppermute | solution.py:76
  924.0 239.2 %collective-permute-start.3 = (bf16[3,256,2048]{2,1,0:T(8,128)(2,1)S(1)}, bf16[3,256,2048]{2,1,0:T(8,128)(2,1)S(1)}, u32[]{:S(2)}, u32[]{:S(2)}) collective-permute-start(bf16[3,256,2048]{2,1,0:T(8,128)(2,1)S(1)} %pad_maximum_fusion.2), channel_id=1, source_target_pairs={{0,16},{16,0},{1,17},{17,1},{2,18},{18,2},{3,19},{19,3},{4,20},{20... | collective-permute-start | bytes 9437192 | tf_op jit(solution)/shard_map/ppermute | solution.py:76
  1073.6 69.0 %collective-permute-start.9 = (bf16[256,256]{1,0:T(8,128)(2,1)S(1)}, bf16[256,256]{1,0:T(8,128)(2,1)S(1)}, u32[]{:S(2)}, u32[]{:S(2)}) collective-permute-start(bf16[256,256]{1,0:T(8,128)(2,1)S(1)} %convolution_convert_fusion.18), channel_id=1, source_target_pairs={{0,16},{16,0},{1,17},{17,1},{2,18},{18,2},{3,19},{19,3},{4,20},{20... | collective-permute-start | bytes 393224 | tf_op jit(solution)/shard_map/ppermute | solution.py:76
  1142.6 5.0 collective-permute-start.8
  1147.5 5.0 collective-permute-start.7
  1168.7 26.4 %all-to-all-start.2 = ((bf16[16,2,8192]{2,1,0:T(2,128)(2,1)}), bf16[16,2,8192]{2,1,0:T(2,128)(2,1)S(1)}, u32[]{:S(2)}, u32[]{:S(2)}) async-start(bf16[16,2,8192]{2,1,0:T(2,128)(2,1)} %reshape.415), calls=%async_computation.4 | async-start | bytes 1048576 | tf_op jit(solution)/shard_map/all_to_all | solution.py:227
  1196.6 7.0 copy-start.39
  1202.1 36.3 %collective-permute-start.2 = (bf16[128,2048]{1,0:T(8,128)(2,1)}, bf16[128,2048]{1,0:T(8,128)(2,1)}, u32[]{:S(2)}, u32[]{:S(2)}) collective-permute-start(bf16[128,2048]{1,0:T(8,128)(2,1)} %fusion.56), channel_id=1, source_target_pairs={{0,16},{16,0},{1,17},{17,1},{2,18},{18,2},{3,19},{19,3},{4,20},{20... | collective-permute-start | bytes 1572872 | tf_op jit(solution)/shard_map/ppermute | solution.py:76
  1203.5 9.2 copy-start.37
  1203.5 16.0 %copy-start.57 = (f32[128]{0:T(128)S(1)}, f32[128]{0:T(128)}, u32[]{:S(2)}) copy-start(f32[128]{0:T(128)} %copy-done.56) | copy-start | bytes 1540
  1203.5 16.0 %copy-start.34 = (f32[2048]{0:T(1024)S(1)}, f32[2048]{0:T(1024)}, u32[]{:S(2)}) copy-start(f32[2048]{0:T(1024)} %copy-done.33) | copy-start | bytes 24580
  1203.6 16.0 %copy-start.42 = (f32[128]{0:T(128)S(1)}, f32[128]{0:T(128)}, u32[]{:S(2)}) copy-start(f32[128]{0:T(128)} %copy-done.41) | copy-start | bytes 1540
  1203.6 16.0 %copy-start.54 = (f32[128]{0:T(128)S(1)}, f32[128]{0:T(128)}, u32[]{:S(2)}) copy-start(f32[128]{0:T(128)} %copy-done.53) | copy-start | bytes 1540
  1209.7 9.9 copy-start.1
  1209.7 9.9 copy-start.7
  1209.8 9.9 copy-start.8
  1213.3 12.7 %all-to-all-start = ((f32[16,128,2]{1,2,0:T(2,128)}), f32[16,128,2]{1,2,0:T(2,128)S(1)}, u32[]{:S(2)}, u32[]{:S(2)}) async-start(f32[16,128,2]{1,2,0:T(2,128)} %copy.61), calls=%async_computation.2 | async-start | bytes 32768 | tf_op jit(solution)/shard_map/all_to_all | solution.py:275
  1226.1 11.8 collective-permute-start
  1236.3 20.4 %collective-permute-start.1 = (bf16[128,3328]{1,0:T(8,128)(2,1)S(1)}, bf16[128,3328]{1,0:T(8,128)(2,1)S(1)}, u32[]{:S(2)}, u32[]{:S(2)}) collective-permute-start(bf16[128,3328]{1,0:T(8,128)(2,1)S(1)} %pad_maximum_fusion.9), channel_id=1, source_target_pairs={{0,16},{16,0},{1,17},{17,1},{2,18},{18,2},{3,19},{19,3},{4,20},{20... | collective-permute-start | bytes 2555912 | tf_op jit(solution)/shard_map/ppermute | solution.py:76
  (44 other events, 157.9 us)
Sparse Core Ops, SparseCore 0:
  12.2 106.3 all-gather.7
  131.1 39.7 all-gather.9
  173.7 79.6 all-gather.11
  255.4 72.7 all-gather.15
  330.8 72.8 all-gather.13
  482.0 101.9 reduce-scatter.4
  605.6 97.6 all-reduce.2
  707.4 110.6 reduce-scatter.2
  820.4 90.3 all-gather.19
  912.9 98.8 all-gather.17

commit v2 on v1

--- a/solution.py
+++ b/solution.py
@@ -199,27 +199,17 @@
     gate_grad = jnp.concatenate(gate_parts, axis=1)
     up_grad = jnp.concatenate(up_parts, axis=1)
     hidden_act = jnp.concatenate(hidden_parts, axis=1)
+    gate_grad, kept_all = lax.optimization_barrier((gate_grad, kept_all))
     normed_two_grad = sum_rows(
         low(
             contract(gate_grad, ffn_weight[:, 0, :], 1, 0)
             + contract(up_grad, ffn_weight[:, 1, :], 1, 0)
         ).reshape(micro, seq_len, model_dim)
     )
+    normed_two_grad, _ = lax.optimization_barrier(
+        (normed_two_grad, [pair[0] for pair in ffn_parts] + [ffn_parts[0][1]])
+    )
     normed_two_grad = normed_two_grad.reshape(count, model_dim).astype(jnp.float32)
-    down_mine = sum_rows(
-        jnp.concatenate(
-            [
-                low(contract(hidden_act, ffn_weight[:, 2, :], 1, 0)),
-                low(contract(hidden_act, ffn_adapter, 1, 0)),
-            ],
-            axis=1,
-        ).reshape(micro, seq_len, model_dim + RANK)
-    ).reshape(count, model_dim + RANK)
-    down_low = down_mine[:, model_dim:]
-    result = (
-        mixed_sum + down_mine[:, :model_dim].astype(jnp.float32) + contract(down_low, bd_t, 1, 1)
-    )
-
     cot_full = cotangent.reshape(count, model_dim).astype(jnp.float32)
     mixed_part, gain_two_grad = norm_back_two(normed_two_grad)
     mixed_grad = cot_full + mixed_part
@@ -235,17 +225,35 @@
     score_grad = low(score_grad).reshape(micro, local_len * HEADS, seq_len)
     query_grad = batched(score_grad, keys_all, 2, 1) * score_scale
     query_grad = query_grad.reshape(count, HEADS, HD)
-    kv_grad = sum_rows(
-        low(
-            jnp.concatenate(
-                [
-                    batched(score_grad, queries, 1, 1) * score_scale,
-                    batched(weights_low, context_rows, 1, 1),
-                ],
-                axis=2,
-            )
-        )
-    ).reshape(count, 2 * HD)
+    kv_part = low(
+        jnp.concatenate(
+            [
+                batched(score_grad, queries, 1, 1) * score_scale,
+                batched(weights_low, context_rows, 1, 1),
+            ],
+            axis=2,
+        )
+    )
+    kv_part, _ = lax.optimization_barrier((kv_part, ffn_parts[1][1]))
+    sums = sum_rows(
+        jnp.concatenate(
+            [
+                low(contract(hidden_act, ffn_weight[:, 2, :], 1, 0)).reshape(
+                    micro, seq_len, model_dim
+                ),
+                low(contract(hidden_act, ffn_adapter, 1, 0)).reshape(micro, seq_len, RANK),
+                kv_part,
+            ],
+            axis=2,
+        )
+    )
+    sums, _ = lax.optimization_barrier((sums, ffn_parts[2][1]))
+    sums = sums.reshape(count, model_dim + RANK + 2 * HD)
+    kv_grad = sums[:, model_dim + RANK :]
+    down_low = sums[:, model_dim : model_dim + RANK]
+    result = (
+        mixed_sum + sums[:, :model_dim].astype(jnp.float32) + contract(down_low, bd_t, 1, 1)
+    )
     query_pre_grad = low(rotate(query_grad, -angles[:, None, :]).reshape(count, q_width))
     key_grad = low(rotate(kv_grad[:, :HD].astype(jnp.float32), -angles))
     value_grad = kv_grad[:, HD:]

time: 1280 us -> 1070 us (0.84)
  waiting for transfers between devices: 858 us -> 659 us
  matrix products: 246 us -> 228 us
  other arithmetic: 68.8 us -> 86.1 us
    reduce_scatter x2, waiting for transfers between devices: 198 us -> 69.9 us  [sum_rows(): return lax.psum_scatter(values, 'fsdp', scatter_dimension=1, tiled=True)]
    unnamed x11 -> x9, waiting for transfers between devices: 65.6 us -> 0.65 us
    ppermute x11, waiting for transfers between devices: 237 us -> 213 us  [swap_rep(): return lax.ppermute(values, 'rep', [(0, 1), (1, 0)])]
    dot_general x50, matrix products: 236 us -> 218 us  [contract(): lax.dot_general(left_op, right_op, (((left_dim,), (right_dim,)), ((), ())...]
    all_gather x7, waiting for transfers between devices: 332 us -> 349 us  [gather_rows(): return lax.all_gather(values, 'fsdp', axis=values.ndim - 2, tiled=True)]
  transfers between devices with their start and end apart: 24 -> 23, of which waited for: 15 -> 18; matrix products, arithmetic and copies ran while one was open for 18% -> 25% of each run, Pallas kernels for 0% -> 0%
where the time goes in v2:
time: 1070 us; the launch traced here: 1060 us
  waiting for transfers between devices  659 us (62%)
  matrix products  228 us (21%)
  other arithmetic  86.1 us (8%)
  local copies, waits for them, and re-layouts  34.5 us (3%)
  starting transfers between devices  33.5 us (3%)
  between operations  16.1 us (2%)
    all_gather x7, waiting for transfers between devices, gather_rows(): return lax.all_gather(values, 'fsdp', axis=values.ndim - 2, tiled=True)  349 us
    dot_general x50, matrix products, contract(): lax.dot_general(left_op, right_op, (((left_dim,), (right_dim,)), ((), ())...  218 us
    ppermute x11, waiting for transfers between devices, swap_rep(): return lax.ppermute(values, 'rep', [(0, 1), (1, 0)])  213 us
    reduce_scatter x2, waiting for transfers between devices, sum_rows(): return lax.psum_scatter(values, 'fsdp', scatter_dimension=1, tiled=True)  69.9 us
    all_to_all x1, waiting for transfers between devices, local(): lax.all_to_all(normed_low.reshape(micro, local_len, model_dim), 'fsdp', 2...  23.1 us
    add x11, other arithmetic, total(): return mine.astype(jnp.float32) + other.astype(jnp.float32)  22.5 us
  transfers between devices with their start and end apart: 23, of which 18 were waited for; matrix products, arithmetic and copies ran while one was open for 25% of the time, Pallas kernels for 0%

profile of v2, /device:TPU:0, one launch (start us, length us, event | category | flops | bytes accessed | tf_op | source)
XLA Modules:
  0.0 1057.9 jit_solution(7047098858831415282)
XLA Ops:
  13.1 105.5 %all-gather.8.cloned.1.call-done = bf16[2048,3200]{1,0:T(8,128)(2,1)} async-done(((bf16[128,3200]{1,0:T(8,128)(2,1)}), bf16[2048,3200]{1,0:T(8,128)(2,1)}) %all-gather.8.cloned.1.call-update) | async-done | bytes 13107216 | tf_op jit(solution)/shard_map/all_gather | solution.py:68
  121.4 5.6 fusion.5
  136.6 34.3 %all-gather.10.cloned.1.call-done = bf16[2,1024,512]{2,1,0:T(8,128)(2,1)} async-done(((bf16[2,64,512]{2,1,0:T(8,128)(2,1)}), bf16[2,1024,512]{2,1,0:T(8,128)(2,1)}) %all-gather.10.cloned.1.call-update) | async-done | bytes 2097168 | tf_op jit(solution)/shard_map/all_gather | solution.py:68
  178.1 75.3 %all-gather.12.cloned.1.call-done = bf16[2048,2304]{1,0:T(8,128)(2,1)} async-done(((bf16[128,2304]{1,0:T(8,128)(2,1)}), bf16[2048,2304]{1,0:T(8,128)(2,1)}) %all-gather.12.cloned.1.call-update) | async-done | bytes 9437200 | tf_op jit(solution)/shard_map/all_gather | solution.py:68
  253.4 6.4 multiply_reduce_fusion.1
  263.1 65.1 %all-gather.16.cloned.1.call-done = bf16[2,1024,2048]{2,1,0:T(8,128)(2,1)} async-done(((bf16[2,64,2048]{2,1,0:T(8,128)(2,1)}), bf16[2,1024,2048]{2,1,0:T(8,128)(2,1)}) %all-gather.16.cloned.1.call-update) | async-done | bytes 8388624 | tf_op jit(solution)/shard_map/all_gather | solution.py:68
  328.2 6.1 fusion.92
  334.4 3.6 fusion.94
  338.0 3.7 fusion.96
  341.7 3.6 fusion.98
  345.3 3.7 convolution_convert_fusion.14
  355.0 48.7 %all-gather.14.cloned.1.call-done = bf16[2,1024,2048]{2,1,0:T(8,128)(2,1)} async-done(((bf16[2,64,2048]{2,1,0:T(8,128)(2,1)}), bf16[2,1024,2048]{2,1,0:T(8,128)(2,1)}) %all-gather.14.cloned.1.call-update) | async-done | bytes 8388624 | tf_op jit(solution)/shard_map/all_gather | solution.py:68
  403.7 7.4 fusion.102
  411.2 7.9 fusion.106
  419.2 3.7 fusion.110
  422.9 2.4 fusion.114
  425.3 9.7 multiply_convert_fusion.6
  435.0 9.9 multiply_convert_fusion.7
  444.9 9.5 multiply_convert_fusion.8
  454.5 7.9 multiply_convert_fusion.9
  465.6 19.8 %all-gather.18.cloned.1.call-done = bf16[2,1024,2304]{2,1,0:T(8,128)(2,1)} async-done(((bf16[2,64,2304]{2,1,0:T(8,128)(2,1)}), bf16[2,1024,2304]{2,1,0:T(8,128)(2,1)}) %all-gather.18.cloned.1.call-update) | async-done | bytes 9437200 | tf_op jit(solution)/shard_map/all_gather | solution.py:68
  485.4 15.6 %fusion.21 = f32[2048,2048]{1,0:T(8,128)} fusion(bf16[2048,1024]{0,1:T(8,128)(2,1)} %pad_maximum_fusion.2, bf16[1024,3,2048]{2,0,1:T(8,128)(2,1)} %param.13), kind=kOutput, calls=%fused_computation.31 | convolution fusion | flops 8589934592 | bytes 25165824 | tf_op jit(solution)/shard_map/dot_general | solution.py:46
  501.1 16.1 %add_convert_fusion = bf16[2048,2048]{1,0:T(8,128)(2,1)} fusion(f32[2048,2048]{1,0:T(8,128)} %fusion.21, bf16[2048,256]{0,1:T(8,128)(2,1)S(1)} %copy-done.94, bf16[2048,256]{0,1:T(8,128)(2,1)S(1)} %copy-done.95, bf16[2048,256]{0,1:T(8,128)(2,1)} %get-tuple-element.35, bf16[2048,256]{0,1:T(8,128)(2,1)} %get-tuple-element.38, bf16[1024,3,2048]{2,0,1:T(8,128)(2,1)} %param.13), kind=kOutput, calls=%fused_computation.2 | convolution fusion | flops 8615100416 | bytes 33554432 | tf_op jit(solution)/shard_map/dot_general | solution.py:46
  517.5 6.3 fusion.32
  523.9 6.9 fusion.31
  530.9 2.4 fusion.33
  535.2 2.3 fusion.35
  537.6 2.3 fusion.34
  540.0 2.3 fusion.38
  542.3 2.8 fusion.37
  549.9 2.4 fusion.36
  552.3 2.4 fusion.39
  554.7 2.4 fusion.42
  564.6 2.5 convolution_convert_fusion.1
  567.1 13.6 %convolution_convert_fusion = bf16[2048,2048]{1,0:T(8,128)(2,1)} fusion(bf16[1024,3,2048]{2,0,1:T(8,128)(2,1)} %param.13, bf16[2048,256]{0,1:T(8,128)(2,1)S(1)} %get-tuple-element.27, bf16[2048,256]{0,1:T(8,128)(2,1)S(1)} %copy-done.45, bf16[2048,256]{0,1:T(8,128)(2,1)S(1)} %copy-done.46, bf16[2048,256]{0,1:T(8,128)(2,1)S(1)} %copy-done.48), kind=kOutput, calls=%fused_computation.12 | convolution fusion | flops 8610906112 | bytes 16777216 | tf_op jit(solution)/shard_map/dot_general | solution.py:46
  580.8 24.1 %collective-permute-done = bf16[3,256,2048]{2,1,0:T(8,128)(2,1)} collective-permute-done((bf16[3,256,2048]{2,1,0:T(8,128)(2,1)S(1)}, bf16[3,256,2048]{2,1,0:T(8,128)(2,1)}, u32[]{:S(2)}, u32[]{:S(2)}) %collective-permute-start) | collective-permute-done | bytes 3145760 | tf_op jit(solution)/shard_map/ppermute | solution.py:76
  604.8 14.4 %reduce-scatter.3.cloned.1.call-done = bf16[2,64,2048]{2,1,0:T(8,128)(2,1)} async-done(((bf16[2,1024,2048]{2,1,0:T(8,128)(2,1)}), bf16[2,64,2048]{2,1,0:T(8,128)(2,1)}) %reduce-scatter.3.cloned.1.call-update) | async-done | bytes 524304 | tf_op jit(solution)/shard_map/reduce_scatter | solution.py:72
  623.4 4.6 fusion.46
  628.3 3.5 multiply_reduce_fusion
  634.9 36.5 %collective-permute-done.1 = bf16[3,256,2048]{2,1,0:T(8,128)(2,1)} collective-permute-done((bf16[3,256,2048]{2,1,0:T(8,128)(2,1)}, bf16[3,256,2048]{2,1,0:T(8,128)(2,1)}, u32[]{:S(2)}, u32[]{:S(2)}) %collective-permute-start.1) | collective-permute-done | bytes 3145760 | tf_op jit(solution)/shard_map/ppermute | solution.py:76
  671.4 2.5 copy.53
  674.0 11.1 %pad_maximum_fusion = bf16[2,1024,2816]{2,1,0:T(8,128)(2,1)} fusion(bf16[2,1024,512]{2,1,0:T(8,128)(2,1)} %copy.53, bf16[2,1024,256]{2,1,0:T(8,128)(2,1)} %bitcast.244, bf16[2,1024,2048]{2,1,0:T(8,128)(2,1)} %bitcast.230), kind=kLoop, calls=%fused_computation.5 | loop fusion | flops 34603008 | bytes 23068672 | tf_op jit(solution)/shard_map/concatenate | solution.py:239
  689.3 65.9 %collective-permute-done.2 = bf16[3,256,2048]{2,1,0:T(8,128)(2,1)} collective-permute-done((bf16[3,256,2048]{2,1,0:T(8,128)(2,1)}, bf16[3,256,2048]{2,1,0:T(8,128)(2,1)}, u32[]{:S(2)}, u32[]{:S(2)}) %collective-permute-start.2) | collective-permute-done | bytes 3145760 | tf_op jit(solution)/shard_map/ppermute | solution.py:76
  755.2 55.5 %reduce-scatter.5.cloned.1.call-done = bf16[2,64,2816]{2,1,0:T(8,128)(2,1)} async-done(((bf16[2,1024,2816]{2,1,0:T(8,128)(2,1)}), bf16[2,64,2816]{2,1,0:T(8,128)(2,1)}) %reduce-scatter.5.cloned.1.call-update) | async-done | bytes 720912 | tf_op jit(solution)/shard_map/reduce_scatter | solution.py:72
  820.7 3.8 reshape.416
  824.5 4.1 all-to-all-start.1
  828.5 23.1 %all-to-all-done.1 = bf16[16,2,8192]{2,1,0:T(2,128)(2,1)S(1)} async-done(((bf16[16,2,8192]{2,1,0:T(2,128)(2,1)}), bf16[16,2,8192]{2,1,0:T(2,128)(2,1)S(1)}, u32[]{:S(2)}, u32[]{:S(2)}) %all-to-all-start.1) | async-done | bytes 524320 | tf_op jit(solution)/shard_map/all_to_all | solution.py:131
  853.2 3.5 copy.64
  866.8 63.9 %collective-permute-done.10 = bf16[256,256]{1,0:T(8,128)(2,1)S(1)} collective-permute-done((bf16[256,256]{1,0:T(8,128)(2,1)S(1)}, bf16[256,256]{1,0:T(8,128)(2,1)S(1)}, u32[]{:S(2)}, u32[]{:S(2)}) %collective-permute-start.10) | collective-permute-done | bytes 131104 | tf_op jit(solution)/shard_map/ppermute | solution.py:76
  930.8 2.8 collective-permute-done.9
  933.6 2.8 collective-permute-done.8
  939.0 4.8 convert_add_fusion.1
  943.9 4.7 convert_add_fusion.2
  950.8 11.3 %all-to-all-start.2 = ((bf16[16,2,8192]{2,1,0:T(2,128)(2,1)}), bf16[16,2,8192]{2,1,0:T(2,128)(2,1)S(1)}, u32[]{:S(2)}, u32[]{:S(2)}) async-start(bf16[16,2,8192]{2,1,0:T(2,128)(2,1)} %reshape.414), calls=%async_computation.4 | async-start | bytes 1048576 | tf_op jit(solution)/shard_map/all_to_all | solution.py:217
  962.2 5.2 convert_add_fusion.3
  967.5 4.6 convert_add_fusion
  972.1 4.4 all-to-all-done.2
  977.9 4.8 fusion.49
  983.9 19.1 %maximum_bitcast_fusion = f32[1024,3,2048]{2,0,1:T(8,128)} fusion(f32[3,256,2048]{2,1,0:T(8,128)} %convert_add_fusion, f32[3,256,2048]{2,1,0:T(8,128)} %convert_add_fusion.1, f32[3,256,2048]{2,1,0:T(8,128)} %convert_add_fusion.2, f32[3,256,2048]{2,1,0:T(8,128)} %convert_add_fusion.3), kind=kLoop, calls=%fused_computation.1 | loop fusion | flops 18874368 | bytes 50331648 | tf_op jit(solution)/shard_map/transpose | solution.py:296
  1004.1 3.5 fusion.3
  1009.8 4.2 all-to-all-start
  1017.7 6.3 fusion.27
  1028.6 2.7 fusion.52
  1031.2 15.3 %collective-permute-done.3 = bf16[128,2]{0,1:T(2,128)(2,1)S(1)} collective-permute-done((bf16[128,2]{0,1:T(2,128)(2,1)S(1)}, bf16[128,2]{0,1:T(2,128)(2,1)S(1)}, u32[]{:S(2)}, u32[]{:S(2)}) %collective-permute-start.3) | collective-permute-done | bytes 544 | tf_op jit(solution)/shard_map/ppermute | solution.py:76
  (370 shorter events, 108.5 us)
Async XLA Ops:
  7.2 111.4 %all-gather.8.cloned.1.call-start = ((), (), s32[]{:S(2)}) async-start(), calls=%async_computation.5 | async-start | bytes 13926400 | tf_op jit(solution)/shard_map/all_gather | solution.py:68
  12.1 158.8 %all-gather.10.cloned.1.call-start = ((), (), s32[]{:S(2)}) async-start(), calls=%async_computation.6 | async-start | bytes 2228224 | tf_op jit(solution)/shard_map/all_gather | solution.py:68
  13.0 107.7 %copy-start.90 = (f32[128]{0:T(128)}, f32[128]{0:T(128)S(1)}, u32[]{:S(2)}) copy-start(f32[128]{0:T(128)S(1)} %add.160) | copy-start | bytes 1540
  13.0 114.0 %copy-start.82 = (f32[128]{0:T(128)}, f32[128]{0:T(128)S(1)}, u32[]{:S(2)}) copy-start(f32[128]{0:T(128)S(1)} %rsqrt.23) | copy-start | bytes 1540
  13.1 116.0 %copy-start.78 = (f32[128]{0:T(128)}, f32[128]{0:T(128)S(1)}, u32[]{:S(2)}) copy-start(f32[128]{0:T(128)S(1)} %multiply_power_fusion) | copy-start | bytes 1540
  120.6 139.2 %copy-start.67 = (f32[2048]{0:T(1024)}, f32[2048]{0:T(1024)S(1)}, u32[]{:S(2)}) copy-start(f32[2048]{0:T(1024)S(1)} %get-tuple-element.21) | copy-start | bytes 24580
  131.0 122.4 %all-gather.12.cloned.1.call-start = ((), (), s32[]{:S(2)}) async-start(), calls=%async_computation.7 | async-start | bytes 10027008 | tf_op jit(solution)/shard_map/all_gather | solution.py:68
  131.9 196.3 %all-gather.16.cloned.1.call-start = ((), (), s32[]{:S(2)}) async-start(), calls=%async_computation.9 | async-start | bytes 8912896 | tf_op jit(solution)/shard_map/all_gather | solution.py:68
  132.5 271.2 %all-gather.14.cloned.1.call-start = ((), (), s32[]{:S(2)}) async-start(), calls=%async_computation.8 | async-start | bytes 8912896 | tf_op jit(solution)/shard_map/all_gather | solution.py:68
  136.6 38.4 %copy-start.50 = (bf16[128,8,128]{2,1,0:T(8,128)(2,1)}, bf16[128,8,128]{2,1,0:T(8,128)(2,1)S(1)}, u32[]{:S(2)}) copy-start(bf16[128,8,128]{2,1,0:T(8,128)(2,1)S(1)} %get-tuple-element.43) | copy-start | bytes 786436
  136.6 38.4 %copy-start.52 = (bf16[128,8,128]{2,1,0:T(8,128)(2,1)}, bf16[128,8,128]{2,1,0:T(8,128)(2,1)S(1)}, u32[]{:S(2)}) copy-start(bf16[128,8,128]{2,1,0:T(8,128)(2,1)S(1)} %get-tuple-element.44) | copy-start | bytes 786436
  259.7 74.6 %copy-start.92 = (f32[128]{0:T(128)}, f32[128]{0:T(128)S(1)}, u32[]{:S(2)}) copy-start(f32[128]{0:T(128)S(1)} %get-tuple-element.57) | copy-start | bytes 1540
  259.8 74.6 %copy-start.75 = (f32[128]{0:T(128)}, f32[128]{0:T(128)S(1)}, u32[]{:S(2)}) copy-start(f32[128]{0:T(128)S(1)} %fusion.169) | copy-start | bytes 1540
  261.7 223.7 %all-gather.18.cloned.1.call-start = ((), (), s32[]{:S(2)}) async-start(), calls=%async_computation.10 | async-start | bytes 10027008 | tf_op jit(solution)/shard_map/all_gather | solution.py:68
  262.9 356.3 %reduce-scatter.3.cloned.1.call-start = ((), (), s32[]{:S(2)}) async-start(), calls=%async_computation.11 | async-start | bytes 8912896 | tf_op jit(solution)/shard_map/reduce_scatter | solution.py:72
  403.7 15.4 %slice-start.9 = ((s8[12582912]{0:T(1024)(128)(4,1)}), s8[4194304]{0:T(1024)(128)(4,1)S(1)}, s32[]{:S(2)}) async-start(s8[12582912]{0:T(1024)(128)(4,1)} %bitcast.282), calls=%async_computation.23 | async-start | bytes 8388608
  403.7 15.4 %slice-start.11 = ((s8[8388608]{0:T(1024)(128)(4,1)}), s8[4194304]{0:T(1024)(128)(4,1)S(1)}, s32[]{:S(2)}) async-start(s8[8388608]{0:T(1024)(128)(4,1)} %bitcast.288), calls=%async_computation.25 | async-start | bytes 8388608
  435.0 27.4 %copy-start.54 = (bf16[2048,256]{0,1:T(8,128)(2,1)}, bf16[2048,256]{0,1:T(8,128)(2,1)S(1)}, u32[]{:S(2)}) copy-start(bf16[2048,256]{0,1:T(8,128)(2,1)S(1)} %get-tuple-element.28) | copy-start | bytes 3145732
  435.0 132.1 %copy-start.44 = (bf16[2048,256]{0,1:T(8,128)(2,1)}, bf16[2048,256]{0,1:T(8,128)(2,1)S(1)}, u32[]{:S(2)}) copy-start(bf16[2048,256]{0,1:T(8,128)(2,1)S(1)} %get-tuple-element.27) | copy-start | bytes 3145732
  444.9 17.5 %copy-start.56 = (bf16[2048,256]{0,1:T(8,128)(2,1)}, bf16[2048,256]{0,1:T(8,128)(2,1)S(1)}, u32[]{:S(2)}) copy-start(bf16[2048,256]{0,1:T(8,128)(2,1)S(1)} %get-tuple-element.31) | copy-start | bytes 3145732
  485.4 15.7 %copy-start.94 = (bf16[2048,256]{0,1:T(8,128)(2,1)S(1)}, bf16[2048,256]{0,1:T(8,128)(2,1)}, u32[]{:S(2)}) copy-start(bf16[2048,256]{0,1:T(8,128)(2,1)} %get-tuple-element.29) | copy-start | bytes 3145732
  485.4 15.7 %copy-start.95 = (bf16[2048,256]{0,1:T(8,128)(2,1)S(1)}, bf16[2048,256]{0,1:T(8,128)(2,1)}, u32[]{:S(2)}) copy-start(bf16[2048,256]{0,1:T(8,128)(2,1)} %get-tuple-element.32) | copy-start | bytes 3145732
  517.2 293.4 %reduce-scatter.5.cloned.1.call-start = ((), (), s32[]{:S(2)}) async-start(), calls=%async_computation.12 | async-start | bytes 12255232 | tf_op jit(solution)/shard_map/reduce_scatter | solution.py:72
  533.7 71.1 %collective-permute-start = (bf16[3,256,2048]{2,1,0:T(8,128)(2,1)S(1)}, bf16[3,256,2048]{2,1,0:T(8,128)(2,1)}, u32[]{:S(2)}, u32[]{:S(2)}) collective-permute-start(bf16[3,256,2048]{2,1,0:T(8,128)(2,1)S(1)} %pad_maximum_fusion.3), channel_id=1, source_target_pairs={{0,16},{16,0},{1,17},{17,1},{2,18},{18,2},{3,19},{19,3},{4,20},{20... | collective-permute-start | bytes 9437192 | tf_op jit(solution)/shard_map/ppermute | solution.py:76
  537.6 19.5 %copy-start.20 = (bf16[1,256,2048]{2,1,0:T(8,128)(2,1)}, bf16[1,256,2048]{2,1,0:T(8,128)(2,1)S(1)}, u32[]{:S(2)}) copy-start(bf16[1,256,2048]{2,1,0:T(8,128)(2,1)S(1)} %fusion.35) | copy-start | bytes 3145732
  540.0 17.2 %copy-start.22 = (bf16[1,256,2048]{2,1,0:T(8,128)(2,1)}, bf16[1,256,2048]{2,1,0:T(8,128)(2,1)S(1)}, u32[]{:S(2)}) copy-start(bf16[1,256,2048]{2,1,0:T(8,128)(2,1)S(1)} %fusion.34) | copy-start | bytes 3145732
  542.3 18.2 %copy-start.24 = (bf16[1,256,2048]{2,1,0:T(8,128)(2,1)}, bf16[1,256,2048]{2,1,0:T(8,128)(2,1)S(1)}, u32[]{:S(2)}) copy-start(bf16[1,256,2048]{2,1,0:T(8,128)(2,1)S(1)} %fusion.38) | copy-start | bytes 3145732
  545.1 15.4 %copy-start.26 = (bf16[1,256,2048]{2,1,0:T(8,128)(2,1)}, bf16[1,256,2048]{2,1,0:T(8,128)(2,1)S(1)}, u32[]{:S(2)}) copy-start(bf16[1,256,2048]{2,1,0:T(8,128)(2,1)S(1)} %fusion.37) | copy-start | bytes 3145732
  559.2 112.3 %collective-permute-start.1 = (bf16[3,256,2048]{2,1,0:T(8,128)(2,1)}, bf16[3,256,2048]{2,1,0:T(8,128)(2,1)}, u32[]{:S(2)}, u32[]{:S(2)}) collective-permute-start(bf16[3,256,2048]{2,1,0:T(8,128)(2,1)} %pad_maximum_fusion.4), channel_id=1, source_target_pairs={{0,16},{16,0},{1,17},{17,1},{2,18},{18,2},{3,19},{19,3},{4,20},{20... | collective-permute-start | bytes 9437192 | tf_op jit(solution)/shard_map/ppermute | solution.py:76
  567.1 52.1 %copy-start.3 = (f32[128,2048]{1,0:T(8,128)S(1)}, f32[128,2048]{1,0:T(8,128)}, u32[]{:S(2)}) copy-start(f32[128,2048]{1,0:T(8,128)} %copy-done.2) | copy-start | bytes 3145732
  567.1 52.1 %copy-start.68 = (f32[2048]{0:T(1024)S(1)}, f32[2048]{0:T(1024)}, u32[]{:S(2)}) copy-start(f32[2048]{0:T(1024)} %copy-done.67) | copy-start | bytes 24580
  567.1 52.1 %copy-start.76 = (f32[128]{0:T(128)S(1)}, f32[128]{0:T(128)}, u32[]{:S(2)}) copy-start(f32[128]{0:T(128)} %copy-done.75) | copy-start | bytes 1540
  567.1 54.1 %copy-start.93 = (f32[128]{0:T(128)S(1)}, f32[128]{0:T(128)}, u32[]{:S(2)}) copy-start(f32[128]{0:T(128)} %copy-done.92) | copy-start | bytes 1540
  567.1 54.1 %copy-start.6 = (bf16[2,64,2048]{2,1,0:T(8,128)(2,1)S(1)}, bf16[2,64,2048]{2,1,0:T(8,128)(2,1)}, u32[]{:S(2)}) copy-start(bf16[2,64,2048]{2,1,0:T(8,128)(2,1)} %param.15) | copy-start | bytes 1572868
  685.2 126.3 %copy-start.79 = (f32[128]{0:T(128)S(1)}, f32[128]{0:T(128)}, u32[]{:S(2)}) copy-start(f32[128]{0:T(128)} %copy-done.78) | copy-start | bytes 1540
  685.2 126.3 %copy-start.81 = (f32[128]{0:T(128)S(1)}, f32[128]{0:T(128)}, u32[]{:S(2)}) copy-start(f32[128]{0:T(128)} %copy-done.80) | copy-start | bytes 1540
  685.2 328.9 %all-gather.20.cloned.1.call-start = ((), (), s32[]{:S(2)}) async-start(), calls=%async_computation.13 | async-start | bytes 13369344 | tf_op jit(solution)/shard_map/all_gather | solution.py:68
  685.5 69.7 %collective-permute-start.2 = (bf16[3,256,2048]{2,1,0:T(8,128)(2,1)}, bf16[3,256,2048]{2,1,0:T(8,128)(2,1)}, u32[]{:S(2)}, u32[]{:S(2)}) collective-permute-start(bf16[3,256,2048]{2,1,0:T(8,128)(2,1)} %pad_maximum_fusion.5), channel_id=1, source_target_pairs={{0,16},{16,0},{1,17},{17,1},{2,18},{18,2},{3,19},{19,3},{4,20},{20... | collective-permute-start | bytes 9437192 | tf_op jit(solution)/shard_map/ppermute | solution.py:76
  688.9 128.8 %copy-start.5 = (bf16[2,64,2048]{2,1,0:T(8,128)(2,1)S(1)}, bf16[2,64,2048]{2,1,0:T(8,128)(2,1)}, u32[]{:S(2)}) copy-start(bf16[2,64,2048]{2,1,0:T(8,128)(2,1)} %param.8) | copy-start | bytes 1572868
  688.9 128.8 %copy-start.70 = (f32[2048]{0:T(1024)S(1)}, f32[2048]{0:T(1024)}, u32[]{:S(2)}) copy-start(f32[2048]{0:T(1024)} %copy-done.69) | copy-start | bytes 24580
  689.3 128.5 %copy-start.37 = (bf16[16,8,8,256]{3,1,2,0:T(8,128)(2,1)}, bf16[16,8,8,256]{3,1,2,0:T(8,128)(2,1)S(1)}, u32[]{:S(2)}) copy-start(bf16[16,8,8,256]{3,1,2,0:T(8,128)(2,1)S(1)} %copy.68) | copy-start | bytes 1572868
  817.7 40.5 %copy-start.1 = (bf16[256,2048]{1,0:T(8,128)(2,1)S(1)}, bf16[256,2048]{1,0:T(8,128)(2,1)}, u32[]{:S(2)}) copy-start(bf16[256,2048]{1,0:T(8,128)(2,1)} %copy-done) | copy-start | bytes 3145732
  824.5 27.1 %all-to-all-start.1 = ((bf16[16,2,8192]{2,1,0:T(2,128)(2,1)}), bf16[16,2,8192]{2,1,0:T(2,128)(2,1)S(1)}, u32[]{:S(2)}, u32[]{:S(2)}) async-start(bf16[16,2,8192]{2,1,0:T(2,128)(2,1)} %reshape.416), calls=%async_computation.3 | async-start | bytes 1048576 | tf_op jit(solution)/shard_map/all_to_all | solution.py:131
  856.8 110.7 %collective-permute-start.6 = (bf16[3,256,2048]{2,1,0:T(8,128)(2,1)}, bf16[3,256,2048]{2,1,0:T(8,128)(2,1)}, u32[]{:S(2)}, u32[]{:S(2)}) collective-permute-start(bf16[3,256,2048]{2,1,0:T(8,128)(2,1)} %pad_maximum_fusion.6), channel_id=1, source_target_pairs={{0,16},{16,0},{1,17},{17,1},{2,18},{18,2},{3,19},{19,3},{4,20},{20... | collective-permute-start | bytes 9437192 | tf_op jit(solution)/shard_map/ppermute | solution.py:76
  859.9 70.8 %collective-permute-start.10 = (bf16[256,256]{1,0:T(8,128)(2,1)S(1)}, bf16[256,256]{1,0:T(8,128)(2,1)S(1)}, u32[]{:S(2)}, u32[]{:S(2)}) collective-permute-start(bf16[256,256]{1,0:T(8,128)(2,1)S(1)} %convolution_convert_fusion.17), channel_id=1, source_target_pairs={{0,16},{16,0},{1,17},{17,1},{2,18},{18,2},{3,19},{19,3},{4,20},{20... | collective-permute-start | bytes 393224 | tf_op jit(solution)/shard_map/ppermute | solution.py:76
  862.3 76.6 %copy-start.25 = (bf16[1,256,2048]{2,1,0:T(8,128)(2,1)S(1)}, bf16[1,256,2048]{2,1,0:T(8,128)(2,1)}, u32[]{:S(2)}) copy-start(bf16[1,256,2048]{2,1,0:T(8,128)(2,1)} %copy-done.24) | copy-start | bytes 3145732
  862.3 76.6 %copy-start.27 = (bf16[1,256,2048]{2,1,0:T(8,128)(2,1)S(1)}, bf16[1,256,2048]{2,1,0:T(8,128)(2,1)}, u32[]{:S(2)}) copy-start(bf16[1,256,2048]{2,1,0:T(8,128)(2,1)} %copy-done.26) | copy-start | bytes 3145732
  862.3 76.6 %copy-start.31 = (bf16[1,256,2048]{2,1,0:T(8,128)(2,1)S(1)}, bf16[1,256,2048]{2,1,0:T(8,128)(2,1)}, u32[]{:S(2)}) copy-start(bf16[1,256,2048]{2,1,0:T(8,128)(2,1)} %copy-done.30) | copy-start | bytes 3145732
  863.3 70.2 %collective-permute-start.9 = (bf16[256,256]{1,0:T(8,128)(2,1)S(1)}, bf16[256,256]{1,0:T(8,128)(2,1)S(1)}, u32[]{:S(2)}, u32[]{:S(2)}) collective-permute-start(bf16[256,256]{1,0:T(8,128)(2,1)S(1)} %convolution_convert_fusion.18), channel_id=1, source_target_pairs={{0,16},{16,0},{1,17},{17,1},{2,18},{18,2},{3,19},{19,3},{4,20},{20... | collective-permute-start | bytes 393224 | tf_op jit(solution)/shard_map/ppermute | solution.py:76
  864.8 71.6 %collective-permute-start.8 = (bf16[256,256]{1,0:T(8,128)(2,1)S(1)}, bf16[256,256]{1,0:T(8,128)(2,1)S(1)}, u32[]{:S(2)}, u32[]{:S(2)}) collective-permute-start(bf16[256,256]{1,0:T(8,128)(2,1)S(1)} %convolution_convert_fusion.19), channel_id=1, source_target_pairs={{0,16},{16,0},{1,17},{17,1},{2,18},{18,2},{3,19},{19,3},{4,20},{20... | collective-permute-start | bytes 393224 | tf_op jit(solution)/shard_map/ppermute | solution.py:76
  865.4 72.5 %collective-permute-start.7 = (bf16[256,256]{1,0:T(8,128)(2,1)S(1)}, bf16[256,256]{1,0:T(8,128)(2,1)S(1)}, u32[]{:S(2)}, u32[]{:S(2)}) collective-permute-start(bf16[256,256]{1,0:T(8,128)(2,1)S(1)} %convolution_convert_fusion.20), channel_id=1, source_target_pairs={{0,16},{16,0},{1,17},{17,1},{2,18},{18,2},{3,19},{19,3},{4,20},{20... | collective-permute-start | bytes 393224 | tf_op jit(solution)/shard_map/ppermute | solution.py:76
  950.8 25.6 %all-to-all-start.2 = ((bf16[16,2,8192]{2,1,0:T(2,128)(2,1)}), bf16[16,2,8192]{2,1,0:T(2,128)(2,1)S(1)}, u32[]{:S(2)}, u32[]{:S(2)}) async-start(bf16[16,2,8192]{2,1,0:T(2,128)(2,1)} %reshape.414), calls=%async_computation.4 | async-start | bytes 1048576 | tf_op jit(solution)/shard_map/all_to_all | solution.py:217
  977.9 26.2 %slice-start.1 = ((s8[13107200]{0:T(1024)(128)(4,1)}), s8[4194304]{0:T(1024)(128)(4,1)S(1)}, s32[]{:S(2)}) async-start(s8[13107200]{0:T(1024)(128)(4,1)} %bitcast.250), calls=%async_computation.15 | async-start | bytes 8388608
  982.7 21.4 %copy-start.38 = (bf16[16,8,8,256]{3,1,2,0:T(8,128)(2,1)S(1)}, bf16[16,8,8,256]{3,1,2,0:T(8,128)(2,1)}, u32[]{:S(2)}) copy-start(bf16[16,8,8,256]{3,1,2,0:T(8,128)(2,1)} %copy-done.37) | copy-start | bytes 1572868
  982.7 21.4 %slice-start.2 = ((s8[13107200]{0:T(1024)(128)(4,1)}), s8[4194304]{0:T(1024)(128)(4,1)S(1)}, s32[]{:S(2)}) async-start(s8[13107200]{0:T(1024)(128)(4,1)} %bitcast.250), calls=%async_computation.16 | async-start | bytes 8388608
  982.7 21.3 %slice-start.3 = ((s8[13107200]{0:T(1024)(128)(4,1)}), s8[4194304]{0:T(1024)(128)(4,1)S(1)}, s32[]{:S(2)}) async-start(s8[13107200]{0:T(1024)(128)(4,1)} %bitcast.250), calls=%async_computation.17 | async-start | bytes 8388608
  982.7 21.3 %slice-start.4 = ((s8[13107200]{0:T(1024)(128)(4,1)}), s8[524288]{0:T(1024)(128)(4,1)S(1)}, s32[]{:S(2)}) async-start(s8[13107200]{0:T(1024)(128)(4,1)} %bitcast.250), calls=%async_computation.18 | async-start | bytes 1048576
  982.7 21.3 %copy-start.73 = (bf16[128,128]{1,0:T(8,128)(2,1)S(1)}, bf16[128,128]{1,0:T(8,128)(2,1)}, u32[]{:S(2)}) copy-start(bf16[128,128]{1,0:T(8,128)(2,1)} %get-tuple-element.26) | copy-start | bytes 98308
  982.8 21.3 %copy-start.74 = (bf16[128,128]{1,0:T(8,128)(2,1)S(1)}, bf16[128,128]{1,0:T(8,128)(2,1)}, u32[]{:S(2)}) copy-start(bf16[128,128]{1,0:T(8,128)(2,1)} %get-tuple-element.24) | copy-start | bytes 98308
  982.8 20.2 %collective-permute-start.5 = (bf16[128,2048]{1,0:T(8,128)(2,1)S(1)}, bf16[128,2048]{1,0:T(8,128)(2,1)S(1)}, u32[]{:S(2)}, u32[]{:S(2)}) collective-permute-start(bf16[128,2048]{1,0:T(8,128)(2,1)S(1)} %fusion.49), channel_id=1, source_target_pairs={{0,16},{16,0},{1,17},{17,1},{2,18},{18,2},{3,19},{19,3},{4,20},{20... | collective-permute-start | bytes 1572872 | tf_op jit(solution)/shard_map/ppermute | solution.py:76
  1009.8 17.6 %all-to-all-start = ((f32[16,128,2]{1,2,0:T(2,128)}), f32[16,128,2]{1,2,0:T(2,128)S(1)}, u32[]{:S(2)}, u32[]{:S(2)}) async-start(f32[16,128,2]{1,2,0:T(2,128)} %copy.54), calls=%async_computation.2 | async-start | bytes 32768 | tf_op jit(solution)/shard_map/all_to_all | solution.py:283
  1025.0 22.1 %collective-permute-start.4 = (bf16[128,3328]{1,0:T(8,128)(2,1)}, bf16[128,3328]{1,0:T(8,128)(2,1)}, u32[]{:S(2)}, u32[]{:S(2)}) collective-permute-start(bf16[128,3328]{1,0:T(8,128)(2,1)} %pad_maximum_fusion.10), channel_id=1, source_target_pairs={{0,16},{16,0},{1,17},{17,1},{2,18},{18,2},{3,19},{19,3},{4,20},{20... | collective-permute-start | bytes 2555912 | tf_op jit(solution)/shard_map/ppermute | solution.py:76
  1027.5 21.9 %copy-start.32 = (f32[128,2048]{1,0:T(8,128)S(1)}, f32[128,2048]{1,0:T(8,128)}, u32[]{:S(2)}) copy-start(f32[128,2048]{1,0:T(8,128)} %convert_add_fusion.5) | copy-start | bytes 3145732
  1027.5 19.1 %collective-permute-start.3 = (bf16[128,2]{0,1:T(2,128)(2,1)S(1)}, bf16[128,2]{0,1:T(2,128)(2,1)S(1)}, u32[]{:S(2)}, u32[]{:S(2)}) collective-permute-start(bf16[128,2]{0,1:T(2,128)(2,1)S(1)} %reduce_sum.118), channel_id=1, source_target_pairs={{0,16},{16,0},{1,17},{17,1},{2,18},{18,2},{3,19},{19,3},{4,20},{20... | collective-permute-start | bytes 1544 | tf_op jit(solution)/shard_map/ppermute | solution.py:76
  (72 other events, 395.7 us)
Sparse Core Ops, SparseCore 0:
  12.2 106.3 all-gather.7
  131.1 39.7 all-gather.9
  173.7 79.6 all-gather.11
  255.4 72.7 all-gather.15
  330.8 72.8 all-gather.13
  405.9 79.5 all-gather.17
  517.4 101.7 reduce-scatter.2
  685.3 125.3 reduce-scatter.4
  817.8 110.9 all-gather.19

commit v3 on v2

--- a/solution.py
+++ b/solution.py
@@ -1,6 +1,10 @@
+import functools
+
 import jax
 import jax.numpy as jnp
 from jax import lax
+from jax.experimental import pallas as pl
+from jax.experimental.pallas import tpu as pltpu
 from jax.sharding import PartitionSpec as P
 
 HEADS = 8
@@ -74,6 +78,198 @@
 
 def swap_rep(values):
     return lax.ppermute(values, "rep", [(0, 1), (1, 0)])
+
+
+def grid_of(shards):
+    short = 2 if shards <= 16 else 4
+    return shards // (2 * short), short
+
+
+def neighbours(shards):
+    long_len, short_len = grid_of(shards)
+    me = lax.axis_index("fsdp")
+    return me, me // (2 * short_len), (me // 2) % short_len, me % 2
+
+
+def greet(shards, across):
+    long_len, short_len = grid_of(shards)
+    me, at_long, at_short, core = neighbours(shards)
+    barrier = pltpu.get_barrier_semaphore()
+    around = [
+        (me >= 0, {"fsdp": me + 1 - 2 * core}),
+        (at_long > 0, {"fsdp": me - 2 * short_len}),
+        (at_long < long_len - 1, {"fsdp": me + 2 * short_len}),
+        (at_short > 0, {"fsdp": me - 2}),
+        (at_short < short_len - 1, {"fsdp": me + 2}),
+    ]
+    if across:
+        around.append((me >= 0, {"rep": 1 - lax.axis_index("rep")}))
+    for has, peer in around:
+        @pl.when(has)
+        def _():
+            pl.semaphore_signal(barrier, inc=1, device_id=peer)
+    pl.semaphore_wait(barrier, sum(has.astype(jnp.int32) for has, _ in around))
+
+
+def gather_kernel(shards, widths, shared, *refs):
+    long_len, short_len = grid_of(shards)
+    count = len(widths)
+    own = refs[:count]
+    out = refs[count : 2 * count]
+    send_sem, recv_sem, own_sem = refs[2 * count :]
+    me, at_long, at_short, core = neighbours(shards)
+    stride = 2 * short_len
+    partner = {"fsdp": me + 1 - 2 * core}
+    half = shared // 2
+    parts = []
+    if shared:
+        rep = lax.axis_index("rep")
+        peer_rep = {"rep": 1 - rep}
+        parts.append((0, pl.multiple_of(rep * half, 128), half))
+        parts.append((0, shared, widths[0] - shared))
+        parts += [(k, 0, widths[k]) for k in range(1, count)]
+        other = (0, pl.multiple_of((1 - rep) * half, 128), half)
+    else:
+        parts += [(k, 0, widths[k]) for k in range(count)]
+        other = None
+    lanes = list(range(len(parts)))
+    away = len(parts)
+    if shared:
+        parts.append(other)
+
+    def copy(lane, way, slot, peer, fresh):
+        k, first, width = parts[lane]
+        columns = pl.ds(first, width)
+        there = out[k].at[:, slot, :, columns]
+        return pltpu.make_async_remote_copy(
+            src_ref=own[k].at[:, :, columns] if fresh else there,
+            dst_ref=there,
+            send_sem=send_sem.at[lane, way, slot],
+            recv_sem=recv_sem.at[away if way == 5 else lane, slot],
+            device_id=peer,
+        )
+
+    greet(shards, bool(shared))
+    done = []
+
+    def start(has, which, way, slot, peer, fresh=False):
+        @pl.when(has)
+        def _():
+            for lane in which:
+                copy(lane, way, slot, peer, fresh).start()
+
+        done.append((has, which, way, slot, peer, fresh))
+
+    def arrive(has, which, slot):
+        @pl.when(has)
+        def _():
+            for lane in which:
+                copy(lane, 0, slot, partner, False).wait_recv()
+
+    late = []
+
+    def got(has, slot):
+        if shared:
+            start(has, [0], 5, slot, peer_rep)
+            late.append((has, slot))
+        start(has, lanes, 4, slot, partner)
+
+    def from_across():
+        for has, slot in late:
+            arrive(has, [away], slot)
+            start(has, [away], 4, slot, partner)
+        late.clear()
+
+    def spread_short(has, slot, fresh=False):
+        start(has & (at_short < short_len - 1), lanes, 2, slot, {"fsdp": me + 2}, fresh)
+        start(has & (at_short > 0), lanes, 3, slot, {"fsdp": me - 2}, fresh)
+
+    def short_arrivals(has, line):
+        for far in range(1, short_len):
+            for sign in (-1, 1):
+                source = at_short + sign * far
+                ok = has & (source >= 0) & (source < short_len)
+                slot = me + 2 * sign * far + (line - at_long) * stride
+                arrive(ok, lanes, slot)
+                if far < short_len - 1:
+                    onward = at_short - sign
+                    start(
+                        ok & (onward >= 0) & (onward < short_len),
+                        lanes,
+                        2 if sign < 0 else 3,
+                        slot,
+                        {"fsdp": me - 2 * sign},
+                    )
+                got(ok, slot)
+
+    true = me >= 0
+    start(at_long < long_len - 1, lanes, 0, me, {"fsdp": me + stride}, True)
+    start(at_long > 0, lanes, 1, me, {"fsdp": me - stride}, True)
+    spread_short(true, me, True)
+    every = list(range(len(parts)))
+    start(true, every, 4, me, partner, True)
+    mine = [pltpu.make_async_copy(own[k], out[k].at[:, me], own_sem.at[k]) for k in range(count)]
+    for each in mine:
+        each.start()
+    for far in range(1, long_len):
+        for sign in (-1, 1):
+            source = at_long + sign * far
+            ok = (source >= 0) & (source < long_len)
+            slot = me + sign * far * stride
+            arrive(ok, lanes, slot)
+            onward = at_long - sign
+            start(
+                ok & (onward >= 0) & (onward < long_len),
+                lanes,
+                0 if sign < 0 else 1,
+                slot,
+                {"fsdp": me - sign * stride},
+            )
+            spread_short(ok, slot)
+            got(ok, slot)
+        if far == 1:
+            short_arrivals(true, at_long)
+        else:
+            for sign in (-1, 1):
+                source = at_long + sign * (far - 1)
+                short_arrivals((source >= 0) & (source < long_len), source)
+        if far > 1:
+            from_across()
+    for sign in (-1, 1):
+        source = at_long + sign * (long_len - 1)
+        short_arrivals((source >= 0) & (source < long_len), source)
+    from_across()
+    for line in range(long_len):
+        for short in range(short_len):
+            arrive(true, every, (line * short_len + short) * 2 + 1 - core)
+    for has, which, way, slot, peer, fresh in done:
+        @pl.when(has)
+        def _():
+            for lane in which:
+                copy(lane, way, slot, peer, fresh).wait_send()
+    for each in mine:
+        each.wait()
+
+
+def gather_all(shards, ident, *values, shared=0):
+    widths = tuple(v.shape[2] for v in values)
+    count = len(values)
+    lanes = count + (2 if shared else 0)
+    return pl.pallas_call(
+        functools.partial(gather_kernel, shards, widths, shared),
+        out_shape=[
+            jax.ShapeDtypeStruct((v.shape[0], shards) + v.shape[1:], v.dtype) for v in values
+        ],
+        in_specs=[pl.BlockSpec(memory_space=pltpu.VMEM)] * count,
+        out_specs=[pl.BlockSpec(memory_space=pl.ANY)] * count,
+        scratch_shapes=[
+            pltpu.SemaphoreType.DMA((lanes, 6, shards)),
+            pltpu.SemaphoreType.DMA((lanes, shards)),
+            pltpu.SemaphoreType.DMA((count,)),
+        ],
+        compiler_params=pltpu.CompilerParams(collective_id=ident, has_side_effects=True),
+        name="gather_%d" % ident,
+    )(*values)
 
 
 def local(
@@ -95,29 +291,22 @@
     seg_cols = count // attn_rows
     seg_block = low(segment_ids).reshape(attn_rows, seg_cols)
     spare = jnp.zeros((attn_rows, 128 - 2 - seg_cols), jnp.bfloat16)
-    first = gather_rows(
-        jnp.concatenate(
-            [
-                attn_weight[:, :kv_end],
-                adapter[:, : 2 * RANK],
-                norm_gains,
-                seg_block,
-                spare,
-            ],
-            axis=1,
-        )
-    )
-    second = gather_rows(jnp.concatenate([attn_weight[:, kv_end:], adapter[:, 2 * RANK :]], axis=1))
-    extra = kv_end + 2 * RANK
-    w_proj = first[:, :kv_end]
-    a_q = first[:, kv_end : kv_end + RANK]
-    bq_t = first[:, kv_end + RANK : extra]
-    gain_two = first[:, extra : extra + 2].astype(jnp.float32)
-    seg_all = first[:, extra + 2 : extra + 2 + seg_cols].reshape(shards, micro, local_len)
+    small = jnp.concatenate([norm_gains, seg_block, spare], axis=1)
+    same = kv_end + 4 * RANK
+    attn_all, adapter_all, small_all = gather_all(
+        shards, 1, attn_weight[None], adapter[None], small[None], shared=same
+    )
+    cotangent_now, small_all = lax.optimization_barrier((cotangent, small_all))
+    cot_all = gather_rows(cotangent_now).reshape(every, model_dim)
+    attn_all = attn_all.reshape(model_dim, attn_weight.shape[1])
+    adapter_all = adapter_all.reshape(model_dim, 3 * RANK)
+    small_all = small_all.reshape(model_dim, 128)
+    w_proj = attn_all[:, :kv_end]
+    w_out = attn_all[:, kv_end:]
+    a_q, bq_t, bd_t = (adapter_all[:, j * RANK : (j + 1) * RANK] for j in range(3))
+    gain_two = small_all[:, :2].astype(jnp.float32)
+    seg_all = small_all[:, 2 : 2 + seg_cols].reshape(shards, micro, local_len)
     seg_all = seg_all.transpose(1, 0, 2).reshape(micro, seq_len).astype(jnp.int32)
-    w_out = second[:, :q_width]
-    bd_t = second[:, q_width:]
-    cot_all = gather_rows(cotangent).reshape(every, model_dim)
 
     hidden_in = tokens.reshape(count, model_dim).astype(jnp.float32)
     key_index = jnp.arange(seq_len, dtype=jnp.int32)
@@ -128,9 +317,6 @@
     angles = angles_of(query_index[None, :] - before).reshape(count, HD // 2)
     normed, norm_back_one = jax.vjp(rms_scale, hidden_in, gain_two[:, 0])
     normed_low = low(normed)
-    normed_cols = lax.all_to_all(
-        normed_low.reshape(micro, local_len, model_dim), "fsdp", 2, 1, tiled=True
-    ).reshape(every, attn_rows)
     projected = contract(normed_low, w_proj, 1, 0)
     query_low = low(contract(normed_low, a_q, 1, 0))
     query_pre = projected[:, :q_width] + contract(query_low, bq_t, 1, 1)
@@ -138,11 +324,15 @@
     queries = queries.reshape(micro, local_len * HEADS, HD)
     keys_low = low(rotate(projected[:, q_width : q_width + HD], angles))
     values_low = low(projected[:, q_width + HD :])
-    kv_all = gather_rows(
-        jnp.concatenate([keys_low, values_low], axis=1).reshape(micro, local_len, 2 * HD)
-    )
-    keys_all = kv_all[..., :HD]
-    values_all = kv_all[..., HD:]
+    keys_all, values_all = (
+        each.reshape(micro, seq_len, HD)
+        for each in gather_all(
+            shards,
+            2,
+            keys_low.reshape(micro, local_len, HD),
+            values_low.reshape(micro, local_len, HD),
+        )
+    )
     allowed = (
         (segment_ids[:, :, None] == seg_all[:, None, :])
         & (key_index[None, None, :] <= query_index[None, :, None])
@@ -158,15 +348,17 @@
     context = low(batched(weights_low, values_all, 2, 1)).reshape(count, q_width)
     mixed_sum = hidden_in + contract(context, w_out, 1, 1)
     normed_two, norm_back_two = jax.vjp(rms_scale, mixed_sum, gain_two[:, 1])
-    inputs_all = gather_rows(low(normed_two).reshape(micro, local_len, model_dim))
+    (inputs_all,) = gather_all(shards, 3, low(normed_two).reshape(micro, local_len, model_dim))
     inputs_all = inputs_all.reshape(every, model_dim)
-    kept_all = gather_rows(
-        jnp.concatenate([context, query_low], axis=1).reshape(micro, local_len, q_width + RANK)
-    ).reshape(every, q_width + RANK)
+    kept, inputs_all = lax.optimization_barrier(
+        (jnp.concatenate([context, query_low], axis=1), inputs_all)
+    )
+    kept_all = gather_rows(kept.reshape(micro, local_len, q_width + RANK))
+    kept_all = kept_all.reshape(every, q_width + RANK)
     low_grad_all = low(contract(cot_all, bd_t, 1, 0))
 
     step = hidden_cols // CHUNKS
-    hidden_parts, gate_parts, up_parts, ffn_parts, low_parts = [], [], [], [], []
+    hidden_parts, gate_parts, up_parts, ffn_parts = [], [], [], []
     for at in range(CHUNKS):
         units = slice(at * step, (at + 1) * step)
         w_gate, w_up, w_down = (ffn_weight[units, j, :] for j in range(3))
@@ -179,19 +371,13 @@
         )
         gate_grad = low(gelu_back(hidden_grad * up_pre)[0])
         up_grad = low(hidden_grad * activated)
-        mine = low(
-            jnp.stack(
-                [
-                    contract(gate_grad, inputs_all, 0, 0),
-                    contract(up_grad, inputs_all, 0, 0),
-                    contract(hidden_act, cot_all, 0, 0),
-                ],
-                axis=0,
-            )
-        )
-        mine_low = low(contract(hidden_act, low_grad_all, 0, 0))
-        ffn_parts.append((mine, swap_rep(mine)))
-        low_parts.append((mine_low, swap_rep(mine_low)))
+        for left, right in (
+            (gate_grad, inputs_all),
+            (up_grad, inputs_all),
+            (hidden_act, cot_all),
+        ):
+            mine = low(contract(left, right, 0, 0))
+            ffn_parts.append((mine, swap_rep(mine)))
         hidden_parts.append(hidden_act)
         gate_parts.append(gate_grad)
         up_parts.append(up_grad)
@@ -199,6 +385,7 @@
     gate_grad = jnp.concatenate(gate_parts, axis=1)
     up_grad = jnp.concatenate(up_parts, axis=1)
     hidden_act = jnp.concatenate(hidden_parts, axis=1)
+    low_mine = low(contract(hidden_act, low_grad_all, 0, 0))
     gate_grad, kept_all = lax.optimization_barrier((gate_grad, kept_all))
     normed_two_grad = sum_rows(
         low(
@@ -207,16 +394,18 @@
         ).reshape(micro, seq_len, model_dim)
     )
     normed_two_grad, _ = lax.optimization_barrier(
-        (normed_two_grad, [pair[0] for pair in ffn_parts] + [ffn_parts[0][1]])
+        (normed_two_grad, [pair[0] for pair in ffn_parts] + [pair[1] for pair in ffn_parts[:4]])
     )
     normed_two_grad = normed_two_grad.reshape(count, model_dim).astype(jnp.float32)
     cot_full = cotangent.reshape(count, model_dim).astype(jnp.float32)
     mixed_part, gain_two_grad = norm_back_two(normed_two_grad)
     mixed_grad = cot_full + mixed_part
     out_grad_low = low(mixed_grad)
-    out_cols = lax.all_to_all(
-        out_grad_low.reshape(micro, local_len, model_dim), "fsdp", 2, 1, tiled=True
-    ).reshape(every, attn_rows)
+    both = jnp.concatenate([normed_low, out_grad_low], axis=0)
+    both_cols = lax.all_to_all(
+        both.reshape(2 * micro, local_len, model_dim), "fsdp", 2, 1, tiled=True
+    ).reshape(2, every, attn_rows)
+    normed_cols, out_cols = both_cols[0], both_cols[1]
     wout_grad = contract(out_cols, kept_all[:, :q_width], 0, 0)
     context_grad = contract(out_grad_low, w_out, 1, 0)
     context_rows = low(context_grad).reshape(micro, local_len * HEADS, HD)
@@ -234,7 +423,7 @@
             axis=2,
         )
     )
-    kv_part, _ = lax.optimization_barrier((kv_part, ffn_parts[1][1]))
+    kv_part, _ = lax.optimization_barrier((kv_part, [pair[1] for pair in ffn_parts[4:6]]))
     sums = sum_rows(
         jnp.concatenate(
             [
@@ -247,7 +436,7 @@
             axis=2,
         )
     )
-    sums, _ = lax.optimization_barrier((sums, ffn_parts[2][1]))
+    sums, _ = lax.optimization_barrier((sums, [pair[1] for pair in ffn_parts[6:10]]))
     sums = sums.reshape(count, model_dim + RANK + 2 * HD)
     kv_grad = sums[:, model_dim + RANK :]
     down_low = sums[:, model_dim : model_dim + RANK]
@@ -263,19 +452,31 @@
     hidden_part, gain_one_grad = norm_back_one(normed_grad)
     input_grad = low(mixed_grad + hidden_part)
 
-    back_all = gather_rows(
-        jnp.concatenate([proj_grad, rank_grad, down_low], axis=1).reshape(
-            micro, local_len, kv_end + 2 * RANK
-        )
-    ).reshape(every, kv_end + 2 * RANK)
+    narrow = jnp.concatenate([key_grad, value_grad, rank_grad, down_low], axis=1)
+    q_all, narrow_all = (
+        each.reshape(every, -1)
+        for each in gather_all(
+            shards,
+            4,
+            query_pre_grad.reshape(micro, local_len, q_width),
+            narrow.reshape(micro, local_len, 2 * HD + 2 * RANK),
+        )
+    )
+    narrow_all, _ = lax.optimization_barrier((narrow_all, [pair[1] for pair in ffn_parts[10:]]))
     my_cols = me * attn_rows
-    attn_in = contract(normed_cols, back_all[:, : kv_end + RANK], 0, 0)
+    attn_in = jnp.concatenate(
+        [
+            contract(normed_cols, q_all, 0, 0),
+            contract(normed_cols, narrow_all[:, : 2 * HD + RANK], 0, 0),
+        ],
+        axis=1,
+    )
     bq_grad = contract(
-        lax.dynamic_slice_in_dim(back_all, my_cols, attn_rows, 1), kept_all[:, q_width:], 0, 0
+        lax.dynamic_slice_in_dim(q_all, my_cols, attn_rows, 1), kept_all[:, q_width:], 0, 0
     )
     bd_grad = contract(
         lax.dynamic_slice_in_dim(cot_all, my_cols, attn_rows, 1),
-        back_all[:, kv_end + RANK :],
+        narrow_all[:, 2 * HD + RANK :],
         0,
         0,
     )
@@ -293,8 +494,13 @@
     gains_grad = total(tail_gain, swap_rep(tail_gain))
     attn_grad = jnp.concatenate([tail[:, :kv_end], tail_out], axis=1)
     adapter_grad = tail[:, kv_end:]
-    ffn_grad = jnp.concatenate([total(*pair) for pair in ffn_parts], axis=1).transpose(1, 0, 2)
-    ffn_low_grad = jnp.concatenate([total(*pair) for pair in low_parts], axis=0)
+    ffn_grad = jnp.zeros((3, hidden_cols, model_dim), jnp.float32)
+    for at, pair in enumerate(ffn_parts):
+        ffn_grad = lax.dynamic_update_slice(
+            ffn_grad, total(*pair)[None], (at % 3, at // 3 * step, 0)
+        )
+    ffn_grad = ffn_grad.transpose(1, 0, 2)
+    ffn_low_grad = total(low_mine, swap_rep(low_mine))
     return (
         low(result).reshape(micro, local_len, model_dim),
         input_grad.reshape(micro, local_len, model_dim),

time: 1070 us -> 850 us (0.79)
  waiting for transfers between devices: 659 us -> 166 us
  Pallas kernels: 0 us -> 287 us
  other arithmetic: 86.1 us -> 74 us
    all_gather x7 -> x2, waiting for transfers between devices: 349 us -> 2.64 us  [gather_rows(): return lax.all_gather(values, 'fsdp', axis=values.ndim - 2, tiled=True)]
    pallas_call x0 -> x4, Pallas kernels: none -> 287 us  [gather_all(): pl.pallas_call(functools.partial(gather_kernel, shards, widths, shared),...]
    reduce_scatter x2, waiting for transfers between devices: 69.9 us -> 1.77 us  [sum_rows(): return lax.psum_scatter(values, 'fsdp', scatter_dimension=1, tiled=True)]
    ppermute x11 -> x16, waiting for transfers between devices: 213 us -> 162 us  [swap_rep(): return lax.ppermute(values, 'rep', [(0, 1), (1, 0)])]
    dynamic_update_slice x0 -> x11, other arithmetic: none -> 33.9 us  [local(): lax.dynamic_update_slice(ffn_grad, total(*pair)[None], (at % 3, at // 3 *...]
    all_to_all x2 -> x1, waiting for transfers between devices: 27.4 us -> 0.01 us  [local(): lax.all_to_all(both.reshape(2 * micro, local_len, model_dim), 'fsdp', 2,...]
    transpose x1 -> x0, other arithmetic: 19.1 us -> none  [local(): jnp.concatenate([total(*pair) for pair in ffn_parts], axis=1)]
    add x11 -> x4, other arithmetic: 22.5 us -> 5.3 us  [total(): return mine.astype(jnp.float32) + other.astype(jnp.float32)]
  transfers between devices with their start and end apart: 23 -> 22, of which waited for: 18 -> 14; matrix products, arithmetic and copies ran while one was open for 25% -> 32% of each run, Pallas kernels for 0% -> 21%
where the time goes in v3:
time: 850 us; the launch traced here: 842 us
  Pallas kernels  287 us (34%)
  matrix products  228 us (27%)
  waiting for transfers between devices  166 us (20%)
  other arithmetic  74 us (9%)
  local copies, waits for them, and re-layouts  45.1 us (5%)
  starting transfers between devices  25.9 us (3%)
  between operations  15.3 us (2%)
    pallas_call x4, Pallas kernels, gather_all(): pl.pallas_call(functools.partial(gather_kernel, shards, widths, shared),...  287 us
    dot_general x48, matrix products, contract(): lax.dot_general(left_op, right_op, (((left_dim,), (right_dim,)), ((), ())...  219 us
    ppermute x16, waiting for transfers between devices, swap_rep(): return lax.ppermute(values, 'rep', [(0, 1), (1, 0)])  162 us
    dynamic_update_slice x11, other arithmetic, local(): lax.dynamic_update_slice(ffn_grad, total(*pair)[None], (at % 3, at // 3 *...  33.9 us
    ppermute x16, starting transfers between devices, swap_rep(): return lax.ppermute(values, 'rep', [(0, 1), (1, 0)])  17.8 us
  transfers between devices with their start and end apart: 22, of which 14 were waited for; matrix products, arithmetic and copies ran while one was open for 32% of the time, Pallas kernels for 21%

profile of v3, /device:TPU:0, one launch (start us, length us, event | category | flops | bytes accessed | tf_op | source)
XLA Modules:
  0.0 841.6 jit_solution(9710566024879038442)
XLA Ops:
  9.7 109.0 %gather_1.1 = (bf16[1,16,128,4608]{3,2,1,0:T(8,128)(2,1)}, bf16[1,16,128,768]{3,2,1,0:T(8,128)(2,1)}, bf16[1,16,128,128]{3,2,1,0:T(8,128)(2,1)}) custom-call(bf16[1,128,4608]{2,1,0:T(8,128)(2,1)} %bitcast.287, bf16[1,128,768]{2,1,0:T(8,128)(2,1)} %bitcast.307, bf16[1,128,128]{2,1,0:T(8,128)(2,1)} %maximum_bitcast_fusion.refs_2_), custom_call_target="tpu_custom_call" | custom-call | tf_op jit(solution)/shard_map/gather_1/pallas_call | solution.py:258
  123.9 5.9 fusion.3
  133.5 33.2 %gather_2.1 = (bf16[2,16,64,256]{3,2,1,0:T(8,128)(2,1)}, bf16[2,16,64,256]{3,2,1,0:T(8,128)(2,1)}) custom-call(bf16[2,64,256]{2,1,0:T(8,128)(2,1)} %pad_maximum_fusion.11.refs_0_, bf16[2,64,256]{2,1,0:T(8,128)(2,1)} %bitcast.302), custom_call_target="tpu_custom_call" | custom-call | tf_op jit(solution)/shard_map/gather_2/pallas_call | solution.py:258
  174.4 6.4 multiply_reduce_fusion.1
  182.8 64.5 %gather_3.1 = bf16[2,16,64,2048]{3,2,1,0:T(8,128)(2,1)} custom-call(bf16[2,64,2048]{2,1,0:T(8,128)(2,1)} %bitcast.284), custom_call_target="tpu_custom_call" | custom-call | tf_op jit(solution)/shard_map/gather_3/pallas_call | solution.py:258
  248.7 6.1 fusion.90
  254.8 7.6 fusion.94
  262.5 4.9 fusion.98
  267.4 4.9 fusion.102
  272.3 6.1 fusion.80
  278.5 3.9 convolution_convert_fusion.14
  282.9 3.8 fusion.82
  287.1 3.6 fusion.84
  291.2 3.9 fusion.86
  295.7 6.7 multiply_convert_fusion.6
  302.3 6.4 multiply_convert_fusion.7
  308.8 6.5 multiply_convert_fusion.8
  315.3 6.3 multiply_convert_fusion.9
  327.5 15.8 %fusion.19 = f32[2048,2048]{1,0:T(8,128)} fusion(bf16[2048,1024]{0,1:T(8,128)(2,1)} %pad_maximum_fusion.2, bf16[1024,3,2048]{2,0,1:T(8,128)(2,1)} %param.13), kind=kOutput, calls=%fused_computation.24 | convolution fusion | flops 8589934592 | bytes 25165824 | tf_op jit(solution)/shard_map/dot_general | solution.py:50
  343.3 16.4 %add_convert_fusion = bf16[2048,2048]{1,0:T(8,128)(2,1)} fusion(f32[2048,2048]{1,0:T(8,128)} %fusion.19, bf16[2048,256]{0,1:T(8,128)(2,1)} %get-tuple-element.51, bf16[2048,256]{0,1:T(8,128)(2,1)} %get-tuple-element.54, bf16[2048,256]{0,1:T(8,128)(2,1)} %get-tuple-element.57, bf16[2048,256]{0,1:T(8,128)(2,1)} %get-tuple-element.60, ...), kind=kOutput, calls=%fused_computation.1 | convolution fusion | flops 8615100416 | bytes 33554432 | tf_op jit(solution)/shard_map/dot_general | solution.py:50
  359.9 6.3 convolution_convert_fusion.13
  367.7 7.5 convolution_convert_fusion.12
  383.0 3.4 convolution_convert_fusion.9
  386.4 3.4 convolution_convert_fusion.7
  389.8 3.6 convolution_convert_fusion.6
  393.4 3.4 convolution_convert_fusion.4
  396.8 3.4 convolution_convert_fusion.3
  400.2 3.4 convolution_convert_fusion.8
  403.6 3.4 convolution_convert_fusion.5
  407.0 13.7 %convolution_convert_fusion = bf16[2048,2048]{1,0:T(8,128)(2,1)} fusion(bf16[1024,3,2048]{2,0,1:T(8,128)(2,1)} %param.13, bf16[2048,256]{0,1:T(8,128)(2,1)S(1)} %copy-done.68, bf16[2048,256]{0,1:T(8,128)(2,1)S(1)} %copy-done.69, bf16[2048,256]{0,1:T(8,128)(2,1)} %get-tuple-element.55, bf16[2048,256]{0,1:T(8,128)(2,1)} %get-tuple-element.58), kind=kOutput, calls=%fused_computation.9 | convolution fusion | flops 8610906112 | bytes 16777216 | tf_op jit(solution)/shard_map/dot_general | solution.py:50
  424.9 6.9 convolution_convert_fusion.2
  432.7 4.5 collective-permute-done.2
  438.2 21.6 %collective-permute-done.3 = bf16[256,2048]{1,0:T(8,128)(2,1)} collective-permute-done((bf16[256,2048]{1,0:T(8,128)(2,1)S(1)}, bf16[256,2048]{1,0:T(8,128)(2,1)}, u32[]{:S(2)}, u32[]{:S(2)}) %collective-permute-start.3) | collective-permute-done | bytes 1048608 | tf_op jit(solution)/shard_map/ppermute | solution.py:80
  465.2 4.7 fusion.32
  470.2 3.2 multiply_reduce_fusion
  476.5 5.8 collective-permute-done.4
  482.3 21.7 %collective-permute-done.5 = bf16[256,2048]{1,0:T(8,128)(2,1)} collective-permute-done((bf16[256,2048]{1,0:T(8,128)(2,1)}, bf16[256,2048]{1,0:T(8,128)(2,1)}, u32[]{:S(2)}, u32[]{:S(2)}) %collective-permute-start.5) | collective-permute-done | bytes 1048608 | tf_op jit(solution)/shard_map/ppermute | solution.py:80
  506.5 11.3 %pad_maximum_fusion = bf16[2,1024,2816]{2,1,0:T(8,128)(2,1)} fusion(bf16[2,1024,512]{2,1,0:T(8,128)(2,1)} %copy.36, bf16[2,1024,256]{2,1,0:T(8,128)(2,1)} %bitcast.288, bf16[2,1024,2048]{2,1,0:T(8,128)(2,1)} %bitcast.268), kind=kLoop, calls=%fused_computation.2 | loop fusion | flops 34603008 | bytes 23068672 | tf_op jit(solution)/shard_map/concatenate | solution.py:428
  519.0 3.2 convolution_convert_fusion.17
  527.8 9.3 %collective-permute-done.15 = bf16[1024,256]{1,0:T(8,128)(2,1)S(1)} collective-permute-done((bf16[1024,256]{1,0:T(8,128)(2,1)S(1)}, bf16[1024,256]{1,0:T(8,128)(2,1)S(1)}, u32[]{:S(2)}, u32[]{:S(2)}) %collective-permute-start.15) | collective-permute-done | bytes 524320 | tf_op jit(solution)/shard_map/ppermute | solution.py:80
  541.6 12.5 %dynamic_update_slice.36 = f32[3,1024,2048]{2,1,0:T(8,128)} pad(f32[1,256,2048]{2,1,0:T(8,128)S(1)} %add_bitcast_fusion, f32[]{:T(128)} %constant.29.clone.1), padding=0_2x0_768x0_0 | pad | bytes 27262980 | tf_op jit(solution)/shard_map/dynamic_update_slice | solution.py:499
  554.1 3.4 bitcast_dynamic-update-slice_fusion.10
  562.1 3.3 bitcast_dynamic-update-slice_fusion.7
  565.4 3.2 bitcast_dynamic-update-slice_fusion.6
  569.4 3.2 bitcast_dynamic-update-slice_fusion.5
  572.6 9.5 %collective-permute-done.7 = bf16[256,2048]{1,0:T(8,128)(2,1)} collective-permute-done((bf16[256,2048]{1,0:T(8,128)(2,1)}, bf16[256,2048]{1,0:T(8,128)(2,1)}, u32[]{:S(2)}, u32[]{:S(2)}) %collective-permute-start.7) | collective-permute-done | bytes 1048608 | tf_op jit(solution)/shard_map/ppermute | solution.py:80
  582.1 3.2 bitcast_dynamic-update-slice_fusion.4
  591.5 3.9 all-to-all-start.1
  595.4 9.2 %collective-permute-done.8 = bf16[256,2048]{1,0:T(8,128)(2,1)} collective-permute-done((bf16[256,2048]{1,0:T(8,128)(2,1)}, bf16[256,2048]{1,0:T(8,128)(2,1)}, u32[]{:S(2)}, u32[]{:S(2)}) %collective-permute-start.8) | collective-permute-done | bytes 1048608 | tf_op jit(solution)/shard_map/ppermute | solution.py:80
  604.6 3.2 bitcast_dynamic-update-slice_fusion.3
  607.8 19.2 %collective-permute-done.9 = bf16[256,2048]{1,0:T(8,128)(2,1)} collective-permute-done((bf16[256,2048]{1,0:T(8,128)(2,1)}, bf16[256,2048]{1,0:T(8,128)(2,1)}, u32[]{:S(2)}, u32[]{:S(2)}) %collective-permute-start.9) | collective-permute-done | bytes 1048608 | tf_op jit(solution)/shard_map/ppermute | solution.py:80
  627.1 3.2 bitcast_dynamic-update-slice_fusion.2
  630.3 19.2 %collective-permute-done.11 = bf16[256,2048]{1,0:T(8,128)(2,1)} collective-permute-done((bf16[256,2048]{1,0:T(8,128)(2,1)}, bf16[256,2048]{1,0:T(8,128)(2,1)}, u32[]{:S(2)}, u32[]{:S(2)}) %collective-permute-start.11) | collective-permute-done | bytes 1048608 | tf_op jit(solution)/shard_map/ppermute | solution.py:80
  649.5 3.2 bitcast_dynamic-update-slice_fusion.1
  652.8 17.6 %collective-permute-done.12 = bf16[256,2048]{1,0:T(8,128)(2,1)} collective-permute-done((bf16[256,2048]{1,0:T(8,128)(2,1)}, bf16[256,2048]{1,0:T(8,128)(2,1)}, u32[]{:S(2)}, u32[]{:S(2)}) %collective-permute-start.12) | collective-permute-done | bytes 1048608 | tf_op jit(solution)/shard_map/ppermute | solution.py:80
  670.4 3.2 bitcast_dynamic-update-slice_fusion
  675.9 3.0 copy.40
  679.8 5.6 fusion.35
  689.0 9.0 %collective-permute-done.14 = bf16[128,2048]{1,0:T(8,128)(2,1)} collective-permute-done((bf16[128,2048]{1,0:T(8,128)(2,1)}, bf16[128,2048]{1,0:T(8,128)(2,1)}, u32[]{:S(2)}, u32[]{:S(2)}) %collective-permute-start.14) | collective-permute-done | bytes 524320 | tf_op jit(solution)/shard_map/ppermute | solution.py:80
  705.2 6.3 fusion.1
  715.0 3.5 all-to-all-start
  718.5 80.4 %gather_4.1 = (bf16[2,16,64,2048]{3,2,1,0:T(8,128)(2,1)}, bf16[2,16,64,1024]{3,2,1,0:T(8,128)(2,1)}) custom-call(bf16[2,64,2048]{2,1,0:T(8,128)(2,1)} %convert_element_type.362.refs_0_, bf16[2,64,1024]{2,1,0:T(8,128)(2,1)} %bitcast.299), custom_call_target="tpu_custom_call" | custom-call | tf_op jit(solution)/shard_map/gather_4/pallas_call | solution.py:258
  798.9 4.8 fusion.31
  815.0 15.4 %collective-permute-done.10 = bf16[128,2]{0,1:T(2,128)(2,1)S(1)} collective-permute-done((bf16[128,2]{0,1:T(2,128)(2,1)S(1)}, bf16[128,2]{0,1:T(2,128)(2,1)S(1)}, u32[]{:S(2)}, u32[]{:S(2)}) %collective-permute-start.10) | collective-permute-done | bytes 544 | tf_op jit(solution)/shard_map/ppermute | solution.py:80
  (306 shorter events, 112.5 us)
Async XLA Ops:
  7.2 115.6 %copy-start.6 = (bf16[2,64,2048]{2,1,0:T(8,128)(2,1)S(1)}, bf16[2,64,2048]{2,1,0:T(8,128)(2,1)}, u32[]{:S(2)}) copy-start(bf16[2,64,2048]{2,1,0:T(8,128)(2,1)} %param.8) | copy-start | bytes 1572868
  7.2 265.1 %all-gather.3.cloned.1.call-start = ((), (), s32[]{:S(2)}) async-start(), calls=%async_computation.4 | async-start | bytes 8912896 | tf_op jit(solution)/shard_map/all_gather | solution.py:72
  118.7 208.8 %all-gather.5.cloned.1.call-start = ((), (), s32[]{:S(2)}) async-start(), calls=%async_computation.5 | async-start | bytes 10027008 | tf_op jit(solution)/shard_map/all_gather | solution.py:72
  123.7 57.3 %copy-start.43 = (f32[2048,1]{0,1:T(1,128)}, f32[2048,1]{0,1:T(1,128)S(1)}, u32[]{:S(2)}) copy-start(f32[2048,1]{0,1:T(1,128)S(1)} %get-tuple-element.71) | copy-start | bytes 24580
  123.9 6.6 copy-start.19
  123.9 6.6 copy-start.16
  129.8 37.0 %copy-start.58 = (s32[2,64]{1,0:T(2,128)S(1)}, s32[2,64]{1,0:T(2,128)}, u32[]{:S(2)}) copy-start(s32[2,64]{1,0:T(2,128)} %param.9) | copy-start | bytes 1540
  180.9 66.5 %copy-start.63 = (f32[128]{0:T(128)}, f32[128]{0:T(128)S(1)}, u32[]{:S(2)}) copy-start(f32[128]{0:T(128)S(1)} %get-tuple-element.81) | copy-start | bytes 1540
  180.9 66.5 %copy-start.48 = (f32[128]{0:T(128)}, f32[128]{0:T(128)S(1)}, u32[]{:S(2)}) copy-start(f32[128]{0:T(128)S(1)} %fusion.151) | copy-start | bytes 1540
  248.2 213.3 %reduce-scatter.3.cloned.1.call-start = ((), (), s32[]{:S(2)}) async-start(), calls=%async_computation.6 | async-start | bytes 8912896 | tf_op jit(solution)/shard_map/reduce_scatter | solution.py:76
  248.7 13.8 %slice-start = ((s8[8388608]{0:T(1024)(128)(4,1)}), s8[4194304]{0:T(1024)(128)(4,1)S(1)}, s32[]{:S(2)}) async-start(s8[8388608]{0:T(1024)(128)(4,1)} %bitcast.249), calls=%async_computation.8 | async-start | bytes 8388608
  254.8 7.6 slice-start.1
  282.4 12.7 %copy-start.2 = (bf16[2048,256]{1,0:T(8,128)(2,1)}, bf16[2048,256]{1,0:T(8,128)(2,1)S(1)}, u32[]{:S(2)}) copy-start(bf16[2048,256]{1,0:T(8,128)(2,1)S(1)} %convolution_convert_fusion.14) | copy-start | bytes 3145732
  295.6 6.7 copy-start.67
  302.3 6.4 copy-start.66
  308.8 6.5 copy-start.65
  359.7 340.7 %reduce-scatter.5.cloned.1.call-start = ((), (), s32[]{:S(2)}) async-start(), calls=%async_computation.7 | async-start | bytes 12255232 | tf_op jit(solution)/shard_map/reduce_scatter | solution.py:76
  359.9 7.8 copy-start.77
  359.9 16.1 %slice-start.6 = ((s8[8388608]{0:T(1024)(128)(4,1)}), s8[4194304]{0:T(1024)(128)(4,1)S(1)}, s32[]{:S(2)}) async-start(s8[8388608]{0:T(1024)(128)(4,1)} %bitcast.329), calls=%async_computation.14 | async-start | bytes 8388608
  366.2 9.0 %copy-start.25 = (bf16[256,2048]{1,0:T(8,128)(2,1)}, bf16[256,2048]{1,0:T(8,128)(2,1)S(1)}, u32[]{:S(2)}) copy-start(bf16[256,2048]{1,0:T(8,128)(2,1)S(1)} %convolution_convert_fusion.13) | copy-start | bytes 3145732
  366.2 9.8 %slice-start.7 = ((s8[8388608]{0:T(1024)(128)(4,1)}), s8[4194304]{0:T(1024)(128)(4,1)S(1)}, s32[]{:S(2)}) async-start(s8[8388608]{0:T(1024)(128)(4,1)} %bitcast.329), calls=%async_computation.15 | async-start | bytes 8388608
  366.2 9.8 %copy-start.72 = (bf16[2048,256]{0,1:T(8,128)(2,1)S(1)}, bf16[2048,256]{0,1:T(8,128)(2,1)}, u32[]{:S(2)}) copy-start(bf16[2048,256]{0,1:T(8,128)(2,1)} %get-tuple-element.58) | copy-start | bytes 3145732
  366.2 65.6 %collective-permute-start = (bf16[256,2048]{1,0:T(8,128)(2,1)S(1)}, bf16[256,2048]{1,0:T(8,128)(2,1)S(1)}, u32[]{:S(2)}, u32[]{:S(2)}) collective-permute-start(bf16[256,2048]{1,0:T(8,128)(2,1)S(1)} %convolution_convert_fusion.13), channel_id=1, source_target_pairs={{0,16},{16,0},{1,17},{17,1},{2,18},{18,2},{3,19},{19,3},{4,20},{20... | collective-permute-start | bytes 3145736 | tf_op jit(solution)/shard_map/ppermute | solution.py:80
  367.7 12.2 %slice-start.4 = ((s8[8388608]{0:T(1024)(128)(4,1)}), s8[4194304]{0:T(1024)(128)(4,1)S(1)}, s32[]{:S(2)}) async-start(s8[8388608]{0:T(1024)(128)(4,1)} %bitcast.259), calls=%async_computation.12 | async-start | bytes 8388608
  375.2 57.2 %collective-permute-start.1 = (bf16[256,2048]{1,0:T(8,128)(2,1)S(1)}, bf16[256,2048]{1,0:T(8,128)(2,1)S(1)}, u32[]{:S(2)}, u32[]{:S(2)}) collective-permute-start(bf16[256,2048]{1,0:T(8,128)(2,1)S(1)} %convolution_convert_fusion.12), channel_id=1, source_target_pairs={{0,16},{16,0},{1,17},{17,1},{2,18},{18,2},{3,19},{19,3},{4,20},{20... | collective-permute-start | bytes 3145736 | tf_op jit(solution)/shard_map/ppermute | solution.py:80
  378.4 58.8 %collective-permute-start.2 = (bf16[256,2048]{1,0:T(8,128)(2,1)S(1)}, bf16[256,2048]{1,0:T(8,128)(2,1)S(1)}, u32[]{:S(2)}, u32[]{:S(2)}) collective-permute-start(bf16[256,2048]{1,0:T(8,128)(2,1)S(1)} %convolution_convert_fusion.11), channel_id=1, source_target_pairs={{0,16},{16,0},{1,17},{17,1},{2,18},{18,2},{3,19},{19,3},{4,20},{20... | collective-permute-start | bytes 3145736 | tf_op jit(solution)/shard_map/ppermute | solution.py:80
  382.3 77.5 %collective-permute-start.3 = (bf16[256,2048]{1,0:T(8,128)(2,1)S(1)}, bf16[256,2048]{1,0:T(8,128)(2,1)}, u32[]{:S(2)}, u32[]{:S(2)}) collective-permute-start(bf16[256,2048]{1,0:T(8,128)(2,1)S(1)} %convolution_convert_fusion.10), channel_id=1, source_target_pairs={{0,16},{16,0},{1,17},{17,1},{2,18},{18,2},{3,19},{19,3},{4,20},{20... | collective-permute-start | bytes 3145736 | tf_op jit(solution)/shard_map/ppermute | solution.py:80
  407.0 13.7 %copy-start.38 = (bf16[1024,256]{1,0:T(8,128)(2,1)S(1)}, bf16[1024,256]{1,0:T(8,128)(2,1)}, u32[]{:S(2)}) copy-start(bf16[1024,256]{1,0:T(8,128)(2,1)} %param.14) | copy-start | bytes 1572868
  407.0 13.7 %copy-start.71 = (bf16[2048,256]{0,1:T(8,128)(2,1)S(1)}, bf16[2048,256]{0,1:T(8,128)(2,1)}, u32[]{:S(2)}) copy-start(bf16[2048,256]{0,1:T(8,128)(2,1)} %get-tuple-element.55) | copy-start | bytes 3145732
  407.0 13.7 %copy-start.73 = (bf16[2048,256]{0,1:T(8,128)(2,1)S(1)}, bf16[2048,256]{0,1:T(8,128)(2,1)}, u32[]{:S(2)}) copy-start(bf16[2048,256]{0,1:T(8,128)(2,1)} %get-tuple-element.58) | copy-start | bytes 3145732
  423.4 38.2 %copy-start.1 = (f32[128,2048]{1,0:T(8,128)S(1)}, f32[128,2048]{1,0:T(8,128)}, u32[]{:S(2)}) copy-start(f32[128,2048]{1,0:T(8,128)} %copy-done) | copy-start | bytes 3145732
  423.4 38.2 %copy-start.44 = (f32[2048,1]{0,1:T(1,128)S(1)}, f32[2048,1]{0,1:T(1,128)}, u32[]{:S(2)}) copy-start(f32[2048,1]{0,1:T(1,128)} %copy-done.43) | copy-start | bytes 24580
  423.4 38.2 %copy-start.49 = (f32[128]{0:T(128)S(1)}, f32[128]{0:T(128)}, u32[]{:S(2)}) copy-start(f32[128]{0:T(128)} %copy-done.48) | copy-start | bytes 1540
  423.4 39.5 %copy-start.64 = (f32[128]{0:T(128)S(1)}, f32[128]{0:T(128)}, u32[]{:S(2)}) copy-start(f32[128]{0:T(128)} %copy-done.63) | copy-start | bytes 1540
  423.5 39.5 %copy-start.8 = (bf16[2,64,2048]{2,1,0:T(8,128)(2,1)S(1)}, bf16[2,64,2048]{2,1,0:T(8,128)(2,1)}, u32[]{:S(2)}) copy-start(bf16[2,64,2048]{2,1,0:T(8,128)(2,1)} %param.15) | copy-start | bytes 1572868
  423.5 58.8 %collective-permute-start.4 = (bf16[256,2048]{1,0:T(8,128)(2,1)}, bf16[256,2048]{1,0:T(8,128)(2,1)}, u32[]{:S(2)}, u32[]{:S(2)}) collective-permute-start(bf16[256,2048]{1,0:T(8,128)(2,1)} %convolution_convert_fusion.9), channel_id=1, source_target_pairs={{0,16},{16,0},{1,17},{17,1},{2,18},{18,2},{3,19},{19,3},{4,20},{20... | collective-permute-start | bytes 3145736 | tf_op jit(solution)/shard_map/ppermute | solution.py:80
  431.8 72.2 %collective-permute-start.5 = (bf16[256,2048]{1,0:T(8,128)(2,1)}, bf16[256,2048]{1,0:T(8,128)(2,1)}, u32[]{:S(2)}, u32[]{:S(2)}) collective-permute-start(bf16[256,2048]{1,0:T(8,128)(2,1)} %convolution_convert_fusion.8), channel_id=1, source_target_pairs={{0,16},{16,0},{1,17},{17,1},{2,18},{18,2},{3,19},{19,3},{4,20},{20... | collective-permute-start | bytes 3145736 | tf_op jit(solution)/shard_map/ppermute | solution.py:80
  522.2 14.9 %collective-permute-start.15 = (bf16[1024,256]{1,0:T(8,128)(2,1)S(1)}, bf16[1024,256]{1,0:T(8,128)(2,1)S(1)}, u32[]{:S(2)}, u32[]{:S(2)}) collective-permute-start(bf16[1024,256]{1,0:T(8,128)(2,1)S(1)} %convolution_convert_fusion.17), channel_id=1, source_target_pairs={{0,16},{16,0},{1,17},{17,1},{2,18},{18,2},{3,19},{19,3},{4,20},{20... | collective-permute-start | bytes 1572872 | tf_op jit(solution)/shard_map/ppermute | solution.py:80
  523.7 44.9 %collective-permute-start.6 = (bf16[256,2048]{1,0:T(8,128)(2,1)}, bf16[256,2048]{1,0:T(8,128)(2,1)}, u32[]{:S(2)}, u32[]{:S(2)}) collective-permute-start(bf16[256,2048]{1,0:T(8,128)(2,1)} %convolution_convert_fusion.7), channel_id=1, source_target_pairs={{0,16},{16,0},{1,17},{17,1},{2,18},{18,2},{3,19},{19,3},{4,20},{20... | collective-permute-start | bytes 3145736 | tf_op jit(solution)/shard_map/ppermute | solution.py:80
  524.3 57.8 %collective-permute-start.7 = (bf16[256,2048]{1,0:T(8,128)(2,1)}, bf16[256,2048]{1,0:T(8,128)(2,1)}, u32[]{:S(2)}, u32[]{:S(2)}) collective-permute-start(bf16[256,2048]{1,0:T(8,128)(2,1)} %convolution_convert_fusion.6), channel_id=1, source_target_pairs={{0,16},{16,0},{1,17},{17,1},{2,18},{18,2},{3,19},{19,3},{4,20},{20... | collective-permute-start | bytes 3145736 | tf_op jit(solution)/shard_map/ppermute | solution.py:80
  525.8 78.8 %collective-permute-start.8 = (bf16[256,2048]{1,0:T(8,128)(2,1)}, bf16[256,2048]{1,0:T(8,128)(2,1)}, u32[]{:S(2)}, u32[]{:S(2)}) collective-permute-start(bf16[256,2048]{1,0:T(8,128)(2,1)} %convolution_convert_fusion.5), channel_id=1, source_target_pairs={{0,16},{16,0},{1,17},{17,1},{2,18},{18,2},{3,19},{19,3},{4,20},{20... | collective-permute-start | bytes 3145736 | tf_op jit(solution)/shard_map/ppermute | solution.py:80
  526.3 100.7 %collective-permute-start.9 = (bf16[256,2048]{1,0:T(8,128)(2,1)}, bf16[256,2048]{1,0:T(8,128)(2,1)}, u32[]{:S(2)}, u32[]{:S(2)}) collective-permute-start(bf16[256,2048]{1,0:T(8,128)(2,1)} %convolution_convert_fusion.4), channel_id=1, source_target_pairs={{0,16},{16,0},{1,17},{17,1},{2,18},{18,2},{3,19},{19,3},{4,20},{20... | collective-permute-start | bytes 3145736 | tf_op jit(solution)/shard_map/ppermute | solution.py:80
  537.1 112.5 %collective-permute-start.11 = (bf16[256,2048]{1,0:T(8,128)(2,1)}, bf16[256,2048]{1,0:T(8,128)(2,1)}, u32[]{:S(2)}, u32[]{:S(2)}) collective-permute-start(bf16[256,2048]{1,0:T(8,128)(2,1)} %convolution_convert_fusion.3), channel_id=1, source_target_pairs={{0,16},{16,0},{1,17},{17,1},{2,18},{18,2},{3,19},{19,3},{4,20},{20... | collective-permute-start | bytes 3145736 | tf_op jit(solution)/shard_map/ppermute | solution.py:80
  568.6 16.7 %copy-start.18 = (bf16[128,2048]{1,0:T(8,128)(2,1)S(1)}, bf16[128,2048]{1,0:T(8,128)(2,1)}, u32[]{:S(2)}) copy-start(bf16[128,2048]{1,0:T(8,128)(2,1)} %copy-done.17) | copy-start | bytes 1572868
  568.6 16.7 %copy-start.20 = (bf16[128,2048]{1,0:T(8,128)(2,1)S(1)}, bf16[128,2048]{1,0:T(8,128)(2,1)}, u32[]{:S(2)}) copy-start(bf16[128,2048]{1,0:T(8,128)(2,1)} %copy-done.19) | copy-start | bytes 1572868
  568.6 101.8 %collective-permute-start.12 = (bf16[256,2048]{1,0:T(8,128)(2,1)}, bf16[256,2048]{1,0:T(8,128)(2,1)}, u32[]{:S(2)}, u32[]{:S(2)}) collective-permute-start(bf16[256,2048]{1,0:T(8,128)(2,1)} %convolution_convert_fusion.2), channel_id=1, source_target_pairs={{0,16},{16,0},{1,17},{17,1},{2,18},{18,2},{3,19},{19,3},{4,20},{20... | collective-permute-start | bytes 3145736 | tf_op jit(solution)/shard_map/ppermute | solution.py:80
  591.5 82.1 %all-to-all-start.1 = ((bf16[16,2,16384]{2,1,0:T(2,128)(2,1)}), bf16[16,2,16384]{2,1,0:T(2,128)(2,1)S(1)}, u32[]{:S(2)}, u32[]{:S(2)}) async-start(bf16[16,2,16384]{2,1,0:T(2,128)(2,1)} %reshape.436), calls=%async_computation.3 | async-start | bytes 2097152 | tf_op jit(solution)/shard_map/all_to_all | solution.py:405
  679.8 7.1 copy-start.5
  679.8 7.1 copy-start.14
  685.4 12.6 %collective-permute-start.14 = (bf16[128,2048]{1,0:T(8,128)(2,1)}, bf16[128,2048]{1,0:T(8,128)(2,1)}, u32[]{:S(2)}, u32[]{:S(2)}) collective-permute-start(bf16[128,2048]{1,0:T(8,128)(2,1)} %fusion.35), channel_id=1, source_target_pairs={{0,16},{16,0},{1,17},{17,1},{2,18},{18,2},{3,19},{19,3},{4,20},{20... | collective-permute-start | bytes 1572872 | tf_op jit(solution)/shard_map/ppermute | solution.py:80
  687.6 13.6 %copy-start.51 = (f32[128]{0:T(128)S(1)}, f32[128]{0:T(128)}, u32[]{:S(2)}) copy-start(f32[128]{0:T(128)} %copy-done.50) | copy-start | bytes 1540
  687.6 13.6 %copy-start.53 = (f32[128]{0:T(128)S(1)}, f32[128]{0:T(128)}, u32[]{:S(2)}) copy-start(f32[128]{0:T(128)} %copy-done.52) | copy-start | bytes 1540
  705.2 6.3 copy-start.39
  705.2 6.3 copy-start.7
  705.2 6.3 copy-start.46
  705.2 9.1 %copy-start.62 = (f32[128]{0:T(128)S(1)}, f32[128]{0:T(128)}, u32[]{:S(2)}) copy-start(f32[128]{0:T(128)} %copy-done.61) | copy-start | bytes 1540
  715.0 96.8 %all-to-all-start = ((f32[16,128,2]{1,2,0:T(2,128)}), f32[16,128,2]{1,2,0:T(2,128)S(1)}, u32[]{:S(2)}, u32[]{:S(2)}) async-start(f32[16,128,2]{1,2,0:T(2,128)} %copy.37), calls=%async_computation.2 | async-start | bytes 32768 | tf_op jit(solution)/shard_map/all_to_all | solution.py:484
  798.9 8.2 copy-start.36
  803.8 6.6 copy-start.9
  803.8 6.6 copy-start.10
  803.8 6.5 copy-start.15
  808.8 22.3 %collective-permute-start.13 = (bf16[128,3328]{1,0:T(8,128)(2,1)}, bf16[128,3328]{1,0:T(8,128)(2,1)}, u32[]{:S(2)}, u32[]{:S(2)}) collective-permute-start(bf16[128,3328]{1,0:T(8,128)(2,1)} %pad_maximum_fusion.6), channel_id=1, source_target_pairs={{0,16},{16,0},{1,17},{17,1},{2,18},{18,2},{3,19},{19,3},{4,20},{20... | collective-permute-start | bytes 2555912 | tf_op jit(solution)/shard_map/ppermute | solution.py:80
  811.8 21.4 %copy-start.13 = (f32[128,2048]{1,0:T(8,128)S(1)}, f32[128,2048]{1,0:T(8,128)}, u32[]{:S(2)}) copy-start(f32[128,2048]{1,0:T(8,128)} %convert_add_fusion.2) | copy-start | bytes 3145732
  811.8 18.6 %collective-permute-start.10 = (bf16[128,2]{0,1:T(2,128)(2,1)S(1)}, bf16[128,2]{0,1:T(2,128)(2,1)S(1)}, u32[]{:S(2)}, u32[]{:S(2)}) collective-permute-start(bf16[128,2]{0,1:T(2,128)(2,1)S(1)} %reduce_sum.118), channel_id=1, source_target_pairs={{0,16},{16,0},{1,17},{17,1},{2,18},{18,2},{3,19},{19,3},{4,20},{20... | collective-permute-start | bytes 1544 | tf_op jit(solution)/shard_map/ppermute | solution.py:80
  (44 other events, 145.8 us)
Sparse Core Ops, SparseCore 0:
  118.8 80.2 all-gather.2
  248.4 79.0 all-gather.4
  359.8 101.7 reduce-scatter.2
  517.9 135.1 reduce-scatter.4

commit v4 on v3

--- a/solution.py
+++ b/solution.py
@@ -10,7 +10,9 @@
 HEADS = 8
 HD = 256
 RANK = 256
-CHUNKS = 4
+CHUNKS = 1
+PIECES = 2
+EARLY = 3
 
 
 epsilon = 1e-06
@@ -76,6 +78,17 @@
     return lax.psum_scatter(values, "fsdp", scatter_dimension=1, tiled=True)
 
 
+def total(mine, other):
+    return mine.astype(jnp.float32) + other.astype(jnp.float32)
+
+
+def place(whole, at, pair):
+    mine, other = pair
+    return lax.dynamic_update_slice(
+        whole, total(mine, other)[None], (at % 3, at // 3 * mine.shape[0], 0)
+    )
+
+
 def swap_rep(values):
     return lax.ppermute(values, "rep", [(0, 1), (1, 0)])
 
@@ -83,6 +96,20 @@
 def grid_of(shards):
     short = 2 if shards <= 16 else 4
     return shards // (2 * short), short
+
+
+def wire_cost(times, values):
+    moved = times * sum(v.size * v.dtype.itemsize for v in values)
+    return pl.CostEstimate(flops=0, bytes_accessed=24 * moved + (40 << 20), transcendentals=0)
+
+
+def unwritten(shape, dtype):
+    return pl.pallas_call(
+        lambda _: None,
+        out_shape=jax.ShapeDtypeStruct(shape, dtype),
+        out_specs=pl.BlockSpec(memory_space=pl.ANY),
+        name="unwritten",
+    )()
 
 
 def neighbours(shards):
@@ -91,7 +118,7 @@
     return me, me // (2 * short_len), (me // 2) % short_len, me % 2
 
 
-def greet(shards, across):
+def greet(shards, across, everyone=False):
     long_len, short_len = grid_of(shards)
     me, at_long, at_short, core = neighbours(shards)
     barrier = pltpu.get_barrier_semaphore()
@@ -102,6 +129,8 @@
         (at_short > 0, {"fsdp": me - 2}),
         (at_short < short_len - 1, {"fsdp": me + 2}),
     ]
+    if everyone:
+        around = [(me >= 0, {"fsdp": (me + far) % shards}) for far in range(1, shards)]
     if across:
         around.append((me >= 0, {"rep": 1 - lax.axis_index("rep")}))
     for has, peer in around:
@@ -111,12 +140,13 @@
     pl.semaphore_wait(barrier, sum(has.astype(jnp.int32) for has, _ in around))
 
 
-def gather_kernel(shards, widths, shared, *refs):
+def gather_kernel(shards, widths, shared, spread, *refs):
     long_len, short_len = grid_of(shards)
     count = len(widths)
-    own = refs[:count]
-    out = refs[count : 2 * count]
-    send_sem, recv_sem, own_sem = refs[2 * count :]
+    total = count + spread
+    own = refs[:total]
+    out = refs[total : 2 * total]
+    send_sem, recv_sem, own_sem, spread_sem = refs[2 * total :]
     me, at_long, at_short, core = neighbours(shards)
     stride = 2 * short_len
     partner = {"fsdp": me + 1 - 2 * core}
@@ -149,7 +179,7 @@
             device_id=peer,
         )
 
-    greet(shards, bool(shared))
+    greet(shards, bool(shared), bool(spread))
     done = []
 
     def start(has, which, way, slot, peer, fresh=False):
@@ -209,6 +239,27 @@
     every = list(range(len(parts)))
     start(true, every, 4, me, partner, True)
     mine = [pltpu.make_async_copy(own[k], out[k].at[:, me], own_sem.at[k]) for k in range(count)]
+
+    def share(k, peer, target):
+        width = own[k].shape[2] // shards
+        columns = pl.ds(pl.multiple_of(peer * width, 128), width)
+        return own[k].at[:, :, columns], out[k].at[:, target]
+
+    def dealt(k, far, back):
+        peer = (me + far) % shards
+        source, target = share(k, me if back else peer, peer if back else me)
+        return pltpu.make_async_remote_copy(
+            src_ref=source,
+            dst_ref=target,
+            send_sem=spread_sem.at[k - count, 0, peer],
+            recv_sem=spread_sem.at[k - count, 1, peer if back else me],
+            device_id={"fsdp": peer},
+        )
+
+    for k in range(count, total):
+        mine.append(pltpu.make_async_copy(*share(k, me, me), own_sem.at[k]))
+        for far in range(1, shards):
+            dealt(k, far, False).start()
     for each in mine:
         each.start()
     for far in range(1, long_len):
@@ -247,28 +298,231 @@
         def _():
             for lane in which:
                 copy(lane, way, slot, peer, fresh).wait_send()
+    for k in range(count, total):
+        for far in range(1, shards):
+            dealt(k, far, True).wait_recv()
+            dealt(k, far, False).wait_send()
     for each in mine:
         each.wait()
 
 
-def gather_all(shards, ident, *values, shared=0):
+def gather_all(shards, ident, *values, shared=0, spread=()):
     widths = tuple(v.shape[2] for v in values)
     count = len(values)
     lanes = count + (2 if shared else 0)
-    return pl.pallas_call(
-        functools.partial(gather_kernel, shards, widths, shared),
-        out_shape=[
-            jax.ShapeDtypeStruct((v.shape[0], shards) + v.shape[1:], v.dtype) for v in values
-        ],
-        in_specs=[pl.BlockSpec(memory_space=pltpu.VMEM)] * count,
-        out_specs=[pl.BlockSpec(memory_space=pl.ANY)] * count,
+    shapes = [(v.shape[0], shards) + v.shape[1:] for v in values]
+    dealt = []
+    if spread and spread[0].shape[2] % (128 * shards):
+        for v in spread:
+            each = lax.all_to_all(v, "fsdp", 2, 1, tiled=True)
+            dealt.append(each.reshape(v.shape[0], shards, v.shape[1], -1))
+        spread = ()
+    values = values + tuple(spread)
+    shapes += [(v.shape[0], shards, v.shape[1], v.shape[2] // shards) for v in spread]
+    results = pl.pallas_call(
+        functools.partial(gather_kernel, shards, widths, shared, len(values) - count),
+        out_shape=[jax.ShapeDtypeStruct(shape, v.dtype) for shape, v in zip(shapes, values)],
+        in_specs=[pl.BlockSpec(memory_space=pltpu.VMEM)] * len(values),
+        out_specs=[pl.BlockSpec(memory_space=pl.ANY)] * len(values),
         scratch_shapes=[
             pltpu.SemaphoreType.DMA((lanes, 6, shards)),
             pltpu.SemaphoreType.DMA((lanes, shards)),
+            pltpu.SemaphoreType.DMA((len(values),)),
+            pltpu.SemaphoreType.DMA((len(spread) + 1, 2, shards)),
+        ],
+        compiler_params=pltpu.CompilerParams(collective_id=ident, has_side_effects=True),
+        cost_estimate=wire_cost(shards, values[:count]),
+        name="gather_%d" % ident,
+    )(*values)
+    return list(results) + dealt
+
+
+def scatter_kernel(shards, widths, *refs):
+    long_len, short_len = grid_of(shards)
+    count = len(widths)
+    full = refs[:count]
+    out = refs[count : 2 * count]
+    held, core_in, short_in, long_in, load_sem, core_sem, short_sem, long_sem, done_sem = refs[
+        2 * count :
+    ]
+    me, at_long, at_short, core = neighbours(shards)
+    partner = {"fsdp": me + 1 - 2 * core}
+    firsts = [sum(widths[:k]) for k in range(count)]
+
+    def index(line, short):
+        return line * short_len + short
+
+    def block(k, line, short, side):
+        return full[k].at[:, index(line, short) * 2 + side]
+
+    def columns(ref, k):
+        return ref.at[:, :, pl.ds(firsts[k], widths[k])]
+
+    order = []
+    for far in range(long_len - 1, 0, -1):
+        for sign in (-1, 1):
+            line = at_long + sign * far
+            order.append(((line >= 0) & (line < long_len), line, far, sign))
+    order.append((me >= 0, at_long, 0, 0))
+    shorts = []
+    for far in range(short_len - 1, 0, -1):
+        for sign in (-1, 1):
+            short = at_short + sign * far
+            shorts.append(((short >= 0) & (short < short_len), short, far, sign))
+    shorts.append((me >= 0, at_short, 0, 0))
+
+    def to_core(k, line, short):
+        return pltpu.make_async_remote_copy(
+            src_ref=block(k, line, short, 1 - core),
+            dst_ref=columns(core_in.at[index(line, short)], k),
+            send_sem=core_sem.at[0, k, index(line, short)],
+            recv_sem=core_sem.at[1, k, index(line, short)],
+            device_id=partner,
+        )
+
+    def load(k, line, short):
+        return pltpu.make_async_copy(
+            block(k, line, short, core),
+            columns(held.at[index(line, short)], k),
+            load_sem.at[k, index(line, short)],
+        )
+
+    def along_short(line, short, sign):
+        return pltpu.make_async_remote_copy(
+            src_ref=held.at[index(line, short)],
+            dst_ref=short_in.at[(1 - sign) // 2, index(line, short)],
+            send_sem=short_sem.at[0, index(line, short)],
+            recv_sem=short_sem.at[1 + (1 - sign) // 2, index(line, short)],
+            device_id={"fsdp": me + 2 * sign},
+        )
+
+    def along_long(line, sign):
+        return pltpu.make_async_remote_copy(
+            src_ref=held.at[index(line, at_short)],
+            dst_ref=long_in.at[(1 - sign) // 2, line],
+            send_sem=long_sem.at[0, line],
+            recv_sem=long_sem.at[1 + (1 - sign) // 2, line],
+            device_id={"fsdp": me + 2 * short_len * sign},
+        )
+
+    def add(to_ref, from_ref):
+        batch, rows, _ = to_ref.shape
+        step = 16
+
+        @pl.loop(0, batch * rows // step)
+        def _(at):
+            one = at // (rows // step)
+            where = pl.ds(pl.multiple_of((at % (rows // step)) * step, step), step)
+            to_ref[one, where, :] = (
+                to_ref[one, where, :].astype(jnp.float32)
+                + from_ref[one, where, :].astype(jnp.float32)
+            ).astype(jnp.bfloat16)
+
+    for near, short, far, sign in shorts:
+        for has, line, _, _ in order:
+            @pl.when(near & has)
+            def _():
+                for k in range(count):
+                    load(k, line, short).start()
+
+    greet(shards, False)
+    for near, short, far, sign in shorts:
+        for has, line, _, _ in order:
+            @pl.when(near & has)
+            def _():
+                for k in range(count):
+                    to_core(k, line, short).start()
+
+    for near, short, far, sign in shorts:
+        for has, line, far_line, sign_line in order:
+            @pl.when(near & has)
+            def _():
+                at = index(line, short)
+                for k in range(count):
+                    load(k, line, short).wait()
+                    to_core(k, line, short).wait_recv()
+                add(held.at[at], core_in.at[at])
+                if far:
+                    behind = at_short - sign
+
+                    @pl.when((behind >= 0) & (behind < short_len))
+                    def _():
+                        along_short(line, short, sign).wait_recv()
+                        add(held.at[at], short_in.at[(1 - sign) // 2, at])
+
+                    along_short(line, short, sign).start()
+                else:
+                    for way in (-1, 1):
+                        behind = at_short - way
+
+                        @pl.when((behind >= 0) & (behind < short_len))
+                        def _():
+                            along_short(line, short, way).wait_recv()
+                            add(held.at[at], short_in.at[(1 - way) // 2, at])
+
+                    for way in (-1, 1) if not far_line else (sign_line,):
+                        behind = at_long - way
+
+                        @pl.when((behind >= 0) & (behind < long_len))
+                        def _():
+                            along_long(line, way).wait_recv()
+                            add(held.at[at], long_in.at[(1 - way) // 2, line])
+
+                    if far_line:
+                        along_long(line, sign_line).start()
+
+    results = [
+        pltpu.make_async_copy(columns(held.at[index(at_long, at_short)], k), out[k], done_sem.at[k])
+        for k in range(count)
+    ]
+    for each in results:
+        each.start()
+    for near, short, far, sign in shorts:
+        for has, line, far_line, sign_line in order:
+            @pl.when(near & has)
+            def _():
+                for k in range(count):
+                    to_core(k, line, short).wait_send()
+                if far:
+                    along_short(line, short, sign).wait_send()
+                elif far_line:
+                    along_long(line, sign_line).wait_send()
+    for each in results:
+        each.wait()
+
+
+def scatter_sum(shards, ident, *values):
+    batch, _, rows, _ = values[0].shape
+    widths = tuple(v.shape[3] for v in values)
+    if shards > 16:
+        return [
+            sum_rows(v.reshape(batch, shards * rows, w)) for v, w in zip(values, widths)
+        ]
+    count = len(values)
+    long_len, short_len = grid_of(shards)
+    pairs = shards // 2
+    block = (batch, rows, sum(widths))
+    return pl.pallas_call(
+        functools.partial(scatter_kernel, shards, widths),
+        out_shape=[jax.ShapeDtypeStruct((batch, rows, w), jnp.bfloat16) for w in widths],
+        in_specs=[pl.BlockSpec(memory_space=pl.ANY)] * count,
+        out_specs=[pl.BlockSpec(memory_space=pl.ANY)] * count,
+        scratch_shapes=[
+            pltpu.VMEM((pairs,) + block, jnp.bfloat16),
+            pltpu.VMEM((pairs,) + block, jnp.bfloat16),
+            pltpu.VMEM((2, pairs) + block, jnp.bfloat16),
+            pltpu.VMEM((2, long_len) + block, jnp.bfloat16),
+            pltpu.SemaphoreType.DMA((count, pairs)),
+            pltpu.SemaphoreType.DMA((2, count, pairs)),
+            pltpu.SemaphoreType.DMA((3, pairs)),
+            pltpu.SemaphoreType.DMA((3, long_len)),
             pltpu.SemaphoreType.DMA((count,)),
         ],
-        compiler_params=pltpu.CompilerParams(collective_id=ident, has_side_effects=True),
-        name="gather_%d" % ident,
+        compiler_params=pltpu.CompilerParams(
+            collective_id=ident, has_side_effects=True, vmem_limit_bytes=60 << 20
+        ),
+        cost_estimate=wire_cost(1, values),
+        name="scatter_%d" % ident,
     )(*values)
 
 
@@ -325,7 +579,7 @@
     keys_low = low(rotate(projected[:, q_width : q_width + HD], angles))
     values_low = low(projected[:, q_width + HD :])
     keys_all, values_all = (
-        each.reshape(micro, seq_len, HD)
+        each.reshape(micro, seq_len, -1)
         for each in gather_all(
             shards,
             2,
@@ -358,7 +612,7 @@
     low_grad_all = low(contract(cot_all, bd_t, 1, 0))
 
     step = hidden_cols // CHUNKS
-    hidden_parts, gate_parts, up_parts, ffn_parts = [], [], [], []
+    hidden_parts, gate_parts, up_parts = [], [], []
     for at in range(CHUNKS):
         units = slice(at * step, (at + 1) * step)
         w_gate, w_up, w_down = (ffn_weight[units, j, :] for j in range(3))
@@ -371,42 +625,61 @@
         )
         gate_grad = low(gelu_back(hidden_grad * up_pre)[0])
         up_grad = low(hidden_grad * activated)
+        hidden_parts.append(hidden_act)
+        gate_parts.append(gate_grad)
+        up_parts.append(up_grad)
+
+    gate_grad = jnp.concatenate(gate_parts, axis=1)
+    up_grad = jnp.concatenate(up_parts, axis=1)
+    hidden_act = jnp.concatenate(hidden_parts, axis=1)
+    step = hidden_cols // PIECES
+    first_mine = low(contract(gate_grad[:, :step], inputs_all, 0, 0))
+    down_part = low(contract(hidden_act, ffn_weight[:, 2, :], 1, 0))
+    low_part = low(contract(hidden_act, ffn_adapter, 1, 0))
+    first_other = swap_rep(first_mine)
+    down_part, low_part, gate_grad, up_grad, hidden_act, first_mine = lax.optimization_barrier(
+        (down_part, low_part, gate_grad, up_grad, hidden_act, first_mine)
+    )
+    down_sum = sum_rows(down_part.reshape(micro, seq_len, model_dim))
+    ffn_parts = []
+    for at in range(PIECES):
+        units = slice(at * step, (at + 1) * step)
         for left, right in (
             (gate_grad, inputs_all),
             (up_grad, inputs_all),
             (hidden_act, cot_all),
         ):
-            mine = low(contract(left, right, 0, 0))
+            if not ffn_parts:
+                ffn_parts.append((first_mine, first_other))
+                continue
+            mine = low(contract(left[:, units], right, 0, 0))
             ffn_parts.append((mine, swap_rep(mine)))
-        hidden_parts.append(hidden_act)
-        gate_parts.append(gate_grad)
-        up_parts.append(up_grad)
-
-    gate_grad = jnp.concatenate(gate_parts, axis=1)
-    up_grad = jnp.concatenate(up_parts, axis=1)
-    hidden_act = jnp.concatenate(hidden_parts, axis=1)
     low_mine = low(contract(hidden_act, low_grad_all, 0, 0))
-    gate_grad, kept_all = lax.optimization_barrier((gate_grad, kept_all))
-    normed_two_grad = sum_rows(
+    low_other = swap_rep(low_mine)
+    gate_grad, up_grad, kept_all, _ = lax.optimization_barrier(
+        (
+            gate_grad,
+            up_grad,
+            kept_all,
+            [pair[0] for pair in ffn_parts],
+        )
+    )
+    (normed_two_grad,) = scatter_sum(
+        shards,
+        5,
         low(
             contract(gate_grad, ffn_weight[:, 0, :], 1, 0)
             + contract(up_grad, ffn_weight[:, 1, :], 1, 0)
-        ).reshape(micro, seq_len, model_dim)
-    )
-    normed_two_grad, _ = lax.optimization_barrier(
-        (normed_two_grad, [pair[0] for pair in ffn_parts] + [pair[1] for pair in ffn_parts[:4]])
+        ).reshape(micro, shards, local_len, model_dim),
+    )
+    normed_two_grad, down_sum, _ = lax.optimization_barrier(
+        (normed_two_grad, down_sum, [pair[1] for pair in ffn_parts[:2]])
     )
     normed_two_grad = normed_two_grad.reshape(count, model_dim).astype(jnp.float32)
     cot_full = cotangent.reshape(count, model_dim).astype(jnp.float32)
     mixed_part, gain_two_grad = norm_back_two(normed_two_grad)
     mixed_grad = cot_full + mixed_part
     out_grad_low = low(mixed_grad)
-    both = jnp.concatenate([normed_low, out_grad_low], axis=0)
-    both_cols = lax.all_to_all(
-        both.reshape(2 * micro, local_len, model_dim), "fsdp", 2, 1, tiled=True
-    ).reshape(2, every, attn_rows)
-    normed_cols, out_cols = both_cols[0], both_cols[1]
-    wout_grad = contract(out_cols, kept_all[:, :q_width], 0, 0)
     context_grad = contract(out_grad_low, w_out, 1, 0)
     context_rows = low(context_grad).reshape(micro, local_len * HEADS, HD)
     prob_grad = batched(context_rows, values_all, 2, 2).reshape(micro, local_len, HEADS, seq_len)
@@ -414,38 +687,35 @@
     score_grad = low(score_grad).reshape(micro, local_len * HEADS, seq_len)
     query_grad = batched(score_grad, keys_all, 2, 1) * score_scale
     query_grad = query_grad.reshape(count, HEADS, HD)
-    kv_part = low(
-        jnp.concatenate(
-            [
-                batched(score_grad, queries, 1, 1) * score_scale,
-                batched(weights_low, context_rows, 1, 1),
-            ],
-            axis=2,
-        )
-    )
-    kv_part, _ = lax.optimization_barrier((kv_part, [pair[1] for pair in ffn_parts[4:6]]))
-    sums = sum_rows(
-        jnp.concatenate(
-            [
-                low(contract(hidden_act, ffn_weight[:, 2, :], 1, 0)).reshape(
-                    micro, seq_len, model_dim
-                ),
-                low(contract(hidden_act, ffn_adapter, 1, 0)).reshape(micro, seq_len, RANK),
-                kv_part,
-            ],
-            axis=2,
-        )
-    )
-    sums, _ = lax.optimization_barrier((sums, [pair[1] for pair in ffn_parts[6:10]]))
-    sums = sums.reshape(count, model_dim + RANK + 2 * HD)
-    kv_grad = sums[:, model_dim + RANK :]
-    down_low = sums[:, model_dim : model_dim + RANK]
+    query_pre_grad = low(rotate(query_grad, -angles[:, None, :]).reshape(count, q_width))
+    key_part = low(batched(score_grad, queries, 1, 1) * score_scale)
+    value_part = low(batched(weights_low, context_rows, 1, 1))
+    ffn_grad = unwritten((3, hidden_cols, model_dim), jnp.float32)
+    for at in range(EARLY):
+        ffn_grad = place(ffn_grad, at, ffn_parts[at])
+    key_part, value_part, query_pre_grad, ffn_grad, ffn_parts[3:4] = lax.optimization_barrier(
+        (key_part, value_part, query_pre_grad, ffn_grad, ffn_parts[3:4])
+    )
+    q_all = gather_rows(query_pre_grad.reshape(micro, local_len, q_width))
+    q_all = q_all.reshape(every, q_width)
+    key_sum, value_sum, down_low = (
+        each.reshape(count, -1)
+        for each in scatter_sum(
+            shards,
+            6,
+            *(
+                each.reshape(micro, shards, local_len, -1)
+                for each in (key_part, value_part, low_part)
+            ),
+        )
+    )
     result = (
-        mixed_sum + sums[:, :model_dim].astype(jnp.float32) + contract(down_low, bd_t, 1, 1)
-    )
-    query_pre_grad = low(rotate(query_grad, -angles[:, None, :]).reshape(count, q_width))
-    key_grad = low(rotate(kv_grad[:, :HD].astype(jnp.float32), -angles))
-    value_grad = kv_grad[:, HD:]
+        mixed_sum
+        + down_sum.reshape(count, model_dim).astype(jnp.float32)
+        + contract(down_low, bd_t, 1, 1)
+    )
+    key_grad = low(rotate(key_sum.astype(jnp.float32), -angles))
+    value_grad = value_sum
     rank_grad = low(contract(query_pre_grad, bq_t, 1, 0))
     proj_grad = jnp.concatenate([query_pre_grad, key_grad, value_grad], axis=1)
     normed_grad = contract(proj_grad, w_proj, 1, 1) + contract(rank_grad, a_q, 1, 1)
@@ -453,24 +723,26 @@
     input_grad = low(mixed_grad + hidden_part)
 
     narrow = jnp.concatenate([key_grad, value_grad, rank_grad, down_low], axis=1)
-    q_all, narrow_all = (
-        each.reshape(every, -1)
-        for each in gather_all(
-            shards,
-            4,
-            query_pre_grad.reshape(micro, local_len, q_width),
-            narrow.reshape(micro, local_len, 2 * HD + 2 * RANK),
-        )
-    )
-    narrow_all, _ = lax.optimization_barrier((narrow_all, [pair[1] for pair in ffn_parts[10:]]))
+    narrow, ffn_parts[3:5] = lax.optimization_barrier((narrow, ffn_parts[3:5]))
+    gain_parts = jnp.zeros((1, 16, model_dim), jnp.bfloat16)
+    gain_parts = gain_parts.at[0, 0].set(low(gain_one_grad)).at[0, 1].set(low(gain_two_grad))
+    narrow_all, normed_cols, out_cols, gain_cols = gather_all(
+        shards,
+        4,
+        narrow.reshape(micro, local_len, 2 * HD + 2 * RANK),
+        spread=(
+            normed_low.reshape(micro, local_len, model_dim),
+            out_grad_low.reshape(micro, local_len, model_dim),
+            gain_parts,
+        ),
+    )
+    narrow_all = narrow_all.reshape(every, 2 * HD + 2 * RANK)
+    normed_cols = normed_cols.reshape(every, attn_rows)
+    wout_grad = contract(out_cols.reshape(every, attn_rows), kept_all[:, :q_width], 0, 0)
+    gain_now = jnp.sum(gain_cols[0, :, :2].astype(jnp.float32), axis=0)
     my_cols = me * attn_rows
-    attn_in = jnp.concatenate(
-        [
-            contract(normed_cols, q_all, 0, 0),
-            contract(normed_cols, narrow_all[:, : 2 * HD + RANK], 0, 0),
-        ],
-        axis=1,
-    )
+    attn_q = low(contract(normed_cols, q_all, 0, 0))
+    attn_rest = contract(normed_cols, narrow_all[:, : 2 * HD + RANK], 0, 0)
     bq_grad = contract(
         lax.dynamic_slice_in_dim(q_all, my_cols, attn_rows, 1), kept_all[:, q_width:], 0, 0
     )
@@ -480,27 +752,27 @@
         0,
         0,
     )
-    gain_now = jnp.stack([gain_one_grad, gain_two_grad], axis=1).reshape(shards, attn_rows, 2)
-    gain_now = lax.all_to_all(gain_now, "fsdp", 0, 0, tiled=True).sum(axis=0)
-    tail = low(jnp.concatenate([attn_in, bq_grad, bd_grad], axis=1))
+    tail = low(jnp.concatenate([attn_rest, bq_grad, bd_grad], axis=1))
     tail_out = low(wout_grad)
     tail_gain = low(gain_now)
-
-    def total(mine, other):
-        return mine.astype(jnp.float32) + other.astype(jnp.float32)
-
-    tail = total(tail, swap_rep(tail))
-    tail_out = total(tail_out, swap_rep(tail_out))
-    gains_grad = total(tail_gain, swap_rep(tail_gain))
-    attn_grad = jnp.concatenate([tail[:, :kv_end], tail_out], axis=1)
-    adapter_grad = tail[:, kv_end:]
-    ffn_grad = jnp.zeros((3, hidden_cols, model_dim), jnp.float32)
-    for at, pair in enumerate(ffn_parts):
-        ffn_grad = lax.dynamic_update_slice(
-            ffn_grad, total(*pair)[None], (at % 3, at // 3 * step, 0)
-        )
+    crossing = [swap_rep(each) for each in (tail_out, tail, attn_q)]
+    attn_q, tail, tail_out, ffn_parts[3:], low_mine, low_other = lax.optimization_barrier(
+        (attn_q, tail, tail_out, ffn_parts[3:], low_mine, low_other)
+    )
+    gains_grad = total(tail_gain, swap_rep(tail_gain)).transpose(1, 0)
+    for at in range(EARLY, 3 * PIECES):
+        ffn_grad = place(ffn_grad, at, ffn_parts[at])
     ffn_grad = ffn_grad.transpose(1, 0, 2)
-    ffn_low_grad = total(low_mine, swap_rep(low_mine))
+    ffn_low_grad = total(low_mine, low_other)
+    tail = total(tail, crossing[1])
+    attn_grad = unwritten(attn_weight.shape, jnp.float32)
+    for first, part in (
+        (kv_end, total(tail_out, crossing[0])),
+        (q_width, tail[:, : 2 * HD]),
+        (0, total(attn_q, crossing[2])),
+    ):
+        attn_grad = lax.dynamic_update_slice(attn_grad, part, (0, first))
+    adapter_grad = tail[:, 2 * HD :]
     return (
         low(result).reshape(micro, local_len, model_dim),
         input_grad.reshape(micro, local_len, model_dim),

time: 850 us -> 707 us (0.83)
  waiting for transfers between devices: 166 us -> 0.1 us
  Pallas kernels: 287 us -> 383 us
  local copies, waits for them, and re-layouts: 45.1 us -> 19.1 us
  other arithmetic: 74 us -> 48.9 us
  starting transfers between devices: 25.9 us -> 13.4 us
    ppermute x16 -> x11, waiting for transfers between devices: 162 us -> 0.03 us  [swap_rep(): return lax.ppermute(values, 'rep', [(0, 1), (1, 0)])]
    pallas_call x4 -> x8, Pallas kernels: 287 us -> 383 us  [the longest x4 273 us: gather_all(): pl.pallas_call(functools.partial(gather_kernel, shards, widths, shared, l...]
    concatenate x6 -> x1, other arithmetic: 17.3 us -> 0.02 us  [local(): tail = low(jnp.concatenate([attn_rest, bq_grad, bd_grad], axis=1))]
    dynamic_update_slice x1, local copies, waits for them, and re-layouts: 12.5 us -> 0.02 us  [local(): attn_grad = lax.dynamic_update_slice(attn_grad, part, (0, first))]
    dot_general x48 -> x30, matrix products: 219 us -> 209 us  [contract(): lax.dot_general(left_op, right_op, (((left_dim,), (right_dim,)), ((), ())...]
    ppermute x16 -> x11, starting transfers between devices: 17.8 us -> 13.1 us  [swap_rep(): return lax.ppermute(values, 'rep', [(0, 1), (1, 0)])]
    dynamic_update_slice x11 -> x8, other arithmetic: 33.9 us -> 30.1 us  [the longest x6 28.7 us: place(): lax.dynamic_update_slice(whole, total(mine, other)[None], (at % 3, at //...]
  transfers between devices with their start and end apart: 22 -> 15, of which waited for: 14 -> 0; matrix products, arithmetic and copies ran while one was open for 32% -> 40% of each run, Pallas kernels for 21% -> 39%
where the time goes in v4:
time: 707 us; the launch traced here: 700 us
  Pallas kernels  383 us (54%)
  matrix products  220 us (31%)
  other arithmetic  48.9 us (7%)
  local copies, waits for them, and re-layouts  19.1 us (3%)
  between operations  14.9 us (2%)
  starting transfers between devices  13.4 us (2%)
    pallas_call x4, Pallas kernels, gather_all(): pl.pallas_call(functools.partial(gather_kernel, shards, widths, shared, l...  273 us
    dot_general x30, matrix products, contract(): lax.dot_general(left_op, right_op, (((left_dim,), (right_dim,)), ((), ())...  209 us
    pallas_call x2, Pallas kernels, scatter_sum(): pl.pallas_call(functools.partial(scatter_kernel, shards, widths), out_sha...  110 us
    dynamic_update_slice x6, other arithmetic, place(): lax.dynamic_update_slice(whole, total(mine, other)[None], (at % 3, at //...  28.7 us
  transfers between devices with their start and end apart: 15, of which 0 were waited for; matrix products, arithmetic and copies ran while one was open for 40% of the time, Pallas kernels for 39%

profile of v4, /device:TPU:0, one launch (start us, length us, event | category | flops | bytes accessed | tf_op | source)
XLA Modules:
  0.0 699.5 jit_solution(11832918826871232181)
XLA Ops:
  9.7 109.2 %gather_1.1 = (bf16[1,16,128,4608]{3,2,1,0:T(8,128)(2,1)}, bf16[1,16,128,768]{3,2,1,0:T(8,128)(2,1)}, bf16[1,16,128,128]{3,2,1,0:T(8,128)(2,1)}) custom-call(bf16[1,128,4608]{2,1,0:T(8,128)(2,1)} %bitcast.203, bf16[1,128,768]{2,1,0:T(8,128)(2,1)} %bitcast.228, bf16[1,128,128]{2,1,0:T(8,128)(2,1)} %maximum_bitcast_fusion.refs_2_), custom_call_target="tpu_custom_call" | custom-call | bytes 583008256 | tf_op jit(solution)/shard_map/gather_1/pallas_call | solution.py:322
  119.2 1.2 slice.191
  121.8 1.3 copy.29
  124.7 5.7 fusion.3
  132.3 1.2 fusion.95
  134.1 34.8 %gather_2.1 = (bf16[2,16,64,256]{3,2,1,0:T(8,128)(2,1)}, bf16[2,16,64,256]{3,2,1,0:T(8,128)(2,1)}) custom-call(bf16[2,64,256]{2,1,0:T(8,128)(2,1)} %pad_maximum_fusion.6.refs_0_, bf16[2,64,256]{2,1,0:T(8,128)(2,1)} %bitcast.219), custom_call_target="tpu_custom_call" | custom-call | bytes 92274688 | tf_op jit(solution)/shard_map/gather_2/pallas_call | solution.py:322
  169.4 2.2 fusion.93
  171.6 2.1 fusion.107
  173.7 1.9 copy-done.8
  176.7 6.4 multiply_reduce_fusion.1
  183.2 0.9 copy-done.2
  184.1 1.0 multiply_convert_fusion.4
  185.1 63.0 %gather_3.1 = bf16[2,16,64,2048]{3,2,1,0:T(8,128)(2,1)} custom-call(bf16[2,64,2048]{2,1,0:T(8,128)(2,1)} %bitcast.194), custom_call_target="tpu_custom_call" | custom-call | bytes 243269632 | tf_op jit(solution)/shard_map/gather_3/pallas_call | solution.py:322
  249.2 14.5 %fusion.26 = f32[2048,1024]{1,0:T(8,128)} fusion(bf16[2048,2048]{1,0:T(8,128)(2,1)} %bitcast.169, bf16[1024,3,2048]{2,0,1:T(8,128)(2,1)} %param.17), kind=kOutput, calls=%fused_computation.40 | convolution fusion | flops 8589934592 | bytes 20971520 | tf_op jit(solution)/shard_map/dot_general | solution.py:52
  263.7 14.6 %fusion.22 = f32[2048,1024]{1,0:T(8,128)} fusion(bf16[2048,2048]{1,0:T(8,128)(2,1)} %bitcast.170, bf16[1024,3,2048]{2,0,1:T(8,128)(2,1)} %param.17), kind=kOutput, calls=%fused_computation.36 | convolution fusion | flops 8589934592 | bytes 20971520 | tf_op jit(solution)/shard_map/dot_general | solution.py:52
  278.3 6.1 convolution_convert_fusion.8
  284.4 1.1 copy-done.37
  285.5 13.7 %fusion.18 = f32[2048,1024]{1,0:T(8,128)} fusion(bf16[2048,2048]{1,0:T(8,128)(2,1)S(1)} %bitcast.239, bf16[1024,3,2048]{2,0,1:T(8,128)(2,1)} %param.17), kind=kOutput, calls=%fused_computation.32 | convolution fusion | flops 8589934592 | bytes 20971520 | tf_op jit(solution)/shard_map/dot_general | solution.py:52
  299.2 17.3 %multiply_convert_fusion = (bf16[2048,1024]{1,0:T(8,128)(2,1)}, bf16[2048,1024]{1,0:T(8,128)(2,1)}, bf16[2048,1024]{1,0:T(8,128)(2,1)}) fusion(f32[2048,1024]{1,0:T(8,128)} %fusion.26, f32[2048,1024]{1,0:T(8,128)} %fusion.22, f32[2048,1024]{1,0:T(8,128)} %fusion.18, bf16[2048,256]{1,0:T(8,128)(2,1)S(1)} %convolution_convert_fusion.8, ...), kind=kOutput, calls=%fused_computation.17 | convolution fusion | flops 1130364928 | bytes 39321600 | tf_op jit(solution)/shard_map/dot_general | solution.py:52
  316.6 6.6 convolution_convert_fusion.6
  323.2 1.3 collective-permute-start
  324.5 2.3 convolution_convert_fusion.7
  326.7 13.4 %convolution_convert_fusion = bf16[2048,2048]{1,0:T(8,128)(2,1)} fusion(bf16[2048,1024]{1,0:T(8,128)(2,1)S(1)} %copy-done.55, bf16[1024,3,2048]{2,0,1:T(8,128)(2,1)} %param.17), kind=kOutput, calls=%fused_computation.20 | convolution fusion | flops 8594128896 | bytes 16777216 | tf_op jit(solution)/shard_map/dot_general | solution.py:52
  340.3 10.4 %convolution_convert_fusion.5 = bf16[512,2048]{1,0:T(8,128)(2,1)} fusion(bf16[2048,2048]{1,0:T(8,128)(2,1)} %bitcast.171, bf16[2048,1024]{1,0:T(8,128)(2,1)} %get-tuple-element.94), kind=kOutput, calls=%fused_computation.59 | convolution fusion | flops 4296015872 | bytes 12582912 | tf_op jit(solution)/shard_map/dot_general | solution.py:52
  351.6 11.1 %convolution_convert_fusion.4 = bf16[512,2048]{1,0:T(8,128)(2,1)} fusion(bf16[2048,2048]{1,0:T(8,128)(2,1)} %bitcast.237, bf16[2048,1024]{1,0:T(8,128)(2,1)S(1)} %copy-done.56), kind=kOutput, calls=%fused_computation.58 | convolution fusion | flops 4296015872 | bytes 12582912 | tf_op jit(solution)/shard_map/dot_general | solution.py:52
  362.7 1.1 collective-permute-start.2
  363.9 5.8 convolution_convert_fusion.3
  370.5 5.7 convolution_convert_fusion.2
  376.3 5.7 convolution_convert_fusion.1
  382.0 15.4 %fusion.24 = f32[2048,2048]{1,0:T(8,128)} fusion(bf16[2048,1024]{1,0:T(8,128)(2,1)} %get-tuple-element.93, bf16[1024,3,2048]{2,0,1:T(8,128)(2,1)} %param.17), kind=kOutput, calls=%fused_computation.38 | convolution fusion | flops 8589934592 | bytes 25165824 | tf_op jit(solution)/shard_map/dot_general | solution.py:52
  397.4 16.0 %add_convert_fusion = bf16[2048,2048]{1,0:T(8,128)(2,1)} fusion(f32[2048,2048]{1,0:T(8,128)} %fusion.24, bf16[2048,1024]{1,0:T(8,128)(2,1)S(1)} %copy-done.58, bf16[1024,3,2048]{2,0,1:T(8,128)(2,1)} %param.17), kind=kOutput, calls=%fused_computation.1 | convolution fusion | flops 8598323200 | bytes 33554432 | tf_op jit(solution)/shard_map/dot_general | solution.py:52
  413.4 65.7 %scatter_5.1 = bf16[2,64,2048]{2,1,0:T(8,128)(2,1)} custom-call(bf16[2,16,64,2048]{3,2,1,0:T(8,128)(2,1)} %bitcast.180), custom_call_target="tpu_custom_call" | custom-call | bytes 243269632 | tf_op jit(solution)/shard_map/scatter_5/pallas_call | solution.py:505
  479.1 4.4 bitcast_dynamic-update-slice_fusion.5
  483.5 5.0 bitcast_dynamic-update-slice_fusion.4
  488.6 5.2 bitcast_dynamic-update-slice_fusion.3
  494.6 5.6 fusion.40
  500.2 1.3 reshape.502
  501.5 3.6 multiply_reduce_fusion
  507.8 0.9 copy.31
  508.7 1.9 multiply_convert_fusion.3
  510.6 2.1 convolution_convert_fusion.10
  513.4 2.7 collective-permute-start.4
  516.0 1.0 fusion.73.refs_1_
  517.0 4.7 convolution_convert_fusion.12
  521.7 1.9 collective-permute-start.7
  523.6 43.9 %scatter_6.1 = (bf16[2,64,256]{2,1,0:T(8,128)(2,1)}, bf16[2,64,256]{2,1,0:T(8,128)(2,1)}, bf16[2,64,256]{2,1,0:T(8,128)(2,1)}) custom-call(bf16[2,16,64,256]{3,2,1,0:T(8,128)(2,1)} %bitcast.205, bf16[2,16,64,256]{3,2,1,0:T(8,128)(2,1)} %bitcast.206, bf16[2,16,64,256]{3,2,1,0:T(8,128)(2,1)} %bitcast.204), custom_call_target="tpu_custom_call" | custom-call | bytes 117440512 | tf_op jit(solution)/shard_map/scatter_6/pallas_call | solution.py:505
  569.9 1.5 constant_dynamic-update-slice_fusion.1
  572.3 6.3 fusion.1
  578.6 2.8 fusion.70
  582.7 66.0 %gather_4.1 = (bf16[2,16,64,1024]{3,2,1,0:T(8,128)(2,1)}, bf16[2,16,64,128]{3,2,1,0:T(8,128)(2,1)}, bf16[2,16,64,128]{3,2,1,0:T(8,128)(2,1)}, bf16[1,16,16,128]{3,2,1,0:T(8,128)(2,1)}) custom-call(bf16[2,64,1024]{2,1,0:T(8,128)(2,1)} %bitcast.214, bf16[2,64,2048]{2,1,0:T(8,128)(2,1)} %fusion.73.refs_1_, bf16[2,64,2048]{2,1,0:T(8,128)(2,1)} %bitcast.193, ...), custom_call_target="tpu_custom_call" | custom-call | bytes 142606336 | tf_op jit(solution)/shard_map/gather_4/pallas_call | solution.py:322
  649.6 1.3 collective-permute-start.5
  650.9 5.8 fusion.43
  657.4 2.5 fusion.46
  660.6 1.5 fusion.65
  662.0 1.4 convolution_convert_fusion.13
  664.0 1.8 convolution_convert_fusion.14
  665.8 1.3 collective-permute-start.9
  667.1 4.7 convolution_convert_fusion.9
  672.7 5.0 bitcast_dynamic-update-slice_fusion.2
  677.7 4.5 bitcast_dynamic-update-slice_fusion.1
  682.2 4.5 bitcast_dynamic-update-slice_fusion
  686.7 1.3 add_dynamic-update-slice_fusion.1
  688.1 2.3 convert_add_fusion.1
  691.4 1.4 copy-done.14
  (226 shorter events, 25.9 us)
Async XLA Ops:
  7.2 292.1 %copy-start = (bf16[1024,256]{1,0:T(8,128)(2,1)S(1)}, bf16[1024,256]{1,0:T(8,128)(2,1)}, u32[]{:S(2)}) copy-start(bf16[1024,256]{1,0:T(8,128)(2,1)} %param.18) | copy-start | bytes 1572868
  7.2 115.9 %copy-start.4 = (bf16[2,64,2048]{2,1,0:T(8,128)(2,1)S(1)}, bf16[2,64,2048]{2,1,0:T(8,128)(2,1)}, u32[]{:S(2)}) copy-start(bf16[2,64,2048]{2,1,0:T(8,128)(2,1)} %param.12) | copy-start | bytes 1572868
  7.2 271.1 %all-gather.4.cloned.1.call-start = ((), (), s32[]{:S(2)}) async-start(), calls=%async_computation.1 | async-start | bytes 8912896 | tf_op jit(solution)/shard_map/all_gather | solution.py:74
  119.0 263.0 %all-gather.6.cloned.1.call-start = ((), (), s32[]{:S(2)}) async-start(), calls=%async_computation.2 | async-start | bytes 10027008 | tf_op jit(solution)/shard_map/all_gather | solution.py:74
  124.5 5.9 copy-start.44
  124.5 5.9 copy-start.35
  124.5 58.7 %copy-start.33 = (f32[2048,1]{0,1:T(1,128)}, f32[2048,1]{0,1:T(1,128)S(1)}, u32[]{:S(2)}) copy-start(f32[2048,1]{0,1:T(1,128)S(1)} %get-tuple-element.146) | copy-start | bytes 24580
  124.7 6.4 copy-start.12
  130.4 38.6 %copy-start.48 = (s32[2,64]{1,0:T(2,128)S(1)}, s32[2,64]{1,0:T(2,128)}, u32[]{:S(2)}) copy-start(s32[2,64]{1,0:T(2,128)} %param.13) | copy-start | bytes 1540
  169.4 4.3 copy-start.20
  169.4 4.3 copy-start.22
  171.6 4.0 copy-start.50
  183.1 64.9 %copy-start.53 = (f32[128]{0:T(128)}, f32[128]{0:T(128)S(1)}, u32[]{:S(2)}) copy-start(f32[128]{0:T(128)S(1)} %get-tuple-element.158) | copy-start | bytes 1540
  183.2 64.9 %copy-start.38 = (f32[128]{0:T(128)}, f32[128]{0:T(128)S(1)}, u32[]{:S(2)}) copy-start(f32[128]{0:T(128)S(1)} %fusion.98) | copy-start | bytes 1540
  249.0 244.8 %reduce-scatter.2.cloned.1.call-start = ((), (), s32[]{:S(2)}) async-start(), calls=%async_computation.3 | async-start | bytes 8912896 | tf_op jit(solution)/shard_map/reduce_scatter | solution.py:78
  278.3 7.2 %copy-start.37 = (bf16[2,1024,2048]{2,1,0:T(8,128)(2,1)S(1)}, bf16[2,1024,2048]{2,1,0:T(8,128)(2,1)}, u32[]{:S(2)}) copy-start(bf16[2,1024,2048]{2,1,0:T(8,128)(2,1)} %all-gather.4.cloned.1.call-done) | copy-start | bytes 25165828
  278.3 38.3 %slice-start = ((s8[8388608]{0:T(1024)(128)(4,1)}), s8[4194304]{0:T(1024)(128)(4,1)S(1)}, s32[]{:S(2)}) async-start(s8[8388608]{0:T(1024)(128)(4,1)} %bitcast.172), calls=%async_computation.5 | async-start | bytes 8388608
  285.5 13.7 %copy-start.60 = (bf16[2048,256]{1,0:T(8,128)(2,1)}, bf16[2048,256]{1,0:T(8,128)(2,1)S(1)}, u32[]{:S(2)}) copy-start(bf16[2048,256]{1,0:T(8,128)(2,1)S(1)} %convolution_convert_fusion.8) | copy-start | bytes 3145732
  285.5 31.0 %slice-start.1 = ((s8[8388608]{0:T(1024)(128)(4,1)}), s8[4194304]{0:T(1024)(128)(4,1)S(1)}, s32[]{:S(2)}) async-start(s8[8388608]{0:T(1024)(128)(4,1)} %bitcast.172), calls=%async_computation.6 | async-start | bytes 8388608
  316.6 7.9 %copy-start.55 = (bf16[2048,1024]{1,0:T(8,128)(2,1)S(1)}, bf16[2048,1024]{1,0:T(8,128)(2,1)}, u32[]{:S(2)}) copy-start(bf16[2048,1024]{1,0:T(8,128)(2,1)} %get-tuple-element.92) | copy-start | bytes 12582916
  323.2 155.9 %collective-permute-start = (bf16[512,2048]{1,0:T(8,128)(2,1)S(1)}, bf16[512,2048]{1,0:T(8,128)(2,1)}, u32[]{:S(2)}, u32[]{:S(2)}) collective-permute-start(bf16[512,2048]{1,0:T(8,128)(2,1)S(1)} %convolution_convert_fusion.6), channel_id=1, source_target_pairs={{0,16},{16,0},{1,17},{17,1},{2,18},{18,2},{3,19},{19,3},{4,20},{20... | collective-permute-start | bytes 6291464 | tf_op jit(solution)/shard_map/ppermute | solution.py:93
  340.2 323.8 %all-gather.8.cloned.1.call-start = ((), (), s32[]{:S(2)}) async-start(), calls=%async_computation.4 | async-start | bytes 8912896 | tf_op jit(solution)/shard_map/all_gather | solution.py:74
  340.3 11.3 %copy-start.56 = (bf16[2048,1024]{1,0:T(8,128)(2,1)S(1)}, bf16[2048,1024]{1,0:T(8,128)(2,1)}, u32[]{:S(2)}) copy-start(bf16[2048,1024]{1,0:T(8,128)(2,1)} %get-tuple-element.92) | copy-start | bytes 12582916
  340.3 23.6 %slice-start.2 = ((s8[8388608]{0:T(1024)(128)(4,1)}), s8[4194304]{0:T(1024)(128)(4,1)S(1)}, s32[]{:S(2)}) async-start(s8[8388608]{0:T(1024)(128)(4,1)} %bitcast.175), calls=%async_computation.7 | async-start | bytes 8388608
  350.7 13.2 %slice-start.3 = ((s8[8388608]{0:T(1024)(128)(4,1)}), s8[4194304]{0:T(1024)(128)(4,1)S(1)}, s32[]{:S(2)}) async-start(s8[8388608]{0:T(1024)(128)(4,1)} %bitcast.175), calls=%async_computation.8 | async-start | bytes 8388608
  350.7 13.2 %copy-start.59 = (bf16[2048,1024]{1,0:T(8,128)(2,1)S(1)}, bf16[2048,1024]{1,0:T(8,128)(2,1)}, u32[]{:S(2)}) copy-start(bf16[2048,1024]{1,0:T(8,128)(2,1)} %get-tuple-element.93) | copy-start | bytes 12582916
  350.7 132.8 %collective-permute-start.1 = (bf16[512,2048]{1,0:T(8,128)(2,1)}, bf16[512,2048]{1,0:T(8,128)(2,1)}, u32[]{:S(2)}, u32[]{:S(2)}) collective-permute-start(bf16[512,2048]{1,0:T(8,128)(2,1)} %convolution_convert_fusion.5), channel_id=1, source_target_pairs={{0,16},{16,0},{1,17},{17,1},{2,18},{18,2},{3,19},{19,3},{4,20},{20... | collective-permute-start | bytes 6291464 | tf_op jit(solution)/shard_map/ppermute | solution.py:93
  362.7 7.8 %copy-start.57 = (bf16[2048,1024]{1,0:T(8,128)(2,1)S(1)}, bf16[2048,1024]{1,0:T(8,128)(2,1)}, u32[]{:S(2)}) copy-start(bf16[2048,1024]{1,0:T(8,128)(2,1)} %get-tuple-element.94) | copy-start | bytes 12582916
  362.7 125.9 %collective-permute-start.2 = (bf16[512,2048]{1,0:T(8,128)(2,1)}, bf16[512,2048]{1,0:T(8,128)(2,1)}, u32[]{:S(2)}, u32[]{:S(2)}) collective-permute-start(bf16[512,2048]{1,0:T(8,128)(2,1)} %convolution_convert_fusion.4), channel_id=1, source_target_pairs={{0,16},{16,0},{1,17},{17,1},{2,18},{18,2},{3,19},{19,3},{4,20},{20... | collective-permute-start | bytes 6291464 | tf_op jit(solution)/shard_map/ppermute | solution.py:93
  363.9 12.4 %slice-start.4 = ((s8[8388608]{0:T(1024)(128)(4,1)}), s8[4194304]{0:T(1024)(128)(4,1)S(1)}, s32[]{:S(2)}) async-start(s8[8388608]{0:T(1024)(128)(4,1)} %bitcast.240), calls=%async_computation.9 | async-start | bytes 8388608
  369.6 6.6 slice-start.5
  369.6 143.1 %collective-permute-start.3 = (bf16[512,2048]{1,0:T(8,128)(2,1)}, bf16[512,2048]{1,0:T(8,128)(2,1)}, u32[]{:S(2)}, u32[]{:S(2)}) collective-permute-start(bf16[512,2048]{1,0:T(8,128)(2,1)} %convolution_convert_fusion.3), channel_id=1, source_target_pairs={{0,16},{16,0},{1,17},{17,1},{2,18},{18,2},{3,19},{19,3},{4,20},{20... | collective-permute-start | bytes 6291464 | tf_op jit(solution)/shard_map/ppermute | solution.py:93
  382.0 15.4 %copy-start.58 = (bf16[2048,1024]{1,0:T(8,128)(2,1)S(1)}, bf16[2048,1024]{1,0:T(8,128)(2,1)}, u32[]{:S(2)}) copy-start(bf16[2048,1024]{1,0:T(8,128)(2,1)} %get-tuple-element.94) | copy-start | bytes 12582916
  488.5 5.2 copy-start.3
  488.5 5.2 copy-start.6
  488.5 5.2 copy-start.34
  488.5 5.3 copy-start.39
  488.5 5.6 copy-start.54
  488.6 5.6 copy-start.7
  494.5 5.6 copy-start.15
  494.6 6.9 copy-start.47
  510.6 5.4 copy-start.5
  510.6 5.4 copy-start.36
  510.6 5.4 copy-start.49
  513.4 58.9 %collective-permute-start.4 = (bf16[512,2048]{1,0:T(8,128)(2,1)}, bf16[512,2048]{1,0:T(8,128)(2,1)}, u32[]{:S(2)}, u32[]{:S(2)}) collective-permute-start(bf16[512,2048]{1,0:T(8,128)(2,1)} %convolution_convert_fusion.2), channel_id=1, source_target_pairs={{0,16},{16,0},{1,17},{17,1},{2,18},{18,2},{3,19},{19,3},{4,20},{20... | collective-permute-start | bytes 6291464 | tf_op jit(solution)/shard_map/ppermute | solution.py:93
  517.0 51.3 %copy-start.41 = (f32[128]{0:T(128)S(1)}, f32[128]{0:T(128)}, u32[]{:S(2)}) copy-start(f32[128]{0:T(128)} %copy-done.40) | copy-start | bytes 1540
  517.0 51.4 %copy-start.43 = (f32[128]{0:T(128)S(1)}, f32[128]{0:T(128)}, u32[]{:S(2)}) copy-start(f32[128]{0:T(128)} %copy-done.42) | copy-start | bytes 1540
  517.0 52.9 %copy-start.16 = (bf16[16,8,8,256]{3,1,2,0:T(8,128)(2,1)S(1)}, bf16[16,8,8,256]{3,1,2,0:T(8,128)(2,1)}, u32[]{:S(2)}) copy-start(bf16[16,8,8,256]{3,1,2,0:T(8,128)(2,1)} %copy.31) | copy-start | bytes 1572868
  517.0 155.6 %collective-permute-start.6 = (bf16[512,2048]{1,0:T(8,128)(2,1)}, bf16[512,2048]{1,0:T(8,128)(2,1)}, u32[]{:S(2)}, u32[]{:S(2)}) collective-permute-start(bf16[512,2048]{1,0:T(8,128)(2,1)} %convolution_convert_fusion.1), channel_id=1, source_target_pairs={{0,16},{16,0},{1,17},{17,1},{2,18},{18,2},{3,19},{19,3},{4,20},{20... | collective-permute-start | bytes 6291464 | tf_op jit(solution)/shard_map/ppermute | solution.py:93
  521.7 151.0 %collective-permute-start.7 = (bf16[1024,256]{1,0:T(8,128)(2,1)}, bf16[1024,256]{1,0:T(8,128)(2,1)}, u32[]{:S(2)}, u32[]{:S(2)}) collective-permute-start(bf16[1024,256]{1,0:T(8,128)(2,1)} %convolution_convert_fusion.12), channel_id=1, source_target_pairs={{0,16},{16,0},{1,17},{17,1},{2,18},{18,2},{3,19},{19,3},{4,20},{20... | collective-permute-start | bytes 1572872 | tf_op jit(solution)/shard_map/ppermute | solution.py:93
  572.3 6.3 copy-start.27
  572.3 6.3 copy-start.45
  649.6 13.9 %collective-permute-start.5 = (bf16[2,128]{1,0:T(2,128)(2,1)S(1)}, bf16[2,128]{1,0:T(2,128)(2,1)S(1)}, u32[]{:S(2)}, u32[]{:S(2)}) collective-permute-start(bf16[2,128]{1,0:T(2,128)(2,1)S(1)} %slice_reduce_fusion), channel_id=1, source_target_pairs={{0,16},{16,0},{1,17},{17,1},{2,18},{18,2},{3,19},{19,3},{4,20},{20... | collective-permute-start | bytes 1544 | tf_op jit(solution)/shard_map/ppermute | solution.py:93
  650.9 6.6 copy-start.24
  650.9 6.6 copy-start.29
  650.9 9.1 %copy-start.19 = (bf16[2,16,64,128]{3,2,1,0:T(8,128)(2,1)S(1)}, bf16[2,16,64,128]{3,2,1,0:T(8,128)(2,1)}, u32[]{:S(2)}) copy-start(bf16[2,16,64,128]{3,2,1,0:T(8,128)(2,1)} %get-tuple-element.109) | copy-start | bytes 1572868
  650.9 9.1 %copy-start.28 = (bf16[2,16,64,1024]{3,2,1,0:T(8,128)(2,1)S(1)}, bf16[2,16,64,1024]{3,2,1,0:T(8,128)(2,1)}, u32[]{:S(2)}) copy-start(bf16[2,16,64,1024]{3,2,1,0:T(8,128)(2,1)} %get-tuple-element.110) | copy-start | bytes 12582916
  656.6 30.1 %collective-permute-start.8 = (bf16[128,2048]{1,0:T(8,128)(2,1)}, bf16[128,2048]{1,0:T(8,128)(2,1)}, u32[]{:S(2)}, u32[]{:S(2)}) collective-permute-start(bf16[128,2048]{1,0:T(8,128)(2,1)} %fusion.43), channel_id=1, source_target_pairs={{0,16},{16,0},{1,17},{17,1},{2,18},{18,2},{3,19},{19,3},{4,20},{20... | collective-permute-start | bytes 1572872 | tf_op jit(solution)/shard_map/ppermute | solution.py:93
  665.8 24.5 %collective-permute-start.9 = (bf16[128,1280]{1,0:T(8,128)(2,1)S(1)}, bf16[128,1280]{1,0:T(8,128)(2,1)S(1)}, u32[]{:S(2)}, u32[]{:S(2)}) collective-permute-start(bf16[128,1280]{1,0:T(8,128)(2,1)S(1)} %pad_maximum_fusion.5), channel_id=1, source_target_pairs={{0,16},{16,0},{1,17},{17,1},{2,18},{18,2},{3,19},{19,3},{4,20},{20... | collective-permute-start | bytes 983048 | tf_op jit(solution)/shard_map/ppermute | solution.py:93
  671.8 5.9 copy-start.18
  671.8 19.4 %collective-permute-start.10 = (bf16[128,2048]{1,0:T(8,128)(2,1)S(1)}, bf16[128,2048]{1,0:T(8,128)(2,1)S(1)}, u32[]{:S(2)}, u32[]{:S(2)}) collective-permute-start(bf16[128,2048]{1,0:T(8,128)(2,1)S(1)} %convolution_convert_fusion.9), channel_id=1, source_target_pairs={{0,16},{16,0},{1,17},{17,1},{2,18},{18,2},{3,19},{19,3},{4,20},{20... | collective-permute-start | bytes 1572872 | tf_op jit(solution)/shard_map/ppermute | solution.py:93
  677.7 4.5 copy-start.17
  682.2 4.5 copy-start.13
  682.2 10.6 %copy-start.1 = (bf16[1024,256]{1,0:T(8,128)(2,1)S(1)}, bf16[1024,256]{1,0:T(8,128)(2,1)}, u32[]{:S(2)}) copy-start(bf16[1024,256]{1,0:T(8,128)(2,1)} %param.18) | copy-start | bytes 1572868
  (18 other events, 37.4 us)
Sparse Core Ops, SparseCore 0:
  119.1 76.9 all-gather.3
  249.1 78.8 all-gather.5
  340.3 109.9 reduce-scatter.1
  512.9 86.3 all-gather.7

commit v5 on v4

--- a/solution.py
+++ b/solution.py
@@ -526,6 +526,157 @@
     )(*values)
 
 
+def product_kernel(shards, gate, up, weight, out, *scratch):
+    planes, pair, core_in, short_in, long_in = scratch[:5]
+    plane_sem, core_sem, short_sem, long_sem, done_sem = scratch[5:]
+    long_len, _ = grid_of(shards)
+    me, at_long, at_short, core = neighbours(shards)
+    rows = pair.shape[3]
+    load = pltpu.make_async_copy(weight.at[pl.ds(0, 2)], planes, plane_sem)
+    load.start()
+
+    lines = []
+    first, last = me * 0, me * 0 + long_len - 1
+    for _ in range(long_len - 1):
+        up_side = (last - at_long >= at_long - first).astype(jnp.int32)
+        lines.append((first + up_side * (last - first), 2 * up_side - 1))
+        first, last = first + 1 - up_side, last - up_side
+    lines.append((at_long, None))
+    steps = [(line, sign, 1 - at_short) for line, sign in lines]
+    steps += [(line, sign, at_short) for line, sign in lines]
+
+    def held(at):
+        return pair.at[at, :, core]
+
+    def compute(at):
+        where = pl.ds(pl.multiple_of(at * 2 * rows, 2 * rows), 2 * rows)
+        left = gate[:, where, :].reshape(4 * rows, gate.shape[2])
+        right = up[:, where, :].reshape(4 * rows, up.shape[2])
+
+        @pl.loop(0, pair.shape[4] // 512)
+        def _(tile):
+            columns = pl.ds(pl.multiple_of(tile * 512, 512), 512)
+            sums = jnp.dot(left, planes[0, :, columns], preferred_element_type=jnp.float32)
+            sums += jnp.dot(right, planes[1, :, columns], preferred_element_type=jnp.float32)
+            pair[at, :, :, :, columns] = sums.astype(jnp.bfloat16).reshape(2, 2, rows, 512)
+
+    def to_core(at):
+        return pltpu.make_async_remote_copy(
+            src_ref=pair.at[at, :, 1 - core],
+            dst_ref=core_in.at[at],
+            send_sem=core_sem.at[0, at],
+            recv_sem=core_sem.at[1, at],
+            device_id={"fsdp": me + 1 - 2 * core},
+        )
+
+    def along_short(line, short):
+        return pltpu.make_async_remote_copy(
+            src_ref=held(line * 2 + short),
+            dst_ref=short_in.at[line],
+            send_sem=short_sem.at[0, line],
+            recv_sem=short_sem.at[1, line],
+            device_id={"fsdp": me + 2 - 4 * at_short},
+        )
+
+    def along_long(line, sign):
+        return pltpu.make_async_remote_copy(
+            src_ref=held(line * 2 + at_short),
+            dst_ref=long_in.at[(1 - sign) // 2, line],
+            send_sem=long_sem.at[0, line],
+            recv_sem=long_sem.at[1 + (1 - sign) // 2, line],
+            device_id={"fsdp": me + 4 * sign},
+        )
+
+    def add(at, other):
+        @pl.loop(0, 2 * rows // 16)
+        def _(group):
+            one = group // (rows // 16)
+            where = pl.ds(pl.multiple_of((group % (rows // 16)) * 16, 16), 16)
+            pair[at, one, core, where, :] = (
+                pair[at, one, core, where, :].astype(jnp.float32)
+                + other[one, where, :].astype(jnp.float32)
+            ).astype(jnp.bfloat16)
+
+    def from_behind(at, line, sign):
+        behind = at_long - sign
+
+        @pl.when((behind >= 0) & (behind < long_len))
+        def _():
+            along_long(line, sign).wait_recv()
+            add(at, long_in.at[(1 - sign) // 2, line])
+
+    def settle(at_step):
+        line, sign, short = steps[at_step]
+        at = line * 2 + short
+        to_core(at).wait_recv()
+        add(at, core_in.at[at])
+        if at_step < long_len:
+            along_short(line, short).start()
+            return
+        along_short(line, short).wait_recv()
+        add(at, short_in.at[line])
+        if sign is None:
+            from_behind(at, line, 1)
+            from_behind(at, line, -1)
+        else:
+            from_behind(at, line, sign)
+            along_long(line, sign).start()
+
+    greet(shards, False)
+    load.wait()
+    for at_step, (line, _, short) in enumerate(steps):
+        compute(line * 2 + short)
+        to_core(line * 2 + short).start()
+        if at_step:
+            settle(at_step - 1)
+    settle(len(steps) - 1)
+    result = pltpu.make_async_copy(held(at_long * 2 + at_short), out, done_sem)
+    result.start()
+    for at_step, (line, sign, short) in enumerate(steps):
+        to_core(line * 2 + short).wait_send()
+        if at_step < long_len:
+            along_short(line, short).wait_send()
+        elif sign is not None:
+            along_long(line, sign).wait_send()
+    result.wait()
+
+
+def product_sum(shards, ident, gate, up, weight):
+    batch, every, units = gate.shape
+    columns = weight.shape[2]
+    rows = every // shards
+    long_len, short_len = grid_of(shards)
+    block = (batch, rows, columns)
+    pairs = shards // 2
+    return pl.pallas_call(
+        functools.partial(product_kernel, shards),
+        out_shape=jax.ShapeDtypeStruct(block, jnp.bfloat16),
+        in_specs=[
+            pl.BlockSpec(memory_space=pltpu.VMEM),
+            pl.BlockSpec(memory_space=pltpu.VMEM),
+            pl.BlockSpec(memory_space=pl.ANY),
+        ],
+        out_specs=pl.BlockSpec(memory_space=pl.ANY),
+        scratch_shapes=[
+            pltpu.VMEM((2, units, columns), jnp.bfloat16),
+            pltpu.VMEM((pairs, batch, 2, rows, columns), jnp.bfloat16),
+            pltpu.VMEM((pairs,) + block, jnp.bfloat16),
+            pltpu.VMEM((long_len,) + block, jnp.bfloat16),
+            pltpu.VMEM((2, long_len) + block, jnp.bfloat16),
+            pltpu.SemaphoreType.DMA,
+            pltpu.SemaphoreType.DMA((2, pairs)),
+            pltpu.SemaphoreType.DMA((2, long_len)),
+            pltpu.SemaphoreType.DMA((3, long_len)),
+            pltpu.SemaphoreType.DMA,
+        ],
+        compiler_params=pltpu.CompilerParams(
+            collective_id=ident, has_side_effects=True, vmem_limit_bytes=60 << 20
+        ),
+        cost_estimate=wire_cost(shards, [jax.ShapeDtypeStruct(block, jnp.bfloat16)]),
+        name="product_%d" % ident,
+    )(gate, up, weight)
+
+
 def local(
     tokens, segment_ids, norm_gains, attn_weight, adapter, ffn_weight, ffn_adapter, cotangent
 ):
@@ -664,14 +815,23 @@
             [pair[0] for pair in ffn_parts],
         )
     )
-    (normed_two_grad,) = scatter_sum(
-        shards,
-        5,
-        low(
-            contract(gate_grad, ffn_weight[:, 0, :], 1, 0)
-            + contract(up_grad, ffn_weight[:, 1, :], 1, 0)
-        ).reshape(micro, shards, local_len, model_dim),
-    )
+    if grid_of(shards)[1] == 2 and micro == 2:
+        normed_two_grad = product_sum(
+            shards,
+            5,
+            gate_grad.reshape(micro, seq_len, hidden_cols),
+            up_grad.reshape(micro, seq_len, hidden_cols),
+            ffn_weight.transpose(1, 0, 2),
+        )
+    else:
+        (normed_two_grad,) = scatter_sum(
+            shards,
+            5,
+            low(
+                contract(gate_grad, ffn_weight[:, 0, :], 1, 0)
+                + contract(up_grad, ffn_weight[:, 1, :], 1, 0)
+            ).reshape(micro, shards, local_len, model_dim),
+        )
     normed_two_grad, down_sum, _ = lax.optimization_barrier(
         (normed_two_grad, down_sum, [pair[1] for pair in ffn_parts[:2]])
     )

time: 707 us -> 712 us (level)
  matrix products: 220 us -> 190 us
  waiting for transfers between devices: 0.1 us -> 19.7 us
  Pallas kernels: 383 us -> 400 us
    pallas_call x0 -> x1, Pallas kernels: none -> 87.5 us  [product_sum(): pl.pallas_call(functools.partial(product_kernel, shards), out_shape=jax.S...]
    pallas_call x2 -> x1, Pallas kernels: 110 us -> 40.3 us  [scatter_sum(): pl.pallas_call(functools.partial(scatter_kernel, shards, widths), out_sha...]
    dot_general x30 -> x28, matrix products: 209 us -> 178 us  [contract(): lax.dot_general(left_op, right_op, (((left_dim,), (right_dim,)), ((), ())...]
    ppermute x11, waiting for transfers between devices: 0.03 us -> 19.6 us  [swap_rep(): return lax.ppermute(values, 'rep', [(0, 1), (1, 0)])]
  transfers between devices with their start and end apart: 15 -> 15, of which waited for: 0 -> 1; matrix products, arithmetic and copies ran while one was open for 40% -> 35% of each run, Pallas kernels for 39% -> 41%
where the time goes in v5:
time: 712 us; the launch traced here: 704 us
  Pallas kernels  400 us (56%)
  matrix products  190 us (27%)
  other arithmetic  49.1 us (7%)
  waiting for transfers between devices  19.7 us (3%)
  local copies, waits for them, and re-layouts  19.5 us (3%)
  between operations  14.9 us (2%)
  starting transfers between devices  11.3 us (2%)
    pallas_call x4, Pallas kernels, gather_all(): pl.pallas_call(functools.partial(gather_kernel, shards, widths, shared, l...  272 us
    dot_general x28, matrix products, contract(): lax.dot_general(left_op, right_op, (((left_dim,), (right_dim,)), ((), ())...  178 us
    pallas_call x1, Pallas kernels, product_sum(): pl.pallas_call(functools.partial(product_kernel, shards), out_shape=jax.S...  87.5 us
    pallas_call x1, Pallas kernels, scatter_sum(): pl.pallas_call(functools.partial(scatter_kernel, shards, widths), out_sha...  40.3 us
    dynamic_update_slice x6, other arithmetic, place(): lax.dynamic_update_slice(whole, total(mine, other)[None], (at % 3, at //...  28.9 us
    ppermute x11, waiting for transfers between devices, swap_rep(): return lax.ppermute(values, 'rep', [(0, 1), (1, 0)])  19.6 us
  transfers between devices with their start and end apart: 15, of which 1 were waited for; matrix products, arithmetic and copies ran while one was open for 35% of the time, Pallas kernels for 41%

profile of v5, /device:TPU:0, one launch (start us, length us, event | category | flops | bytes accessed | tf_op | source)
XLA Modules:
  0.0 703.8 jit_solution(14277760234102750781)
XLA Ops:
  9.7 109.2 %gather_1.1 = (bf16[1,16,128,4608]{3,2,1,0:T(8,128)(2,1)}, bf16[1,16,128,768]{3,2,1,0:T(8,128)(2,1)}, bf16[1,16,128,128]{3,2,1,0:T(8,128)(2,1)}) custom-call(bf16[1,128,4608]{2,1,0:T(8,128)(2,1)} %bitcast.201, bf16[1,128,768]{2,1,0:T(8,128)(2,1)} %bitcast.226, bf16[1,128,128]{2,1,0:T(8,128)(2,1)} %maximum_bitcast_fusion.refs_2_), custom_call_target="tpu_custom_call" | custom-call | bytes 583008256 | tf_op jit(solution)/shard_map/gather_1/pallas_call | solution.py:322
  119.2 1.2 slice.189
  120.9 0.9 convert_reduce_fusion
  121.8 1.3 copy.29
  124.8 5.7 fusion.3
  132.3 1.2 fusion.90
  134.2 34.9 %gather_2.1 = (bf16[2,16,64,256]{3,2,1,0:T(8,128)(2,1)}, bf16[2,16,64,256]{3,2,1,0:T(8,128)(2,1)}) custom-call(bf16[2,64,256]{2,1,0:T(8,128)(2,1)} %pad_maximum_fusion.6.refs_0_, bf16[2,64,256]{2,1,0:T(8,128)(2,1)} %bitcast.217), custom_call_target="tpu_custom_call" | custom-call | bytes 92274688 | tf_op jit(solution)/shard_map/gather_2/pallas_call | solution.py:322
  169.6 2.2 fusion.88
  171.7 2.1 fusion.102
  173.9 2.0 copy-done.8
  176.9 6.4 multiply_reduce_fusion.1
  183.3 0.9 copy-done.2
  184.2 1.0 multiply_convert_fusion.4
  185.2 63.0 %gather_3.1 = bf16[2,16,64,2048]{3,2,1,0:T(8,128)(2,1)} custom-call(bf16[2,64,2048]{2,1,0:T(8,128)(2,1)} %bitcast.192), custom_call_target="tpu_custom_call" | custom-call | bytes 243269632 | tf_op jit(solution)/shard_map/gather_3/pallas_call | solution.py:322
  248.2 0.9 pad_maximum_fusion
  249.3 14.6 %fusion.23 = f32[2048,1024]{1,0:T(8,128)} fusion(bf16[2048,2048]{1,0:T(8,128)(2,1)} %bitcast.167, bf16[1024,3,2048]{2,0,1:T(8,128)(2,1)} %param.17), kind=kOutput, calls=%fused_computation.36 | convolution fusion | flops 8589934592 | bytes 20971520 | tf_op jit(solution)/shard_map/dot_general | solution.py:52
  263.9 14.5 %fusion.21 = f32[2048,1024]{1,0:T(8,128)} fusion(bf16[2048,2048]{1,0:T(8,128)(2,1)} %bitcast.168, bf16[1024,3,2048]{2,0,1:T(8,128)(2,1)} %param.17), kind=kOutput, calls=%fused_computation.34 | convolution fusion | flops 8589934592 | bytes 20971520 | tf_op jit(solution)/shard_map/dot_general | solution.py:52
  278.4 6.1 convolution_convert_fusion.8
  284.5 1.1 copy-done.40
  285.6 13.5 %fusion.18 = f32[2048,1024]{1,0:T(8,128)} fusion(bf16[2048,2048]{1,0:T(8,128)(2,1)S(1)} %bitcast.236, bf16[1024,3,2048]{2,0,1:T(8,128)(2,1)} %param.17), kind=kOutput, calls=%fused_computation.31 | convolution fusion | flops 8589934592 | bytes 20971520 | tf_op jit(solution)/shard_map/dot_general | solution.py:52
  299.1 17.6 %multiply_convert_fusion = (bf16[2048,1024]{1,0:T(8,128)(2,1)}, bf16[2048,1024]{1,0:T(8,128)(2,1)}, bf16[2048,1024]{1,0:T(8,128)(2,1)}) fusion(f32[2048,1024]{1,0:T(8,128)} %fusion.23, f32[2048,1024]{1,0:T(8,128)} %fusion.21, f32[2048,1024]{1,0:T(8,128)} %fusion.18, bf16[2048,256]{1,0:T(8,128)(2,1)S(1)} %convolution_convert_fusion.8, ...), kind=kOutput, calls=%fused_computation.16 | convolution fusion | flops 1130364928 | bytes 39321600 | tf_op jit(solution)/shard_map/dot_general | solution.py:52
  316.7 4.6 convolution_convert_fusion.7
  321.3 4.7 convolution_convert_fusion.6
  326.1 13.6 %convolution_convert_fusion = bf16[2048,2048]{1,0:T(8,128)(2,1)} fusion(bf16[2048,1024]{1,0:T(8,128)(2,1)S(1)} %copy-done.58, bf16[1024,3,2048]{2,0,1:T(8,128)(2,1)} %param.17), kind=kOutput, calls=%fused_computation.19 | convolution fusion | flops 8594128896 | bytes 16777216 | tf_op jit(solution)/shard_map/dot_general | solution.py:52
  340.6 11.0 %convolution_convert_fusion.5 = bf16[512,2048]{1,0:T(8,128)(2,1)} fusion(bf16[2048,2048]{1,0:T(8,128)(2,1)} %bitcast.169, bf16[2048,1024]{1,0:T(8,128)(2,1)} %get-tuple-element.94), kind=kOutput, calls=%fused_computation.53 | convolution fusion | flops 4296015872 | bytes 12582912 | tf_op jit(solution)/shard_map/dot_general | solution.py:52
  351.6 10.3 %convolution_convert_fusion.2 = bf16[512,2048]{1,0:T(8,128)(2,1)} fusion(bf16[2048,2048]{1,0:T(8,128)(2,1)} %bitcast.170, bf16[2048,1024]{1,0:T(8,128)(2,1)S(1)} %copy-done.11), kind=kOutput, calls=%fused_computation.50 | convolution fusion | flops 4296015872 | bytes 12582912 | tf_op jit(solution)/shard_map/dot_general | solution.py:52
  361.9 5.8 convolution_convert_fusion.4
  367.7 5.8 convolution_convert_fusion.3
  374.2 1.3 collective-permute-start.2
  376.2 5.8 convolution_convert_fusion.1
  382.0 87.5 %product_5.1 = bf16[2,64,2048]{2,1,0:T(8,128)(2,1)} custom-call(bf16[2,1024,1024]{2,1,0:T(8,128)(2,1)} %bitcast.181, bf16[2,1024,1024]{2,1,0:T(8,128)(2,1)} %bitcast.180, bf16[3,1024,2048]{2,1,0:T(8,128)(2,1)} %bitcast.165), custom_call_target="tpu_custom_call" | custom-call | bytes 243269632 | tf_op jit(solution)/shard_map/product_5/pallas_call | solution.py:651
  469.5 4.4 bitcast_dynamic-update-slice_fusion.5
  473.9 5.0 bitcast_dynamic-update-slice_fusion.4
  478.9 5.2 bitcast_dynamic-update-slice_fusion.3
  484.9 5.6 fusion.35
  490.6 1.3 reshape.506
  491.9 3.6 multiply_reduce_fusion
  498.1 0.9 copy.31
  499.0 1.9 multiply_convert_fusion.3
  501.0 2.1 convolution_convert_fusion.10
  503.1 19.6 %collective-permute-done.3 = bf16[512,2048]{1,0:T(8,128)(2,1)} collective-permute-done((bf16[512,2048]{1,0:T(8,128)(2,1)}, bf16[512,2048]{1,0:T(8,128)(2,1)}, u32[]{:S(2)}, u32[]{:S(2)}) %collective-permute-start.3) | collective-permute-done | bytes 2097184 | tf_op jit(solution)/shard_map/ppermute | solution.py:93
  523.4 1.2 collective-permute-start.4
  524.6 1.0 fusion.68.refs_1_
  526.4 5.0 convolution_convert_fusion.12
  531.4 1.1 collective-permute-start.7
  532.5 40.3 %scatter_6.1 = (bf16[2,64,256]{2,1,0:T(8,128)(2,1)}, bf16[2,64,256]{2,1,0:T(8,128)(2,1)}, bf16[2,64,256]{2,1,0:T(8,128)(2,1)}) custom-call(bf16[2,16,64,256]{3,2,1,0:T(8,128)(2,1)} %bitcast.203, bf16[2,16,64,256]{3,2,1,0:T(8,128)(2,1)} %bitcast.204, bf16[2,16,64,256]{3,2,1,0:T(8,128)(2,1)} %bitcast.202), custom_call_target="tpu_custom_call" | custom-call | bytes 117440512 | tf_op jit(solution)/shard_map/scatter_6/pallas_call | solution.py:505
  575.2 1.6 constant_dynamic-update-slice_fusion.1
  577.6 6.3 fusion.1
  583.9 2.8 fusion.65
  588.2 64.6 %gather_4.1 = (bf16[2,16,64,1024]{3,2,1,0:T(8,128)(2,1)}, bf16[2,16,64,128]{3,2,1,0:T(8,128)(2,1)}, bf16[2,16,64,128]{3,2,1,0:T(8,128)(2,1)}, bf16[1,16,16,128]{3,2,1,0:T(8,128)(2,1)}) custom-call(bf16[2,64,1024]{2,1,0:T(8,128)(2,1)} %bitcast.212, bf16[2,64,2048]{2,1,0:T(8,128)(2,1)} %fusion.68.refs_1_, bf16[2,64,2048]{2,1,0:T(8,128)(2,1)} %bitcast.191, ...), custom_call_target="tpu_custom_call" | custom-call | bytes 142606336 | tf_op jit(solution)/shard_map/gather_4/pallas_call | solution.py:322
  653.6 1.8 collective-permute-start.5
  655.4 5.8 fusion.38
  661.5 2.5 fusion.41
  664.7 1.5 fusion.60
  666.2 1.4 convolution_convert_fusion.13
  668.1 1.8 convolution_convert_fusion.14
  669.9 1.8 collective-permute-start.9
  671.7 4.7 convolution_convert_fusion.9
  676.8 5.2 bitcast_dynamic-update-slice_fusion.2
  682.0 4.5 bitcast_dynamic-update-slice_fusion.1
  686.6 4.5 bitcast_dynamic-update-slice_fusion
  691.1 1.3 add_dynamic-update-slice_fusion.1
  692.4 2.3 convert_add_fusion.1
  695.7 1.4 copy-done.17
  (224 shorter events, 24.7 us)
Async XLA Ops:
  7.2 292.0 %copy-start = (bf16[1024,256]{1,0:T(8,128)(2,1)S(1)}, bf16[1024,256]{1,0:T(8,128)(2,1)}, u32[]{:S(2)}) copy-start(bf16[1024,256]{1,0:T(8,128)(2,1)} %param.18) | copy-start | bytes 1572868
  7.2 115.9 %copy-start.4 = (bf16[2,64,2048]{2,1,0:T(8,128)(2,1)S(1)}, bf16[2,64,2048]{2,1,0:T(8,128)(2,1)}, u32[]{:S(2)}) copy-start(bf16[2,64,2048]{2,1,0:T(8,128)(2,1)} %param.12) | copy-start | bytes 1572868
  7.2 271.2 %all-gather.4.cloned.1.call-start = ((), (), s32[]{:S(2)}) async-start(), calls=%async_computation.1 | async-start | bytes 8912896 | tf_op jit(solution)/shard_map/all_gather | solution.py:74
  119.0 263.0 %all-gather.6.cloned.1.call-start = ((), (), s32[]{:S(2)}) async-start(), calls=%async_computation.2 | async-start | bytes 10027008 | tf_op jit(solution)/shard_map/all_gather | solution.py:74
  124.5 5.9 copy-start.47
  124.6 5.9 copy-start.38
  124.6 58.7 %copy-start.36 = (f32[2048,1]{0,1:T(1,128)}, f32[2048,1]{0,1:T(1,128)S(1)}, u32[]{:S(2)}) copy-start(f32[2048,1]{0,1:T(1,128)S(1)} %get-tuple-element.146) | copy-start | bytes 24580
  124.8 6.4 copy-start.15
  130.5 38.7 %copy-start.51 = (s32[2,64]{1,0:T(2,128)S(1)}, s32[2,64]{1,0:T(2,128)}, u32[]{:S(2)}) copy-start(s32[2,64]{1,0:T(2,128)} %param.13) | copy-start | bytes 1540
  169.5 4.3 copy-start.23
  169.6 4.3 copy-start.25
  171.7 4.1 copy-start.53
  183.3 64.9 %copy-start.56 = (f32[128]{0:T(128)}, f32[128]{0:T(128)S(1)}, u32[]{:S(2)}) copy-start(f32[128]{0:T(128)S(1)} %get-tuple-element.158) | copy-start | bytes 1540
  183.3 64.9 %copy-start.41 = (f32[128]{0:T(128)}, f32[128]{0:T(128)S(1)}, u32[]{:S(2)}) copy-start(f32[128]{0:T(128)S(1)} %fusion.93) | copy-start | bytes 1540
  249.1 235.1 %reduce-scatter.2.cloned.1.call-start = ((), (), s32[]{:S(2)}) async-start(), calls=%async_computation.3 | async-start | bytes 8912896 | tf_op jit(solution)/shard_map/reduce_scatter | solution.py:78
  278.4 7.2 %copy-start.40 = (bf16[2,1024,2048]{2,1,0:T(8,128)(2,1)S(1)}, bf16[2,1024,2048]{2,1,0:T(8,128)(2,1)}, u32[]{:S(2)}) copy-start(bf16[2,1024,2048]{2,1,0:T(8,128)(2,1)} %all-gather.4.cloned.1.call-done) | copy-start | bytes 25165828
  285.6 13.5 %copy-start.60 = (bf16[2048,256]{1,0:T(8,128)(2,1)}, bf16[2048,256]{1,0:T(8,128)(2,1)S(1)}, u32[]{:S(2)}) copy-start(bf16[2048,256]{1,0:T(8,128)(2,1)S(1)} %convolution_convert_fusion.8) | copy-start | bytes 3145732
  285.6 35.7 %slice-start = ((s8[8388608]{0:T(1024)(128)(4,1)}), s8[4194304]{0:T(1024)(128)(4,1)S(1)}, s32[]{:S(2)}) async-start(s8[8388608]{0:T(1024)(128)(4,1)} %bitcast.171), calls=%async_computation.5 | async-start | bytes 8388608
  299.1 22.2 %slice-start.1 = ((s8[8388608]{0:T(1024)(128)(4,1)}), s8[4194304]{0:T(1024)(128)(4,1)S(1)}, s32[]{:S(2)}) async-start(s8[8388608]{0:T(1024)(128)(4,1)} %bitcast.171), calls=%async_computation.6 | async-start | bytes 8388608
  316.7 4.6 copy-start.12
  321.3 4.8 copy-start.58
  339.7 328.4 %all-gather.8.cloned.1.call-start = ((), (), s32[]{:S(2)}) async-start(), calls=%async_computation.4 | async-start | bytes 8912896 | tf_op jit(solution)/shard_map/all_gather | solution.py:74
  339.8 11.9 %copy-start.11 = (bf16[2048,1024]{1,0:T(8,128)(2,1)S(1)}, bf16[2048,1024]{1,0:T(8,128)(2,1)}, u32[]{:S(2)}) copy-start(bf16[2048,1024]{1,0:T(8,128)(2,1)} %get-tuple-element.94) | copy-start | bytes 12582916
  339.8 129.7 %collective-permute-start = (bf16[512,2048]{1,0:T(8,128)(2,1)S(1)}, bf16[512,2048]{1,0:T(8,128)(2,1)}, u32[]{:S(2)}, u32[]{:S(2)}) collective-permute-start(bf16[512,2048]{1,0:T(8,128)(2,1)S(1)} %convolution_convert_fusion.6), channel_id=1, source_target_pairs={{0,16},{16,0},{1,17},{17,1},{2,18},{18,2},{3,19},{19,3},{4,20},{20... | collective-permute-start | bytes 6291464 | tf_op jit(solution)/shard_map/ppermute | solution.py:93
  340.6 21.3 %slice-start.4 = ((s8[8388608]{0:T(1024)(128)(4,1)}), s8[4194304]{0:T(1024)(128)(4,1)S(1)}, s32[]{:S(2)}) async-start(s8[8388608]{0:T(1024)(128)(4,1)} %bitcast.237), calls=%async_computation.9 | async-start | bytes 8388608
  351.6 10.3 %slice-start.5 = ((s8[8388608]{0:T(1024)(128)(4,1)}), s8[4194304]{0:T(1024)(128)(4,1)S(1)}, s32[]{:S(2)}) async-start(s8[8388608]{0:T(1024)(128)(4,1)} %bitcast.237), calls=%async_computation.10 | async-start | bytes 8388608
  351.6 10.3 %copy-start.59 = (bf16[2048,1024]{1,0:T(8,128)(2,1)S(1)}, bf16[2048,1024]{1,0:T(8,128)(2,1)}, u32[]{:S(2)}) copy-start(bf16[2048,1024]{1,0:T(8,128)(2,1)} %get-tuple-element.92) | copy-start | bytes 12582916
  351.6 16.1 %slice-start.2 = ((s8[8388608]{0:T(1024)(128)(4,1)}), s8[4194304]{0:T(1024)(128)(4,1)S(1)}, s32[]{:S(2)}) async-start(s8[8388608]{0:T(1024)(128)(4,1)} %bitcast.174), calls=%async_computation.7 | async-start | bytes 8388608
  361.9 5.8 slice-start.3
  361.9 5.8 copy-start.13
  373.5 100.4 %collective-permute-start.1 = (bf16[512,2048]{1,0:T(8,128)(2,1)}, bf16[512,2048]{1,0:T(8,128)(2,1)}, u32[]{:S(2)}, u32[]{:S(2)}) collective-permute-start(bf16[512,2048]{1,0:T(8,128)(2,1)} %convolution_convert_fusion.5), channel_id=1, source_target_pairs={{0,16},{16,0},{1,17},{17,1},{2,18},{18,2},{3,19},{19,3},{4,20},{20... | collective-permute-start | bytes 6291464 | tf_op jit(solution)/shard_map/ppermute | solution.py:93
  374.2 104.8 %collective-permute-start.2 = (bf16[512,2048]{1,0:T(8,128)(2,1)}, bf16[512,2048]{1,0:T(8,128)(2,1)}, u32[]{:S(2)}, u32[]{:S(2)}) collective-permute-start(bf16[512,2048]{1,0:T(8,128)(2,1)} %convolution_convert_fusion.4), channel_id=1, source_target_pairs={{0,16},{16,0},{1,17},{17,1},{2,18},{18,2},{3,19},{19,3},{4,20},{20... | collective-permute-start | bytes 6291464 | tf_op jit(solution)/shard_map/ppermute | solution.py:93
  375.5 147.2 %collective-permute-start.3 = (bf16[512,2048]{1,0:T(8,128)(2,1)}, bf16[512,2048]{1,0:T(8,128)(2,1)}, u32[]{:S(2)}, u32[]{:S(2)}) collective-permute-start(bf16[512,2048]{1,0:T(8,128)(2,1)} %convolution_convert_fusion.3), channel_id=1, source_target_pairs={{0,16},{16,0},{1,17},{17,1},{2,18},{18,2},{3,19},{19,3},{4,20},{20... | collective-permute-start | bytes 6291464 | tf_op jit(solution)/shard_map/ppermute | solution.py:93
  478.9 5.2 copy-start.3
  478.9 5.2 copy-start.6
  478.9 5.2 copy-start.37
  478.9 5.3 copy-start.42
  478.9 5.6 copy-start.57
  478.9 5.6 copy-start.7
  484.9 5.6 copy-start.18
  484.9 6.9 copy-start.50
  501.0 23.7 %copy-start.5 = (bf16[2,64,2048]{2,1,0:T(8,128)(2,1)S(1)}, bf16[2,64,2048]{2,1,0:T(8,128)(2,1)}, u32[]{:S(2)}) copy-start(bf16[2,64,2048]{2,1,0:T(8,128)(2,1)} %param.12) | copy-start | bytes 1572868
  501.0 23.7 %copy-start.39 = (f32[2048,1]{0,1:T(1,128)S(1)}, f32[2048,1]{0,1:T(1,128)}, u32[]{:S(2)}) copy-start(f32[2048,1]{0,1:T(1,128)} %copy-done.38) | copy-start | bytes 24580
  501.0 23.7 %copy-start.52 = (f32[2,64]{1,0:T(2,128)S(1)}, f32[2,64]{1,0:T(2,128)}, u32[]{:S(2)}) copy-start(f32[2,64]{1,0:T(2,128)} %get-tuple-element.148) | copy-start | bytes 1540
  523.4 54.2 %collective-permute-start.4 = (bf16[512,2048]{1,0:T(8,128)(2,1)}, bf16[512,2048]{1,0:T(8,128)(2,1)}, u32[]{:S(2)}, u32[]{:S(2)}) collective-permute-start(bf16[512,2048]{1,0:T(8,128)(2,1)} %convolution_convert_fusion.2), channel_id=1, source_target_pairs={{0,16},{16,0},{1,17},{17,1},{2,18},{18,2},{3,19},{19,3},{4,20},{20... | collective-permute-start | bytes 6291464 | tf_op jit(solution)/shard_map/ppermute | solution.py:93
  525.6 48.0 %copy-start.44 = (f32[128]{0:T(128)S(1)}, f32[128]{0:T(128)}, u32[]{:S(2)}) copy-start(f32[128]{0:T(128)} %copy-done.43) | copy-start | bytes 1540
  525.6 48.0 %copy-start.46 = (f32[128]{0:T(128)S(1)}, f32[128]{0:T(128)}, u32[]{:S(2)}) copy-start(f32[128]{0:T(128)} %copy-done.45) | copy-start | bytes 1540
  525.6 49.6 %copy-start.19 = (bf16[16,8,8,256]{3,1,2,0:T(8,128)(2,1)S(1)}, bf16[16,8,8,256]{3,1,2,0:T(8,128)(2,1)}, u32[]{:S(2)}) copy-start(bf16[16,8,8,256]{3,1,2,0:T(8,128)(2,1)} %copy.31) | copy-start | bytes 1572868
  525.6 151.2 %collective-permute-start.6 = (bf16[512,2048]{1,0:T(8,128)(2,1)}, bf16[512,2048]{1,0:T(8,128)(2,1)}, u32[]{:S(2)}, u32[]{:S(2)}) collective-permute-start(bf16[512,2048]{1,0:T(8,128)(2,1)} %convolution_convert_fusion.1), channel_id=1, source_target_pairs={{0,16},{16,0},{1,17},{17,1},{2,18},{18,2},{3,19},{19,3},{4,20},{20... | collective-permute-start | bytes 6291464 | tf_op jit(solution)/shard_map/ppermute | solution.py:93
  531.4 145.4 %collective-permute-start.7 = (bf16[1024,256]{1,0:T(8,128)(2,1)}, bf16[1024,256]{1,0:T(8,128)(2,1)}, u32[]{:S(2)}, u32[]{:S(2)}) collective-permute-start(bf16[1024,256]{1,0:T(8,128)(2,1)} %convolution_convert_fusion.12), channel_id=1, source_target_pairs={{0,16},{16,0},{1,17},{17,1},{2,18},{18,2},{3,19},{19,3},{4,20},{20... | collective-permute-start | bytes 1572872 | tf_op jit(solution)/shard_map/ppermute | solution.py:93
  577.6 6.3 copy-start.30
  577.6 6.3 copy-start.48
  653.6 13.9 %collective-permute-start.5 = (bf16[2,128]{1,0:T(2,128)(2,1)S(1)}, bf16[2,128]{1,0:T(2,128)(2,1)S(1)}, u32[]{:S(2)}, u32[]{:S(2)}) collective-permute-start(bf16[2,128]{1,0:T(2,128)(2,1)S(1)} %slice_reduce_fusion), channel_id=1, source_target_pairs={{0,16},{16,0},{1,17},{17,1},{2,18},{18,2},{3,19},{19,3},{4,20},{20... | collective-permute-start | bytes 1544 | tf_op jit(solution)/shard_map/ppermute | solution.py:93
  655.4 6.1 copy-start.27
  655.4 6.1 copy-start.32
  655.4 8.6 %copy-start.22 = (bf16[2,16,64,128]{3,2,1,0:T(8,128)(2,1)S(1)}, bf16[2,16,64,128]{3,2,1,0:T(8,128)(2,1)}, u32[]{:S(2)}) copy-start(bf16[2,16,64,128]{3,2,1,0:T(8,128)(2,1)} %get-tuple-element.109) | copy-start | bytes 1572868
  655.4 8.6 %copy-start.31 = (bf16[2,16,64,1024]{3,2,1,0:T(8,128)(2,1)S(1)}, bf16[2,16,64,1024]{3,2,1,0:T(8,128)(2,1)}, u32[]{:S(2)}) copy-start(bf16[2,16,64,1024]{3,2,1,0:T(8,128)(2,1)} %get-tuple-element.110) | copy-start | bytes 12582916
  661.2 29.8 %collective-permute-start.8 = (bf16[128,2048]{1,0:T(8,128)(2,1)}, bf16[128,2048]{1,0:T(8,128)(2,1)}, u32[]{:S(2)}, u32[]{:S(2)}) collective-permute-start(bf16[128,2048]{1,0:T(8,128)(2,1)} %fusion.38), channel_id=1, source_target_pairs={{0,16},{16,0},{1,17},{17,1},{2,18},{18,2},{3,19},{19,3},{4,20},{20... | collective-permute-start | bytes 1572872 | tf_op jit(solution)/shard_map/ppermute | solution.py:93
  669.9 24.7 %collective-permute-start.9 = (bf16[128,1280]{1,0:T(8,128)(2,1)S(1)}, bf16[128,1280]{1,0:T(8,128)(2,1)S(1)}, u32[]{:S(2)}, u32[]{:S(2)}) collective-permute-start(bf16[128,1280]{1,0:T(8,128)(2,1)S(1)} %pad_maximum_fusion.5), channel_id=1, source_target_pairs={{0,16},{16,0},{1,17},{17,1},{2,18},{18,2},{3,19},{19,3},{4,20},{20... | collective-permute-start | bytes 983048 | tf_op jit(solution)/shard_map/ppermute | solution.py:93
  676.4 5.6 copy-start.20
  676.4 19.1 %collective-permute-start.10 = (bf16[128,2048]{1,0:T(8,128)(2,1)S(1)}, bf16[128,2048]{1,0:T(8,128)(2,1)S(1)}, u32[]{:S(2)}, u32[]{:S(2)}) collective-permute-start(bf16[128,2048]{1,0:T(8,128)(2,1)S(1)} %convolution_convert_fusion.9), channel_id=1, source_target_pairs={{0,16},{16,0},{1,17},{17,1},{2,18},{18,2},{3,19},{19,3},{4,20},{20... | collective-permute-start | bytes 1572872 | tf_op jit(solution)/shard_map/ppermute | solution.py:93
  682.0 4.5 copy-start.21
  686.6 4.5 copy-start.16
  686.6 10.6 %copy-start.1 = (bf16[1024,256]{1,0:T(8,128)(2,1)S(1)}, bf16[1024,256]{1,0:T(8,128)(2,1)}, u32[]{:S(2)}) copy-start(bf16[1024,256]{1,0:T(8,128)(2,1)} %param.18) | copy-start | bytes 1572868
  (18 other events, 36.7 us)
Sparse Core Ops, SparseCore 0:
  119.1 77.1 all-gather.3
  249.2 78.8 all-gather.5
  339.8 125.8 reduce-scatter.1
  522.8 78.1 all-gather.7

commit v6 on v5

--- a/solution.py
+++ b/solution.py
@@ -12,7 +12,6 @@
 RANK = 256
 CHUNKS = 1
 PIECES = 2
-EARLY = 3
 
 
 epsilon = 1e-06
@@ -82,11 +81,47 @@
     return mine.astype(jnp.float32) + other.astype(jnp.float32)
 
 
-def place(whole, at, pair):
-    mine, other = pair
-    return lax.dynamic_update_slice(
-        whole, total(mine, other)[None], (at % 3, at // 3 * mine.shape[0], 0)
-    )
+def place_kernel(kinds, *refs):
+    out = refs[-1]
+    for kind in range(kinds):
+
+        @pl.when(pl.program_id(0) == kind)
+        def _():
+            mine, other = refs[2 * kind], refs[2 * kind + 1]
+            out[0] = total(mine[...], other[...])
+
+
+def place(whole, group, groups, pairs):
+    kinds = len(pairs)
+    rows, columns = pairs[0][0].shape
+    tile = min(rows, 128)
+    tiles = rows // tile
+
+    def part(kind):
+        return pl.BlockSpec(
+            (tile, columns),
+            lambda k, j: (jnp.where(k == kind, j, jnp.where(k < kind, 0, tiles - 1)), 0),
+        )
+
+    in_specs = [part(kind) for kind in range(kinds) for _ in range(2)]
+    operands = [each for pair in pairs for each in pair]
+    aliases = {}
+    if whole is not None:
+        aliases = {len(operands): 0}
+        in_specs.append(pl.BlockSpec(memory_space=pl.ANY))
+        operands.append(whole)
+    moved = kinds * rows * columns
+    return pl.pallas_call(
+        functools.partial(place_kernel, kinds),
+        grid=(kinds, tiles),
+        out_shape=jax.ShapeDtypeStruct((kinds, groups * rows, columns), jnp.float32),
+        in_specs=in_specs,
+        out_specs=pl.BlockSpec((1, tile, columns), lambda k, j: (k, group * tiles + j, 0)),
+        input_output_aliases=aliases,
+        cost_estimate=pl.CostEstimate(flops=moved, bytes_accessed=8 * moved, transcendentals=0),
+        compiler_params=pltpu.CompilerParams(vmem_limit_bytes=24 << 20),
+        name="place_%d" % group,
+    )(*operands)
 
 
 def swap_rep(values):
@@ -850,11 +885,9 @@
     query_pre_grad = low(rotate(query_grad, -angles[:, None, :]).reshape(count, q_width))
     key_part = low(batched(score_grad, queries, 1, 1) * score_scale)
     value_part = low(batched(weights_low, context_rows, 1, 1))
-    ffn_grad = unwritten((3, hidden_cols, model_dim), jnp.float32)
-    for at in range(EARLY):
-        ffn_grad = place(ffn_grad, at, ffn_parts[at])
-    key_part, value_part, query_pre_grad, ffn_grad, ffn_parts[3:4] = lax.optimization_barrier(
-        (key_part, value_part, query_pre_grad, ffn_grad, ffn_parts[3:4])
+    ffn_grad = place(None, 0, PIECES, ffn_parts[:3])
+    key_part, value_part, query_pre_grad, ffn_grad = lax.optimization_barrier(
+        (key_part, value_part, query_pre_grad, ffn_grad)
     )
     q_all = gather_rows(query_pre_grad.reshape(micro, local_len, q_width))
     q_all = q_all.reshape(every, q_width)
@@ -883,7 +916,7 @@
     input_grad = low(mixed_grad + hidden_part)
 
     narrow = jnp.concatenate([key_grad, value_grad, rank_grad, down_low], axis=1)
-    narrow, ffn_parts[3:5] = lax.optimization_barrier((narrow, ffn_parts[3:5]))
+    narrow, ffn_parts[3:4] = lax.optimization_barrier((narrow, ffn_parts[3:4]))
     gain_parts = jnp.zeros((1, 16, model_dim), jnp.bfloat16)
     gain_parts = gain_parts.at[0, 0].set(low(gain_one_grad)).at[0, 1].set(low(gain_two_grad))
     narrow_all, normed_cols, out_cols, gain_cols = gather_all(
@@ -920,8 +953,7 @@
         (attn_q, tail, tail_out, ffn_parts[3:], low_mine, low_other)
     )
     gains_grad = total(tail_gain, swap_rep(tail_gain)).transpose(1, 0)
-    for at in range(EARLY, 3 * PIECES):
-        ffn_grad = place(ffn_grad, at, ffn_parts[at])
+    ffn_grad = place(ffn_grad, 1, PIECES, ffn_parts[3:])
     ffn_grad = ffn_grad.transpose(1, 0, 2)
     ffn_low_grad = total(low_mine, low_other)
     tail = total(tail, crossing[1])

time: 712 us -> 709 us (level)
  other arithmetic: 49.1 us -> 22.7 us
  Pallas kernels: 400 us -> 426 us
    dynamic_update_slice x6 -> x0, other arithmetic: 28.9 us -> none  [place(): lax.dynamic_update_slice(whole, total(mine, other)[None], (at % 3, at //...]
    pallas_call x0 -> x2, Pallas kernels: none -> 25.2 us  [place(): pl.pallas_call(functools.partial(place_kernel, kinds), grid=(kinds, tiles...]
  transfers between devices with their start and end apart: 15 -> 15, of which waited for: 1 -> 4; matrix products, arithmetic and copies ran while one was open for 35% -> 29% of each run, Pallas kernels for 41% -> 45%
where the time goes in v6:
time: 709 us; the launch traced here: 702 us
  Pallas kernels  426 us (60%)
  matrix products  191 us (27%)
  other arithmetic  22.7 us (3%)
  local copies, waits for them, and re-layouts  19.8 us (3%)
  waiting for transfers between devices  15 us (2%)
  between operations  15 us (2%)
  starting transfers between devices  11.8 us (2%)
    pallas_call x4, Pallas kernels, gather_all(): pl.pallas_call(functools.partial(gather_kernel, shards, widths, shared, l...  271 us
    dot_general x28, matrix products, contract(): lax.dot_general(left_op, right_op, (((left_dim,), (right_dim,)), ((), ())...  180 us
    pallas_call x1, Pallas kernels, product_sum(): pl.pallas_call(functools.partial(product_kernel, shards), out_shape=jax.S...  89.5 us
    pallas_call x1, Pallas kernels, scatter_sum(): pl.pallas_call(functools.partial(scatter_kernel, shards, widths), out_sha...  40.9 us
    pallas_call x2, Pallas kernels, place(): pl.pallas_call(functools.partial(place_kernel, kinds), grid=(kinds, tiles...  25.2 us
    ppermute x11, waiting for transfers between devices, swap_rep(): return lax.ppermute(values, 'rep', [(0, 1), (1, 0)])  15 us
  transfers between devices with their start and end apart: 15, of which 4 were waited for; matrix products, arithmetic and copies ran while one was open for 29% of the time, Pallas kernels for 45%

profile of v6, /device:TPU:0, one launch (start us, length us, event | category | flops | bytes accessed | tf_op | source)
XLA Modules:
  0.0 701.5 jit_solution(16669543957134653415)
XLA Ops:
  9.7 109.2 %gather_1.1 = (bf16[1,16,128,4608]{3,2,1,0:T(8,128)(2,1)}, bf16[1,16,128,768]{3,2,1,0:T(8,128)(2,1)}, bf16[1,16,128,128]{3,2,1,0:T(8,128)(2,1)}) custom-call(bf16[1,128,4608]{2,1,0:T(8,128)(2,1)} %bitcast.189, bf16[1,128,768]{2,1,0:T(8,128)(2,1)} %bitcast.214, bf16[1,128,128]{2,1,0:T(8,128)(2,1)} %maximum_bitcast_fusion.refs_2_), custom_call_target="tpu_custom_call" | custom-call | bytes 583008256 | tf_op jit(solution)/shard_map/gather_1/pallas_call | solution.py:357
  119.2 1.2 slice.189
  121.8 1.3 copy.30
  124.8 5.7 fusion.3
  132.3 1.2 fusion.90
  134.2 35.1 %gather_2.1 = (bf16[2,16,64,256]{3,2,1,0:T(8,128)(2,1)}, bf16[2,16,64,256]{3,2,1,0:T(8,128)(2,1)}) custom-call(bf16[2,64,256]{2,1,0:T(8,128)(2,1)} %pad_maximum_fusion.6.refs_0_, bf16[2,64,256]{2,1,0:T(8,128)(2,1)} %bitcast.205), custom_call_target="tpu_custom_call" | custom-call | bytes 92274688 | tf_op jit(solution)/shard_map/gather_2/pallas_call | solution.py:357
  169.7 2.2 fusion.88
  171.9 2.1 fusion.102
  174.1 2.0 copy-done.11
  177.1 6.4 multiply_reduce_fusion.1
  183.5 0.9 copy-done.4
  184.4 1.0 multiply_convert_fusion.4
  185.4 62.8 %gather_3.1 = bf16[2,16,64,2048]{3,2,1,0:T(8,128)(2,1)} custom-call(bf16[2,64,2048]{2,1,0:T(8,128)(2,1)} %bitcast.180), custom_call_target="tpu_custom_call" | custom-call | bytes 243269632 | tf_op jit(solution)/shard_map/gather_3/pallas_call | solution.py:357
  249.4 14.6 %fusion.23 = f32[2048,1024]{1,0:T(8,128)} fusion(bf16[2048,2048]{1,0:T(8,128)(2,1)} %bitcast.154, bf16[1024,3,2048]{2,0,1:T(8,128)(2,1)} %param.17), kind=kOutput, calls=%fused_computation.30 | convolution fusion | flops 8589934592 | bytes 20971520 | tf_op jit(solution)/shard_map/dot_general | solution.py:51
  263.9 14.6 %fusion.21 = f32[2048,1024]{1,0:T(8,128)} fusion(bf16[2048,2048]{1,0:T(8,128)(2,1)} %bitcast.155, bf16[1024,3,2048]{2,0,1:T(8,128)(2,1)} %param.17), kind=kOutput, calls=%fused_computation.28 | convolution fusion | flops 8589934592 | bytes 20971520 | tf_op jit(solution)/shard_map/dot_general | solution.py:51
  278.5 6.1 convolution_convert_fusion.8
  284.7 1.1 copy-done.39
  285.8 13.8 %fusion.18 = f32[2048,1024]{1,0:T(8,128)} fusion(bf16[2048,2048]{1,0:T(8,128)(2,1)S(1)} %bitcast.225, bf16[1024,3,2048]{2,0,1:T(8,128)(2,1)} %param.17), kind=kOutput, calls=%fused_computation.25 | convolution fusion | flops 8589934592 | bytes 20971520 | tf_op jit(solution)/shard_map/dot_general | solution.py:51
  299.6 17.7 %multiply_convert_fusion = (bf16[2048,1024]{1,0:T(8,128)(2,1)}, bf16[2048,1024]{1,0:T(8,128)(2,1)}, bf16[2048,1024]{1,0:T(8,128)(2,1)}) fusion(f32[2048,1024]{1,0:T(8,128)} %fusion.23, f32[2048,1024]{1,0:T(8,128)} %fusion.21, f32[2048,1024]{1,0:T(8,128)} %fusion.18, bf16[2048,256]{1,0:T(8,128)(2,1)S(1)} %convolution_convert_fusion.8, ...), kind=kOutput, calls=%fused_computation.16 | convolution fusion | flops 1130364928 | bytes 39321600 | tf_op jit(solution)/shard_map/dot_general | solution.py:51
  317.3 4.6 convolution_convert_fusion.7
  321.9 5.7 convolution_convert_fusion.6.refs_0_
  327.7 13.2 %convolution_convert_fusion = bf16[2048,2048]{1,0:T(8,128)(2,1)} fusion(bf16[2048,1024]{1,0:T(8,128)(2,1)S(1)} %copy-done.57, bf16[1024,3,2048]{2,0,1:T(8,128)(2,1)} %param.17), kind=kOutput, calls=%fused_computation.19 | convolution fusion | flops 8594128896 | bytes 16777216 | tf_op jit(solution)/shard_map/dot_general | solution.py:51
  341.0 1.0 collective-permute-start
  342.0 10.8 %convolution_convert_fusion.5.refs_2_ = bf16[512,2048]{1,0:T(8,128)(2,1)} fusion(bf16[2048,2048]{1,0:T(8,128)(2,1)} %bitcast.156, bf16[2048,1024]{1,0:T(8,128)(2,1)} %get-tuple-element.90), kind=kOutput, calls=%fused_computation.47 | convolution fusion | flops 4296015872 | bytes 12582912 | tf_op jit(solution)/shard_map/dot_general | solution.py:51
  353.5 11.1 %convolution_convert_fusion.4.refs_4_ = bf16[512,2048]{1,0:T(8,128)(2,1)} fusion(bf16[2048,2048]{1,0:T(8,128)(2,1)} %bitcast.223, bf16[2048,1024]{1,0:T(8,128)(2,1)S(1)} %copy-done.58), kind=kOutput, calls=%fused_computation.46 | convolution fusion | flops 4296015872 | bytes 12582912 | tf_op jit(solution)/shard_map/dot_general | solution.py:51
  364.6 1.4 collective-permute-start.2
  366.0 4.7 convolution_convert_fusion.2.refs_2_
  370.8 5.7 convolution_convert_fusion.1.refs_4_
  376.5 5.7 convolution_convert_fusion.3.refs_0_
  382.3 89.5 %product_5.1 = bf16[2,64,2048]{2,1,0:T(8,128)(2,1)} custom-call(bf16[2,1024,1024]{2,1,0:T(8,128)(2,1)} %bitcast.169, bf16[2,1024,1024]{2,1,0:T(8,128)(2,1)} %bitcast.168, bf16[3,1024,2048]{2,1,0:T(8,128)(2,1)} %bitcast.153), custom_call_target="tpu_custom_call" | custom-call | bytes 243269632 | tf_op jit(solution)/shard_map/product_5/pallas_call | solution.py:686
  471.8 7.3 %collective-permute-done.2.refs_5_ = bf16[512,2048]{1,0:T(8,128)(2,1)} collective-permute-done((bf16[512,2048]{1,0:T(8,128)(2,1)}, bf16[512,2048]{1,0:T(8,128)(2,1)}, u32[]{:S(2)}, u32[]{:S(2)}) %collective-permute-start.2) | collective-permute-done | bytes 2097184 | tf_op jit(solution)/shard_map/ppermute | solution.py:128
  479.1 14.1 %place_0.1.refs_6_ = f32[3,1024,2048]{2,1,0:T(8,128)} custom-call(bf16[512,2048]{1,0:T(8,128)(2,1)} %convolution_convert_fusion.6.refs_0_, bf16[512,2048]{1,0:T(8,128)(2,1)} %collective-permute-done.refs_1_, bf16[512,2048]{1,0:T(8,128)(2,1)} %convolution_convert_fusion.5.refs_2_, bf16[512,2048]{1,0:T(8,128)(2,1)} %collective-permute-done.1.refs_3_, ...), custom_call_target="tpu_custom_call" | custom-call | flops 3145728 | bytes 25165824 | tf_op jit(solution)/shard_map/place_0/pallas_call | solution.py:114
  493.2 1.6 fusion.57
  494.8 1.6 fusion.100
  497.2 5.4 fusion.35
  502.6 1.3 reshape.506
  503.9 3.5 multiply_reduce_fusion
  507.7 2.2 convolution_convert_fusion.10
  510.9 1.9 multiply_convert_fusion.3
  513.8 0.9 copy.32
  515.4 1.3 collective-permute-start.3
  516.7 1.0 fusion.68.refs_1_
  518.4 1.3 collective-permute-start.6
  519.7 4.9 convolution_convert_fusion.12
  525.4 40.9 %scatter_6.1 = (bf16[2,64,256]{2,1,0:T(8,128)(2,1)}, bf16[2,64,256]{2,1,0:T(8,128)(2,1)}, bf16[2,64,256]{2,1,0:T(8,128)(2,1)}) custom-call(bf16[2,16,64,256]{3,2,1,0:T(8,128)(2,1)} %bitcast.192, bf16[2,16,64,256]{3,2,1,0:T(8,128)(2,1)} %bitcast.191, bf16[2,16,64,256]{3,2,1,0:T(8,128)(2,1)} %bitcast.190), custom_call_target="tpu_custom_call" | custom-call | bytes 117440512 | tf_op jit(solution)/shard_map/scatter_6/pallas_call | solution.py:540
  568.7 1.5 constant_dynamic-update-slice_fusion.1
  571.1 6.3 fusion.1
  577.5 2.8 fusion.65
  581.7 63.5 %gather_4.1 = (bf16[2,16,64,1024]{3,2,1,0:T(8,128)(2,1)}, bf16[2,16,64,128]{3,2,1,0:T(8,128)(2,1)}, bf16[2,16,64,128]{3,2,1,0:T(8,128)(2,1)}, bf16[1,16,16,128]{3,2,1,0:T(8,128)(2,1)}) custom-call(bf16[2,64,1024]{2,1,0:T(8,128)(2,1)} %bitcast.200, bf16[2,64,2048]{2,1,0:T(8,128)(2,1)} %fusion.68.refs_1_, bf16[2,64,2048]{2,1,0:T(8,128)(2,1)} %bitcast.179, ...), custom_call_target="tpu_custom_call" | custom-call | bytes 142606336 | tf_op jit(solution)/shard_map/gather_4/pallas_call | solution.py:357
  646.0 2.1 collective-permute-start.4
  648.1 5.8 fusion.38
  654.0 2.6 fusion.41
  657.3 1.5 fusion.60
  658.8 1.4 convolution_convert_fusion.13
  660.1 5.2 collective-permute-done.4
  665.9 1.8 convolution_convert_fusion.14
  667.8 1.3 collective-permute-start.9
  669.1 5.4 convolution_convert_fusion.9
  675.2 1.4 collective-permute-done.8
  676.6 1.3 add_dynamic-update-slice_fusion.1
  678.0 11.1 %place_1.1 = f32[3,1024,2048]{2,1,0:T(8,128)} custom-call(bf16[512,2048]{1,0:T(8,128)(2,1)S(1)} %copy-done.3, bf16[512,2048]{1,0:T(8,128)(2,1)} %collective-permute-done.3.refs_1_, bf16[512,2048]{1,0:T(8,128)(2,1)S(1)} %convolution_convert_fusion.2.refs_2_, bf16[512,2048]{1,0:T(8,128)(2,1)} %collective-permute-done.5.refs_3_, ...), custom_call_target="tpu_custom_call", output_to_operand_aliasing={{}: (6, {})} | custom-call | flops 3145728 | bytes 25165824 | tf_op jit(solution)/shard_map/place_1/pallas_call | solution.py:114
  689.1 2.3 convert_add_fusion.1
  692.2 1.0 collective-permute-done.10
  693.4 1.4 copy-done.20
  (217 shorter events, 25.3 us)
Async XLA Ops:
  7.2 292.4 %copy-start = (bf16[1024,256]{1,0:T(8,128)(2,1)S(1)}, bf16[1024,256]{1,0:T(8,128)(2,1)}, u32[]{:S(2)}) copy-start(bf16[1024,256]{1,0:T(8,128)(2,1)} %param.18) | copy-start | bytes 1572868
  7.2 115.9 %copy-start.6 = (bf16[2,64,2048]{2,1,0:T(8,128)(2,1)S(1)}, bf16[2,64,2048]{2,1,0:T(8,128)(2,1)}, u32[]{:S(2)}) copy-start(bf16[2,64,2048]{2,1,0:T(8,128)(2,1)} %param.12) | copy-start | bytes 1572868
  7.2 271.3 %all-gather.4.cloned.1.call-start = ((), (), s32[]{:S(2)}) async-start(), calls=%async_computation.1 | async-start | bytes 8912896 | tf_op jit(solution)/shard_map/all_gather | solution.py:73
  119.0 263.2 %all-gather.6.cloned.1.call-start = ((), (), s32[]{:S(2)}) async-start(), calls=%async_computation.2 | async-start | bytes 10027008 | tf_op jit(solution)/shard_map/all_gather | solution.py:73
  124.6 5.9 copy-start.46
  124.6 5.9 copy-start.37
  124.6 58.9 %copy-start.35 = (f32[2048,1]{0,1:T(1,128)}, f32[2048,1]{0,1:T(1,128)S(1)}, u32[]{:S(2)}) copy-start(f32[2048,1]{0,1:T(1,128)S(1)} %get-tuple-element.138) | copy-start | bytes 24580
  124.8 6.4 copy-start.18
  130.5 38.9 %copy-start.50 = (s32[2,64]{1,0:T(2,128)S(1)}, s32[2,64]{1,0:T(2,128)}, u32[]{:S(2)}) copy-start(s32[2,64]{1,0:T(2,128)} %param.13) | copy-start | bytes 1540
  169.7 4.3 copy-start.24
  169.7 4.3 copy-start.26
  171.9 4.1 copy-start.52
  183.5 64.7 %copy-start.55 = (f32[128]{0:T(128)}, f32[128]{0:T(128)S(1)}, u32[]{:S(2)}) copy-start(f32[128]{0:T(128)S(1)} %get-tuple-element.150) | copy-start | bytes 1540
  183.5 64.7 %copy-start.40 = (f32[128]{0:T(128)}, f32[128]{0:T(128)S(1)}, u32[]{:S(2)}) copy-start(f32[128]{0:T(128)S(1)} %fusion.93) | copy-start | bytes 1540
  249.1 244.1 %reduce-scatter.2.cloned.1.call-start = ((), (), s32[]{:S(2)}) async-start(), calls=%async_computation.3 | async-start | bytes 8912896 | tf_op jit(solution)/shard_map/reduce_scatter | solution.py:77
  278.5 7.2 %copy-start.39 = (bf16[2,1024,2048]{2,1,0:T(8,128)(2,1)S(1)}, bf16[2,1024,2048]{2,1,0:T(8,128)(2,1)}, u32[]{:S(2)}) copy-start(bf16[2,1024,2048]{2,1,0:T(8,128)(2,1)} %all-gather.4.cloned.1.call-done) | copy-start | bytes 25165828
  285.8 13.8 %copy-start.59 = (bf16[2048,256]{1,0:T(8,128)(2,1)}, bf16[2048,256]{1,0:T(8,128)(2,1)S(1)}, u32[]{:S(2)}) copy-start(bf16[2048,256]{1,0:T(8,128)(2,1)S(1)} %convolution_convert_fusion.8) | copy-start | bytes 3145732
  285.8 36.1 %slice-start = ((s8[8388608]{0:T(1024)(128)(4,1)}), s8[4194304]{0:T(1024)(128)(4,1)S(1)}, s32[]{:S(2)}) async-start(s8[8388608]{0:T(1024)(128)(4,1)} %bitcast.157), calls=%async_computation.5 | async-start | bytes 8388608
  299.6 22.4 %slice-start.1 = ((s8[8388608]{0:T(1024)(128)(4,1)}), s8[4194304]{0:T(1024)(128)(4,1)S(1)}, s32[]{:S(2)}) async-start(s8[8388608]{0:T(1024)(128)(4,1)} %bitcast.157), calls=%async_computation.6 | async-start | bytes 8388608
  317.3 4.6 copy-start.15
  321.9 5.7 copy-start.57
  340.9 325.0 %all-gather.8.cloned.1.call-start = ((), (), s32[]{:S(2)}) async-start(), calls=%async_computation.4 | async-start | bytes 8912896 | tf_op jit(solution)/shard_map/all_gather | solution.py:73
  341.0 12.5 %copy-start.58 = (bf16[2048,1024]{1,0:T(8,128)(2,1)S(1)}, bf16[2048,1024]{1,0:T(8,128)(2,1)}, u32[]{:S(2)}) copy-start(bf16[2048,1024]{1,0:T(8,128)(2,1)} %get-tuple-element.88) | copy-start | bytes 12582916
  341.0 130.8 %collective-permute-start = (bf16[512,2048]{1,0:T(8,128)(2,1)}, bf16[512,2048]{1,0:T(8,128)(2,1)}, u32[]{:S(2)}, u32[]{:S(2)}) collective-permute-start(bf16[512,2048]{1,0:T(8,128)(2,1)} %convolution_convert_fusion.6.refs_0_), channel_id=1, source_target_pairs={{0,16},{16,0},{1,17},{17,1},{2,18},{18,2},{3,19},{19,3},{4,20},{20... | collective-permute-start | bytes 6291464 | tf_op jit(solution)/shard_map/ppermute | solution.py:128
  342.0 24.0 %slice-start.2 = ((s8[8388608]{0:T(1024)(128)(4,1)}), s8[4194304]{0:T(1024)(128)(4,1)S(1)}, s32[]{:S(2)}) async-start(s8[8388608]{0:T(1024)(128)(4,1)} %bitcast.160), calls=%async_computation.7 | async-start | bytes 8388608
  352.8 13.2 %slice-start.3 = ((s8[8388608]{0:T(1024)(128)(4,1)}), s8[4194304]{0:T(1024)(128)(4,1)S(1)}, s32[]{:S(2)}) async-start(s8[8388608]{0:T(1024)(128)(4,1)} %bitcast.160), calls=%async_computation.8 | async-start | bytes 8388608
  352.8 13.2 %copy-start.14 = (bf16[2048,1024]{1,0:T(8,128)(2,1)S(1)}, bf16[2048,1024]{1,0:T(8,128)(2,1)}, u32[]{:S(2)}) copy-start(bf16[2048,1024]{1,0:T(8,128)(2,1)} %get-tuple-element.90) | copy-start | bytes 12582916
  352.8 119.0 %collective-permute-start.1 = (bf16[512,2048]{1,0:T(8,128)(2,1)}, bf16[512,2048]{1,0:T(8,128)(2,1)}, u32[]{:S(2)}, u32[]{:S(2)}) collective-permute-start(bf16[512,2048]{1,0:T(8,128)(2,1)} %convolution_convert_fusion.5.refs_2_), channel_id=1, source_target_pairs={{0,16},{16,0},{1,17},{17,1},{2,18},{18,2},{3,19},{19,3},{4,20},{20... | collective-permute-start | bytes 6291464 | tf_op jit(solution)/shard_map/ppermute | solution.py:128
  353.5 17.3 %slice-start.4 = ((s8[8388608]{0:T(1024)(128)(4,1)}), s8[4194304]{0:T(1024)(128)(4,1)S(1)}, s32[]{:S(2)}) async-start(s8[8388608]{0:T(1024)(128)(4,1)} %bitcast.226), calls=%async_computation.9 | async-start | bytes 8388608
  364.5 6.2 slice-start.5
  364.6 114.6 %collective-permute-start.2 = (bf16[512,2048]{1,0:T(8,128)(2,1)}, bf16[512,2048]{1,0:T(8,128)(2,1)}, u32[]{:S(2)}, u32[]{:S(2)}) collective-permute-start(bf16[512,2048]{1,0:T(8,128)(2,1)} %convolution_convert_fusion.4.refs_4_), channel_id=1, source_target_pairs={{0,16},{16,0},{1,17},{17,1},{2,18},{18,2},{3,19},{19,3},{4,20},{20... | collective-permute-start | bytes 6291464 | tf_op jit(solution)/shard_map/ppermute | solution.py:128
  370.8 5.8 copy-start.16
  471.8 21.4 %copy-start.8 = (bf16[2,64,2048]{2,1,0:T(8,128)(2,1)S(1)}, bf16[2,64,2048]{2,1,0:T(8,128)(2,1)}, u32[]{:S(2)}) copy-start(bf16[2,64,2048]{2,1,0:T(8,128)(2,1)} %product_5.1) | copy-start | bytes 1572868
  471.8 21.4 %copy-start.36 = (f32[2048,1]{0,1:T(1,128)S(1)}, f32[2048,1]{0,1:T(1,128)}, u32[]{:S(2)}) copy-start(f32[2048,1]{0,1:T(1,128)} %copy-done.35) | copy-start | bytes 24580
  471.8 21.4 %copy-start.41 = (f32[128]{0:T(128)S(1)}, f32[128]{0:T(128)}, u32[]{:S(2)}) copy-start(f32[128]{0:T(128)} %copy-done.40) | copy-start | bytes 1540
  471.8 23.0 %copy-start.56 = (f32[128]{0:T(128)S(1)}, f32[128]{0:T(128)}, u32[]{:S(2)}) copy-start(f32[128]{0:T(128)} %copy-done.55) | copy-start | bytes 1540
  471.8 23.0 %copy-start.9 = (bf16[2,64,2048]{2,1,0:T(8,128)(2,1)S(1)}, bf16[2,64,2048]{2,1,0:T(8,128)(2,1)}, u32[]{:S(2)}) copy-start(bf16[2,64,2048]{2,1,0:T(8,128)(2,1)} %param.19) | copy-start | bytes 1572868
  497.2 6.7 copy-start.49
  503.9 3.7 copy-start.12
  515.4 55.6 %collective-permute-start.3 = (bf16[512,2048]{1,0:T(8,128)(2,1)}, bf16[512,2048]{1,0:T(8,128)(2,1)}, u32[]{:S(2)}, u32[]{:S(2)}) collective-permute-start(bf16[512,2048]{1,0:T(8,128)(2,1)} %convolution_convert_fusion.3.refs_0_), channel_id=1, source_target_pairs={{0,16},{16,0},{1,17},{17,1},{2,18},{18,2},{3,19},{19,3},{4,20},{20... | collective-permute-start | bytes 6291464 | tf_op jit(solution)/shard_map/ppermute | solution.py:128
  517.7 49.5 %copy-start.43 = (f32[128]{0:T(128)S(1)}, f32[128]{0:T(128)}, u32[]{:S(2)}) copy-start(f32[128]{0:T(128)} %copy-done.42) | copy-start | bytes 1540
  517.7 49.5 %copy-start.45 = (f32[128]{0:T(128)S(1)}, f32[128]{0:T(128)}, u32[]{:S(2)}) copy-start(f32[128]{0:T(128)} %copy-done.44) | copy-start | bytes 1540
  517.7 51.0 %copy-start.22 = (bf16[16,8,8,256]{3,1,2,0:T(8,128)(2,1)S(1)}, bf16[16,8,8,256]{3,1,2,0:T(8,128)(2,1)}, u32[]{:S(2)}) copy-start(bf16[16,8,8,256]{3,1,2,0:T(8,128)(2,1)} %copy.32) | copy-start | bytes 1572868
  517.7 157.5 %collective-permute-start.5 = (bf16[512,2048]{1,0:T(8,128)(2,1)S(1)}, bf16[512,2048]{1,0:T(8,128)(2,1)}, u32[]{:S(2)}, u32[]{:S(2)}) collective-permute-start(bf16[512,2048]{1,0:T(8,128)(2,1)S(1)} %convolution_convert_fusion.2.refs_2_), channel_id=1, source_target_pairs={{0,16},{16,0},{1,17},{17,1},{2,18},{18,2},{3,19},{19,3},{4,20},{20... | collective-permute-start | bytes 6291464 | tf_op jit(solution)/shard_map/ppermute | solution.py:128
  518.4 156.7 %collective-permute-start.6 = (bf16[512,2048]{1,0:T(8,128)(2,1)}, bf16[512,2048]{1,0:T(8,128)(2,1)}, u32[]{:S(2)}, u32[]{:S(2)}) collective-permute-start(bf16[512,2048]{1,0:T(8,128)(2,1)} %convolution_convert_fusion.1.refs_4_), channel_id=1, source_target_pairs={{0,16},{16,0},{1,17},{17,1},{2,18},{18,2},{3,19},{19,3},{4,20},{20... | collective-permute-start | bytes 6291464 | tf_op jit(solution)/shard_map/ppermute | solution.py:128
  524.6 149.9 %collective-permute-start.7 = (bf16[1024,256]{1,0:T(8,128)(2,1)}, bf16[1024,256]{1,0:T(8,128)(2,1)}, u32[]{:S(2)}, u32[]{:S(2)}) collective-permute-start(bf16[1024,256]{1,0:T(8,128)(2,1)} %convolution_convert_fusion.12), channel_id=1, source_target_pairs={{0,16},{16,0},{1,17},{17,1},{2,18},{18,2},{3,19},{19,3},{4,20},{20... | collective-permute-start | bytes 1572872 | tf_op jit(solution)/shard_map/ppermute | solution.py:128
  571.1 6.4 copy-start.29
  571.1 6.4 copy-start.47
  646.0 19.4 %collective-permute-start.4 = (bf16[2,128]{1,0:T(2,128)(2,1)S(1)}, bf16[2,128]{1,0:T(2,128)(2,1)S(1)}, u32[]{:S(2)}, u32[]{:S(2)}) collective-permute-start(bf16[2,128]{1,0:T(2,128)(2,1)S(1)} %slice_reduce_fusion), channel_id=1, source_target_pairs={{0,16},{16,0},{1,17},{17,1},{2,18},{18,2},{3,19},{19,3},{4,20},{20... | collective-permute-start | bytes 1544 | tf_op jit(solution)/shard_map/ppermute | solution.py:128
  648.1 5.9 copy-start.5
  648.1 5.9 copy-start.28
  648.1 5.9 copy-start.31
  648.1 8.5 %copy-start.23 = (bf16[2,16,64,128]{3,2,1,0:T(8,128)(2,1)S(1)}, bf16[2,16,64,128]{3,2,1,0:T(8,128)(2,1)}, u32[]{:S(2)}) copy-start(bf16[2,16,64,128]{3,2,1,0:T(8,128)(2,1)} %get-tuple-element.103) | copy-start | bytes 1572868
  648.1 8.5 %copy-start.30 = (bf16[2,16,64,1024]{3,2,1,0:T(8,128)(2,1)S(1)}, bf16[2,16,64,1024]{3,2,1,0:T(8,128)(2,1)}, u32[]{:S(2)}) copy-start(bf16[2,16,64,1024]{3,2,1,0:T(8,128)(2,1)} %get-tuple-element.104) | copy-start | bytes 12582916
  654.0 3.3 copy-start.54
  654.0 3.3 copy-start.10
  654.0 3.3 copy-start.13
  654.0 22.6 %collective-permute-start.8 = (bf16[128,2048]{1,0:T(8,128)(2,1)}, bf16[128,2048]{1,0:T(8,128)(2,1)}, u32[]{:S(2)}, u32[]{:S(2)}) collective-permute-start(bf16[128,2048]{1,0:T(8,128)(2,1)} %fusion.38), channel_id=1, source_target_pairs={{0,16},{16,0},{1,17},{17,1},{2,18},{18,2},{3,19},{19,3},{4,20},{20... | collective-permute-start | bytes 1572872 | tf_op jit(solution)/shard_map/ppermute | solution.py:128
  667.7 8.9 %copy-start.19 = (f32[128,4608]{1,0:T(8,128)S(1)}, f32[128,4608]{1,0:T(8,128)}, u32[]{:S(2)}) copy-start(f32[128,4608]{1,0:T(8,128)} %unwritten.1) | copy-start | bytes 7077892
  667.7 10.2 %copy-start.2 = (bf16[512,2048]{1,0:T(8,128)(2,1)S(1)}, bf16[512,2048]{1,0:T(8,128)(2,1)}, u32[]{:S(2)}) copy-start(bf16[512,2048]{1,0:T(8,128)(2,1)} %convolution_convert_fusion.1.refs_4_) | copy-start | bytes 6291460
  667.8 10.2 %copy-start.3 = (bf16[512,2048]{1,0:T(8,128)(2,1)S(1)}, bf16[512,2048]{1,0:T(8,128)(2,1)}, u32[]{:S(2)}) copy-start(bf16[512,2048]{1,0:T(8,128)(2,1)} %convolution_convert_fusion.3.refs_0_) | copy-start | bytes 6291460
  667.8 23.6 %collective-permute-start.9 = (bf16[128,1280]{1,0:T(8,128)(2,1)S(1)}, bf16[128,1280]{1,0:T(8,128)(2,1)S(1)}, u32[]{:S(2)}, u32[]{:S(2)}) collective-permute-start(bf16[128,1280]{1,0:T(8,128)(2,1)S(1)} %pad_maximum_fusion.5), channel_id=1, source_target_pairs={{0,16},{16,0},{1,17},{17,1},{2,18},{18,2},{3,19},{19,3},{4,20},{20... | collective-permute-start | bytes 983048 | tf_op jit(solution)/shard_map/ppermute | solution.py:128
  674.5 18.8 %collective-permute-start.10 = (bf16[128,2048]{1,0:T(8,128)(2,1)S(1)}, bf16[128,2048]{1,0:T(8,128)(2,1)S(1)}, u32[]{:S(2)}, u32[]{:S(2)}) collective-permute-start(bf16[128,2048]{1,0:T(8,128)(2,1)S(1)} %convolution_convert_fusion.9), channel_id=1, source_target_pairs={{0,16},{16,0},{1,17},{17,1},{2,18},{18,2},{3,19},{19,3},{4,20},{20... | collective-permute-start | bytes 1572872 | tf_op jit(solution)/shard_map/ppermute | solution.py:128
  678.0 16.9 %copy-start.1 = (bf16[1024,256]{1,0:T(8,128)(2,1)S(1)}, bf16[1024,256]{1,0:T(8,128)(2,1)}, u32[]{:S(2)}) copy-start(bf16[1024,256]{1,0:T(8,128)(2,1)} %param.18) | copy-start | bytes 1572868
  (17 other events, 31.7 us)
Sparse Core Ops, SparseCore 0:
  119.1 77.1 all-gather.3
  249.2 78.7 all-gather.5
  341.0 126.8 reduce-scatter.1
  514.9 78.0 all-gather.7

commit v7 on v6

--- a/solution.py
+++ b/solution.py
@@ -819,36 +819,22 @@
     up_grad = jnp.concatenate(up_parts, axis=1)
     hidden_act = jnp.concatenate(hidden_parts, axis=1)
     step = hidden_cols // PIECES
-    first_mine = low(contract(gate_grad[:, :step], inputs_all, 0, 0))
-    down_part = low(contract(hidden_act, ffn_weight[:, 2, :], 1, 0))
-    low_part = low(contract(hidden_act, ffn_adapter, 1, 0))
-    first_other = swap_rep(first_mine)
-    down_part, low_part, gate_grad, up_grad, hidden_act, first_mine = lax.optimization_barrier(
-        (down_part, low_part, gate_grad, up_grad, hidden_act, first_mine)
-    )
-    down_sum = sum_rows(down_part.reshape(micro, seq_len, model_dim))
-    ffn_parts = []
-    for at in range(PIECES):
+
+    def weight_grads(at, gate_now, up_now, hidden_now):
         units = slice(at * step, (at + 1) * step)
+        made = []
         for left, right in (
-            (gate_grad, inputs_all),
-            (up_grad, inputs_all),
-            (hidden_act, cot_all),
+            (gate_now, inputs_all),
+            (up_now, inputs_all),
+            (hidden_now, cot_all),
         ):
-            if not ffn_parts:
-                ffn_parts.append((first_mine, first_other))
-                continue
             mine = low(contract(left[:, units], right, 0, 0))
-            ffn_parts.append((mine, swap_rep(mine)))
-    low_mine = low(contract(hidden_act, low_grad_all, 0, 0))
-    low_other = swap_rep(low_mine)
+            made.append((mine, swap_rep(mine)))
+        return made
+
+    ffn_parts = weight_grads(0, gate_grad, up_grad, hidden_act)
     gate_grad, up_grad, kept_all, _ = lax.optimization_barrier(
-        (
-            gate_grad,
-            up_grad,
-            kept_all,
-            [pair[0] for pair in ffn_parts],
-        )
+        (gate_grad, up_grad, kept_all, [pair[0] for pair in ffn_parts])
     )
     if grid_of(shards)[1] == 2 and micro == 2:
         normed_two_grad = product_sum(
@@ -867,8 +853,20 @@
                 + contract(up_grad, ffn_weight[:, 1, :], 1, 0)
             ).reshape(micro, shards, local_len, model_dim),
         )
-    normed_two_grad, down_sum, _ = lax.optimization_barrier(
-        (normed_two_grad, down_sum, [pair[1] for pair in ffn_parts[:2]])
+    normed_two_grad, gate_grad, up_grad, hidden_act, _ = lax.optimization_barrier(
+        (normed_two_grad, gate_grad, up_grad, hidden_act, [pair[1] for pair in ffn_parts[:2]])
+    )
+    down_part = low(contract(hidden_act, ffn_weight[:, 2, :], 1, 0))
+    low_part = low(contract(hidden_act, ffn_adapter, 1, 0))
+    down_part, gate_grad, up_grad, hidden_act = lax.optimization_barrier(
+        (down_part, gate_grad, up_grad, hidden_act)
+    )
+    down_sum = sum_rows(down_part.reshape(micro, seq_len, model_dim))
+    ffn_parts += weight_grads(1, gate_grad, up_grad, hidden_act)
+    low_mine = low(contract(hidden_act, low_grad_all, 0, 0))
+    low_other = swap_rep(low_mine)
+    normed_two_grad, low_part, low_mine, _ = lax.optimization_barrier(
+        (normed_two_grad, low_part, low_mine, [pair[0] for pair in ffn_parts])
     )
     normed_two_grad = normed_two_grad.reshape(count, model_dim).astype(jnp.float32)
     cot_full = cotangent.reshape(count, model_dim).astype(jnp.float32)
@@ -885,9 +883,8 @@
     query_pre_grad = low(rotate(query_grad, -angles[:, None, :]).reshape(count, q_width))
     key_part = low(batched(score_grad, queries, 1, 1) * score_scale)
     value_part = low(batched(weights_low, context_rows, 1, 1))
-    ffn_grad = place(None, 0, PIECES, ffn_parts[:3])
-    key_part, value_part, query_pre_grad, ffn_grad = lax.optimization_barrier(
-        (key_part, value_part, query_pre_grad, ffn_grad)
+    key_part, value_part, query_pre_grad, ffn_parts[2:3] = lax.optimization_barrier(
+        (key_part, value_part, query_pre_grad, ffn_parts[2:3])
     )
     q_all = gather_rows(query_pre_grad.reshape(micro, local_len, q_width))
     q_all = q_all.reshape(every, q_width)
@@ -929,6 +926,8 @@
             gain_parts,
         ),
     )
+    narrow_all, ffn_parts[:3] = lax.optimization_barrier((narrow_all, ffn_parts[:3]))
+    ffn_grad = place(None, 0, PIECES, ffn_parts[:3])
     narrow_all = narrow_all.reshape(every, 2 * HD + 2 * RANK)
     normed_cols = normed_cols.reshape(every, attn_rows)
     wout_grad = contract(out_cols.reshape(every, attn_rows), kept_all[:, :q_width], 0, 0)

time: 709 us -> 712 us (level)
    pallas_call x4, Pallas kernels: 271 us -> 300 us  [gather_all(): pl.pallas_call(functools.partial(gather_kernel, shards, widths, shared, l...]
    pallas_call x1, Pallas kernels: 89.5 us -> 66.7 us  [product_sum(): pl.pallas_call(functools.partial(product_kernel, shards), out_shape=jax.S...]
  transfers between devices with their start and end apart: 15 -> 15, of which waited for: 4 -> 1; matrix products, arithmetic and copies ran while one was open for 29% -> 30% of each run, Pallas kernels for 45% -> 45%
where the time goes in v7:
time: 712 us; the launch traced here: 705 us
  Pallas kernels  425 us (60%)
  matrix products  191 us (27%)
  other arithmetic  23.3 us (3%)
  local copies, waits for them, and re-layouts  19.1 us (3%)
  waiting for transfers between devices  18.6 us (3%)
  between operations  15.3 us (2%)
  starting transfers between devices  11.9 us (2%)
    pallas_call x4, Pallas kernels, gather_all(): pl.pallas_call(functools.partial(gather_kernel, shards, widths, shared, l...  300 us
    dot_general x28, matrix products, contract(): lax.dot_general(left_op, right_op, (((left_dim,), (right_dim,)), ((), ())...  180 us
    pallas_call x1, Pallas kernels, product_sum(): pl.pallas_call(functools.partial(product_kernel, shards), out_shape=jax.S...  66.7 us
    pallas_call x1, Pallas kernels, scatter_sum(): pl.pallas_call(functools.partial(scatter_kernel, shards, widths), out_sha...  34.2 us
    pallas_call x2, Pallas kernels, place(): pl.pallas_call(functools.partial(place_kernel, kinds), grid=(kinds, tiles...  24.5 us
    ppermute x11, waiting for transfers between devices, swap_rep(): return lax.ppermute(values, 'rep', [(0, 1), (1, 0)])  18.6 us
  transfers between devices with their start and end apart: 15, of which 1 were waited for; matrix products, arithmetic and copies ran while one was open for 30% of the time, Pallas kernels for 45%

profile of v7, /device:TPU:0, one launch (start us, length us, event | category | flops | bytes accessed | tf_op | source)
XLA Modules:
  0.0 704.5 jit_solution(15237519314510150210)
XLA Ops:
  9.7 109.2 %gather_1.1 = (bf16[1,16,128,4608]{3,2,1,0:T(8,128)(2,1)}, bf16[1,16,128,768]{3,2,1,0:T(8,128)(2,1)}, bf16[1,16,128,128]{3,2,1,0:T(8,128)(2,1)}) custom-call(bf16[1,128,4608]{2,1,0:T(8,128)(2,1)} %bitcast.189, bf16[1,128,768]{2,1,0:T(8,128)(2,1)} %bitcast.214, bf16[1,128,128]{2,1,0:T(8,128)(2,1)} %maximum_bitcast_fusion.refs_2_), custom_call_target="tpu_custom_call" | custom-call | bytes 583008256 | tf_op jit(solution)/shard_map/gather_1/pallas_call | solution.py:357
  119.2 1.2 slice.189
  120.9 0.9 convert_reduce_fusion
  121.8 1.3 copy.30
  124.8 5.7 fusion.3
  132.3 1.2 fusion.90
  134.2 34.9 %gather_2.1 = (bf16[2,16,64,256]{3,2,1,0:T(8,128)(2,1)}, bf16[2,16,64,256]{3,2,1,0:T(8,128)(2,1)}) custom-call(bf16[2,64,256]{2,1,0:T(8,128)(2,1)} %pad_maximum_fusion.6.refs_0_, bf16[2,64,256]{2,1,0:T(8,128)(2,1)} %bitcast.205), custom_call_target="tpu_custom_call" | custom-call | bytes 92274688 | tf_op jit(solution)/shard_map/gather_2/pallas_call | solution.py:357
  169.5 2.2 fusion.88
  171.7 2.1 fusion.102
  173.8 1.9 copy-done.11
  176.8 6.4 multiply_reduce_fusion.1
  183.2 0.9 copy-done.5
  184.1 1.0 multiply_convert_fusion.4
  185.1 63.0 %gather_3.1 = bf16[2,16,64,2048]{3,2,1,0:T(8,128)(2,1)} custom-call(bf16[2,64,2048]{2,1,0:T(8,128)(2,1)} %bitcast.180), custom_call_target="tpu_custom_call" | custom-call | bytes 243269632 | tf_op jit(solution)/shard_map/gather_3/pallas_call | solution.py:357
  248.1 0.9 pad_maximum_fusion
  249.3 14.6 %fusion.18 = f32[2048,1024]{1,0:T(8,128)} fusion(bf16[2048,2048]{1,0:T(8,128)(2,1)} %bitcast.157, bf16[1024,3,2048]{2,0,1:T(8,128)(2,1)} %param.17), kind=kOutput, calls=%fused_computation.25 | convolution fusion | flops 8589934592 | bytes 20971520 | tf_op jit(solution)/shard_map/dot_general | solution.py:51
  263.8 6.2 convolution_convert_fusion.8
  270.0 14.7 %fusion.23 = f32[2048,1024]{1,0:T(8,128)S(1)} fusion(bf16[2048,2048]{1,0:T(8,128)(2,1)S(1)} %bitcast.225, bf16[1024,3,2048]{2,0,1:T(8,128)(2,1)} %param.17), kind=kOutput, calls=%fused_computation.30 | convolution fusion | flops 8589934592 | bytes 20971520 | tf_op jit(solution)/shard_map/dot_general | solution.py:51
  284.7 4.5 convolution_add_fusion
  289.2 26.4 %multiply_convert_fusion = (bf16[2048,1024]{1,0:T(8,128)(2,1)}, bf16[2048,1024]{1,0:T(8,128)(2,1)}, bf16[2048,1024]{1,0:T(8,128)(2,1)}) fusion(f32[2048,1024]{1,0:T(8,128)} %fusion.18, f32[2048,1024]{1,0:T(8,128)} %convolution_add_fusion, bf16[2048,2048]{1,0:T(8,128)(2,1)} %bitcast.158, bf16[1024,3,2048]{2,0,1:T(8,128)(2,1)} %param.17), kind=kOutput, calls=%fused_computation.16 | convolution fusion | flops 8644460544 | bytes 41943040 | tf_op jit(solution)/shard_map/dot_general | solution.py:51
  315.6 8.8 %convolution_convert_fusion.6.refs_0_ = bf16[512,2048]{1,0:T(8,128)(2,1)S(1)} fusion(bf16[2048,2048]{1,0:T(8,128)(2,1)} %bitcast.159, bf16[2048,1024]{1,0:T(8,128)(2,1)} %get-tuple-element.104), kind=kOutput, calls=%fused_computation.48 | convolution fusion | flops 4296015872 | bytes 12582912 | tf_op jit(solution)/shard_map/dot_general | solution.py:51
  324.4 10.1 %convolution_convert_fusion.5.refs_2_ = bf16[512,2048]{1,0:T(8,128)(2,1)} fusion(bf16[2048,2048]{1,0:T(8,128)(2,1)} %bitcast.160, bf16[2048,1024]{1,0:T(8,128)(2,1)S(1)} %copy-done.13), kind=kOutput, calls=%fused_computation.47 | convolution fusion | flops 4296015872 | bytes 12582912 | tf_op jit(solution)/shard_map/dot_general | solution.py:51
  334.5 1.3 collective-permute-start
  336.5 5.7 convolution_convert_fusion.4.refs_4_
  342.2 66.7 %product_5.1 = bf16[2,64,2048]{2,1,0:T(8,128)(2,1)} custom-call(bf16[2,1024,1024]{2,1,0:T(8,128)(2,1)} %bitcast.169, bf16[2,1024,1024]{2,1,0:T(8,128)(2,1)} %bitcast.168, bf16[3,1024,2048]{2,1,0:T(8,128)(2,1)} %bitcast.155), custom_call_target="tpu_custom_call" | custom-call | bytes 243269632 | tf_op jit(solution)/shard_map/product_5/pallas_call | solution.py:686
  409.0 18.5 %collective-permute-done.1.refs_3_ = bf16[512,2048]{1,0:T(8,128)(2,1)} collective-permute-done((bf16[512,2048]{1,0:T(8,128)(2,1)}, bf16[512,2048]{1,0:T(8,128)(2,1)}, u32[]{:S(2)}, u32[]{:S(2)}) %collective-permute-start.1) | collective-permute-done | bytes 2097184 | tf_op jit(solution)/shard_map/ppermute | solution.py:128
  427.5 13.9 %convolution_convert_fusion = bf16[2048,2048]{1,0:T(8,128)(2,1)} fusion(bf16[2048,1024]{1,0:T(8,128)(2,1)} %get-tuple-element.103, bf16[1024,3,2048]{2,0,1:T(8,128)(2,1)} %param.17), kind=kOutput, calls=%fused_computation.19 | convolution fusion | flops 8594128896 | bytes 16777216 | tf_op jit(solution)/shard_map/dot_general | solution.py:51
  441.5 1.4 collective-permute-start.2
  442.9 4.7 convolution_convert_fusion.7
  447.7 2.1 convolution_convert_fusion.12
  449.8 9.1 %convolution_convert_fusion.1.refs_4_ = bf16[512,2048]{1,0:T(8,128)(2,1)S(1)} fusion(bf16[2048,2048]{1,0:T(8,128)(2,1)} %bitcast.223, bf16[2048,1024]{1,0:T(8,128)(2,1)S(1)} %copy-done.62), kind=kOutput, calls=%fused_computation.43 | convolution fusion | flops 4296015872 | bytes 12582912 | tf_op jit(solution)/shard_map/dot_general | solution.py:51
  459.0 5.8 convolution_convert_fusion.3.refs_0_
  464.8 6.0 convolution_convert_fusion.2.refs_2_
  470.8 0.9 fusion.57
  473.2 5.4 fusion.35
  478.6 1.3 reshape.506
  479.9 3.6 multiply_reduce_fusion
  486.3 0.9 copy.32
  487.2 1.9 multiply_convert_fusion.3
  489.2 2.1 convolution_convert_fusion.10
  491.9 1.0 fusion.68.refs_1_
  493.7 1.3 collective-permute-start.5
  495.7 1.3 collective-permute-start.7
  497.0 34.2 %scatter_6.1 = (bf16[2,64,256]{2,1,0:T(8,128)(2,1)}, bf16[2,64,256]{2,1,0:T(8,128)(2,1)}, bf16[2,64,256]{2,1,0:T(8,128)(2,1)}) custom-call(bf16[2,16,64,256]{3,2,1,0:T(8,128)(2,1)} %bitcast.191, bf16[2,16,64,256]{3,2,1,0:T(8,128)(2,1)} %bitcast.192, bf16[2,16,64,256]{3,2,1,0:T(8,128)(2,1)} %bitcast.190), custom_call_target="tpu_custom_call" | custom-call | bytes 117440512 | tf_op jit(solution)/shard_map/scatter_6/pallas_call | solution.py:540
  531.2 0.9 bitcast_convert_fusion
  532.8 0.8 constant_dynamic-update-slice_fusion.2
  533.6 1.6 constant_dynamic-update-slice_fusion.1
  535.3 6.4 fusion.1
  541.7 3.3 fusion.65
  545.7 1.5 scatter.9.refs_3_
  547.9 3.3 fusion.60
  551.2 92.4 %gather_4.1 = (bf16[2,16,64,1024]{3,2,1,0:T(8,128)(2,1)}, bf16[2,16,64,128]{3,2,1,0:T(8,128)(2,1)}, bf16[2,16,64,128]{3,2,1,0:T(8,128)(2,1)}, bf16[1,16,16,128]{3,2,1,0:T(8,128)(2,1)}) custom-call(bf16[2,64,1024]{2,1,0:T(8,128)(2,1)} %bitcast.200, bf16[2,64,2048]{2,1,0:T(8,128)(2,1)} %fusion.68.refs_1_, bf16[2,64,2048]{2,1,0:T(8,128)(2,1)} %bitcast.179, ...), custom_call_target="tpu_custom_call" | custom-call | bytes 142606336 | tf_op jit(solution)/shard_map/gather_4/pallas_call | solution.py:357
  644.5 1.3 collective-permute-start.4
  645.8 5.9 fusion.38
  652.5 1.4 convolution_convert_fusion.13
  654.5 13.4 %place_0.1.refs_6_ = f32[3,1024,2048]{2,1,0:T(8,128)} custom-call(bf16[512,2048]{1,0:T(8,128)(2,1)S(1)} %copy-done.4, bf16[512,2048]{1,0:T(8,128)(2,1)} %collective-permute-done.refs_1_, bf16[512,2048]{1,0:T(8,128)(2,1)} %convolution_convert_fusion.5.refs_2_, bf16[512,2048]{1,0:T(8,128)(2,1)} %collective-permute-done.1.refs_3_, ...), custom_call_target="tpu_custom_call" | custom-call | flops 3145728 | bytes 25165824 | tf_op jit(solution)/shard_map/place_0/pallas_call | solution.py:114
  668.5 3.0 fusion.41
  671.4 1.8 convolution_convert_fusion.14
  673.3 1.5 collective-permute-start.9
  674.7 5.1 convolution_convert_fusion.9
  680.5 1.3 add_dynamic-update-slice_fusion.1
  681.9 11.1 %place_1.1 = f32[3,1024,2048]{2,1,0:T(8,128)} custom-call(bf16[512,2048]{1,0:T(8,128)(2,1)S(1)} %copy-done.1, bf16[512,2048]{1,0:T(8,128)(2,1)} %collective-permute-done.3.refs_1_, bf16[512,2048]{1,0:T(8,128)(2,1)S(1)} %copy-done.2, bf16[512,2048]{1,0:T(8,128)(2,1)} %collective-permute-done.5.refs_3_, ...), custom_call_target="tpu_custom_call", output_to_operand_aliasing={{}: (6, {})} | custom-call | flops 3145728 | bytes 25165824 | tf_op jit(solution)/shard_map/place_1/pallas_call | solution.py:114
  693.0 2.1 convert_add_fusion.1
  696.1 1.4 copy-done.19
  (218 shorter events, 22.4 us)
Async XLA Ops:
  7.2 277.5 %copy-start = (bf16[1024,256]{1,0:T(8,128)(2,1)S(1)}, bf16[1024,256]{1,0:T(8,128)(2,1)}, u32[]{:S(2)}) copy-start(bf16[1024,256]{1,0:T(8,128)(2,1)} %param.18) | copy-start | bytes 1572868
  7.2 115.9 %copy-start.7 = (bf16[2,64,2048]{2,1,0:T(8,128)(2,1)S(1)}, bf16[2,64,2048]{2,1,0:T(8,128)(2,1)}, u32[]{:S(2)}) copy-start(bf16[2,64,2048]{2,1,0:T(8,128)(2,1)} %param.12) | copy-start | bytes 1572868
  7.2 256.6 %all-gather.4.cloned.1.call-start = ((), (), s32[]{:S(2)}) async-start(), calls=%async_computation.1 | async-start | bytes 8912896 | tf_op jit(solution)/shard_map/all_gather | solution.py:73
  119.0 223.2 %all-gather.6.cloned.1.call-start = ((), (), s32[]{:S(2)}) async-start(), calls=%async_computation.2 | async-start | bytes 10027008 | tf_op jit(solution)/shard_map/all_gather | solution.py:73
  124.5 5.9 copy-start.50
  124.5 5.9 copy-start.40
  124.6 58.7 %copy-start.38 = (f32[2048,1]{0,1:T(1,128)}, f32[2048,1]{0,1:T(1,128)S(1)}, u32[]{:S(2)}) copy-start(f32[2048,1]{0,1:T(1,128)S(1)} %get-tuple-element.160) | copy-start | bytes 24580
  124.8 6.4 copy-start.17
  130.5 38.7 %copy-start.54 = (s32[2,64]{1,0:T(2,128)S(1)}, s32[2,64]{1,0:T(2,128)}, u32[]{:S(2)}) copy-start(s32[2,64]{1,0:T(2,128)} %param.13) | copy-start | bytes 1540
  169.5 4.3 copy-start.25
  169.5 4.3 copy-start.27
  171.7 4.1 copy-start.57
  183.2 64.9 %copy-start.59 = (f32[128]{0:T(128)}, f32[128]{0:T(128)S(1)}, u32[]{:S(2)}) copy-start(f32[128]{0:T(128)S(1)} %get-tuple-element.172) | copy-start | bytes 1540
  183.2 64.9 %copy-start.44 = (f32[128]{0:T(128)}, f32[128]{0:T(128)S(1)}, u32[]{:S(2)}) copy-start(f32[128]{0:T(128)S(1)} %fusion.93) | copy-start | bytes 1540
  249.0 419.4 %reduce-scatter.2.cloned.1.call-start = ((), (), s32[]{:S(2)}) async-start(), calls=%async_computation.3 | async-start | bytes 8912896 | tf_op jit(solution)/shard_map/reduce_scatter | solution.py:77
  263.8 6.2 copy-start.42
  270.0 14.7 %copy-start.23 = (bf16[2048,256]{1,0:T(8,128)(2,1)}, bf16[2048,256]{1,0:T(8,128)(2,1)S(1)}, u32[]{:S(2)}) copy-start(bf16[2048,256]{1,0:T(8,128)(2,1)S(1)} %convolution_convert_fusion.8) | copy-start | bytes 3145732
  315.6 8.8 %copy-start.13 = (bf16[2048,1024]{1,0:T(8,128)(2,1)S(1)}, bf16[2048,1024]{1,0:T(8,128)(2,1)}, u32[]{:S(2)}) copy-start(bf16[2048,1024]{1,0:T(8,128)(2,1)} %get-tuple-element.105) | copy-start | bytes 12582916
  315.6 20.9 %slice-start.2 = ((s8[8388608]{0:T(1024)(128)(4,1)}), s8[4194304]{0:T(1024)(128)(4,1)S(1)}, s32[]{:S(2)}) async-start(s8[8388608]{0:T(1024)(128)(4,1)} %bitcast.226), calls=%async_computation.7 | async-start | bytes 8388608
  324.4 10.1 %copy-start.3 = (bf16[512,2048]{1,0:T(8,128)(2,1)}, bf16[512,2048]{1,0:T(8,128)(2,1)S(1)}, u32[]{:S(2)}) copy-start(bf16[512,2048]{1,0:T(8,128)(2,1)S(1)} %convolution_convert_fusion.6.refs_0_) | copy-start | bytes 6291460
  324.4 12.1 %slice-start.3 = ((s8[8388608]{0:T(1024)(128)(4,1)}), s8[4194304]{0:T(1024)(128)(4,1)S(1)}, s32[]{:S(2)}) async-start(s8[8388608]{0:T(1024)(128)(4,1)} %bitcast.226), calls=%async_computation.8 | async-start | bytes 8388608
  324.4 12.1 %copy-start.61 = (bf16[2048,1024]{1,0:T(8,128)(2,1)S(1)}, bf16[2048,1024]{1,0:T(8,128)(2,1)}, u32[]{:S(2)}) copy-start(bf16[2048,1024]{1,0:T(8,128)(2,1)} %get-tuple-element.103) | copy-start | bytes 12582916
  334.5 74.5 %collective-permute-start = (bf16[512,2048]{1,0:T(8,128)(2,1)S(1)}, bf16[512,2048]{1,0:T(8,128)(2,1)}, u32[]{:S(2)}, u32[]{:S(2)}) collective-permute-start(bf16[512,2048]{1,0:T(8,128)(2,1)S(1)} %convolution_convert_fusion.6.refs_0_), channel_id=1, source_target_pairs={{0,16},{16,0},{1,17},{17,1},{2,18},{18,2},{3,19},{19,3},{4,20},{20... | collective-permute-start | bytes 6291464 | tf_op jit(solution)/shard_map/ppermute | solution.py:128
  335.8 91.7 %collective-permute-start.1 = (bf16[512,2048]{1,0:T(8,128)(2,1)}, bf16[512,2048]{1,0:T(8,128)(2,1)}, u32[]{:S(2)}, u32[]{:S(2)}) collective-permute-start(bf16[512,2048]{1,0:T(8,128)(2,1)} %convolution_convert_fusion.5.refs_2_), channel_id=1, source_target_pairs={{0,16},{16,0},{1,17},{17,1},{2,18},{18,2},{3,19},{19,3},{4,20},{20... | collective-permute-start | bytes 6291464 | tf_op jit(solution)/shard_map/ppermute | solution.py:128
  441.4 6.2 copy-start.24
  441.5 230.0 %all-gather.8.cloned.1.call-start = ((), (), s32[]{:S(2)}) async-start(), calls=%async_computation.4 | async-start | bytes 8912896 | tf_op jit(solution)/shard_map/all_gather | solution.py:73
  441.5 6.1 copy-start.62
  441.5 49.8 %collective-permute-start.2 = (bf16[512,2048]{1,0:T(8,128)(2,1)}, bf16[512,2048]{1,0:T(8,128)(2,1)}, u32[]{:S(2)}, u32[]{:S(2)}) collective-permute-start(bf16[512,2048]{1,0:T(8,128)(2,1)} %convolution_convert_fusion.4.refs_4_), channel_id=1, source_target_pairs={{0,16},{16,0},{1,17},{17,1},{2,18},{18,2},{3,19},{19,3},{4,20},{20... | collective-permute-start | bytes 6291464 | tf_op jit(solution)/shard_map/ppermute | solution.py:128
  447.7 11.3 %slice-start = ((s8[8388608]{0:T(1024)(128)(4,1)}), s8[4194304]{0:T(1024)(128)(4,1)S(1)}, s32[]{:S(2)}) async-start(s8[8388608]{0:T(1024)(128)(4,1)} %bitcast.161), calls=%async_computation.5 | async-start | bytes 8388608
  449.8 9.1 %slice-start.1 = ((s8[8388608]{0:T(1024)(128)(4,1)}), s8[4194304]{0:T(1024)(128)(4,1)S(1)}, s32[]{:S(2)}) async-start(s8[8388608]{0:T(1024)(128)(4,1)} %bitcast.161), calls=%async_computation.6 | async-start | bytes 8388608
  449.8 9.2 %copy-start.15 = (bf16[2048,1024]{1,0:T(8,128)(2,1)S(1)}, bf16[2048,1024]{1,0:T(8,128)(2,1)}, u32[]{:S(2)}) copy-start(bf16[2048,1024]{1,0:T(8,128)(2,1)} %get-tuple-element.104) | copy-start | bytes 12582916
  459.0 5.8 copy-start.14
  464.7 6.0 copy-start.6
  464.7 6.0 copy-start.9
  464.7 6.1 copy-start.39
  464.8 6.1 copy-start.45
  464.8 7.0 copy-start.60
  464.8 7.0 copy-start.10
  473.2 6.7 copy-start.53
  479.9 3.6 copy-start.29
  479.9 4.0 copy-start.12
  485.9 3.3 copy-start.30
  491.3 40.8 %copy-start.47 = (f32[128]{0:T(128)S(1)}, f32[128]{0:T(128)}, u32[]{:S(2)}) copy-start(f32[128]{0:T(128)} %copy-done.46) | copy-start | bytes 1540
  491.3 40.8 %copy-start.49 = (f32[128]{0:T(128)S(1)}, f32[128]{0:T(128)}, u32[]{:S(2)}) copy-start(f32[128]{0:T(128)} %copy-done.48) | copy-start | bytes 1540
  491.9 41.7 %copy-start.21 = (bf16[16,8,8,256]{3,1,2,0:T(8,128)(2,1)S(1)}, bf16[16,8,8,256]{3,1,2,0:T(8,128)(2,1)}, u32[]{:S(2)}) copy-start(bf16[16,8,8,256]{3,1,2,0:T(8,128)(2,1)} %copy.32) | copy-start | bytes 1572868
  492.9 58.3 %collective-permute-start.3 = (bf16[512,2048]{1,0:T(8,128)(2,1)}, bf16[512,2048]{1,0:T(8,128)(2,1)}, u32[]{:S(2)}, u32[]{:S(2)}) collective-permute-start(bf16[512,2048]{1,0:T(8,128)(2,1)} %convolution_convert_fusion.3.refs_0_), channel_id=1, source_target_pairs={{0,16},{16,0},{1,17},{17,1},{2,18},{18,2},{3,19},{19,3},{4,20},{20... | collective-permute-start | bytes 6291464 | tf_op jit(solution)/shard_map/ppermute | solution.py:128
  493.7 186.8 %collective-permute-start.5 = (bf16[512,2048]{1,0:T(8,128)(2,1)}, bf16[512,2048]{1,0:T(8,128)(2,1)}, u32[]{:S(2)}, u32[]{:S(2)}) collective-permute-start(bf16[512,2048]{1,0:T(8,128)(2,1)} %convolution_convert_fusion.2.refs_2_), channel_id=1, source_target_pairs={{0,16},{16,0},{1,17},{17,1},{2,18},{18,2},{3,19},{19,3},{4,20},{20... | collective-permute-start | bytes 6291464 | tf_op jit(solution)/shard_map/ppermute | solution.py:128
  495.0 185.5 %collective-permute-start.6 = (bf16[512,2048]{1,0:T(8,128)(2,1)S(1)}, bf16[512,2048]{1,0:T(8,128)(2,1)}, u32[]{:S(2)}, u32[]{:S(2)}) collective-permute-start(bf16[512,2048]{1,0:T(8,128)(2,1)S(1)} %convolution_convert_fusion.1.refs_4_), channel_id=1, source_target_pairs={{0,16},{16,0},{1,17},{17,1},{2,18},{18,2},{3,19},{19,3},{4,20},{20... | collective-permute-start | bytes 6291464 | tf_op jit(solution)/shard_map/ppermute | solution.py:128
  495.7 184.2 %collective-permute-start.7 = (bf16[1024,256]{1,0:T(8,128)(2,1)}, bf16[1024,256]{1,0:T(8,128)(2,1)}, u32[]{:S(2)}, u32[]{:S(2)}) collective-permute-start(bf16[1024,256]{1,0:T(8,128)(2,1)} %convolution_convert_fusion.12), channel_id=1, source_target_pairs={{0,16},{16,0},{1,17},{17,1},{2,18},{18,2},{3,19},{19,3},{4,20},{20... | collective-permute-start | bytes 1572872 | tf_op jit(solution)/shard_map/ppermute | solution.py:128
  535.3 6.5 copy-start.51
  535.3 9.8 %copy-start.43 = (bf16[2048]{0:T(1024)(128)(2,1)S(1)}, bf16[2048]{0:T(1024)(128)(2,1)}, u32[]{:S(2)}) copy-start(bf16[2048]{0:T(1024)(128)(2,1)} %get-tuple-element.143) | copy-start | bytes 12292
  535.3 11.9 %copy-start.34 = (bf16[2,64,256]{2,1,0:T(8,128)(2,1)S(1)}, bf16[2,64,256]{2,1,0:T(8,128)(2,1)}, u32[]{:S(2)}) copy-start(bf16[2,64,256]{2,1,0:T(8,128)(2,1)} %get-tuple-element.110) | copy-start | bytes 196612
  547.2 4.1 copy-start.37
  547.2 4.0 copy-start.32
  644.5 23.4 %collective-permute-start.4 = (bf16[2,128]{1,0:T(2,128)(2,1)S(1)}, bf16[2,128]{1,0:T(2,128)(2,1)S(1)}, u32[]{:S(2)}, u32[]{:S(2)}) collective-permute-start(bf16[2,128]{1,0:T(2,128)(2,1)S(1)} %slice_reduce_fusion), channel_id=1, source_target_pairs={{0,16},{16,0},{1,17},{17,1},{2,18},{18,2},{3,19},{19,3},{4,20},{20... | collective-permute-start | bytes 1544 | tf_op jit(solution)/shard_map/ppermute | solution.py:128
  645.8 6.7 copy-start.33
  645.8 8.1 %copy-start.22 = (bf16[2,16,64,128]{3,2,1,0:T(8,128)(2,1)S(1)}, bf16[2,16,64,128]{3,2,1,0:T(8,128)(2,1)}, u32[]{:S(2)}) copy-start(bf16[2,16,64,128]{3,2,1,0:T(8,128)(2,1)} %get-tuple-element.116) | copy-start | bytes 1572868
  651.7 28.8 %collective-permute-start.8 = (bf16[128,2048]{1,0:T(8,128)(2,1)}, bf16[128,2048]{1,0:T(8,128)(2,1)}, u32[]{:S(2)}, u32[]{:S(2)}) collective-permute-start(bf16[128,2048]{1,0:T(8,128)(2,1)} %fusion.38), channel_id=1, source_target_pairs={{0,16},{16,0},{1,17},{17,1},{2,18},{18,2},{3,19},{19,3},{4,20},{20... | collective-permute-start | bytes 1572872 | tf_op jit(solution)/shard_map/ppermute | solution.py:128
  673.3 7.2 %copy-start.18 = (f32[128,4608]{1,0:T(8,128)S(1)}, f32[128,4608]{1,0:T(8,128)}, u32[]{:S(2)}) copy-start(f32[128,4608]{1,0:T(8,128)} %unwritten.1) | copy-start | bytes 7077892
  673.3 8.6 %copy-start.1 = (bf16[512,2048]{1,0:T(8,128)(2,1)S(1)}, bf16[512,2048]{1,0:T(8,128)(2,1)}, u32[]{:S(2)}) copy-start(bf16[512,2048]{1,0:T(8,128)(2,1)} %convolution_convert_fusion.3.refs_0_) | copy-start | bytes 6291460
  673.3 8.6 %copy-start.2 = (bf16[512,2048]{1,0:T(8,128)(2,1)S(1)}, bf16[512,2048]{1,0:T(8,128)(2,1)}, u32[]{:S(2)}) copy-start(bf16[512,2048]{1,0:T(8,128)(2,1)} %convolution_convert_fusion.2.refs_2_) | copy-start | bytes 6291460
  673.3 21.8 %collective-permute-start.9 = (bf16[128,1280]{1,0:T(8,128)(2,1)S(1)}, bf16[128,1280]{1,0:T(8,128)(2,1)S(1)}, u32[]{:S(2)}, u32[]{:S(2)}) collective-permute-start(bf16[128,1280]{1,0:T(8,128)(2,1)S(1)} %pad_maximum_fusion.5), channel_id=1, source_target_pairs={{0,16},{16,0},{1,17},{17,1},{2,18},{18,2},{3,19},{19,3},{4,20},{20... | collective-permute-start | bytes 983048 | tf_op jit(solution)/shard_map/ppermute | solution.py:128
  679.9 16.1 %collective-permute-start.10 = (bf16[128,2048]{1,0:T(8,128)(2,1)S(1)}, bf16[128,2048]{1,0:T(8,128)(2,1)S(1)}, u32[]{:S(2)}, u32[]{:S(2)}) collective-permute-start(bf16[128,2048]{1,0:T(8,128)(2,1)S(1)} %convolution_convert_fusion.9), channel_id=1, source_target_pairs={{0,16},{16,0},{1,17},{17,1},{2,18},{18,2},{3,19},{19,3},{4,20},{20... | collective-permute-start | bytes 1572872 | tf_op jit(solution)/shard_map/ppermute | solution.py:128
  681.9 11.1 %copy-start.31 = (bf16[1024,256]{1,0:T(8,128)(2,1)S(1)}, bf16[1024,256]{1,0:T(8,128)(2,1)}, u32[]{:S(2)}) copy-start(bf16[1024,256]{1,0:T(8,128)(2,1)} %convolution_convert_fusion.12) | copy-start | bytes 1572868
  (18 other events, 30.9 us)
Sparse Core Ops, SparseCore 0:
  119.1 77.0 all-gather.3
  249.2 78.7 all-gather.5
  441.6 112.8 reduce-scatter.1
  556.5 98.8 all-gather.7

commit v8 on v7

--- a/solution.py
+++ b/solution.py
@@ -833,8 +833,10 @@
         return made
 
     ffn_parts = weight_grads(0, gate_grad, up_grad, hidden_act)
-    gate_grad, up_grad, kept_all, _ = lax.optimization_barrier(
-        (gate_grad, up_grad, kept_all, [pair[0] for pair in ffn_parts])
+    down_part = low(contract(hidden_act, ffn_weight[:, 2, :], 1, 0))
+    low_part = low(contract(hidden_act, ffn_adapter, 1, 0))
+    gate_grad, up_grad, kept_all, down_part, low_part, _ = lax.optimization_barrier(
+        (gate_grad, up_grad, kept_all, down_part, low_part, [pair[0] for pair in ffn_parts])
     )
     if grid_of(shards)[1] == 2 and micro == 2:
         normed_two_grad = product_sum(
@@ -853,13 +855,15 @@
                 + contract(up_grad, ffn_weight[:, 1, :], 1, 0)
             ).reshape(micro, shards, local_len, model_dim),
         )
-    normed_two_grad, gate_grad, up_grad, hidden_act, _ = lax.optimization_barrier(
-        (normed_two_grad, gate_grad, up_grad, hidden_act, [pair[1] for pair in ffn_parts[:2]])
-    )
-    down_part = low(contract(hidden_act, ffn_weight[:, 2, :], 1, 0))
-    low_part = low(contract(hidden_act, ffn_adapter, 1, 0))
-    down_part, gate_grad, up_grad, hidden_act = lax.optimization_barrier(
-        (down_part, gate_grad, up_grad, hidden_act)
+    normed_two_grad, down_part, gate_grad, up_grad, hidden_act, _ = lax.optimization_barrier(
+        (
+            normed_two_grad,
+            down_part,
+            gate_grad,
+            up_grad,
+            hidden_act,
+            [pair[1] for pair in ffn_parts[:2]],
+        )
     )
     down_sum = sum_rows(down_part.reshape(micro, seq_len, model_dim))
     ffn_parts += weight_grads(1, gate_grad, up_grad, hidden_act)

time: 712 us -> 691 us (0.971)
  waiting for transfers between devices: 18.6 us -> 0.1 us
    ppermute x11, waiting for transfers between devices: 18.6 us -> 0.03 us  [swap_rep(): return lax.ppermute(values, 'rep', [(0, 1), (1, 0)])]
  transfers between devices with their start and end apart: 15 -> 15, of which waited for: 1 -> 0; matrix products, arithmetic and copies ran while one was open for 30% -> 32% of each run, Pallas kernels for 45% -> 46%
where the time goes in v8:
time: 691 us; the launch traced here: 684 us
  Pallas kernels  425 us (62%)
  matrix products  189 us (27%)
  other arithmetic  23 us (3%)
  local copies, waits for them, and re-layouts  18.8 us (3%)
  between operations  15.3 us (2%)
  starting transfers between devices  12.1 us (2%)
    pallas_call x4, Pallas kernels, gather_all(): pl.pallas_call(functools.partial(gather_kernel, shards, widths, shared, l...  299 us
    dot_general x28, matrix products, contract(): lax.dot_general(left_op, right_op, (((left_dim,), (right_dim,)), ((), ())...  178 us
    pallas_call x1, Pallas kernels, product_sum(): pl.pallas_call(functools.partial(product_kernel, shards), out_shape=jax.S...  67.1 us
    pallas_call x1, Pallas kernels, scatter_sum(): pl.pallas_call(functools.partial(scatter_kernel, shards, widths), out_sha...  34.7 us
    pallas_call x2, Pallas kernels, place(): pl.pallas_call(functools.partial(place_kernel, kinds), grid=(kinds, tiles...  24.6 us
  transfers between devices with their start and end apart: 15, of which 0 were waited for; matrix products, arithmetic and copies ran while one was open for 32% of the time, Pallas kernels for 46%

profile of v8, /device:TPU:0, one launch (start us, length us, event | category | flops | bytes accessed | tf_op | source)
XLA Modules:
  0.0 683.5 jit_solution(3118600032390185683)
XLA Ops:
  9.7 109.2 %gather_1.1 = (bf16[1,16,128,4608]{3,2,1,0:T(8,128)(2,1)}, bf16[1,16,128,768]{3,2,1,0:T(8,128)(2,1)}, bf16[1,16,128,128]{3,2,1,0:T(8,128)(2,1)}) custom-call(bf16[1,128,4608]{2,1,0:T(8,128)(2,1)} %bitcast.189, bf16[1,128,768]{2,1,0:T(8,128)(2,1)} %bitcast.214, bf16[1,128,128]{2,1,0:T(8,128)(2,1)} %maximum_bitcast_fusion.refs_2_), custom_call_target="tpu_custom_call" | custom-call | bytes 583008256 | tf_op jit(solution)/shard_map/gather_1/pallas_call | solution.py:357
  119.2 1.2 slice.189
  120.9 0.9 convert_reduce_fusion
  121.8 1.3 copy.30
  124.7 5.7 fusion.3
  132.3 1.2 fusion.90
  134.1 34.8 %gather_2.1 = (bf16[2,16,64,256]{3,2,1,0:T(8,128)(2,1)}, bf16[2,16,64,256]{3,2,1,0:T(8,128)(2,1)}) custom-call(bf16[2,64,256]{2,1,0:T(8,128)(2,1)} %pad_maximum_fusion.6.refs_0_, bf16[2,64,256]{2,1,0:T(8,128)(2,1)} %bitcast.205), custom_call_target="tpu_custom_call" | custom-call | bytes 92274688 | tf_op jit(solution)/shard_map/gather_2/pallas_call | solution.py:357
  169.4 2.2 fusion.88
  171.6 2.1 fusion.102
  173.7 1.9 copy-done.12
  176.7 6.4 multiply_reduce_fusion.1
  183.1 0.9 copy-done.6
  184.0 1.0 multiply_convert_fusion.4
  185.0 63.1 %gather_3.1 = bf16[2,16,64,2048]{3,2,1,0:T(8,128)(2,1)} custom-call(bf16[2,64,2048]{2,1,0:T(8,128)(2,1)} %bitcast.180), custom_call_target="tpu_custom_call" | custom-call | bytes 243269632 | tf_op jit(solution)/shard_map/gather_3/pallas_call | solution.py:357
  248.1 0.9 pad_maximum_fusion
  249.2 14.6 %fusion.18 = f32[2048,1024]{1,0:T(8,128)} fusion(bf16[2048,2048]{1,0:T(8,128)(2,1)} %bitcast.157, bf16[1024,3,2048]{2,0,1:T(8,128)(2,1)} %param.17), kind=kOutput, calls=%fused_computation.25 | convolution fusion | flops 8589934592 | bytes 20971520 | tf_op jit(solution)/shard_map/dot_general | solution.py:51
  263.8 6.1 convolution_convert_fusion.8
  270.0 14.7 %fusion.23 = f32[2048,1024]{1,0:T(8,128)S(1)} fusion(bf16[2048,2048]{1,0:T(8,128)(2,1)S(1)} %bitcast.225, bf16[1024,3,2048]{2,0,1:T(8,128)(2,1)} %param.17), kind=kOutput, calls=%fused_computation.30 | convolution fusion | flops 8589934592 | bytes 20971520 | tf_op jit(solution)/shard_map/dot_general | solution.py:51
  284.7 4.5 convolution_add_fusion
  289.2 26.4 %multiply_convert_fusion = (bf16[2048,1024]{1,0:T(8,128)(2,1)}, bf16[2048,1024]{1,0:T(8,128)(2,1)}, bf16[2048,1024]{1,0:T(8,128)(2,1)}) fusion(f32[2048,1024]{1,0:T(8,128)} %fusion.18, f32[2048,1024]{1,0:T(8,128)} %convolution_add_fusion, bf16[2048,2048]{1,0:T(8,128)(2,1)} %bitcast.158, bf16[1024,3,2048]{2,0,1:T(8,128)(2,1)} %param.17), kind=kOutput, calls=%fused_computation.16 | convolution fusion | flops 8644460544 | bytes 41943040 | tf_op jit(solution)/shard_map/dot_general | solution.py:51
  315.6 8.7 %convolution_convert_fusion.6.refs_0_ = bf16[512,2048]{1,0:T(8,128)(2,1)S(1)} fusion(bf16[2048,2048]{1,0:T(8,128)(2,1)} %bitcast.159, bf16[2048,1024]{1,0:T(8,128)(2,1)} %get-tuple-element.102), kind=kOutput, calls=%fused_computation.48 | convolution fusion | flops 4296015872 | bytes 12582912 | tf_op jit(solution)/shard_map/dot_general | solution.py:51
  324.3 1.4 collective-permute-start
  325.7 9.4 %convolution_convert_fusion.5.refs_2_ = bf16[512,2048]{1,0:T(8,128)(2,1)} fusion(bf16[2048,2048]{1,0:T(8,128)(2,1)} %bitcast.160, bf16[2048,1024]{1,0:T(8,128)(2,1)S(1)} %copy-done.14), kind=kOutput, calls=%fused_computation.47 | convolution fusion | flops 4296015872 | bytes 12582912 | tf_op jit(solution)/shard_map/dot_general | solution.py:51
  335.1 0.8 collective-permute-start.1
  336.0 5.7 convolution_convert_fusion.4.refs_4_
  341.7 2.3 convolution_convert_fusion.7
  344.0 13.0 %convolution_convert_fusion = bf16[2048,2048]{1,0:T(8,128)(2,1)} fusion(bf16[2048,1024]{1,0:T(8,128)(2,1)S(1)} %copy-done.62, bf16[1024,3,2048]{2,0,1:T(8,128)(2,1)} %param.17), kind=kOutput, calls=%fused_computation.19 | convolution fusion | flops 8594128896 | bytes 16777216 | tf_op jit(solution)/shard_map/dot_general | solution.py:51
  357.0 67.1 %product_5.1 = bf16[2,64,2048]{2,1,0:T(8,128)(2,1)} custom-call(bf16[2,1024,1024]{2,1,0:T(8,128)(2,1)} %bitcast.169, bf16[2,1024,1024]{2,1,0:T(8,128)(2,1)} %bitcast.168, bf16[3,1024,2048]{2,1,0:T(8,128)(2,1)} %bitcast.155), custom_call_target="tpu_custom_call" | custom-call | bytes 243269632 | tf_op jit(solution)/shard_map/product_5/pallas_call | solution.py:686
  424.2 1.2 collective-permute-start.2
  425.5 4.6 convolution_convert_fusion.12
  430.1 9.1 %convolution_convert_fusion.1.refs_4_ = bf16[512,2048]{1,0:T(8,128)(2,1)S(1)} fusion(bf16[2048,2048]{1,0:T(8,128)(2,1)} %bitcast.223, bf16[2048,1024]{1,0:T(8,128)(2,1)S(1)} %copy-done.63), kind=kOutput, calls=%fused_computation.43 | convolution fusion | flops 4296015872 | bytes 12582912 | tf_op jit(solution)/shard_map/dot_general | solution.py:51
  439.3 5.8 convolution_convert_fusion.3.refs_0_
  445.1 5.9 convolution_convert_fusion.2.refs_2_
  451.1 0.9 fusion.57
  453.3 5.9 fusion.35
  459.2 1.3 reshape.506
  460.5 3.6 multiply_reduce_fusion
  466.8 0.9 copy.32
  467.7 1.9 multiply_convert_fusion.3
  469.7 2.2 convolution_convert_fusion.10
  472.5 1.0 fusion.68.refs_1_
  473.5 1.4 collective-permute-start.3
  475.5 1.4 collective-permute-start.6
  477.5 34.7 %scatter_6.1 = (bf16[2,64,256]{2,1,0:T(8,128)(2,1)}, bf16[2,64,256]{2,1,0:T(8,128)(2,1)}, bf16[2,64,256]{2,1,0:T(8,128)(2,1)}) custom-call(bf16[2,16,64,256]{3,2,1,0:T(8,128)(2,1)} %bitcast.191, bf16[2,16,64,256]{3,2,1,0:T(8,128)(2,1)} %bitcast.192, bf16[2,16,64,256]{3,2,1,0:T(8,128)(2,1)} %bitcast.190), custom_call_target="tpu_custom_call" | custom-call | bytes 117440512 | tf_op jit(solution)/shard_map/scatter_6/pallas_call | solution.py:540
  512.2 0.9 bitcast_convert_fusion
  513.8 0.8 constant_dynamic-update-slice_fusion.2
  514.6 1.5 constant_dynamic-update-slice_fusion.1
  516.2 6.5 fusion.1
  522.8 3.3 fusion.65
  526.7 1.5 scatter.9.refs_3_
  528.9 3.2 fusion.60
  532.1 91.4 %gather_4.1 = (bf16[2,16,64,1024]{3,2,1,0:T(8,128)(2,1)}, bf16[2,16,64,128]{3,2,1,0:T(8,128)(2,1)}, bf16[2,16,64,128]{3,2,1,0:T(8,128)(2,1)}, bf16[1,16,16,128]{3,2,1,0:T(8,128)(2,1)}) custom-call(bf16[2,64,1024]{2,1,0:T(8,128)(2,1)} %bitcast.200, bf16[2,64,2048]{2,1,0:T(8,128)(2,1)} %fusion.68.refs_1_, bf16[2,64,2048]{2,1,0:T(8,128)(2,1)} %bitcast.179, ...), custom_call_target="tpu_custom_call" | custom-call | bytes 142606336 | tf_op jit(solution)/shard_map/gather_4/pallas_call | solution.py:357
  624.3 1.5 collective-permute-start.4
  625.8 5.1 fusion.38
  631.6 1.4 convolution_convert_fusion.13
  633.6 13.5 %place_0.1.refs_6_ = f32[3,1024,2048]{2,1,0:T(8,128)} custom-call(bf16[512,2048]{1,0:T(8,128)(2,1)S(1)} %copy-done.5, bf16[512,2048]{1,0:T(8,128)(2,1)} %collective-permute-done.refs_1_, bf16[512,2048]{1,0:T(8,128)(2,1)} %convolution_convert_fusion.5.refs_2_, bf16[512,2048]{1,0:T(8,128)(2,1)} %collective-permute-done.1.refs_3_, ...), custom_call_target="tpu_custom_call" | custom-call | flops 3145728 | bytes 25165824 | tf_op jit(solution)/shard_map/place_0/pallas_call | solution.py:114
  647.7 3.0 fusion.41
  650.7 1.8 convolution_convert_fusion.14
  652.5 1.5 collective-permute-start.9
  654.0 5.0 convolution_convert_fusion.9
  659.7 1.2 add_dynamic-update-slice_fusion.1
  660.9 11.1 %place_1.1 = f32[3,1024,2048]{2,1,0:T(8,128)} custom-call(bf16[512,2048]{1,0:T(8,128)(2,1)S(1)} %copy-done.2, bf16[512,2048]{1,0:T(8,128)(2,1)} %collective-permute-done.3.refs_1_, bf16[512,2048]{1,0:T(8,128)(2,1)S(1)} %copy-done.3, bf16[512,2048]{1,0:T(8,128)(2,1)} %collective-permute-done.5.refs_3_, ...), custom_call_target="tpu_custom_call", output_to_operand_aliasing={{}: (6, {})} | custom-call | flops 3145728 | bytes 25165824 | tf_op jit(solution)/shard_map/place_1/pallas_call | solution.py:114
  672.0 2.1 convert_add_fusion.1
  675.2 1.4 copy-done.20
  (220 shorter events, 21.2 us)
Async XLA Ops:
  7.2 277.5 %copy-start = (bf16[1024,256]{1,0:T(8,128)(2,1)S(1)}, bf16[1024,256]{1,0:T(8,128)(2,1)}, u32[]{:S(2)}) copy-start(bf16[1024,256]{1,0:T(8,128)(2,1)} %param.18) | copy-start | bytes 1572868
  7.2 115.9 %copy-start.8 = (bf16[2,64,2048]{2,1,0:T(8,128)(2,1)S(1)}, bf16[2,64,2048]{2,1,0:T(8,128)(2,1)}, u32[]{:S(2)}) copy-start(bf16[2,64,2048]{2,1,0:T(8,128)(2,1)} %param.12) | copy-start | bytes 1572868
  7.2 256.6 %all-gather.4.cloned.1.call-start = ((), (), s32[]{:S(2)}) async-start(), calls=%async_computation.1 | async-start | bytes 8912896 | tf_op jit(solution)/shard_map/all_gather | solution.py:73
  119.0 238.0 %all-gather.6.cloned.1.call-start = ((), (), s32[]{:S(2)}) async-start(), calls=%async_computation.2 | async-start | bytes 10027008 | tf_op jit(solution)/shard_map/all_gather | solution.py:73
  124.5 5.9 copy-start.51
  124.5 5.9 copy-start.41
  124.5 58.6 %copy-start.39 = (f32[2048,1]{0,1:T(1,128)}, f32[2048,1]{0,1:T(1,128)S(1)}, u32[]{:S(2)}) copy-start(f32[2048,1]{0,1:T(1,128)S(1)} %get-tuple-element.158) | copy-start | bytes 24580
  124.7 6.4 copy-start.18
  130.4 38.6 %copy-start.55 = (s32[2,64]{1,0:T(2,128)S(1)}, s32[2,64]{1,0:T(2,128)}, u32[]{:S(2)}) copy-start(s32[2,64]{1,0:T(2,128)} %param.13) | copy-start | bytes 1540
  169.4 4.3 copy-start.26
  169.4 4.3 copy-start.28
  171.6 4.1 copy-start.58
  183.1 65.0 %copy-start.60 = (f32[128]{0:T(128)}, f32[128]{0:T(128)S(1)}, u32[]{:S(2)}) copy-start(f32[128]{0:T(128)S(1)} %get-tuple-element.170) | copy-start | bytes 1540
  183.1 65.0 %copy-start.45 = (f32[128]{0:T(128)}, f32[128]{0:T(128)S(1)}, u32[]{:S(2)}) copy-start(f32[128]{0:T(128)S(1)} %fusion.93) | copy-start | bytes 1540
  249.0 398.7 %reduce-scatter.2.cloned.1.call-start = ((), (), s32[]{:S(2)}) async-start(), calls=%async_computation.3 | async-start | bytes 8912896 | tf_op jit(solution)/shard_map/reduce_scatter | solution.py:77
  263.8 6.2 copy-start.43
  270.0 14.7 %copy-start.24 = (bf16[2048,256]{1,0:T(8,128)(2,1)}, bf16[2048,256]{1,0:T(8,128)(2,1)S(1)}, u32[]{:S(2)}) copy-start(bf16[2048,256]{1,0:T(8,128)(2,1)S(1)} %convolution_convert_fusion.8) | copy-start | bytes 3145732
  315.6 10.2 %copy-start.14 = (bf16[2048,1024]{1,0:T(8,128)(2,1)S(1)}, bf16[2048,1024]{1,0:T(8,128)(2,1)}, u32[]{:S(2)}) copy-start(bf16[2048,1024]{1,0:T(8,128)(2,1)} %get-tuple-element.103) | copy-start | bytes 12582916
  315.6 20.4 %slice-start.2 = ((s8[8388608]{0:T(1024)(128)(4,1)}), s8[4194304]{0:T(1024)(128)(4,1)S(1)}, s32[]{:S(2)}) async-start(s8[8388608]{0:T(1024)(128)(4,1)} %bitcast.226), calls=%async_computation.7 | async-start | bytes 8388608
  324.3 10.8 %copy-start.4 = (bf16[512,2048]{1,0:T(8,128)(2,1)}, bf16[512,2048]{1,0:T(8,128)(2,1)S(1)}, u32[]{:S(2)}) copy-start(bf16[512,2048]{1,0:T(8,128)(2,1)S(1)} %convolution_convert_fusion.6.refs_0_) | copy-start | bytes 6291460
  324.3 99.8 %collective-permute-start = (bf16[512,2048]{1,0:T(8,128)(2,1)S(1)}, bf16[512,2048]{1,0:T(8,128)(2,1)}, u32[]{:S(2)}, u32[]{:S(2)}) collective-permute-start(bf16[512,2048]{1,0:T(8,128)(2,1)S(1)} %convolution_convert_fusion.6.refs_0_), channel_id=1, source_target_pairs={{0,16},{16,0},{1,17},{17,1},{2,18},{18,2},{3,19},{19,3},{4,20},{20... | collective-permute-start | bytes 6291464 | tf_op jit(solution)/shard_map/ppermute | solution.py:128
  325.7 10.3 %slice-start.3 = ((s8[8388608]{0:T(1024)(128)(4,1)}), s8[4194304]{0:T(1024)(128)(4,1)S(1)}, s32[]{:S(2)}) async-start(s8[8388608]{0:T(1024)(128)(4,1)} %bitcast.226), calls=%async_computation.8 | async-start | bytes 8388608
  325.7 10.3 %copy-start.62 = (bf16[2048,1024]{1,0:T(8,128)(2,1)S(1)}, bf16[2048,1024]{1,0:T(8,128)(2,1)}, u32[]{:S(2)}) copy-start(bf16[2048,1024]{1,0:T(8,128)(2,1)} %get-tuple-element.101) | copy-start | bytes 12582916
  335.1 89.0 %collective-permute-start.1 = (bf16[512,2048]{1,0:T(8,128)(2,1)}, bf16[512,2048]{1,0:T(8,128)(2,1)}, u32[]{:S(2)}, u32[]{:S(2)}) collective-permute-start(bf16[512,2048]{1,0:T(8,128)(2,1)} %convolution_convert_fusion.5.refs_2_), channel_id=1, source_target_pairs={{0,16},{16,0},{1,17},{17,1},{2,18},{18,2},{3,19},{19,3},{4,20},{20... | collective-permute-start | bytes 6291464 | tf_op jit(solution)/shard_map/ppermute | solution.py:128
  424.2 226.5 %all-gather.8.cloned.1.call-start = ((), (), s32[]{:S(2)}) async-start(), calls=%async_computation.4 | async-start | bytes 8912896 | tf_op jit(solution)/shard_map/all_gather | solution.py:73
  424.2 5.9 copy-start.63
  424.2 47.6 %collective-permute-start.2 = (bf16[512,2048]{1,0:T(8,128)(2,1)}, bf16[512,2048]{1,0:T(8,128)(2,1)}, u32[]{:S(2)}, u32[]{:S(2)}) collective-permute-start(bf16[512,2048]{1,0:T(8,128)(2,1)} %convolution_convert_fusion.4.refs_4_), channel_id=1, source_target_pairs={{0,16},{16,0},{1,17},{17,1},{2,18},{18,2},{3,19},{19,3},{4,20},{20... | collective-permute-start | bytes 6291464 | tf_op jit(solution)/shard_map/ppermute | solution.py:128
  425.5 13.8 %slice-start = ((s8[8388608]{0:T(1024)(128)(4,1)}), s8[4194304]{0:T(1024)(128)(4,1)S(1)}, s32[]{:S(2)}) async-start(s8[8388608]{0:T(1024)(128)(4,1)} %bitcast.161), calls=%async_computation.5 | async-start | bytes 8388608
  430.1 9.2 %slice-start.1 = ((s8[8388608]{0:T(1024)(128)(4,1)}), s8[4194304]{0:T(1024)(128)(4,1)S(1)}, s32[]{:S(2)}) async-start(s8[8388608]{0:T(1024)(128)(4,1)} %bitcast.161), calls=%async_computation.6 | async-start | bytes 8388608
  430.1 9.2 %copy-start.16 = (bf16[2048,1024]{1,0:T(8,128)(2,1)S(1)}, bf16[2048,1024]{1,0:T(8,128)(2,1)}, u32[]{:S(2)}) copy-start(bf16[2048,1024]{1,0:T(8,128)(2,1)} %get-tuple-element.102) | copy-start | bytes 12582916
  439.3 5.8 copy-start.15
  445.1 6.0 copy-start.7
  445.1 6.0 copy-start.10
  445.1 6.0 copy-start.40
  445.1 6.0 copy-start.46
  445.1 6.9 %copy-start.61 = (f32[128]{0:T(128)S(1)}, f32[128]{0:T(128)}, u32[]{:S(2)}) copy-start(f32[128]{0:T(128)} %copy-done.60) | copy-start | bytes 1540
  445.1 7.0 %copy-start.11 = (bf16[2,64,2048]{2,1,0:T(8,128)(2,1)S(1)}, bf16[2,64,2048]{2,1,0:T(8,128)(2,1)}, u32[]{:S(2)}) copy-start(bf16[2,64,2048]{2,1,0:T(8,128)(2,1)} %param.19) | copy-start | bytes 1572868
  452.1 7.1 %copy-start.57 = (f32[128]{0:T(128)}, f32[128]{0:T(128)S(1)}, u32[]{:S(2)}) copy-start(f32[128]{0:T(128)S(1)} %multiply_multiply_fusion.4) | copy-start | bytes 1540
  453.3 7.2 %copy-start.54 = (f32[2,512]{1,0:T(2,128)S(1)}, f32[2,512]{1,0:T(2,128)}, u32[]{:S(2)}) copy-start(f32[2,512]{1,0:T(2,128)} %copy-done.53) | copy-start | bytes 12292
  460.5 3.6 copy-start.30
  460.5 4.0 copy-start.13
  471.9 41.2 %copy-start.48 = (f32[128]{0:T(128)S(1)}, f32[128]{0:T(128)}, u32[]{:S(2)}) copy-start(f32[128]{0:T(128)} %copy-done.47) | copy-start | bytes 1540
  471.9 41.2 %copy-start.50 = (f32[128]{0:T(128)S(1)}, f32[128]{0:T(128)}, u32[]{:S(2)}) copy-start(f32[128]{0:T(128)} %copy-done.49) | copy-start | bytes 1540
  472.5 42.1 %copy-start.22 = (bf16[16,8,8,256]{3,1,2,0:T(8,128)(2,1)S(1)}, bf16[16,8,8,256]{3,1,2,0:T(8,128)(2,1)}, u32[]{:S(2)}) copy-start(bf16[16,8,8,256]{3,1,2,0:T(8,128)(2,1)} %copy.32) | copy-start | bytes 1572868
  473.5 58.6 %collective-permute-start.3 = (bf16[512,2048]{1,0:T(8,128)(2,1)}, bf16[512,2048]{1,0:T(8,128)(2,1)}, u32[]{:S(2)}, u32[]{:S(2)}) collective-permute-start(bf16[512,2048]{1,0:T(8,128)(2,1)} %convolution_convert_fusion.3.refs_0_), channel_id=1, source_target_pairs={{0,16},{16,0},{1,17},{17,1},{2,18},{18,2},{3,19},{19,3},{4,20},{20... | collective-permute-start | bytes 6291464 | tf_op jit(solution)/shard_map/ppermute | solution.py:128
  474.8 184.8 %collective-permute-start.5 = (bf16[512,2048]{1,0:T(8,128)(2,1)}, bf16[512,2048]{1,0:T(8,128)(2,1)}, u32[]{:S(2)}, u32[]{:S(2)}) collective-permute-start(bf16[512,2048]{1,0:T(8,128)(2,1)} %convolution_convert_fusion.2.refs_2_), channel_id=1, source_target_pairs={{0,16},{16,0},{1,17},{17,1},{2,18},{18,2},{3,19},{19,3},{4,20},{20... | collective-permute-start | bytes 6291464 | tf_op jit(solution)/shard_map/ppermute | solution.py:128
  475.5 184.1 %collective-permute-start.6 = (bf16[512,2048]{1,0:T(8,128)(2,1)S(1)}, bf16[512,2048]{1,0:T(8,128)(2,1)}, u32[]{:S(2)}, u32[]{:S(2)}) collective-permute-start(bf16[512,2048]{1,0:T(8,128)(2,1)S(1)} %convolution_convert_fusion.1.refs_4_), channel_id=1, source_target_pairs={{0,16},{16,0},{1,17},{17,1},{2,18},{18,2},{3,19},{19,3},{4,20},{20... | collective-permute-start | bytes 6291464 | tf_op jit(solution)/shard_map/ppermute | solution.py:128
  476.9 182.2 %collective-permute-start.7 = (bf16[1024,256]{1,0:T(8,128)(2,1)}, bf16[1024,256]{1,0:T(8,128)(2,1)}, u32[]{:S(2)}, u32[]{:S(2)}) collective-permute-start(bf16[1024,256]{1,0:T(8,128)(2,1)} %convolution_convert_fusion.12), channel_id=1, source_target_pairs={{0,16},{16,0},{1,17},{17,1},{2,18},{18,2},{3,19},{19,3},{4,20},{20... | collective-permute-start | bytes 1572872 | tf_op jit(solution)/shard_map/ppermute | solution.py:128
  516.2 6.6 copy-start.52
  516.2 9.9 %copy-start.44 = (bf16[2048]{0:T(1024)(128)(2,1)S(1)}, bf16[2048]{0:T(1024)(128)(2,1)}, u32[]{:S(2)}) copy-start(bf16[2048]{0:T(1024)(128)(2,1)} %get-tuple-element.141) | copy-start | bytes 12292
  516.2 12.0 %copy-start.35 = (bf16[2,64,256]{2,1,0:T(8,128)(2,1)S(1)}, bf16[2,64,256]{2,1,0:T(8,128)(2,1)}, u32[]{:S(2)}) copy-start(bf16[2,64,256]{2,1,0:T(8,128)(2,1)} %get-tuple-element.108) | copy-start | bytes 196612
  528.2 3.9 copy-start.38
  528.2 3.9 copy-start.33
  624.3 22.8 %collective-permute-start.4 = (bf16[2,128]{1,0:T(2,128)(2,1)S(1)}, bf16[2,128]{1,0:T(2,128)(2,1)S(1)}, u32[]{:S(2)}, u32[]{:S(2)}) collective-permute-start(bf16[2,128]{1,0:T(2,128)(2,1)S(1)} %slice_reduce_fusion), channel_id=1, source_target_pairs={{0,16},{16,0},{1,17},{17,1},{2,18},{18,2},{3,19},{19,3},{4,20},{20... | collective-permute-start | bytes 1544 | tf_op jit(solution)/shard_map/ppermute | solution.py:128
  625.8 5.7 copy-start.34
  625.8 7.2 %copy-start.23 = (bf16[2,16,64,128]{3,2,1,0:T(8,128)(2,1)S(1)}, bf16[2,16,64,128]{3,2,1,0:T(8,128)(2,1)}, u32[]{:S(2)}) copy-start(bf16[2,16,64,128]{3,2,1,0:T(8,128)(2,1)} %get-tuple-element.114) | copy-start | bytes 1572868
  631.0 28.7 %collective-permute-start.8 = (bf16[128,2048]{1,0:T(8,128)(2,1)S(1)}, bf16[128,2048]{1,0:T(8,128)(2,1)}, u32[]{:S(2)}, u32[]{:S(2)}) collective-permute-start(bf16[128,2048]{1,0:T(8,128)(2,1)S(1)} %fusion.38), channel_id=1, source_target_pairs={{0,16},{16,0},{1,17},{17,1},{2,18},{18,2},{3,19},{19,3},{4,20},{20... | collective-permute-start | bytes 1572872 | tf_op jit(solution)/shard_map/ppermute | solution.py:128
  652.5 7.2 %copy-start.19 = (f32[128,4608]{1,0:T(8,128)S(1)}, f32[128,4608]{1,0:T(8,128)}, u32[]{:S(2)}) copy-start(f32[128,4608]{1,0:T(8,128)} %unwritten.1) | copy-start | bytes 7077892
  652.5 8.4 %copy-start.2 = (bf16[512,2048]{1,0:T(8,128)(2,1)S(1)}, bf16[512,2048]{1,0:T(8,128)(2,1)}, u32[]{:S(2)}) copy-start(bf16[512,2048]{1,0:T(8,128)(2,1)} %convolution_convert_fusion.3.refs_0_) | copy-start | bytes 6291460
  652.5 8.4 %copy-start.3 = (bf16[512,2048]{1,0:T(8,128)(2,1)S(1)}, bf16[512,2048]{1,0:T(8,128)(2,1)}, u32[]{:S(2)}) copy-start(bf16[512,2048]{1,0:T(8,128)(2,1)} %convolution_convert_fusion.2.refs_2_) | copy-start | bytes 6291460
  652.5 21.7 %collective-permute-start.9 = (bf16[128,1280]{1,0:T(8,128)(2,1)S(1)}, bf16[128,1280]{1,0:T(8,128)(2,1)S(1)}, u32[]{:S(2)}, u32[]{:S(2)}) collective-permute-start(bf16[128,1280]{1,0:T(8,128)(2,1)S(1)} %pad_maximum_fusion.5), channel_id=1, source_target_pairs={{0,16},{16,0},{1,17},{17,1},{2,18},{18,2},{3,19},{19,3},{4,20},{20... | collective-permute-start | bytes 983048 | tf_op jit(solution)/shard_map/ppermute | solution.py:128
  659.1 15.9 %collective-permute-start.10 = (bf16[128,2048]{1,0:T(8,128)(2,1)S(1)}, bf16[128,2048]{1,0:T(8,128)(2,1)S(1)}, u32[]{:S(2)}, u32[]{:S(2)}) collective-permute-start(bf16[128,2048]{1,0:T(8,128)(2,1)S(1)} %convolution_convert_fusion.9), channel_id=1, source_target_pairs={{0,16},{16,0},{1,17},{17,1},{2,18},{18,2},{3,19},{19,3},{4,20},{20... | collective-permute-start | bytes 1572872 | tf_op jit(solution)/shard_map/ppermute | solution.py:128
  660.9 11.2 %copy-start.32 = (bf16[1024,256]{1,0:T(8,128)(2,1)S(1)}, bf16[1024,256]{1,0:T(8,128)(2,1)}, u32[]{:S(2)}) copy-start(bf16[1024,256]{1,0:T(8,128)(2,1)} %convolution_convert_fusion.12) | copy-start | bytes 1572868
  660.9 15.7 %copy-start.1 = (bf16[1024,256]{1,0:T(8,128)(2,1)S(1)}, bf16[1024,256]{1,0:T(8,128)(2,1)}, u32[]{:S(2)}) copy-start(bf16[1024,256]{1,0:T(8,128)(2,1)} %param.18) | copy-start | bytes 1572868
  (19 other events, 34.8 us)
Sparse Core Ops, SparseCore 0:
  119.1 76.9 all-gather.3
  249.1 78.8 all-gather.5
  424.3 112.9 reduce-scatter.1
  539.3 95.8 all-gather.7

commit v9 on v8

--- a/solution.py
+++ b/solution.py
@@ -94,7 +94,7 @@
 def place(whole, group, groups, pairs):
     kinds = len(pairs)
     rows, columns = pairs[0][0].shape
-    tile = min(rows, 128)
+    tile = min(rows, 256)
     tiles = rows // tile
 
     def part(kind):
@@ -917,7 +917,10 @@
     input_grad = low(mixed_grad + hidden_part)
 
     narrow = jnp.concatenate([key_grad, value_grad, rank_grad, down_low], axis=1)
-    narrow, ffn_parts[3:4] = lax.optimization_barrier((narrow, ffn_parts[3:4]))
+    ffn_grad = place(None, 0, PIECES, ffn_parts[:3])
+    narrow, ffn_grad, ffn_parts[3:4] = lax.optimization_barrier(
+        (narrow, ffn_grad, ffn_parts[3:4])
+    )
     gain_parts = jnp.zeros((1, 16, model_dim), jnp.bfloat16)
     gain_parts = gain_parts.at[0, 0].set(low(gain_one_grad)).at[0, 1].set(low(gain_two_grad))
     narrow_all, normed_cols, out_cols, gain_cols = gather_all(
@@ -930,8 +933,6 @@
             gain_parts,
         ),
     )
-    narrow_all, ffn_parts[:3] = lax.optimization_barrier((narrow_all, ffn_parts[:3]))
-    ffn_grad = place(None, 0, PIECES, ffn_parts[:3])
     narrow_all = narrow_all.reshape(every, 2 * HD + 2 * RANK)
     normed_cols = normed_cols.reshape(every, attn_rows)
     wout_grad = contract(out_cols.reshape(every, attn_rows), kept_all[:, :q_width], 0, 0)

time: 691 us -> 700 us (1.013)
  Pallas kernels: 425 us -> 433 us
    pallas_call x4, Pallas kernels: 299 us -> 311 us  [gather_all(): pl.pallas_call(functools.partial(gather_kernel, shards, widths, shared, l...]
  transfers between devices with their start and end apart: 15 -> 15, of which waited for: 0 -> 1; matrix products, arithmetic and copies ran while one was open for 32% -> 31% of each run, Pallas kernels for 46% -> 47%
where the time goes in v9:
time: 700 us; the launch traced here: 692 us
  Pallas kernels  433 us (62%)
  matrix products  189 us (27%)
  other arithmetic  20.6 us (3%)
  local copies, waits for them, and re-layouts  19.3 us (3%)
  between operations  15.4 us (2%)
  starting transfers between devices  11.8 us (2%)
    pallas_call x4, Pallas kernels, gather_all(): pl.pallas_call(functools.partial(gather_kernel, shards, widths, shared, l...  311 us
    dot_general x28, matrix products, contract(): lax.dot_general(left_op, right_op, (((left_dim,), (right_dim,)), ((), ())...  178 us
    pallas_call x1, Pallas kernels, product_sum(): pl.pallas_call(functools.partial(product_kernel, shards), out_shape=jax.S...  67.1 us
    pallas_call x1, Pallas kernels, scatter_sum(): pl.pallas_call(functools.partial(scatter_kernel, shards, widths), out_sha...  34.7 us
    pallas_call x2, Pallas kernels, place(): pl.pallas_call(functools.partial(place_kernel, kinds), grid=(kinds, tiles...  20.5 us
  transfers between devices with their start and end apart: 15, of which 1 were waited for; matrix products, arithmetic and copies ran while one was open for 31% of the time, Pallas kernels for 47%

profile of v9, /device:TPU:0, one launch (start us, length us, event | category | flops | bytes accessed | tf_op | source)
XLA Modules:
  0.0 692.1 jit_solution(4707810645730565321)
XLA Ops:
  9.7 109.2 %gather_1.1 = (bf16[1,16,128,4608]{3,2,1,0:T(8,128)(2,1)}, bf16[1,16,128,768]{3,2,1,0:T(8,128)(2,1)}, bf16[1,16,128,128]{3,2,1,0:T(8,128)(2,1)}) custom-call(bf16[1,128,4608]{2,1,0:T(8,128)(2,1)} %bitcast.189, bf16[1,128,768]{2,1,0:T(8,128)(2,1)} %bitcast.214, bf16[1,128,128]{2,1,0:T(8,128)(2,1)} %maximum_bitcast_fusion.refs_2_), custom_call_target="tpu_custom_call" | custom-call | bytes 583008256 | tf_op jit(solution)/shard_map/gather_1/pallas_call | solution.py:357
  119.2 1.2 slice.189
  120.9 0.9 convert_reduce_fusion
  121.8 1.3 copy.30
  124.8 5.7 fusion.3
  132.3 1.2 fusion.90
  134.2 34.9 %gather_2.1 = (bf16[2,16,64,256]{3,2,1,0:T(8,128)(2,1)}, bf16[2,16,64,256]{3,2,1,0:T(8,128)(2,1)}) custom-call(bf16[2,64,256]{2,1,0:T(8,128)(2,1)} %pad_maximum_fusion.6.refs_0_, bf16[2,64,256]{2,1,0:T(8,128)(2,1)} %bitcast.205), custom_call_target="tpu_custom_call" | custom-call | bytes 92274688 | tf_op jit(solution)/shard_map/gather_2/pallas_call | solution.py:357
  169.6 2.2 fusion.88
  171.7 2.1 fusion.102
  173.9 2.0 copy-done.14
  176.9 6.4 multiply_reduce_fusion.1
  183.3 0.9 copy-done.6
  184.2 1.0 multiply_convert_fusion.4
  185.1 63.0 %gather_3.1 = bf16[2,16,64,2048]{3,2,1,0:T(8,128)(2,1)} custom-call(bf16[2,64,2048]{2,1,0:T(8,128)(2,1)} %bitcast.180), custom_call_target="tpu_custom_call" | custom-call | bytes 243269632 | tf_op jit(solution)/shard_map/gather_3/pallas_call | solution.py:357
  248.2 0.9 pad_maximum_fusion
  249.3 14.6 %fusion.18 = f32[2048,1024]{1,0:T(8,128)} fusion(bf16[2048,2048]{1,0:T(8,128)(2,1)} %bitcast.157, bf16[1024,3,2048]{2,0,1:T(8,128)(2,1)} %param.17), kind=kOutput, calls=%fused_computation.25 | convolution fusion | flops 8589934592 | bytes 20971520 | tf_op jit(solution)/shard_map/dot_general | solution.py:51
  263.8 6.2 convolution_convert_fusion.8
  270.0 14.7 %fusion.23 = f32[2048,1024]{1,0:T(8,128)S(1)} fusion(bf16[2048,2048]{1,0:T(8,128)(2,1)S(1)} %bitcast.225, bf16[1024,3,2048]{2,0,1:T(8,128)(2,1)} %param.17), kind=kOutput, calls=%fused_computation.30 | convolution fusion | flops 8589934592 | bytes 20971520 | tf_op jit(solution)/shard_map/dot_general | solution.py:51
  284.7 4.5 convolution_add_fusion
  289.2 26.4 %multiply_convert_fusion = (bf16[2048,1024]{1,0:T(8,128)(2,1)}, bf16[2048,1024]{1,0:T(8,128)(2,1)}, bf16[2048,1024]{1,0:T(8,128)(2,1)}) fusion(f32[2048,1024]{1,0:T(8,128)} %fusion.18, f32[2048,1024]{1,0:T(8,128)} %convolution_add_fusion, bf16[2048,2048]{1,0:T(8,128)(2,1)} %bitcast.158, bf16[1024,3,2048]{2,0,1:T(8,128)(2,1)} %param.17), kind=kOutput, calls=%fused_computation.16 | convolution fusion | flops 8644460544 | bytes 41943040 | tf_op jit(solution)/shard_map/dot_general | solution.py:51
  315.6 8.8 %convolution_convert_fusion.6.refs_0_ = bf16[512,2048]{1,0:T(8,128)(2,1)S(1)} fusion(bf16[2048,2048]{1,0:T(8,128)(2,1)} %bitcast.159, bf16[2048,1024]{1,0:T(8,128)(2,1)} %get-tuple-element.96), kind=kOutput, calls=%fused_computation.48 | convolution fusion | flops 4296015872 | bytes 12582912 | tf_op jit(solution)/shard_map/dot_general | solution.py:51
  324.4 1.3 collective-permute-start
  325.7 9.4 %convolution_convert_fusion.5.refs_2_ = bf16[512,2048]{1,0:T(8,128)(2,1)} fusion(bf16[2048,2048]{1,0:T(8,128)(2,1)} %bitcast.160, bf16[2048,1024]{1,0:T(8,128)(2,1)S(1)} %copy-done.17), kind=kOutput, calls=%fused_computation.47 | convolution fusion | flops 4296015872 | bytes 12582912 | tf_op jit(solution)/shard_map/dot_general | solution.py:51
  335.1 0.9 collective-permute-start.1
  336.0 5.7 convolution_convert_fusion.4.refs_4_
  341.7 2.3 convolution_convert_fusion.7
  344.0 13.0 %convolution_convert_fusion = bf16[2048,2048]{1,0:T(8,128)(2,1)} fusion(bf16[2048,1024]{1,0:T(8,128)(2,1)S(1)} %copy-done.70, bf16[1024,3,2048]{2,0,1:T(8,128)(2,1)} %param.17), kind=kOutput, calls=%fused_computation.19 | convolution fusion | flops 8594128896 | bytes 16777216 | tf_op jit(solution)/shard_map/dot_general | solution.py:51
  357.0 67.1 %product_5.1 = bf16[2,64,2048]{2,1,0:T(8,128)(2,1)} custom-call(bf16[2,1024,1024]{2,1,0:T(8,128)(2,1)} %bitcast.169, bf16[2,1024,1024]{2,1,0:T(8,128)(2,1)} %bitcast.168, bf16[3,1024,2048]{2,1,0:T(8,128)(2,1)} %bitcast.155), custom_call_target="tpu_custom_call" | custom-call | bytes 243269632 | tf_op jit(solution)/shard_map/product_5/pallas_call | solution.py:686
  424.3 1.1 collective-permute-start.2
  425.4 4.8 convolution_convert_fusion.12
  430.2 9.1 %convolution_convert_fusion.1.refs_4_ = bf16[512,2048]{1,0:T(8,128)(2,1)S(1)} fusion(bf16[2048,2048]{1,0:T(8,128)(2,1)} %bitcast.223, bf16[2048,1024]{1,0:T(8,128)(2,1)S(1)} %copy-done.71), kind=kOutput, calls=%fused_computation.43 | convolution fusion | flops 4296015872 | bytes 12582912 | tf_op jit(solution)/shard_map/dot_general | solution.py:51
  439.4 5.8 convolution_convert_fusion.3.refs_0_
  445.2 5.9 convolution_convert_fusion.2.refs_2_
  451.2 1.0 fusion.57
  453.4 5.8 fusion.35
  459.2 1.3 reshape.506
  460.5 3.6 multiply_reduce_fusion
  466.8 0.9 copy.32
  467.7 2.0 multiply_convert_fusion.3
  469.7 2.1 convolution_convert_fusion.10
  472.5 1.0 fusion.68.refs_1_
  473.5 1.3 collective-permute-start.3
  475.5 1.3 collective-permute-start.6
  477.5 34.7 %scatter_6.1 = (bf16[2,64,256]{2,1,0:T(8,128)(2,1)}, bf16[2,64,256]{2,1,0:T(8,128)(2,1)}, bf16[2,64,256]{2,1,0:T(8,128)(2,1)}) custom-call(bf16[2,16,64,256]{3,2,1,0:T(8,128)(2,1)} %bitcast.191, bf16[2,16,64,256]{3,2,1,0:T(8,128)(2,1)} %bitcast.192, bf16[2,16,64,256]{3,2,1,0:T(8,128)(2,1)} %bitcast.190), custom_call_target="tpu_custom_call" | custom-call | bytes 117440512 | tf_op jit(solution)/shard_map/scatter_6/pallas_call | solution.py:540
  512.2 0.9 bitcast_convert_fusion
  514.6 1.5 constant_dynamic-update-slice_fusion.1
  516.2 6.5 fusion.1
  522.7 3.3 fusion.65
  526.9 1.6 copy-done.5
  528.6 11.5 %place_0.1.refs_6_ = f32[3,1024,2048]{2,1,0:T(8,128)} custom-call(bf16[512,2048]{1,0:T(8,128)(2,1)S(1)} %copy-done.5, bf16[512,2048]{1,0:T(8,128)(2,1)} %collective-permute-done.refs_1_, bf16[512,2048]{1,0:T(8,128)(2,1)} %convolution_convert_fusion.5.refs_2_, bf16[512,2048]{1,0:T(8,128)(2,1)} %collective-permute-done.1.refs_3_, ...), custom_call_target="tpu_custom_call" | custom-call | flops 3145728 | bytes 25165824 | tf_op jit(solution)/shard_map/place_0/pallas_call | solution.py:114
  540.2 1.4 fusion.60
  541.6 103.6 %gather_4.1 = (bf16[2,16,64,1024]{3,2,1,0:T(8,128)(2,1)}, bf16[2,16,64,128]{3,2,1,0:T(8,128)(2,1)}, bf16[2,16,64,128]{3,2,1,0:T(8,128)(2,1)}, bf16[1,16,16,128]{3,2,1,0:T(8,128)(2,1)}) custom-call(bf16[2,64,1024]{2,1,0:T(8,128)(2,1)} %bitcast.200, bf16[2,64,2048]{2,1,0:T(8,128)(2,1)} %fusion.68.refs_1_, bf16[2,64,2048]{2,1,0:T(8,128)(2,1)} %bitcast.179, ...), custom_call_target="tpu_custom_call" | custom-call | bytes 142606336 | tf_op jit(solution)/shard_map/gather_4/pallas_call | solution.py:357
  646.1 5.0 fusion.38
  651.0 2.1 collective-permute-start.8
  653.7 1.4 convolution_convert_fusion.13
  655.7 3.0 fusion.41
  658.7 1.8 convolution_convert_fusion.14
  660.6 4.8 convolution_convert_fusion.9
  665.4 1.9 collective-permute-start.10
  667.4 1.2 add_dynamic-update-slice_fusion.1
  668.6 9.1 %place_1.1 = f32[3,1024,2048]{2,1,0:T(8,128)} custom-call(bf16[512,2048]{1,0:T(8,128)(2,1)S(1)} %copy-done.2, bf16[512,2048]{1,0:T(8,128)(2,1)} %collective-permute-done.3.refs_1_, bf16[512,2048]{1,0:T(8,128)(2,1)S(1)} %copy-done.3, bf16[512,2048]{1,0:T(8,128)(2,1)} %collective-permute-done.5.refs_3_, ...), custom_call_target="tpu_custom_call", output_to_operand_aliasing={{}: (6, {})} | custom-call | flops 3145728 | bytes 25165824 | tf_op jit(solution)/shard_map/place_1/pallas_call | solution.py:114
  677.6 2.1 convert_add_fusion.1
  680.6 3.0 collective-permute-done.10
  683.8 1.4 copy-done.23
  (236 shorter events, 20.7 us)
Async XLA Ops:
  7.2 277.6 %copy-start = (bf16[1024,256]{1,0:T(8,128)(2,1)S(1)}, bf16[1024,256]{1,0:T(8,128)(2,1)}, u32[]{:S(2)}) copy-start(bf16[1024,256]{1,0:T(8,128)(2,1)} %param.18) | copy-start | bytes 1572868
  7.2 115.9 %copy-start.9 = (bf16[2,64,2048]{2,1,0:T(8,128)(2,1)S(1)}, bf16[2,64,2048]{2,1,0:T(8,128)(2,1)}, u32[]{:S(2)}) copy-start(bf16[2,64,2048]{2,1,0:T(8,128)(2,1)} %param.12) | copy-start | bytes 1572868
  7.2 256.6 %all-gather.4.cloned.1.call-start = ((), (), s32[]{:S(2)}) async-start(), calls=%async_computation.1 | async-start | bytes 8912896 | tf_op jit(solution)/shard_map/all_gather | solution.py:73
  119.0 238.0 %all-gather.6.cloned.1.call-start = ((), (), s32[]{:S(2)}) async-start(), calls=%async_computation.2 | async-start | bytes 10027008 | tf_op jit(solution)/shard_map/all_gather | solution.py:73
  124.6 5.9 copy-start.55
  124.6 58.7 %copy-start.42 = (f32[2048,1]{0,1:T(1,128)}, f32[2048,1]{0,1:T(1,128)S(1)}, u32[]{:S(2)}) copy-start(f32[2048,1]{0,1:T(1,128)S(1)} %get-tuple-element.146) | copy-start | bytes 24580
  124.8 6.4 copy-start.21
  130.5 38.7 %copy-start.60 = (s32[2,64]{1,0:T(2,128)S(1)}, s32[2,64]{1,0:T(2,128)}, u32[]{:S(2)}) copy-start(s32[2,64]{1,0:T(2,128)} %param.13) | copy-start | bytes 1540
  183.2 64.9 %copy-start.68 = (f32[128]{0:T(128)}, f32[128]{0:T(128)S(1)}, u32[]{:S(2)}) copy-start(f32[128]{0:T(128)S(1)} %get-tuple-element.158) | copy-start | bytes 1540
  183.2 64.9 %copy-start.48 = (f32[128]{0:T(128)}, f32[128]{0:T(128)S(1)}, u32[]{:S(2)}) copy-start(f32[128]{0:T(128)S(1)} %fusion.93) | copy-start | bytes 1540
  249.0 406.7 %reduce-scatter.2.cloned.1.call-start = ((), (), s32[]{:S(2)}) async-start(), calls=%async_computation.3 | async-start | bytes 8912896 | tf_op jit(solution)/shard_map/reduce_scatter | solution.py:77
  263.8 6.2 copy-start.46
  270.0 14.7 %copy-start.27 = (bf16[2048,256]{1,0:T(8,128)(2,1)}, bf16[2048,256]{1,0:T(8,128)(2,1)S(1)}, u32[]{:S(2)}) copy-start(bf16[2048,256]{1,0:T(8,128)(2,1)S(1)} %convolution_convert_fusion.8) | copy-start | bytes 3145732
  315.6 10.1 %copy-start.17 = (bf16[2048,1024]{1,0:T(8,128)(2,1)S(1)}, bf16[2048,1024]{1,0:T(8,128)(2,1)}, u32[]{:S(2)}) copy-start(bf16[2048,1024]{1,0:T(8,128)(2,1)} %get-tuple-element.97) | copy-start | bytes 12582916
  315.6 20.4 %slice-start.2 = ((s8[8388608]{0:T(1024)(128)(4,1)}), s8[4194304]{0:T(1024)(128)(4,1)S(1)}, s32[]{:S(2)}) async-start(s8[8388608]{0:T(1024)(128)(4,1)} %bitcast.226), calls=%async_computation.7 | async-start | bytes 8388608
  324.4 10.7 %copy-start.4 = (bf16[512,2048]{1,0:T(8,128)(2,1)}, bf16[512,2048]{1,0:T(8,128)(2,1)S(1)}, u32[]{:S(2)}) copy-start(bf16[512,2048]{1,0:T(8,128)(2,1)S(1)} %convolution_convert_fusion.6.refs_0_) | copy-start | bytes 6291460
  324.4 99.7 %collective-permute-start = (bf16[512,2048]{1,0:T(8,128)(2,1)S(1)}, bf16[512,2048]{1,0:T(8,128)(2,1)}, u32[]{:S(2)}, u32[]{:S(2)}) collective-permute-start(bf16[512,2048]{1,0:T(8,128)(2,1)S(1)} %convolution_convert_fusion.6.refs_0_), channel_id=1, source_target_pairs={{0,16},{16,0},{1,17},{17,1},{2,18},{18,2},{3,19},{19,3},{4,20},{20... | collective-permute-start | bytes 6291464 | tf_op jit(solution)/shard_map/ppermute | solution.py:128
  325.7 10.3 %slice-start.3 = ((s8[8388608]{0:T(1024)(128)(4,1)}), s8[4194304]{0:T(1024)(128)(4,1)S(1)}, s32[]{:S(2)}) async-start(s8[8388608]{0:T(1024)(128)(4,1)} %bitcast.226), calls=%async_computation.8 | async-start | bytes 8388608
  325.7 10.3 %copy-start.70 = (bf16[2048,1024]{1,0:T(8,128)(2,1)S(1)}, bf16[2048,1024]{1,0:T(8,128)(2,1)}, u32[]{:S(2)}) copy-start(bf16[2048,1024]{1,0:T(8,128)(2,1)} %get-tuple-element.95) | copy-start | bytes 12582916
  335.1 89.0 %collective-permute-start.1 = (bf16[512,2048]{1,0:T(8,128)(2,1)}, bf16[512,2048]{1,0:T(8,128)(2,1)}, u32[]{:S(2)}, u32[]{:S(2)}) collective-permute-start(bf16[512,2048]{1,0:T(8,128)(2,1)} %convolution_convert_fusion.5.refs_2_), channel_id=1, source_target_pairs={{0,16},{16,0},{1,17},{17,1},{2,18},{18,2},{3,19},{19,3},{4,20},{20... | collective-permute-start | bytes 6291464 | tf_op jit(solution)/shard_map/ppermute | solution.py:128
  424.2 234.5 %all-gather.8.cloned.1.call-start = ((), (), s32[]{:S(2)}) async-start(), calls=%async_computation.4 | async-start | bytes 8912896 | tf_op jit(solution)/shard_map/all_gather | solution.py:73
  424.2 6.0 copy-start.71
  424.3 47.6 %collective-permute-start.2 = (bf16[512,2048]{1,0:T(8,128)(2,1)}, bf16[512,2048]{1,0:T(8,128)(2,1)}, u32[]{:S(2)}, u32[]{:S(2)}) collective-permute-start(bf16[512,2048]{1,0:T(8,128)(2,1)} %convolution_convert_fusion.4.refs_4_), channel_id=1, source_target_pairs={{0,16},{16,0},{1,17},{17,1},{2,18},{18,2},{3,19},{19,3},{4,20},{20... | collective-permute-start | bytes 6291464 | tf_op jit(solution)/shard_map/ppermute | solution.py:128
  425.4 14.0 %slice-start = ((s8[8388608]{0:T(1024)(128)(4,1)}), s8[4194304]{0:T(1024)(128)(4,1)S(1)}, s32[]{:S(2)}) async-start(s8[8388608]{0:T(1024)(128)(4,1)} %bitcast.161), calls=%async_computation.5 | async-start | bytes 8388608
  430.2 9.2 %slice-start.1 = ((s8[8388608]{0:T(1024)(128)(4,1)}), s8[4194304]{0:T(1024)(128)(4,1)S(1)}, s32[]{:S(2)}) async-start(s8[8388608]{0:T(1024)(128)(4,1)} %bitcast.161), calls=%async_computation.6 | async-start | bytes 8388608
  430.2 9.2 %copy-start.19 = (bf16[2048,1024]{1,0:T(8,128)(2,1)S(1)}, bf16[2048,1024]{1,0:T(8,128)(2,1)}, u32[]{:S(2)}) copy-start(bf16[2048,1024]{1,0:T(8,128)(2,1)} %get-tuple-element.96) | copy-start | bytes 12582916
  445.1 6.0 copy-start.7
  445.1 6.0 copy-start.11
  445.2 6.0 copy-start.43
  445.2 6.0 copy-start.49
  445.2 7.0 %copy-start.69 = (f32[128]{0:T(128)S(1)}, f32[128]{0:T(128)}, u32[]{:S(2)}) copy-start(f32[128]{0:T(128)} %copy-done.68) | copy-start | bytes 1540
  445.2 7.0 %copy-start.12 = (bf16[2,64,2048]{2,1,0:T(8,128)(2,1)S(1)}, bf16[2,64,2048]{2,1,0:T(8,128)(2,1)}, u32[]{:S(2)}) copy-start(bf16[2,64,2048]{2,1,0:T(8,128)(2,1)} %param.19) | copy-start | bytes 1572868
  452.2 7.0 %copy-start.62 = (f32[128]{0:T(128)}, f32[128]{0:T(128)S(1)}, u32[]{:S(2)}) copy-start(f32[128]{0:T(128)S(1)} %multiply_multiply_fusion.4) | copy-start | bytes 1540
  453.4 7.1 %copy-start.59 = (f32[2,512]{1,0:T(2,128)S(1)}, f32[2,512]{1,0:T(2,128)}, u32[]{:S(2)}) copy-start(f32[2,512]{1,0:T(2,128)} %copy-done.58) | copy-start | bytes 12292
  471.9 41.2 %copy-start.52 = (f32[128]{0:T(128)S(1)}, f32[128]{0:T(128)}, u32[]{:S(2)}) copy-start(f32[128]{0:T(128)} %copy-done.51) | copy-start | bytes 1540
  471.9 41.2 %copy-start.54 = (f32[128]{0:T(128)S(1)}, f32[128]{0:T(128)}, u32[]{:S(2)}) copy-start(f32[128]{0:T(128)} %copy-done.53) | copy-start | bytes 1540
  472.5 42.2 %copy-start.25 = (bf16[16,8,8,256]{3,1,2,0:T(8,128)(2,1)S(1)}, bf16[16,8,8,256]{3,1,2,0:T(8,128)(2,1)}, u32[]{:S(2)}) copy-start(bf16[16,8,8,256]{3,1,2,0:T(8,128)(2,1)} %copy.32) | copy-start | bytes 1572868
  473.5 68.1 %collective-permute-start.3 = (bf16[512,2048]{1,0:T(8,128)(2,1)}, bf16[512,2048]{1,0:T(8,128)(2,1)}, u32[]{:S(2)}, u32[]{:S(2)}) collective-permute-start(bf16[512,2048]{1,0:T(8,128)(2,1)} %convolution_convert_fusion.3.refs_0_), channel_id=1, source_target_pairs={{0,16},{16,0},{1,17},{17,1},{2,18},{18,2},{3,19},{19,3},{4,20},{20... | collective-permute-start | bytes 6291464 | tf_op jit(solution)/shard_map/ppermute | solution.py:128
  474.8 192.5 %collective-permute-start.5 = (bf16[512,2048]{1,0:T(8,128)(2,1)}, bf16[512,2048]{1,0:T(8,128)(2,1)}, u32[]{:S(2)}, u32[]{:S(2)}) collective-permute-start(bf16[512,2048]{1,0:T(8,128)(2,1)} %convolution_convert_fusion.2.refs_2_), channel_id=1, source_target_pairs={{0,16},{16,0},{1,17},{17,1},{2,18},{18,2},{3,19},{19,3},{4,20},{20... | collective-permute-start | bytes 6291464 | tf_op jit(solution)/shard_map/ppermute | solution.py:128
  475.5 191.8 %collective-permute-start.6 = (bf16[512,2048]{1,0:T(8,128)(2,1)S(1)}, bf16[512,2048]{1,0:T(8,128)(2,1)}, u32[]{:S(2)}, u32[]{:S(2)}) collective-permute-start(bf16[512,2048]{1,0:T(8,128)(2,1)S(1)} %convolution_convert_fusion.1.refs_4_), channel_id=1, source_target_pairs={{0,16},{16,0},{1,17},{17,1},{2,18},{18,2},{3,19},{19,3},{4,20},{20... | collective-permute-start | bytes 6291464 | tf_op jit(solution)/shard_map/ppermute | solution.py:128
  476.8 188.6 %collective-permute-start.7 = (bf16[1024,256]{1,0:T(8,128)(2,1)}, bf16[1024,256]{1,0:T(8,128)(2,1)}, u32[]{:S(2)}, u32[]{:S(2)}) collective-permute-start(bf16[1024,256]{1,0:T(8,128)(2,1)} %convolution_convert_fusion.12), channel_id=1, source_target_pairs={{0,16},{16,0},{1,17},{17,1},{2,18},{18,2},{3,19},{19,3},{4,20},{20... | collective-permute-start | bytes 1572872 | tf_op jit(solution)/shard_map/ppermute | solution.py:128
  516.2 6.5 copy-start.56
  516.2 9.9 %copy-start.47 = (bf16[2048]{0:T(1024)(128)(2,1)S(1)}, bf16[2048]{0:T(1024)(128)(2,1)}, u32[]{:S(2)}) copy-start(bf16[2048]{0:T(1024)(128)(2,1)} %get-tuple-element.129) | copy-start | bytes 12292
  528.5 11.6 %copy-start.41 = (bf16[1,16,2048]{2,1,0:T(8,128)(2,1)}, bf16[1,16,2048]{2,1,0:T(8,128)(2,1)S(1)}, u32[]{:S(2)}) copy-start(bf16[1,16,2048]{2,1,0:T(8,128)(2,1)S(1)} %scatter.9.refs_3_) | copy-start | bytes 196612
  528.5 11.6 %copy-start.38 = (bf16[2,64,256]{2,1,0:T(8,128)(2,1)S(1)}, bf16[2,64,256]{2,1,0:T(8,128)(2,1)}, u32[]{:S(2)}) copy-start(bf16[2,64,256]{2,1,0:T(8,128)(2,1)} %get-tuple-element.102) | copy-start | bytes 196612
  528.5 11.6 %copy-start.64 = (f32[128]{0:T(128)S(1)}, f32[128]{0:T(128)}, u32[]{:S(2)}) copy-start(f32[128]{0:T(128)} %get-tuple-element.132) | copy-start | bytes 1540
  528.5 11.6 %copy-start.67 = (f32[128]{0:T(128)S(1)}, f32[128]{0:T(128)}, u32[]{:S(2)}) copy-start(f32[128]{0:T(128)} %copy-done.66) | copy-start | bytes 1540
  528.5 11.6 %copy-start.8 = (f32[128,2048]{1,0:T(8,128)S(1)}, f32[128,2048]{1,0:T(8,128)}, u32[]{:S(2)}) copy-start(f32[128,2048]{1,0:T(8,128)} %copy-done.6) | copy-start | bytes 3145732
  528.5 11.6 %copy-start.13 = (bf16[2,64,2048]{2,1,0:T(8,128)(2,1)S(1)}, bf16[2,64,2048]{2,1,0:T(8,128)(2,1)}, u32[]{:S(2)}) copy-start(bf16[2,64,2048]{2,1,0:T(8,128)(2,1)} %param.19) | copy-start | bytes 1572868
  528.5 11.6 %copy-start.16 = (f32[128,2048]{1,0:T(8,128)S(1)}, f32[128,2048]{1,0:T(8,128)}, u32[]{:S(2)}) copy-start(f32[128,2048]{1,0:T(8,128)} %get-tuple-element.162) | copy-start | bytes 3145732
  528.5 11.6 %copy-start.50 = (f32[128]{0:T(128)S(1)}, f32[128]{0:T(128)}, u32[]{:S(2)}) copy-start(f32[128]{0:T(128)} %copy-done.48) | copy-start | bytes 1540
  528.5 11.6 %copy-start.57 = (f32[128]{0:T(128)S(1)}, f32[128]{0:T(128)}, u32[]{:S(2)}) copy-start(f32[128]{0:T(128)} %copy-done.55) | copy-start | bytes 1540
  528.5 11.6 %copy-start.63 = (f32[128]{0:T(128)S(1)}, f32[128]{0:T(128)}, u32[]{:S(2)}) copy-start(f32[128]{0:T(128)} %copy-done.62) | copy-start | bytes 1540
  646.0 9.2 %collective-permute-start.4 = (bf16[2,128]{1,0:T(2,128)(2,1)S(1)}, bf16[2,128]{1,0:T(2,128)(2,1)S(1)}, u32[]{:S(2)}, u32[]{:S(2)}) collective-permute-start(bf16[2,128]{1,0:T(2,128)(2,1)S(1)} %slice_reduce_fusion), channel_id=1, source_target_pairs={{0,16},{16,0},{1,17},{17,1},{2,18},{18,2},{3,19},{19,3},{4,20},{20... | collective-permute-start | bytes 1544 | tf_op jit(solution)/shard_map/ppermute | solution.py:128
  646.0 7.1 %copy-start.26 = (bf16[2,16,64,128]{3,2,1,0:T(8,128)(2,1)S(1)}, bf16[2,16,64,128]{3,2,1,0:T(8,128)(2,1)}, u32[]{:S(2)}) copy-start(bf16[2,16,64,128]{3,2,1,0:T(8,128)(2,1)} %get-tuple-element.110) | copy-start | bytes 1572868
  646.0 7.1 %copy-start.37 = (bf16[2,16,64,1024]{3,2,1,0:T(8,128)(2,1)S(1)}, bf16[2,16,64,1024]{3,2,1,0:T(8,128)(2,1)}, u32[]{:S(2)}) copy-start(bf16[2,16,64,1024]{3,2,1,0:T(8,128)(2,1)} %get-tuple-element.111) | copy-start | bytes 12582916
  651.0 16.3 %collective-permute-start.8 = (bf16[128,2048]{1,0:T(8,128)(2,1)S(1)}, bf16[128,2048]{1,0:T(8,128)(2,1)}, u32[]{:S(2)}, u32[]{:S(2)}) collective-permute-start(bf16[128,2048]{1,0:T(8,128)(2,1)S(1)} %fusion.38), channel_id=1, source_target_pairs={{0,16},{16,0},{1,17},{17,1},{2,18},{18,2},{3,19},{19,3},{4,20},{20... | collective-permute-start | bytes 1572872 | tf_op jit(solution)/shard_map/ppermute | solution.py:128
  660.5 6.9 copy-start.22
  660.5 8.0 %copy-start.2 = (bf16[512,2048]{1,0:T(8,128)(2,1)S(1)}, bf16[512,2048]{1,0:T(8,128)(2,1)}, u32[]{:S(2)}) copy-start(bf16[512,2048]{1,0:T(8,128)(2,1)} %convolution_convert_fusion.3.refs_0_) | copy-start | bytes 6291460
  660.5 8.0 %copy-start.3 = (bf16[512,2048]{1,0:T(8,128)(2,1)S(1)}, bf16[512,2048]{1,0:T(8,128)(2,1)}, u32[]{:S(2)}) copy-start(bf16[512,2048]{1,0:T(8,128)(2,1)} %convolution_convert_fusion.2.refs_2_) | copy-start | bytes 6291460
  660.5 19.3 %collective-permute-start.9 = (bf16[128,1280]{1,0:T(8,128)(2,1)S(1)}, bf16[128,1280]{1,0:T(8,128)(2,1)S(1)}, u32[]{:S(2)}, u32[]{:S(2)}) collective-permute-start(bf16[128,1280]{1,0:T(8,128)(2,1)S(1)} %pad_maximum_fusion.5), channel_id=1, source_target_pairs={{0,16},{16,0},{1,17},{17,1},{2,18},{18,2},{3,19},{19,3},{4,20},{20... | collective-permute-start | bytes 983048 | tf_op jit(solution)/shard_map/ppermute | solution.py:128
  665.4 18.2 %collective-permute-start.10 = (bf16[128,2048]{1,0:T(8,128)(2,1)S(1)}, bf16[128,2048]{1,0:T(8,128)(2,1)S(1)}, u32[]{:S(2)}, u32[]{:S(2)}) collective-permute-start(bf16[128,2048]{1,0:T(8,128)(2,1)S(1)} %convolution_convert_fusion.9), channel_id=1, source_target_pairs={{0,16},{16,0},{1,17},{17,1},{2,18},{18,2},{3,19},{19,3},{4,20},{20... | collective-permute-start | bytes 1572872 | tf_op jit(solution)/shard_map/ppermute | solution.py:128
  668.5 9.1 %copy-start.35 = (bf16[1024,256]{1,0:T(8,128)(2,1)S(1)}, bf16[1024,256]{1,0:T(8,128)(2,1)}, u32[]{:S(2)}) copy-start(bf16[1024,256]{1,0:T(8,128)(2,1)} %convolution_convert_fusion.12) | copy-start | bytes 1572868
  668.6 16.6 %copy-start.1 = (bf16[1024,256]{1,0:T(8,128)(2,1)S(1)}, bf16[1024,256]{1,0:T(8,128)(2,1)}, u32[]{:S(2)}) copy-start(bf16[1024,256]{1,0:T(8,128)(2,1)} %param.18) | copy-start | bytes 1572868
  (27 other events, 67.2 us)
Sparse Core Ops, SparseCore 0:
  119.1 77.1 all-gather.3
  249.2 78.8 all-gather.5
  424.3 112.8 reduce-scatter.1
  539.2 98.8 all-gather.7
